TPU v7x, 128 devices: a whole 4x4x4 slice. The times are simulated.
128 devices in a mesh: pipe: 2 (over core), space: 64 (over x, z, y).
Axes of the slice: x: 4, y: 4, z: 4, core: 2. Of those that a mesh axis runs over, the one named last changes fastest.
Arguments:
- saved_inputs: bfloat16 [2, 4, 16384, 512], P('pipe', None, 'space'), may hold values from -50 to 50
- project_in: bfloat16 [2, 512, 1536], P('pipe'), may hold values from -1.5 to 1.5
- project_out: bfloat16 [2, 512, 512], P('pipe'), may hold values from -0.25 to 0.25
- norm_gains: float32 [2, 512], P('pipe'), may hold values from 0.5 to 1.5
- neighbour_blocks: int32 [2, 4, 64, 2], P('pipe', None, 'space'), may hold values from 0 to 127, as said below
- cotangent: bfloat16 [4, 16384, 512], P(None, 'space'), may hold values from -6 to 6
Outputs:
- input_grads: bfloat16 [2, 4, 16384, 512], P('pipe', None, 'space')
Inputs may be any that keep to these rules, and one draw needn't show every extreme that they name: `neighbour_blocks`: entry e of patch p names block q * 2 + r of patch q, with q != p and |q - p| <= 2; a distance of 2 occurs; entries of one patch may repeat.
All inputs are finite; a program needn't handle non-finite values.
Results may differ from a plain program's by a relative error of at most 0.014.
Values may be sent and summed in bfloat16 or wider, within the bound.
A program may use at most 128 MiB of HBM per device.

v0:
```python
import jax
import jax.numpy as jnp
from jax import lax
from jax.sharding import PartitionSpec as P

HEADS = 32
HD = 16
BLK = 128
REACH = 2


epsilon = 1e-05


def shifted(x, axis, by):
    peers = lax.axis_size(axis)
    pairs = [(i, i + by) for i in range(peers) if 0 <= i + by < peers]
    return lax.ppermute(x, axis, pairs)


def normalize(points, gain_row):
    values = points.astype(jnp.float32)
    centre = jnp.mean(values, axis=-1, keepdims=True)
    spread = jnp.mean(jnp.square(values - centre), axis=-1, keepdims=True)
    inverse = lax.rsqrt(spread + epsilon)
    scaled = (values - centre) * inverse
    return (scaled, inverse, (scaled * gain_row).astype(jnp.bfloat16))


def norm_backward(grad_normed, scaled, inverse, gain_row):
    weighted = grad_normed * gain_row
    return inverse * (
        weighted
        - jnp.mean(weighted, axis=-1, keepdims=True)
        - scaled * jnp.mean(weighted * scaled, axis=-1, keepdims=True)
    )


def attend_backward(queries, key_rows, value_rows, grad_attn):
    group_heads = min(HEADS, max(1, 128 // HD))
    group_width = group_heads * HD
    factor = HD ** (-0.5)
    row_count = queries.shape[0]
    key_count = key_rows.shape[0]
    grad_query, grad_key, grad_value = ([], [], [])
    for column in range(0, queries.shape[1], group_width):
        query_group = queries[:, column : column + group_width].reshape(row_count, group_heads, HD)
        key_group = key_rows[:, column : column + group_width].reshape(key_count, group_heads, HD)
        value_group = value_rows[:, column : column + group_width].reshape(
            key_count, group_heads, HD
        )
        grad_group = grad_attn[:, column : column + group_width].reshape(row_count, group_heads, HD)
        scores = (
            jnp.einsum("qhd,khd->hqk", query_group, key_group, preferred_element_type=jnp.float32)
            * factor
        )
        attention = jax.nn.softmax(scores, axis=-1)
        grad_probs = jnp.einsum(
            "qhd,khd->hqk", grad_group, value_group, preferred_element_type=jnp.float32
        )
        grad_scores = (
            attention
            * (grad_probs - jnp.sum(attention * grad_probs, axis=-1, keepdims=True))
            * factor
        ).astype(jnp.bfloat16)
        grad_query.append(
            jnp.einsum(
                "hqk,khd->qhd", grad_scores, key_group, preferred_element_type=jnp.float32
            ).reshape(row_count, group_width)
        )
        grad_key.append(
            jnp.einsum(
                "hqk,qhd->khd", grad_scores, query_group, preferred_element_type=jnp.float32
            ).reshape(key_count, group_width)
        )
        grad_value.append(
            jnp.einsum(
                "hqk,qhd->khd",
                attention.astype(jnp.bfloat16),
                grad_group,
                preferred_element_type=jnp.float32,
            ).reshape(key_count, group_width)
        )
    return (
        jnp.concatenate(grad_query, 1),
        jnp.concatenate(grad_key, 1),
        jnp.concatenate(grad_value, 1),
    )


def shards(saved_inputs, project_in, project_out, norm_gains, neighbour_blocks, cotangent):
    sections = lax.axis_size("pipe")
    segment_index = lax.axis_index("pipe")
    myself = lax.axis_index("space")
    micro_count = cotangent.shape[0]
    points = cotangent.shape[1]
    model_width = cotangent.shape[2]
    weight_in = project_in[0]
    weight_out = project_out[0]
    gain_row = norm_gains[0]
    block_count = points // BLK
    offsets = [shift_by for shift_by in range(-REACH, REACH + 1) if shift_by != 0]
    local_lists = neighbour_blocks[0, :, 0, :]

    def step(step_index, state_pair):
        incoming, collected = state_pair
        micro_index = step_index - (sections - 1 - segment_index)
        active = (micro_index >= 0) & (micro_index < micro_count)
        chosen = jnp.clip(micro_index, 0, micro_count - 1)
        grad_out = jnp.where(
            segment_index == sections - 1,
            lax.dynamic_index_in_dim(cotangent, chosen, 0, keepdims=False),
            incoming,
        )
        points_in = lax.dynamic_index_in_dim(saved_inputs[0], chosen, 0, keepdims=False)
        block_ids = lax.dynamic_index_in_dim(local_lists, chosen, 0, keepdims=False)
        owners = block_ids // block_count
        within = block_ids % block_count
        distance = owners - myself
        scaled, inverse, normed = normalize(points_in, gain_row)
        projected = jnp.dot(normed, weight_in, preferred_element_type=jnp.float32).astype(
            jnp.bfloat16
        )
        queries = projected[:, :model_width]
        own_pairs = projected[:, model_width:]
        grad_attn = jnp.dot(grad_out, weight_out.T, preferred_element_type=jnp.float32).astype(
            jnp.bfloat16
        )
        received = []
        for shift_by in offsets:
            received.append(shifted(own_pairs, "space", -shift_by))
        window_blocks = jnp.stack(received).reshape(
            len(offsets) * block_count, BLK, 2 * model_width
        )
        position = (
            jnp.where(distance < 0, distance + REACH, distance + REACH - 1) * block_count + within
        )
        fetched = jnp.take(window_blocks, position, axis=0)
        combined = jnp.concatenate([own_pairs, fetched.reshape(-1, 2 * model_width)], 0)
        grad_query, grad_key, grad_value = attend_backward(
            queries, combined[:, :model_width], combined[:, model_width:], grad_attn
        )
        grad_pairs = jnp.concatenate([grad_key, grad_value], 1)
        grad_own = grad_pairs[:points]
        grad_remote = grad_pairs[points:].reshape(-1, BLK, 2 * model_width)
        window_grads = (
            jnp.zeros((len(offsets) * block_count, BLK, 2 * model_width), jnp.float32)
            .at[position]
            .add(grad_remote)
        )
        window_grads = window_grads.reshape(len(offsets), points, 2 * model_width)
        for slot_index, shift_by in enumerate(offsets):
            grad_own = grad_own + shifted(window_grads[slot_index], "space", shift_by)
        grad_project = jnp.concatenate([grad_query, grad_own], 1).astype(jnp.bfloat16)
        grad_normed = jnp.dot(grad_project, weight_in.T, preferred_element_type=jnp.float32)
        result = (
            grad_out.astype(jnp.float32) + norm_backward(grad_normed, scaled, inverse, gain_row)
        ).astype(jnp.bfloat16)
        collected = jnp.where(
            active, lax.dynamic_update_index_in_dim(collected, result, chosen, 0), collected
        )
        passed = shifted(result, "pipe", -1)
        return (passed, collected)

    start_state = (
        jnp.zeros((points, model_width), jnp.bfloat16),
        jnp.zeros((micro_count, points, model_width), jnp.bfloat16),
    )
    final_state = lax.fori_loop(0, micro_count + sections - 1, step, start_state)
    return final_state[1][None]


def solution(mesh):
    return jax.shard_map(
        shards,
        mesh=mesh,
        in_specs=(
            P("pipe", None, "space", None),
            P("pipe", None, None),
            P("pipe", None, None),
            P("pipe", None),
            P("pipe", None, "space", None),
            P(None, "space", None),
        ),
        out_specs=P("pipe", None, "space", None),
        check_vma=False,
    )
```

profile of v0, /device:TPU:15, one launch (start us, length us, event | category | flops | bytes accessed | tf_op | source)
XLA Modules:
  0.0 1470.6 jit_solution(11146871088003046813)
XLA Ops:
  2.4 1467.1 %while.20 = (s32[]{:T(128)}, bf16[256,512]{1,0:T(8,128)(2,1)S(1)}, bf16[4,256,512]{2,1,0:T(8,128)(2,1)}, pred[]{:T(512)}, s32[]{:T(128)}, /*index=5*/bf16[4,256,...) while((s32[]{:T(128)}, bf16[256,512]{1,0:T(8,128)(2,1)S(1)}, ...), condition=%wide.region_18.19_spmd, body=%wide.region_0.18_spmd.sunk | while | flops 1844741504 | bytes 218177424 | solution.py:169
  37.9 9.2 collective-permute-done
  57.5 17.8 %fusion.403 = bf16[8,16,256]{2,1,0:T(8,128)(2,1)} fusion(bf16[512,8,16]{0,2,1:T(8,128)(2,1)S(1)} %bitcast.413, f32[8,256,512]{2,1,0:T(8,128)} %fusion.400, f32[8,256,512]{2,1,0:T(8,128)} %get-tuple-element.604, f32[8,256]{1,0:T(8,128)S(1)} %get-tuple-element.605), kind=kOutput, calls=%fused_computation.87.clone.1 | convolution fusion | flops 40929792 | bytes 8593408 | tf_op jit(solution)/shard_map/while/body/eval_jaxpr/hqk,khd->qhd/dot_general | solution.py:67
  75.3 16.6 %fusion.413 = f32[8,16,512]{2,1,0:T(8,128)S(1)} fusion(bf16[256,8,16]{0,2,1:T(8,128)(2,1)S(1)} %bitcast.426, f32[8,256,512]{2,1,0:T(8,128)} %fusion.400, f32[8,256,512]{2,1,0:T(8,128)} %get-tuple-element.604, f32[8,256]{1,0:T(8,128)S(1)} %get-tuple-element.605), kind=kOutput, calls=%fused_computation.35.clone.1 | convolution fusion | flops 40897024 | bytes 8724480 | tf_op jit(solution)/shard_map/while/body/eval_jaxpr/hqk,qhd->khd/dot_general | solution.py:72
  117.7 16.6 %fusion.416 = f32[8,16,512]{2,1,0:T(8,128)S(1)} fusion(bf16[256,8,16]{0,2,1:T(8,128)(2,1)S(1)} %bitcast.424, f32[8,256,512]{2,1,0:T(8,128)} %fusion.410, f32[8,256,512]{2,1,0:T(8,128)} %get-tuple-element.622, f32[8,256]{1,0:T(8,128)S(1)} %get-tuple-element.623), kind=kOutput, calls=%fused_computation.41.clone.1 | convolution fusion | flops 40897024 | bytes 8724480 | tf_op jit(solution)/shard_map/while/body/eval_jaxpr/hqk,qhd->khd/dot_general | solution.py:72
  134.3 16.4 %fusion.415 = f32[8,16,512]{2,1,0:T(8,128)S(1)} fusion(bf16[256,8,16]{0,2,1:T(8,128)(2,1)S(1)} %bitcast.421, f32[8,256,512]{2,1,0:T(8,128)} %fusion.407, f32[8,256,512]{2,1,0:T(8,128)} %get-tuple-element.616, f32[8,256]{1,0:T(8,128)S(1)} %get-tuple-element.617), kind=kOutput, calls=%fused_computation.39.clone.1 | convolution fusion | flops 40897024 | bytes 8724480 | tf_op jit(solution)/shard_map/while/body/eval_jaxpr/hqk,qhd->khd/dot_general | solution.py:72
  150.8 16.5 %fusion.414 = f32[8,16,512]{2,1,0:T(8,128)S(1)} fusion(bf16[256,8,16]{0,2,1:T(8,128)(2,1)S(1)} %bitcast.418, f32[8,256,512]{2,1,0:T(8,128)} %fusion.404, f32[8,256,512]{2,1,0:T(8,128)} %get-tuple-element.610, f32[8,256]{1,0:T(8,128)S(1)} %get-tuple-element.611), kind=kOutput, calls=%fused_computation.37.clone.1 | convolution fusion | flops 40897024 | bytes 8724480 | tf_op jit(solution)/shard_map/while/body/eval_jaxpr/hqk,qhd->khd/dot_general | solution.py:72
  192.7 12.4 collective-permute-start.6
  210.8 17.8 %fusion.406 = bf16[8,16,256]{2,1,0:T(8,128)(2,1)} fusion(bf16[512,8,16]{0,2,1:T(8,128)(2,1)S(1)} %bitcast.411, f32[8,256,512]{2,1,0:T(8,128)} %fusion.404, f32[8,256,512]{2,1,0:T(8,128)} %get-tuple-element.610, f32[8,256]{1,0:T(8,128)S(1)} %copy-done.22), kind=kOutput, calls=%fused_computation.86.clone.1 | convolution fusion | flops 40929792 | bytes 8593408 | tf_op jit(solution)/shard_map/while/body/eval_jaxpr/hqk,khd->qhd/dot_general | solution.py:67
  230.1 17.9 %fusion.409 = bf16[8,16,256]{2,1,0:T(8,128)(2,1)} fusion(bf16[512,8,16]{0,2,1:T(8,128)(2,1)} %bitcast.408, f32[8,256,512]{2,1,0:T(8,128)} %fusion.407, f32[8,256,512]{2,1,0:T(8,128)} %get-tuple-element.616, f32[8,256]{1,0:T(8,128)} %copy-done.20), kind=kOutput, calls=%fused_computation.85.clone.1 | convolution fusion | flops 40929792 | bytes 8593408 | tf_op jit(solution)/shard_map/while/body/eval_jaxpr/hqk,khd->qhd/dot_general | solution.py:67
  249.4 17.8 %fusion.412 = bf16[8,16,256]{2,1,0:T(8,128)(2,1)} fusion(bf16[512,8,16]{0,2,1:T(8,128)(2,1)S(1)} %bitcast.405, f32[8,256,512]{2,1,0:T(8,128)} %fusion.410, f32[8,256,512]{2,1,0:T(8,128)} %get-tuple-element.622, f32[8,256]{1,0:T(8,128)S(1)} %copy-done.19), kind=kOutput, calls=%fused_computation.84.clone.1 | convolution fusion | flops 40929792 | bytes 8593408 | tf_op jit(solution)/shard_map/while/body/eval_jaxpr/hqk,khd->qhd/dot_general | solution.py:67
  268.9 11.4 collective-permute-done.4
  304.9 13.4 collective-permute-start
  327.9 7.2 collective-permute-done
  345.6 17.8 %fusion.403 = bf16[8,16,256]{2,1,0:T(8,128)(2,1)} fusion(bf16[512,8,16]{0,2,1:T(8,128)(2,1)S(1)} %bitcast.413, f32[8,256,512]{2,1,0:T(8,128)} %fusion.400, f32[8,256,512]{2,1,0:T(8,128)} %get-tuple-element.604, f32[8,256]{1,0:T(8,128)S(1)} %get-tuple-element.605), kind=kOutput, calls=%fused_computation.87.clone.1 | convolution fusion | flops 40929792 | bytes 8593408 | tf_op jit(solution)/shard_map/while/body/eval_jaxpr/hqk,khd->qhd/dot_general | solution.py:67
  363.3 16.6 %fusion.413 = f32[8,16,512]{2,1,0:T(8,128)S(1)} fusion(bf16[256,8,16]{0,2,1:T(8,128)(2,1)S(1)} %bitcast.426, f32[8,256,512]{2,1,0:T(8,128)} %fusion.400, f32[8,256,512]{2,1,0:T(8,128)} %get-tuple-element.604, f32[8,256]{1,0:T(8,128)S(1)} %get-tuple-element.605), kind=kOutput, calls=%fused_computation.35.clone.1 | convolution fusion | flops 40897024 | bytes 8724480 | tf_op jit(solution)/shard_map/while/body/eval_jaxpr/hqk,qhd->khd/dot_general | solution.py:72
  405.8 16.8 %fusion.416 = f32[8,16,512]{2,1,0:T(8,128)S(1)} fusion(bf16[256,8,16]{0,2,1:T(8,128)(2,1)S(1)} %bitcast.424, f32[8,256,512]{2,1,0:T(8,128)} %fusion.410, f32[8,256,512]{2,1,0:T(8,128)} %get-tuple-element.622, f32[8,256]{1,0:T(8,128)S(1)} %get-tuple-element.623), kind=kOutput, calls=%fused_computation.41.clone.1 | convolution fusion | flops 40897024 | bytes 8724480 | tf_op jit(solution)/shard_map/while/body/eval_jaxpr/hqk,qhd->khd/dot_general | solution.py:72
  422.6 16.4 %fusion.415 = f32[8,16,512]{2,1,0:T(8,128)S(1)} fusion(bf16[256,8,16]{0,2,1:T(8,128)(2,1)S(1)} %bitcast.421, f32[8,256,512]{2,1,0:T(8,128)} %fusion.407, f32[8,256,512]{2,1,0:T(8,128)} %get-tuple-element.616, f32[8,256]{1,0:T(8,128)S(1)} %get-tuple-element.617), kind=kOutput, calls=%fused_computation.39.clone.1 | convolution fusion | flops 40897024 | bytes 8724480 | tf_op jit(solution)/shard_map/while/body/eval_jaxpr/hqk,qhd->khd/dot_general | solution.py:72
  439.0 16.5 %fusion.414 = f32[8,16,512]{2,1,0:T(8,128)S(1)} fusion(bf16[256,8,16]{0,2,1:T(8,128)(2,1)S(1)} %bitcast.418, f32[8,256,512]{2,1,0:T(8,128)} %fusion.404, f32[8,256,512]{2,1,0:T(8,128)} %get-tuple-element.610, f32[8,256]{1,0:T(8,128)S(1)} %get-tuple-element.611), kind=kOutput, calls=%fused_computation.37.clone.1 | convolution fusion | flops 40897024 | bytes 8724480 | tf_op jit(solution)/shard_map/while/body/eval_jaxpr/hqk,qhd->khd/dot_general | solution.py:72
  476.8 11.9 collective-permute-start.7
  488.7 8.8 collective-permute-start.6
  503.0 17.8 %fusion.406 = bf16[8,16,256]{2,1,0:T(8,128)(2,1)} fusion(bf16[512,8,16]{0,2,1:T(8,128)(2,1)S(1)} %bitcast.411, f32[8,256,512]{2,1,0:T(8,128)} %fusion.404, f32[8,256,512]{2,1,0:T(8,128)} %get-tuple-element.610, f32[8,256]{1,0:T(8,128)S(1)} %copy-done.22), kind=kOutput, calls=%fused_computation.86.clone.1 | convolution fusion | flops 40929792 | bytes 8593408 | tf_op jit(solution)/shard_map/while/body/eval_jaxpr/hqk,khd->qhd/dot_general | solution.py:67
  522.3 17.9 %fusion.409 = bf16[8,16,256]{2,1,0:T(8,128)(2,1)} fusion(bf16[512,8,16]{0,2,1:T(8,128)(2,1)} %bitcast.408, f32[8,256,512]{2,1,0:T(8,128)} %fusion.407, f32[8,256,512]{2,1,0:T(8,128)} %get-tuple-element.616, f32[8,256]{1,0:T(8,128)} %copy-done.20), kind=kOutput, calls=%fused_computation.85.clone.1 | convolution fusion | flops 40929792 | bytes 8593408 | tf_op jit(solution)/shard_map/while/body/eval_jaxpr/hqk,khd->qhd/dot_general | solution.py:67
  541.6 17.8 %fusion.412 = bf16[8,16,256]{2,1,0:T(8,128)(2,1)} fusion(bf16[512,8,16]{0,2,1:T(8,128)(2,1)S(1)} %bitcast.405, f32[8,256,512]{2,1,0:T(8,128)} %fusion.410, f32[8,256,512]{2,1,0:T(8,128)} %get-tuple-element.622, f32[8,256]{1,0:T(8,128)S(1)} %copy-done.19), kind=kOutput, calls=%fused_computation.84.clone.1 | convolution fusion | flops 40929792 | bytes 8593408 | tf_op jit(solution)/shard_map/while/body/eval_jaxpr/hqk,khd->qhd/dot_general | solution.py:67
  561.1 12.5 collective-permute-done.4
  597.7 13.0 collective-permute-start
  620.7 6.8 collective-permute-done
  638.0 17.8 %fusion.403 = bf16[8,16,256]{2,1,0:T(8,128)(2,1)} fusion(bf16[512,8,16]{0,2,1:T(8,128)(2,1)S(1)} %bitcast.413, f32[8,256,512]{2,1,0:T(8,128)} %fusion.400, f32[8,256,512]{2,1,0:T(8,128)} %get-tuple-element.604, f32[8,256]{1,0:T(8,128)S(1)} %get-tuple-element.605), kind=kOutput, calls=%fused_computation.87.clone.1 | convolution fusion | flops 40929792 | bytes 8593408 | tf_op jit(solution)/shard_map/while/body/eval_jaxpr/hqk,khd->qhd/dot_general | solution.py:67
  655.8 16.8 %fusion.413 = f32[8,16,512]{2,1,0:T(8,128)S(1)} fusion(bf16[256,8,16]{0,2,1:T(8,128)(2,1)S(1)} %bitcast.426, f32[8,256,512]{2,1,0:T(8,128)} %fusion.400, f32[8,256,512]{2,1,0:T(8,128)} %get-tuple-element.604, f32[8,256]{1,0:T(8,128)S(1)} %get-tuple-element.605), kind=kOutput, calls=%fused_computation.35.clone.1 | convolution fusion | flops 40897024 | bytes 8724480 | tf_op jit(solution)/shard_map/while/body/eval_jaxpr/hqk,qhd->khd/dot_general | solution.py:72
  698.4 16.5 %fusion.416 = f32[8,16,512]{2,1,0:T(8,128)S(1)} fusion(bf16[256,8,16]{0,2,1:T(8,128)(2,1)S(1)} %bitcast.424, f32[8,256,512]{2,1,0:T(8,128)} %fusion.410, f32[8,256,512]{2,1,0:T(8,128)} %get-tuple-element.622, f32[8,256]{1,0:T(8,128)S(1)} %get-tuple-element.623), kind=kOutput, calls=%fused_computation.41.clone.1 | convolution fusion | flops 40897024 | bytes 8724480 | tf_op jit(solution)/shard_map/while/body/eval_jaxpr/hqk,qhd->khd/dot_general | solution.py:72
  715.0 16.4 %fusion.415 = f32[8,16,512]{2,1,0:T(8,128)S(1)} fusion(bf16[256,8,16]{0,2,1:T(8,128)(2,1)S(1)} %bitcast.421, f32[8,256,512]{2,1,0:T(8,128)} %fusion.407, f32[8,256,512]{2,1,0:T(8,128)} %get-tuple-element.616, f32[8,256]{1,0:T(8,128)S(1)} %get-tuple-element.617), kind=kOutput, calls=%fused_computation.39.clone.1 | convolution fusion | flops 40897024 | bytes 8724480 | tf_op jit(solution)/shard_map/while/body/eval_jaxpr/hqk,qhd->khd/dot_general | solution.py:72
  731.4 16.5 %fusion.414 = f32[8,16,512]{2,1,0:T(8,128)S(1)} fusion(bf16[256,8,16]{0,2,1:T(8,128)(2,1)S(1)} %bitcast.418, f32[8,256,512]{2,1,0:T(8,128)} %fusion.404, f32[8,256,512]{2,1,0:T(8,128)} %get-tuple-element.610, f32[8,256]{1,0:T(8,128)S(1)} %get-tuple-element.611), kind=kOutput, calls=%fused_computation.37.clone.1 | convolution fusion | flops 40897024 | bytes 8724480 | tf_op jit(solution)/shard_map/while/body/eval_jaxpr/hqk,qhd->khd/dot_general | solution.py:72
  769.3 11.7 collective-permute-start.7
  781.0 8.7 collective-permute-start.6
  795.2 17.8 %fusion.406 = bf16[8,16,256]{2,1,0:T(8,128)(2,1)} fusion(bf16[512,8,16]{0,2,1:T(8,128)(2,1)S(1)} %bitcast.411, f32[8,256,512]{2,1,0:T(8,128)} %fusion.404, f32[8,256,512]{2,1,0:T(8,128)} %get-tuple-element.610, f32[8,256]{1,0:T(8,128)S(1)} %copy-done.22), kind=kOutput, calls=%fused_computation.86.clone.1 | convolution fusion | flops 40929792 | bytes 8593408 | tf_op jit(solution)/shard_map/while/body/eval_jaxpr/hqk,khd->qhd/dot_general | solution.py:67
  814.4 17.9 %fusion.409 = bf16[8,16,256]{2,1,0:T(8,128)(2,1)} fusion(bf16[512,8,16]{0,2,1:T(8,128)(2,1)} %bitcast.408, f32[8,256,512]{2,1,0:T(8,128)} %fusion.407, f32[8,256,512]{2,1,0:T(8,128)} %get-tuple-element.616, f32[8,256]{1,0:T(8,128)} %copy-done.20), kind=kOutput, calls=%fused_computation.85.clone.1 | convolution fusion | flops 40929792 | bytes 8593408 | tf_op jit(solution)/shard_map/while/body/eval_jaxpr/hqk,khd->qhd/dot_general | solution.py:67
  833.8 17.8 %fusion.412 = bf16[8,16,256]{2,1,0:T(8,128)(2,1)} fusion(bf16[512,8,16]{0,2,1:T(8,128)(2,1)S(1)} %bitcast.405, f32[8,256,512]{2,1,0:T(8,128)} %fusion.410, f32[8,256,512]{2,1,0:T(8,128)} %get-tuple-element.622, f32[8,256]{1,0:T(8,128)S(1)} %copy-done.19), kind=kOutput, calls=%fused_computation.84.clone.1 | convolution fusion | flops 40929792 | bytes 8593408 | tf_op jit(solution)/shard_map/while/body/eval_jaxpr/hqk,khd->qhd/dot_general | solution.py:67
  853.2 12.3 collective-permute-done.4
  890.0 13.1 collective-permute-start
  912.9 6.9 collective-permute-done
  930.3 17.8 %fusion.403 = bf16[8,16,256]{2,1,0:T(8,128)(2,1)} fusion(bf16[512,8,16]{0,2,1:T(8,128)(2,1)S(1)} %bitcast.413, f32[8,256,512]{2,1,0:T(8,128)} %fusion.400, f32[8,256,512]{2,1,0:T(8,128)} %get-tuple-element.604, f32[8,256]{1,0:T(8,128)S(1)} %get-tuple-element.605), kind=kOutput, calls=%fused_computation.87.clone.1 | convolution fusion | flops 40929792 | bytes 8593408 | tf_op jit(solution)/shard_map/while/body/eval_jaxpr/hqk,khd->qhd/dot_general | solution.py:67
  948.1 16.6 %fusion.413 = f32[8,16,512]{2,1,0:T(8,128)S(1)} fusion(bf16[256,8,16]{0,2,1:T(8,128)(2,1)S(1)} %bitcast.426, f32[8,256,512]{2,1,0:T(8,128)} %fusion.400, f32[8,256,512]{2,1,0:T(8,128)} %get-tuple-element.604, f32[8,256]{1,0:T(8,128)S(1)} %get-tuple-element.605), kind=kOutput, calls=%fused_computation.35.clone.1 | convolution fusion | flops 40897024 | bytes 8724480 | tf_op jit(solution)/shard_map/while/body/eval_jaxpr/hqk,qhd->khd/dot_general | solution.py:72
  990.5 16.6 %fusion.416 = f32[8,16,512]{2,1,0:T(8,128)S(1)} fusion(bf16[256,8,16]{0,2,1:T(8,128)(2,1)S(1)} %bitcast.424, f32[8,256,512]{2,1,0:T(8,128)} %fusion.410, f32[8,256,512]{2,1,0:T(8,128)} %get-tuple-element.622, f32[8,256]{1,0:T(8,128)S(1)} %get-tuple-element.623), kind=kOutput, calls=%fused_computation.41.clone.1 | convolution fusion | flops 40897024 | bytes 8724480 | tf_op jit(solution)/shard_map/while/body/eval_jaxpr/hqk,qhd->khd/dot_general | solution.py:72
  1007.1 16.4 %fusion.415 = f32[8,16,512]{2,1,0:T(8,128)S(1)} fusion(bf16[256,8,16]{0,2,1:T(8,128)(2,1)S(1)} %bitcast.421, f32[8,256,512]{2,1,0:T(8,128)} %fusion.407, f32[8,256,512]{2,1,0:T(8,128)} %get-tuple-element.616, f32[8,256]{1,0:T(8,128)S(1)} %get-tuple-element.617), kind=kOutput, calls=%fused_computation.39.clone.1 | convolution fusion | flops 40897024 | bytes 8724480 | tf_op jit(solution)/shard_map/while/body/eval_jaxpr/hqk,qhd->khd/dot_general | solution.py:72
  1023.5 16.5 %fusion.414 = f32[8,16,512]{2,1,0:T(8,128)S(1)} fusion(bf16[256,8,16]{0,2,1:T(8,128)(2,1)S(1)} %bitcast.418, f32[8,256,512]{2,1,0:T(8,128)} %fusion.404, f32[8,256,512]{2,1,0:T(8,128)} %get-tuple-element.610, f32[8,256]{1,0:T(8,128)S(1)} %get-tuple-element.611), kind=kOutput, calls=%fused_computation.37.clone.1 | convolution fusion | flops 40897024 | bytes 8724480 | tf_op jit(solution)/shard_map/while/body/eval_jaxpr/hqk,qhd->khd/dot_general | solution.py:72
  1061.3 16.3 %collective-permute-start.7 = (f32[256,1024]{0,1:T(8,128)S(1)}, f32[256,1024]{0,1:T(8,128)S(1)}, u32[]{:S(2)}, u32[]{:S(2)}) collective-permute-start(f32[256,1024]{0,1:T(8,128)S(1)} %copy.99), channel_id=1, source_target_pairs={{2,0},{3,1},{4,2},{5,3},{6,4},{7,5},{8,6},{9,7},{10,8},{11,9},{12,... | collective-permute-start | bytes 3145736 | tf_op jit(solution)/shard_map/while/body/eval_jaxpr/ppermute | solution.py:18
  1077.7 6.6 collective-permute-start.6
  1090.0 17.8 %fusion.406 = bf16[8,16,256]{2,1,0:T(8,128)(2,1)} fusion(bf16[512,8,16]{0,2,1:T(8,128)(2,1)S(1)} %bitcast.411, f32[8,256,512]{2,1,0:T(8,128)} %fusion.404, f32[8,256,512]{2,1,0:T(8,128)} %get-tuple-element.610, f32[8,256]{1,0:T(8,128)S(1)} %copy-done.22), kind=kOutput, calls=%fused_computation.86.clone.1 | convolution fusion | flops 40929792 | bytes 8593408 | tf_op jit(solution)/shard_map/while/body/eval_jaxpr/hqk,khd->qhd/dot_general | solution.py:67
  1109.3 17.9 %fusion.409 = bf16[8,16,256]{2,1,0:T(8,128)(2,1)} fusion(bf16[512,8,16]{0,2,1:T(8,128)(2,1)} %bitcast.408, f32[8,256,512]{2,1,0:T(8,128)} %fusion.407, f32[8,256,512]{2,1,0:T(8,128)} %get-tuple-element.616, f32[8,256]{1,0:T(8,128)} %copy-done.20), kind=kOutput, calls=%fused_computation.85.clone.1 | convolution fusion | flops 40929792 | bytes 8593408 | tf_op jit(solution)/shard_map/while/body/eval_jaxpr/hqk,khd->qhd/dot_general | solution.py:67
  1128.6 17.8 %fusion.412 = bf16[8,16,256]{2,1,0:T(8,128)(2,1)} fusion(bf16[512,8,16]{0,2,1:T(8,128)(2,1)S(1)} %bitcast.405, f32[8,256,512]{2,1,0:T(8,128)} %fusion.410, f32[8,256,512]{2,1,0:T(8,128)} %get-tuple-element.622, f32[8,256]{1,0:T(8,128)S(1)} %copy-done.19), kind=kOutput, calls=%fused_computation.84.clone.1 | convolution fusion | flops 40929792 | bytes 8593408 | tf_op jit(solution)/shard_map/while/body/eval_jaxpr/hqk,khd->qhd/dot_general | solution.py:67
  1148.1 11.7 collective-permute-done.4
  1184.2 17.1 %collective-permute-start = (bf16[256,1024]{1,0:T(8,128)(2,1)S(1)}, bf16[256,1024]{1,0:T(8,128)(2,1)}, u32[]{:S(2)}, u32[]{:S(2)}) collective-permute-start(bf16[256,1024]{1,0:T(8,128)(2,1)S(1)} %slice.473), channel_id=1, source_target_pairs={{2,0},{3,1},{4,2},{5,3},{6,4},{7,5},{8,6},{9,7},{10,8},{11,9},{12,... | collective-permute-start | bytes 1572872 | tf_op jit(solution)/shard_map/while/body/eval_jaxpr/ppermute | solution.py:18
  1208.0 10.0 collective-permute-done
  1228.5 17.8 %fusion.403 = bf16[8,16,256]{2,1,0:T(8,128)(2,1)} fusion(bf16[512,8,16]{0,2,1:T(8,128)(2,1)S(1)} %bitcast.413, f32[8,256,512]{2,1,0:T(8,128)} %fusion.400, f32[8,256,512]{2,1,0:T(8,128)} %get-tuple-element.604, f32[8,256]{1,0:T(8,128)S(1)} %get-tuple-element.605), kind=kOutput, calls=%fused_computation.87.clone.1 | convolution fusion | flops 40929792 | bytes 8593408 | tf_op jit(solution)/shard_map/while/body/eval_jaxpr/hqk,khd->qhd/dot_general | solution.py:67
  1246.3 16.6 %fusion.413 = f32[8,16,512]{2,1,0:T(8,128)S(1)} fusion(bf16[256,8,16]{0,2,1:T(8,128)(2,1)S(1)} %bitcast.426, f32[8,256,512]{2,1,0:T(8,128)} %fusion.400, f32[8,256,512]{2,1,0:T(8,128)} %get-tuple-element.604, f32[8,256]{1,0:T(8,128)S(1)} %get-tuple-element.605), kind=kOutput, calls=%fused_computation.35.clone.1 | convolution fusion | flops 40897024 | bytes 8724480 | tf_op jit(solution)/shard_map/while/body/eval_jaxpr/hqk,qhd->khd/dot_general | solution.py:72
  1288.8 16.8 %fusion.416 = f32[8,16,512]{2,1,0:T(8,128)S(1)} fusion(bf16[256,8,16]{0,2,1:T(8,128)(2,1)S(1)} %bitcast.424, f32[8,256,512]{2,1,0:T(8,128)} %fusion.410, f32[8,256,512]{2,1,0:T(8,128)} %get-tuple-element.622, f32[8,256]{1,0:T(8,128)S(1)} %get-tuple-element.623), kind=kOutput, calls=%fused_computation.41.clone.1 | convolution fusion | flops 40897024 | bytes 8724480 | tf_op jit(solution)/shard_map/while/body/eval_jaxpr/hqk,qhd->khd/dot_general | solution.py:72
  1305.6 16.4 %fusion.415 = f32[8,16,512]{2,1,0:T(8,128)S(1)} fusion(bf16[256,8,16]{0,2,1:T(8,128)(2,1)S(1)} %bitcast.421, f32[8,256,512]{2,1,0:T(8,128)} %fusion.407, f32[8,256,512]{2,1,0:T(8,128)} %get-tuple-element.616, f32[8,256]{1,0:T(8,128)S(1)} %get-tuple-element.617), kind=kOutput, calls=%fused_computation.39.clone.1 | convolution fusion | flops 40897024 | bytes 8724480 | tf_op jit(solution)/shard_map/while/body/eval_jaxpr/hqk,qhd->khd/dot_general | solution.py:72
  1322.0 16.5 %fusion.414 = f32[8,16,512]{2,1,0:T(8,128)S(1)} fusion(bf16[256,8,16]{0,2,1:T(8,128)(2,1)S(1)} %bitcast.418, f32[8,256,512]{2,1,0:T(8,128)} %fusion.404, f32[8,256,512]{2,1,0:T(8,128)} %get-tuple-element.610, f32[8,256]{1,0:T(8,128)S(1)} %get-tuple-element.611), kind=kOutput, calls=%fused_computation.37.clone.1 | convolution fusion | flops 40897024 | bytes 8724480 | tf_op jit(solution)/shard_map/while/body/eval_jaxpr/hqk,qhd->khd/dot_general | solution.py:72
  1359.8 9.7 collective-permute-start.7
  1369.5 11.0 collective-permute-start.6
  1386.0 17.8 %fusion.406 = bf16[8,16,256]{2,1,0:T(8,128)(2,1)} fusion(bf16[512,8,16]{0,2,1:T(8,128)(2,1)S(1)} %bitcast.411, f32[8,256,512]{2,1,0:T(8,128)} %fusion.404, f32[8,256,512]{2,1,0:T(8,128)} %get-tuple-element.610, f32[8,256]{1,0:T(8,128)S(1)} %copy-done.22), kind=kOutput, calls=%fused_computation.86.clone.1 | convolution fusion | flops 40929792 | bytes 8593408 | tf_op jit(solution)/shard_map/while/body/eval_jaxpr/hqk,khd->qhd/dot_general | solution.py:67
  1405.2 17.9 %fusion.409 = bf16[8,16,256]{2,1,0:T(8,128)(2,1)} fusion(bf16[512,8,16]{0,2,1:T(8,128)(2,1)} %bitcast.408, f32[8,256,512]{2,1,0:T(8,128)} %fusion.407, f32[8,256,512]{2,1,0:T(8,128)} %get-tuple-element.616, f32[8,256]{1,0:T(8,128)} %copy-done.20), kind=kOutput, calls=%fused_computation.85.clone.1 | convolution fusion | flops 40929792 | bytes 8593408 | tf_op jit(solution)/shard_map/while/body/eval_jaxpr/hqk,khd->qhd/dot_general | solution.py:67
  1424.6 17.8 %fusion.412 = bf16[8,16,256]{2,1,0:T(8,128)(2,1)} fusion(bf16[512,8,16]{0,2,1:T(8,128)(2,1)S(1)} %bitcast.405, f32[8,256,512]{2,1,0:T(8,128)} %fusion.410, f32[8,256,512]{2,1,0:T(8,128)} %get-tuple-element.622, f32[8,256]{1,0:T(8,128)S(1)} %copy-done.19), kind=kOutput, calls=%fused_computation.84.clone.1 | convolution fusion | flops 40929792 | bytes 8593408 | tf_op jit(solution)/shard_map/while/body/eval_jaxpr/hqk,khd->qhd/dot_general | solution.py:67
  1444.0 12.5 collective-permute-done.4
  (650 shorter events, 524.3 us)
Async XLA Ops:
  6.9 22.3 %collective-permute-start.3 = (bf16[256,1024]{1,0:T(8,128)(2,1)S(1)}, bf16[256,1024]{1,0:T(8,128)(2,1)S(1)}, u32[]{:S(2)}, u32[]{:S(2)}) collective-permute-start(bf16[256,1024]{1,0:T(8,128)(2,1)S(1)} %slice.473), channel_id=1, source_target_pairs={{0,2},{1,3},{2,4},{3,5},{4,6},{5,7},{6,8},{7,9},{8,10},{9,11},{10,... | collective-permute-start | bytes 1572872 | tf_op jit(solution)/shard_map/while/body/eval_jaxpr/ppermute | solution.py:18
  10.9 23.8 %collective-permute-start.2 = (bf16[256,1024]{1,0:T(8,128)(2,1)S(1)}, bf16[256,1024]{1,0:T(8,128)(2,1)}, u32[]{:S(2)}, u32[]{:S(2)}) collective-permute-start(bf16[256,1024]{1,0:T(8,128)(2,1)S(1)} %slice.473), channel_id=1, source_target_pairs={{0,1},{1,2},{2,3},{3,4},{4,5},{5,6},{6,7},{7,8},{8,9},{9,10},{10,1... | collective-permute-start | bytes 1572872 | tf_op jit(solution)/shard_map/while/body/eval_jaxpr/ppermute | solution.py:18
  13.5 24.4 %collective-permute-start.1 = (bf16[256,1024]{1,0:T(8,128)(2,1)S(1)}, bf16[256,1024]{1,0:T(8,128)(2,1)}, u32[]{:S(2)}, u32[]{:S(2)}) collective-permute-start(bf16[256,1024]{1,0:T(8,128)(2,1)S(1)} %slice.473), channel_id=1, source_target_pairs={{1,0},{2,1},{3,2},{4,3},{5,4},{6,5},{7,6},{8,7},{9,8},{10,9},{11,1... | collective-permute-start | bytes 1572872 | tf_op jit(solution)/shard_map/while/body/eval_jaxpr/ppermute | solution.py:18
  16.2 30.9 %collective-permute-start = (bf16[256,1024]{1,0:T(8,128)(2,1)S(1)}, bf16[256,1024]{1,0:T(8,128)(2,1)}, u32[]{:S(2)}, u32[]{:S(2)}) collective-permute-start(bf16[256,1024]{1,0:T(8,128)(2,1)S(1)} %slice.473), channel_id=1, source_target_pairs={{2,0},{3,1},{4,2},{5,3},{6,4},{7,5},{8,6},{9,7},{10,8},{11,9},{12,... | collective-permute-start | bytes 1572872 | tf_op jit(solution)/shard_map/while/body/eval_jaxpr/ppermute | solution.py:18
  115.5 35.3 %copy-start.21 = (f32[8,256]{1,0:T(8,128)}, f32[8,256]{1,0:T(8,128)S(1)}, u32[]{:S(2)}) copy-start(f32[8,256]{1,0:T(8,128)S(1)} %get-tuple-element.611) | copy-start | bytes 24580 | tf_op jit(solution)/shard_map/while
  182.9 27.9 %copy-start.22 = (f32[8,256]{1,0:T(8,128)S(1)}, f32[8,256]{1,0:T(8,128)}, u32[]{:S(2)}) copy-start(f32[8,256]{1,0:T(8,128)} %copy-done.21) | copy-start | bytes 24580 | tf_op jit(solution)/shard_map/while
  188.4 80.4 %collective-permute-start.7 = (f32[256,1024]{0,1:T(8,128)S(1)}, f32[256,1024]{0,1:T(8,128)S(1)}, u32[]{:S(2)}, u32[]{:S(2)}) collective-permute-start(f32[256,1024]{0,1:T(8,128)S(1)} %copy.99), channel_id=1, source_target_pairs={{2,0},{3,1},{4,2},{5,3},{6,4},{7,5},{8,6},{9,7},{10,8},{11,9},{12,... | collective-permute-start | bytes 3145736 | tf_op jit(solution)/shard_map/while/body/eval_jaxpr/ppermute | solution.py:18
  192.7 76.2 %collective-permute-start.6 = (f32[256,1024]{0,1:T(8,128)}, f32[256,1024]{0,1:T(8,128)}, u32[]{:S(2)}, u32[]{:S(2)}) collective-permute-start(f32[256,1024]{0,1:T(8,128)} %copy.98), channel_id=1, source_target_pairs={{1,0},{2,1},{3,2},{4,3},{5,4},{6,5},{7,6},{8,7},{9,8},{10,9},{11,1... | collective-permute-start | bytes 3145736 | tf_op jit(solution)/shard_map/while/body/eval_jaxpr/ppermute | solution.py:18
  205.1 63.8 %collective-permute-start.5 = (f32[256,1024]{0,1:T(8,128)}, f32[256,1024]{0,1:T(8,128)}, u32[]{:S(2)}, u32[]{:S(2)}) collective-permute-start(f32[256,1024]{0,1:T(8,128)} %copy.97), channel_id=1, source_target_pairs={{0,1},{1,2},{2,3},{3,4},{4,5},{5,6},{6,7},{7,8},{8,9},{9,10},{10,1... | collective-permute-start | bytes 3145736 | tf_op jit(solution)/shard_map/while/body/eval_jaxpr/ppermute | solution.py:18
  207.0 73.3 %collective-permute-start.4 = (f32[256,1024]{0,1:T(8,128)S(1)}, f32[256,1024]{0,1:T(8,128)}, u32[]{:S(2)}, u32[]{:S(2)}) collective-permute-start(f32[256,1024]{0,1:T(8,128)S(1)} %copy-done), channel_id=1, source_target_pairs={{0,2},{1,3},{2,4},{3,5},{4,6},{5,7},{6,8},{7,9},{8,10},{9,11},{10,... | collective-permute-start | bytes 3145736 | tf_op jit(solution)/shard_map/while/body/eval_jaxpr/ppermute | solution.py:18
  287.6 5.4 collective-permute-start.8
  295.4 28.9 %copy-start.15 = (s32[4,2]{1,0:T(4,128)S(1)}, s32[4,2]{1,0:T(4,128)}, u32[]{:S(2)}) copy-start(s32[4,2]{1,0:T(4,128)} %get-tuple-element.678) | copy-start | bytes 100 | tf_op jit(solution)/shard_map/while
  297.7 27.4 %collective-permute-start.3 = (bf16[256,1024]{1,0:T(8,128)(2,1)S(1)}, bf16[256,1024]{1,0:T(8,128)(2,1)S(1)}, u32[]{:S(2)}, u32[]{:S(2)}) collective-permute-start(bf16[256,1024]{1,0:T(8,128)(2,1)S(1)} %slice.473), channel_id=1, source_target_pairs={{0,2},{1,3},{2,4},{3,5},{4,6},{5,7},{6,8},{7,9},{8,10},{9,11},{10,... | collective-permute-start | bytes 1572872 | tf_op jit(solution)/shard_map/while/body/eval_jaxpr/ppermute | solution.py:18
  299.6 25.4 %collective-permute-start.2 = (bf16[256,1024]{1,0:T(8,128)(2,1)S(1)}, bf16[256,1024]{1,0:T(8,128)(2,1)}, u32[]{:S(2)}, u32[]{:S(2)}) collective-permute-start(bf16[256,1024]{1,0:T(8,128)(2,1)S(1)} %slice.473), channel_id=1, source_target_pairs={{0,1},{1,2},{2,3},{3,4},{4,5},{5,6},{6,7},{7,8},{8,9},{9,10},{10,1... | collective-permute-start | bytes 1572872 | tf_op jit(solution)/shard_map/while/body/eval_jaxpr/ppermute | solution.py:18
  301.5 26.4 %collective-permute-start.1 = (bf16[256,1024]{1,0:T(8,128)(2,1)S(1)}, bf16[256,1024]{1,0:T(8,128)(2,1)}, u32[]{:S(2)}, u32[]{:S(2)}) collective-permute-start(bf16[256,1024]{1,0:T(8,128)(2,1)S(1)} %slice.473), channel_id=1, source_target_pairs={{1,0},{2,1},{3,2},{4,3},{5,4},{6,5},{7,6},{8,7},{9,8},{10,9},{11,1... | collective-permute-start | bytes 1572872 | tf_op jit(solution)/shard_map/while/body/eval_jaxpr/ppermute | solution.py:18
  304.9 30.2 %collective-permute-start = (bf16[256,1024]{1,0:T(8,128)(2,1)S(1)}, bf16[256,1024]{1,0:T(8,128)(2,1)}, u32[]{:S(2)}, u32[]{:S(2)}) collective-permute-start(bf16[256,1024]{1,0:T(8,128)(2,1)S(1)} %slice.473), channel_id=1, source_target_pairs={{2,0},{3,1},{4,2},{5,3},{6,4},{7,5},{8,6},{9,7},{10,8},{11,9},{12,... | collective-permute-start | bytes 1572872 | tf_op jit(solution)/shard_map/while/body/eval_jaxpr/ppermute | solution.py:18
  403.5 35.5 %copy-start.21 = (f32[8,256]{1,0:T(8,128)}, f32[8,256]{1,0:T(8,128)S(1)}, u32[]{:S(2)}) copy-start(f32[8,256]{1,0:T(8,128)S(1)} %get-tuple-element.611) | copy-start | bytes 24580 | tf_op jit(solution)/shard_map/while
  471.3 31.7 %copy-start.10 = (bf16[512,128]{0,1:T(8,128)(2,1)S(1)}, bf16[512,128]{0,1:T(8,128)(2,1)}, u32[]{:S(2)}) copy-start(bf16[512,128]{0,1:T(8,128)(2,1)} %copy-done.9) | copy-start | bytes 393220 | tf_op jit(solution)/shard_map/while
  471.3 31.7 %copy-start.22 = (f32[8,256]{1,0:T(8,128)S(1)}, f32[8,256]{1,0:T(8,128)}, u32[]{:S(2)}) copy-start(f32[8,256]{1,0:T(8,128)} %copy-done.21) | copy-start | bytes 24580 | tf_op jit(solution)/shard_map/while
  476.8 84.2 %collective-permute-start.7 = (f32[256,1024]{0,1:T(8,128)S(1)}, f32[256,1024]{0,1:T(8,128)S(1)}, u32[]{:S(2)}, u32[]{:S(2)}) collective-permute-start(f32[256,1024]{0,1:T(8,128)S(1)} %copy.99), channel_id=1, source_target_pairs={{2,0},{3,1},{4,2},{5,3},{6,4},{7,5},{8,6},{9,7},{10,8},{11,9},{12,... | collective-permute-start | bytes 3145736 | tf_op jit(solution)/shard_map/while/body/eval_jaxpr/ppermute | solution.py:18
  488.7 72.4 %collective-permute-start.6 = (f32[256,1024]{0,1:T(8,128)}, f32[256,1024]{0,1:T(8,128)}, u32[]{:S(2)}, u32[]{:S(2)}) collective-permute-start(f32[256,1024]{0,1:T(8,128)} %copy.98), channel_id=1, source_target_pairs={{1,0},{2,1},{3,2},{4,3},{5,4},{6,5},{7,6},{8,7},{9,8},{10,9},{11,1... | collective-permute-start | bytes 3145736 | tf_op jit(solution)/shard_map/while/body/eval_jaxpr/ppermute | solution.py:18
  497.5 63.6 %collective-permute-start.5 = (f32[256,1024]{0,1:T(8,128)}, f32[256,1024]{0,1:T(8,128)}, u32[]{:S(2)}, u32[]{:S(2)}) collective-permute-start(f32[256,1024]{0,1:T(8,128)} %copy.97), channel_id=1, source_target_pairs={{0,1},{1,2},{2,3},{3,4},{4,5},{5,6},{6,7},{7,8},{8,9},{9,10},{10,1... | collective-permute-start | bytes 3145736 | tf_op jit(solution)/shard_map/while/body/eval_jaxpr/ppermute | solution.py:18
  499.4 74.1 %collective-permute-start.4 = (f32[256,1024]{0,1:T(8,128)S(1)}, f32[256,1024]{0,1:T(8,128)}, u32[]{:S(2)}, u32[]{:S(2)}) collective-permute-start(f32[256,1024]{0,1:T(8,128)S(1)} %copy-done), channel_id=1, source_target_pairs={{0,2},{1,3},{2,4},{3,5},{4,6},{5,7},{6,8},{7,9},{8,10},{9,11},{10,... | collective-permute-start | bytes 3145736 | tf_op jit(solution)/shard_map/while/body/eval_jaxpr/ppermute | solution.py:18
  580.8 5.0 collective-permute-start.8
  588.3 28.5 %copy-start.15 = (s32[4,2]{1,0:T(4,128)S(1)}, s32[4,2]{1,0:T(4,128)}, u32[]{:S(2)}) copy-start(s32[4,2]{1,0:T(4,128)} %get-tuple-element.678) | copy-start | bytes 100 | tf_op jit(solution)/shard_map/while
  590.5 27.0 %collective-permute-start.3 = (bf16[256,1024]{1,0:T(8,128)(2,1)S(1)}, bf16[256,1024]{1,0:T(8,128)(2,1)S(1)}, u32[]{:S(2)}, u32[]{:S(2)}) collective-permute-start(bf16[256,1024]{1,0:T(8,128)(2,1)S(1)} %slice.473), channel_id=1, source_target_pairs={{0,2},{1,3},{2,4},{3,5},{4,6},{5,7},{6,8},{7,9},{8,10},{9,11},{10,... | collective-permute-start | bytes 1572872 | tf_op jit(solution)/shard_map/while/body/eval_jaxpr/ppermute | solution.py:18
  592.4 25.0 %collective-permute-start.2 = (bf16[256,1024]{1,0:T(8,128)(2,1)S(1)}, bf16[256,1024]{1,0:T(8,128)(2,1)}, u32[]{:S(2)}, u32[]{:S(2)}) collective-permute-start(bf16[256,1024]{1,0:T(8,128)(2,1)S(1)} %slice.473), channel_id=1, source_target_pairs={{0,1},{1,2},{2,3},{3,4},{4,5},{5,6},{6,7},{7,8},{8,9},{9,10},{10,1... | collective-permute-start | bytes 1572872 | tf_op jit(solution)/shard_map/while/body/eval_jaxpr/ppermute | solution.py:18
  594.4 26.4 %collective-permute-start.1 = (bf16[256,1024]{1,0:T(8,128)(2,1)S(1)}, bf16[256,1024]{1,0:T(8,128)(2,1)}, u32[]{:S(2)}, u32[]{:S(2)}) collective-permute-start(bf16[256,1024]{1,0:T(8,128)(2,1)S(1)} %slice.473), channel_id=1, source_target_pairs={{1,0},{2,1},{3,2},{4,3},{5,4},{6,5},{7,6},{8,7},{9,8},{10,9},{11,1... | collective-permute-start | bytes 1572872 | tf_op jit(solution)/shard_map/while/body/eval_jaxpr/ppermute | solution.py:18
  597.7 29.8 %collective-permute-start = (bf16[256,1024]{1,0:T(8,128)(2,1)S(1)}, bf16[256,1024]{1,0:T(8,128)(2,1)}, u32[]{:S(2)}, u32[]{:S(2)}) collective-permute-start(bf16[256,1024]{1,0:T(8,128)(2,1)S(1)} %slice.473), channel_id=1, source_target_pairs={{2,0},{3,1},{4,2},{5,3},{6,4},{7,5},{8,6},{9,7},{10,8},{11,9},{12,... | collective-permute-start | bytes 1572872 | tf_op jit(solution)/shard_map/while/body/eval_jaxpr/ppermute | solution.py:18
  696.1 35.3 %copy-start.21 = (f32[8,256]{1,0:T(8,128)}, f32[8,256]{1,0:T(8,128)S(1)}, u32[]{:S(2)}) copy-start(f32[8,256]{1,0:T(8,128)S(1)} %get-tuple-element.611) | copy-start | bytes 24580 | tf_op jit(solution)/shard_map/while
  763.7 31.4 %copy-start.10 = (bf16[512,128]{0,1:T(8,128)(2,1)S(1)}, bf16[512,128]{0,1:T(8,128)(2,1)}, u32[]{:S(2)}) copy-start(bf16[512,128]{0,1:T(8,128)(2,1)} %copy-done.9) | copy-start | bytes 393220 | tf_op jit(solution)/shard_map/while
  763.7 31.4 %copy-start.22 = (f32[8,256]{1,0:T(8,128)S(1)}, f32[8,256]{1,0:T(8,128)}, u32[]{:S(2)}) copy-start(f32[8,256]{1,0:T(8,128)} %copy-done.21) | copy-start | bytes 24580 | tf_op jit(solution)/shard_map/while
  769.3 84.0 %collective-permute-start.7 = (f32[256,1024]{0,1:T(8,128)S(1)}, f32[256,1024]{0,1:T(8,128)S(1)}, u32[]{:S(2)}, u32[]{:S(2)}) collective-permute-start(f32[256,1024]{0,1:T(8,128)S(1)} %copy.99), channel_id=1, source_target_pairs={{2,0},{3,1},{4,2},{5,3},{6,4},{7,5},{8,6},{9,7},{10,8},{11,9},{12,... | collective-permute-start | bytes 3145736 | tf_op jit(solution)/shard_map/while/body/eval_jaxpr/ppermute | solution.py:18
  781.0 72.3 %collective-permute-start.6 = (f32[256,1024]{0,1:T(8,128)}, f32[256,1024]{0,1:T(8,128)}, u32[]{:S(2)}, u32[]{:S(2)}) collective-permute-start(f32[256,1024]{0,1:T(8,128)} %copy.98), channel_id=1, source_target_pairs={{1,0},{2,1},{3,2},{4,3},{5,4},{6,5},{7,6},{8,7},{9,8},{10,9},{11,1... | collective-permute-start | bytes 3145736 | tf_op jit(solution)/shard_map/while/body/eval_jaxpr/ppermute | solution.py:18
  789.6 63.6 %collective-permute-start.5 = (f32[256,1024]{0,1:T(8,128)}, f32[256,1024]{0,1:T(8,128)}, u32[]{:S(2)}, u32[]{:S(2)}) collective-permute-start(f32[256,1024]{0,1:T(8,128)} %copy.97), channel_id=1, source_target_pairs={{0,1},{1,2},{2,3},{3,4},{4,5},{5,6},{6,7},{7,8},{8,9},{9,10},{10,1... | collective-permute-start | bytes 3145736 | tf_op jit(solution)/shard_map/while/body/eval_jaxpr/ppermute | solution.py:18
  791.6 73.9 %collective-permute-start.4 = (f32[256,1024]{0,1:T(8,128)S(1)}, f32[256,1024]{0,1:T(8,128)}, u32[]{:S(2)}, u32[]{:S(2)}) collective-permute-start(f32[256,1024]{0,1:T(8,128)S(1)} %copy-done), channel_id=1, source_target_pairs={{0,2},{1,3},{2,4},{3,5},{4,6},{5,7},{6,8},{7,9},{8,10},{9,11},{10,... | collective-permute-start | bytes 3145736 | tf_op jit(solution)/shard_map/while/body/eval_jaxpr/ppermute | solution.py:18
  872.7 5.1 collective-permute-start.8
  880.5 28.6 %copy-start.15 = (s32[4,2]{1,0:T(4,128)S(1)}, s32[4,2]{1,0:T(4,128)}, u32[]{:S(2)}) copy-start(s32[4,2]{1,0:T(4,128)} %get-tuple-element.678) | copy-start | bytes 100 | tf_op jit(solution)/shard_map/while
  882.7 27.1 %collective-permute-start.3 = (bf16[256,1024]{1,0:T(8,128)(2,1)S(1)}, bf16[256,1024]{1,0:T(8,128)(2,1)S(1)}, u32[]{:S(2)}, u32[]{:S(2)}) collective-permute-start(bf16[256,1024]{1,0:T(8,128)(2,1)S(1)} %slice.473), channel_id=1, source_target_pairs={{0,2},{1,3},{2,4},{3,5},{4,6},{5,7},{6,8},{7,9},{8,10},{9,11},{10,... | collective-permute-start | bytes 1572872 | tf_op jit(solution)/shard_map/while/body/eval_jaxpr/ppermute | solution.py:18
  884.7 25.1 %collective-permute-start.2 = (bf16[256,1024]{1,0:T(8,128)(2,1)S(1)}, bf16[256,1024]{1,0:T(8,128)(2,1)}, u32[]{:S(2)}, u32[]{:S(2)}) collective-permute-start(bf16[256,1024]{1,0:T(8,128)(2,1)S(1)} %slice.473), channel_id=1, source_target_pairs={{0,1},{1,2},{2,3},{3,4},{4,5},{5,6},{6,7},{7,8},{8,9},{9,10},{10,1... | collective-permute-start | bytes 1572872 | tf_op jit(solution)/shard_map/while/body/eval_jaxpr/ppermute | solution.py:18
  886.6 26.4 %collective-permute-start.1 = (bf16[256,1024]{1,0:T(8,128)(2,1)S(1)}, bf16[256,1024]{1,0:T(8,128)(2,1)}, u32[]{:S(2)}, u32[]{:S(2)}) collective-permute-start(bf16[256,1024]{1,0:T(8,128)(2,1)S(1)} %slice.473), channel_id=1, source_target_pairs={{1,0},{2,1},{3,2},{4,3},{5,4},{6,5},{7,6},{8,7},{9,8},{10,9},{11,1... | collective-permute-start | bytes 1572872 | tf_op jit(solution)/shard_map/while/body/eval_jaxpr/ppermute | solution.py:18
  890.0 29.9 %collective-permute-start = (bf16[256,1024]{1,0:T(8,128)(2,1)S(1)}, bf16[256,1024]{1,0:T(8,128)(2,1)}, u32[]{:S(2)}, u32[]{:S(2)}) collective-permute-start(bf16[256,1024]{1,0:T(8,128)(2,1)S(1)} %slice.473), channel_id=1, source_target_pairs={{2,0},{3,1},{4,2},{5,3},{6,4},{7,5},{8,6},{9,7},{10,8},{11,9},{12,... | collective-permute-start | bytes 1572872 | tf_op jit(solution)/shard_map/while/body/eval_jaxpr/ppermute | solution.py:18
  988.2 35.3 %copy-start.21 = (f32[8,256]{1,0:T(8,128)}, f32[8,256]{1,0:T(8,128)S(1)}, u32[]{:S(2)}) copy-start(f32[8,256]{1,0:T(8,128)S(1)} %get-tuple-element.611) | copy-start | bytes 24580 | tf_op jit(solution)/shard_map/while
  1055.8 34.2 %copy-start.10 = (bf16[512,128]{0,1:T(8,128)(2,1)S(1)}, bf16[512,128]{0,1:T(8,128)(2,1)}, u32[]{:S(2)}) copy-start(bf16[512,128]{0,1:T(8,128)(2,1)} %copy-done.9) | copy-start | bytes 393220 | tf_op jit(solution)/shard_map/while
  1055.8 34.2 %copy-start.22 = (f32[8,256]{1,0:T(8,128)S(1)}, f32[8,256]{1,0:T(8,128)}, u32[]{:S(2)}) copy-start(f32[8,256]{1,0:T(8,128)} %copy-done.21) | copy-start | bytes 24580 | tf_op jit(solution)/shard_map/while
  1061.3 86.7 %collective-permute-start.7 = (f32[256,1024]{0,1:T(8,128)S(1)}, f32[256,1024]{0,1:T(8,128)S(1)}, u32[]{:S(2)}, u32[]{:S(2)}) collective-permute-start(f32[256,1024]{0,1:T(8,128)S(1)} %copy.99), channel_id=1, source_target_pairs={{2,0},{3,1},{4,2},{5,3},{6,4},{7,5},{8,6},{9,7},{10,8},{11,9},{12,... | collective-permute-start | bytes 3145736 | tf_op jit(solution)/shard_map/while/body/eval_jaxpr/ppermute | solution.py:18
  1077.7 70.4 %collective-permute-start.6 = (f32[256,1024]{0,1:T(8,128)}, f32[256,1024]{0,1:T(8,128)}, u32[]{:S(2)}, u32[]{:S(2)}) collective-permute-start(f32[256,1024]{0,1:T(8,128)} %copy.98), channel_id=1, source_target_pairs={{1,0},{2,1},{3,2},{4,3},{5,4},{6,5},{7,6},{8,7},{9,8},{10,9},{11,1... | collective-permute-start | bytes 3145736 | tf_op jit(solution)/shard_map/while/body/eval_jaxpr/ppermute | solution.py:18
  1084.3 63.8 %collective-permute-start.5 = (f32[256,1024]{0,1:T(8,128)}, f32[256,1024]{0,1:T(8,128)}, u32[]{:S(2)}, u32[]{:S(2)}) collective-permute-start(f32[256,1024]{0,1:T(8,128)} %copy.97), channel_id=1, source_target_pairs={{0,1},{1,2},{2,3},{3,4},{4,5},{5,6},{6,7},{7,8},{8,9},{9,10},{10,1... | collective-permute-start | bytes 3145736 | tf_op jit(solution)/shard_map/while/body/eval_jaxpr/ppermute | solution.py:18
  1086.2 73.6 %collective-permute-start.4 = (f32[256,1024]{0,1:T(8,128)S(1)}, f32[256,1024]{0,1:T(8,128)}, u32[]{:S(2)}, u32[]{:S(2)}) collective-permute-start(f32[256,1024]{0,1:T(8,128)S(1)} %copy-done), channel_id=1, source_target_pairs={{0,2},{1,3},{2,4},{3,5},{4,6},{5,7},{6,8},{7,9},{8,10},{9,11},{10,... | collective-permute-start | bytes 3145736 | tf_op jit(solution)/shard_map/while/body/eval_jaxpr/ppermute | solution.py:18
  1167.0 5.2 collective-permute-start.8
  1172.4 28.9 %copy-start.2 = (bf16[512,512]{1,0:T(8,128)(2,1)S(1)}, bf16[512,512]{1,0:T(8,128)(2,1)}, u32[]{:S(2)}) copy-start(bf16[512,512]{1,0:T(8,128)(2,1)} %get-tuple-element.680) | copy-start | bytes 1572868 | tf_op jit(solution)/shard_map/while
  1174.7 32.6 %copy-start.15 = (s32[4,2]{1,0:T(4,128)S(1)}, s32[4,2]{1,0:T(4,128)}, u32[]{:S(2)}) copy-start(s32[4,2]{1,0:T(4,128)} %get-tuple-element.678) | copy-start | bytes 100 | tf_op jit(solution)/shard_map/while
  1177.0 31.0 %collective-permute-start.3 = (bf16[256,1024]{1,0:T(8,128)(2,1)S(1)}, bf16[256,1024]{1,0:T(8,128)(2,1)S(1)}, u32[]{:S(2)}, u32[]{:S(2)}) collective-permute-start(bf16[256,1024]{1,0:T(8,128)(2,1)S(1)} %slice.473), channel_id=1, source_target_pairs={{0,2},{1,3},{2,4},{3,5},{4,6},{5,7},{6,8},{7,9},{8,10},{9,11},{10,... | collective-permute-start | bytes 1572872 | tf_op jit(solution)/shard_map/while/body/eval_jaxpr/ppermute | solution.py:18
  1178.9 29.1 %collective-permute-start.2 = (bf16[256,1024]{1,0:T(8,128)(2,1)S(1)}, bf16[256,1024]{1,0:T(8,128)(2,1)}, u32[]{:S(2)}, u32[]{:S(2)}) collective-permute-start(bf16[256,1024]{1,0:T(8,128)(2,1)S(1)} %slice.473), channel_id=1, source_target_pairs={{0,1},{1,2},{2,3},{3,4},{4,5},{5,6},{6,7},{7,8},{8,9},{9,10},{10,1... | collective-permute-start | bytes 1572872 | tf_op jit(solution)/shard_map/while/body/eval_jaxpr/ppermute | solution.py:18
  1180.8 27.2 %collective-permute-start.1 = (bf16[256,1024]{1,0:T(8,128)(2,1)S(1)}, bf16[256,1024]{1,0:T(8,128)(2,1)}, u32[]{:S(2)}, u32[]{:S(2)}) collective-permute-start(bf16[256,1024]{1,0:T(8,128)(2,1)S(1)} %slice.473), channel_id=1, source_target_pairs={{1,0},{2,1},{3,2},{4,3},{5,4},{6,5},{7,6},{8,7},{9,8},{10,9},{11,1... | collective-permute-start | bytes 1572872 | tf_op jit(solution)/shard_map/while/body/eval_jaxpr/ppermute | solution.py:18
  1184.2 33.9 %collective-permute-start = (bf16[256,1024]{1,0:T(8,128)(2,1)S(1)}, bf16[256,1024]{1,0:T(8,128)(2,1)}, u32[]{:S(2)}, u32[]{:S(2)}) collective-permute-start(bf16[256,1024]{1,0:T(8,128)(2,1)S(1)} %slice.473), channel_id=1, source_target_pairs={{2,0},{3,1},{4,2},{5,3},{6,4},{7,5},{8,6},{9,7},{10,8},{11,9},{12,... | collective-permute-start | bytes 1572872 | tf_op jit(solution)/shard_map/while/body/eval_jaxpr/ppermute | solution.py:18
  1286.5 35.5 %copy-start.21 = (f32[8,256]{1,0:T(8,128)}, f32[8,256]{1,0:T(8,128)S(1)}, u32[]{:S(2)}) copy-start(f32[8,256]{1,0:T(8,128)S(1)} %get-tuple-element.611) | copy-start | bytes 24580 | tf_op jit(solution)/shard_map/while
  1354.3 31.7 %copy-start.10 = (bf16[512,128]{0,1:T(8,128)(2,1)S(1)}, bf16[512,128]{0,1:T(8,128)(2,1)}, u32[]{:S(2)}) copy-start(bf16[512,128]{0,1:T(8,128)(2,1)} %copy-done.9) | copy-start | bytes 393220 | tf_op jit(solution)/shard_map/while
  1354.3 31.7 %copy-start.22 = (f32[8,256]{1,0:T(8,128)S(1)}, f32[8,256]{1,0:T(8,128)}, u32[]{:S(2)}) copy-start(f32[8,256]{1,0:T(8,128)} %copy-done.21) | copy-start | bytes 24580 | tf_op jit(solution)/shard_map/while
  1359.8 84.2 %collective-permute-start.7 = (f32[256,1024]{0,1:T(8,128)S(1)}, f32[256,1024]{0,1:T(8,128)S(1)}, u32[]{:S(2)}, u32[]{:S(2)}) collective-permute-start(f32[256,1024]{0,1:T(8,128)S(1)} %copy.99), channel_id=1, source_target_pairs={{2,0},{3,1},{4,2},{5,3},{6,4},{7,5},{8,6},{9,7},{10,8},{11,9},{12,... | collective-permute-start | bytes 3145736 | tf_op jit(solution)/shard_map/while/body/eval_jaxpr/ppermute | solution.py:18
  1369.5 74.5 %collective-permute-start.6 = (f32[256,1024]{0,1:T(8,128)}, f32[256,1024]{0,1:T(8,128)}, u32[]{:S(2)}, u32[]{:S(2)}) collective-permute-start(f32[256,1024]{0,1:T(8,128)} %copy.98), channel_id=1, source_target_pairs={{1,0},{2,1},{3,2},{4,3},{5,4},{6,5},{7,6},{8,7},{9,8},{10,9},{11,1... | collective-permute-start | bytes 3145736 | tf_op jit(solution)/shard_map/while/body/eval_jaxpr/ppermute | solution.py:18
  1380.5 63.6 %collective-permute-start.5 = (f32[256,1024]{0,1:T(8,128)}, f32[256,1024]{0,1:T(8,128)}, u32[]{:S(2)}, u32[]{:S(2)}) collective-permute-start(f32[256,1024]{0,1:T(8,128)} %copy.97), channel_id=1, source_target_pairs={{0,1},{1,2},{2,3},{3,4},{4,5},{5,6},{6,7},{7,8},{8,9},{9,10},{10,1... | collective-permute-start | bytes 3145736 | tf_op jit(solution)/shard_map/while/body/eval_jaxpr/ppermute | solution.py:18
  1382.4 74.1 %collective-permute-start.4 = (f32[256,1024]{0,1:T(8,128)S(1)}, f32[256,1024]{0,1:T(8,128)}, u32[]{:S(2)}, u32[]{:S(2)}) collective-permute-start(f32[256,1024]{0,1:T(8,128)S(1)} %copy-done), channel_id=1, source_target_pairs={{0,2},{1,3},{2,4},{3,5},{4,6},{5,7},{6,8},{7,9},{8,10},{9,11},{10,... | collective-permute-start | bytes 3145736 | tf_op jit(solution)/shard_map/while/body/eval_jaxpr/ppermute | solution.py:18
  1463.7 5.0 collective-permute-start.8
  (96 other events, 1365.7 us)
where the time goes:
time: 1480 us; the launch traced here: 1470 us
  matrix products  870 us (59%)
  starting transfers between devices  243 us (16%)
  local copies, waits for them, and re-layouts  162 us (11%)
  waiting for transfers between devices  124 us (8%)
  other arithmetic  67.2 us (5%)
    dot_general x20, matrix products, attend_backward(): jnp.einsum('hqk,khd->qhd', grad_scores, key_group, preferred_element_type...  356 us
    dot_general x20, matrix products, attend_backward(): jnp.einsum('hqk,qhd->khd', grad_scores, query_group, preferred_element_ty...  331 us
    ppermute x45, starting transfers between devices, shifted(): return lax.ppermute(x, axis, pairs)  243 us
    ppermute x45, waiting for transfers between devices, shifted(): return lax.ppermute(x, axis, pairs)  124 us
    sub x20, matrix products, attend_backward(): attention = jax.nn.softmax(scores, axis=-1)  66.7 us
    dot_general x20, matrix products, attend_backward(): jnp.einsum('qhd,khd->hqk', grad_group, value_group, preferred_element_typ...  58 us
    while x285, local copies, waits for them, and re-layouts  55.7 us
    dot_general x20, matrix products, attend_backward(): jnp.einsum('hqk,qhd->khd', attention.astype(jnp.bfloat16), grad_group, pr...  31 us
  transfers between devices with their start and end apart: 45, of which 20 were waited for; matrix products, arithmetic and copies ran while one was open for 22% of the time, Pallas kernels for 0%

commit v1 on v0

--- a/solution.py
+++ b/solution.py
@@ -1,6 +1,8 @@
 import jax
 import jax.numpy as jnp
 from jax import lax
+from jax.experimental import pallas as pl
+from jax.experimental.pallas import tpu as pltpu
 from jax.sharding import PartitionSpec as P
 
 HEADS = 32
@@ -36,56 +38,66 @@
     )
 
 
+def attention_kernel(q_ref, k_ref, v_ref, g_ref, dq_ref, dk_ref, dv_ref):
+    factor = HD ** (-0.5)
+    width = q_ref.shape[1]
+    q = q_ref[...]
+    k = k_ref[...]
+    v = v_ref[...]
+    g = g_ref[...]
+    head_of = lax.broadcasted_iota(jnp.int32, (1, width), 1) // HD
+    dq_ref[...] = jnp.zeros_like(dq_ref)
+    dk_ref[...] = jnp.zeros_like(dk_ref)
+    dv_ref[...] = jnp.zeros_like(dv_ref)
+    nt = (((1,), (1,)), ((), ()))
+    tn = (((0,), (0,)), ((), ()))
+
+    def head(h, carry):
+        mask = head_of == h
+        qm = jnp.where(mask, q, jnp.zeros_like(q))
+        km = jnp.where(mask, k, jnp.zeros_like(k))
+        gm = jnp.where(mask, g, jnp.zeros_like(g))
+        scores = lax.dot_general(qm, k, nt, preferred_element_type=jnp.float32) * factor
+        top = jnp.max(scores, axis=-1, keepdims=True)
+        exps = jnp.exp(scores - top)
+        attention = exps / jnp.sum(exps, axis=-1, keepdims=True)
+        grad_probs = lax.dot_general(gm, v, nt, preferred_element_type=jnp.float32)
+        row = jnp.sum(attention * grad_probs, axis=-1, keepdims=True)
+        grad_scores = (attention * (grad_probs - row) * factor).astype(jnp.bfloat16)
+        dq_ref[...] += jnp.dot(grad_scores, km, preferred_element_type=jnp.float32)
+        dk_ref[...] += lax.dot_general(grad_scores, qm, tn, preferred_element_type=jnp.float32)
+        dv_ref[...] += lax.dot_general(
+            attention.astype(jnp.bfloat16), gm, tn, preferred_element_type=jnp.float32
+        )
+        return carry
+
+    lax.fori_loop(0, width // HD, head, 0)
+
+
 def attend_backward(queries, key_rows, value_rows, grad_attn):
-    group_heads = min(HEADS, max(1, 128 // HD))
-    group_width = group_heads * HD
-    factor = HD ** (-0.5)
-    row_count = queries.shape[0]
-    key_count = key_rows.shape[0]
-    grad_query, grad_key, grad_value = ([], [], [])
-    for column in range(0, queries.shape[1], group_width):
-        query_group = queries[:, column : column + group_width].reshape(row_count, group_heads, HD)
-        key_group = key_rows[:, column : column + group_width].reshape(key_count, group_heads, HD)
-        value_group = value_rows[:, column : column + group_width].reshape(
-            key_count, group_heads, HD
-        )
-        grad_group = grad_attn[:, column : column + group_width].reshape(row_count, group_heads, HD)
-        scores = (
-            jnp.einsum("qhd,khd->hqk", query_group, key_group, preferred_element_type=jnp.float32)
-            * factor
-        )
-        attention = jax.nn.softmax(scores, axis=-1)
-        grad_probs = jnp.einsum(
-            "qhd,khd->hqk", grad_group, value_group, preferred_element_type=jnp.float32
-        )
-        grad_scores = (
-            attention
-            * (grad_probs - jnp.sum(attention * grad_probs, axis=-1, keepdims=True))
-            * factor
-        ).astype(jnp.bfloat16)
-        grad_query.append(
-            jnp.einsum(
-                "hqk,khd->qhd", grad_scores, key_group, preferred_element_type=jnp.float32
-            ).reshape(row_count, group_width)
-        )
-        grad_key.append(
-            jnp.einsum(
-                "hqk,qhd->khd", grad_scores, query_group, preferred_element_type=jnp.float32
-            ).reshape(key_count, group_width)
-        )
-        grad_value.append(
-            jnp.einsum(
-                "hqk,qhd->khd",
-                attention.astype(jnp.bfloat16),
-                grad_group,
-                preferred_element_type=jnp.float32,
-            ).reshape(key_count, group_width)
-        )
-    return (
-        jnp.concatenate(grad_query, 1),
-        jnp.concatenate(grad_key, 1),
-        jnp.concatenate(grad_value, 1),
-    )
+    rows, width = queries.shape
+    keys = key_rows.shape[0]
+    group = 128
+    groups = width // group
+    row_spec = pl.BlockSpec((rows, group), lambda i: (0, i))
+    key_spec = pl.BlockSpec((keys, group), lambda i: (0, i))
+    flops = 2 * 5 * rows * keys * width * (group // HD)
+    return pl.pallas_call(
+        attention_kernel,
+        grid=(groups,),
+        in_specs=[row_spec, key_spec, key_spec, row_spec],
+        out_specs=[row_spec, key_spec, key_spec],
+        out_shape=[
+            jax.ShapeDtypeStruct((rows, width), jnp.float32),
+            jax.ShapeDtypeStruct((keys, width), jnp.float32),
+            jax.ShapeDtypeStruct((keys, width), jnp.float32),
+        ],
+        cost_estimate=pl.CostEstimate(
+            flops=flops,
+            transcendentals=rows * keys * width // HD,
+            bytes_accessed=2 * (2 * rows + 2 * keys) * width + 4 * (rows + 2 * keys) * width,
+        ),
+    )(queries, key_rows, value_rows, grad_attn)
 
 
 def shards(saved_inputs, project_in, project_out, norm_gains, neighbour_blocks, cotangent):

time: 1480 us -> 941 us (0.64)
  the two profiles are of different devices: /device:TPU:15 before, /device:TPU:5 now
where the time goes in v1:
time: 941 us; the launch traced here: 938 us
  waiting for transfers between devices  480 us (51%)
  starting transfers between devices  172 us (18%)
  Pallas kernels  148 us (16%)
  other arithmetic  60.9 us (6%)
  local copies, waits for them, and re-layouts  52 us (6%)
  matrix products  24.5 us (3%)
    ppermute x45, waiting for transfers between devices, shifted(): return lax.ppermute(x, axis, pairs)  480 us
    ppermute x45, starting transfers between devices, shifted(): return lax.ppermute(x, axis, pairs)  172 us
    pallas_call x5, Pallas kernels, attend_backward(): pl.pallas_call(attention_kernel, grid=(groups,), in_specs=[row_spec, key_...  148 us
    slice x5, local copies, waits for them, and re-layouts, step(): grad_own = grad_own + shifted(window_grads[slot_index], 'space', shift_by)  21.9 us
  transfers between devices with their start and end apart: 45, of which 34 were waited for; matrix products, arithmetic and copies ran while one was open for 2% of the time, Pallas kernels for 0%

profile of v1, /device:TPU:5, one launch (start us, length us, event | category | flops | bytes accessed | tf_op | source)
XLA Modules:
  0.0 938.5 jit_solution(7951212474397323950)
XLA Ops:
  1.8 936.6 %while.20 = (s32[]{:T(128)}, bf16[256,512]{1,0:T(8,128)(2,1)S(1)}, bf16[4,256,512]{2,1,0:T(8,128)(2,1)}, pred[]{:T(512)}, s32[]{:T(128)}, /*index=5*/bf16[4,256,...) while((s32[]{:T(128)}, bf16[256,512]{1,0:T(8,128)(2,1)S(1)}, ...), condition=%wide.region_6.7_spmd, body=%wide.region_0.6_spmd.sunk | while | flops 6321604096 | bytes 95460656 | solution.py:181
  6.4 4.8 collective-permute-start.3
  13.5 7.2 collective-permute-start.1
  26.3 11.2 %collective-permute-done.2 = bf16[256,1024]{1,0:T(8,128)(2,1)S(1)} collective-permute-done((bf16[256,1024]{1,0:T(8,128)(2,1)S(1)}, bf16[256,1024]{1,0:T(8,128)(2,1)S(1)}, u32[]{:S(2)}, u32[]{:S(2)}) %collective-permute-start.2) | collective-permute-done | bytes 524320 | tf_op jit(solution)/shard_map/while/body/eval_jaxpr/ppermute | solution.py:20
  37.6 16.7 %collective-permute-done.1 = bf16[256,1024]{1,0:T(8,128)(2,1)S(1)} collective-permute-done((bf16[256,1024]{1,0:T(8,128)(2,1)S(1)}, bf16[256,1024]{1,0:T(8,128)(2,1)S(1)}, u32[]{:S(2)}, u32[]{:S(2)}) %collective-permute-start.1) | collective-permute-done | bytes 524320 | tf_op jit(solution)/shard_map/while/body/eval_jaxpr/ppermute | solution.py:20
  56.4 29.6 %eval_jaxpr.12 = (f32[256,512]{1,0:T(8,128)}, f32[512,512]{1,0:T(8,128)}, f32[512,512]{1,0:T(8,128)}) custom-call(bf16[256,512]{1,0:T(8,128)(2,1)} %slice.157.q_ref, bf16[512,512]{1,0:T(8,128)(2,1)} %get-tuple-element.550.k_ref, bf16[512,512]{1,0:T(8,128)(2,1)} %get-tuple-element.551.v_ref, bf16[256,512]{1,0:T(8,128)(2,1)} %convolution_convert_fusion.5.g_ref), custom_call_target="tpu_custom_call" | custom-call | flops 5368709120 | bytes 4194304 | tf_op jit(solution)/shard_map/while/body/eval_jaxpr/pallas_call | solution.py:85
  90.1 3.1 scatter_fusion
  93.2 4.4 fusion.57
  101.4 7.6 collective-permute-start.6
  109.0 4.3 collective-permute-start.7
  114.4 34.6 %collective-permute-done.5 = f32[256,1024]{1,0:T(8,128)S(1)} collective-permute-done((f32[256,1024]{1,0:T(8,128)}, f32[256,1024]{1,0:T(8,128)S(1)}, u32[]{:S(2)}, u32[]{:S(2)}) %collective-permute-start.5) | collective-permute-done | bytes 1048608 | tf_op jit(solution)/shard_map/while/body/eval_jaxpr/ppermute | solution.py:20
  149.0 41.2 %collective-permute-done.6 = f32[256,1024]{1,0:T(8,128)} collective-permute-done((f32[256,1024]{1,0:T(8,128)}, f32[256,1024]{1,0:T(8,128)}, u32[]{:S(2)}, u32[]{:S(2)}) %collective-permute-start.6) | collective-permute-done | bytes 1048608 | tf_op jit(solution)/shard_map/while/body/eval_jaxpr/ppermute | solution.py:20
  195.3 4.1 collective-permute-start.8
  209.0 7.6 collective-permute-start.1
  216.6 3.7 collective-permute-start
  225.2 19.5 %collective-permute-done.2 = bf16[256,1024]{1,0:T(8,128)(2,1)S(1)} collective-permute-done((bf16[256,1024]{1,0:T(8,128)(2,1)S(1)}, bf16[256,1024]{1,0:T(8,128)(2,1)S(1)}, u32[]{:S(2)}, u32[]{:S(2)}) %collective-permute-start.2) | collective-permute-done | bytes 524320 | tf_op jit(solution)/shard_map/while/body/eval_jaxpr/ppermute | solution.py:20
  244.7 3.5 collective-permute-done.1
  250.3 29.6 %eval_jaxpr.12 = (f32[256,512]{1,0:T(8,128)}, f32[512,512]{1,0:T(8,128)}, f32[512,512]{1,0:T(8,128)}) custom-call(bf16[256,512]{1,0:T(8,128)(2,1)} %slice.157.q_ref, bf16[512,512]{1,0:T(8,128)(2,1)} %get-tuple-element.550.k_ref, bf16[512,512]{1,0:T(8,128)(2,1)} %get-tuple-element.551.v_ref, bf16[256,512]{1,0:T(8,128)(2,1)} %convolution_convert_fusion.5.g_ref), custom_call_target="tpu_custom_call" | custom-call | flops 5368709120 | bytes 4194304 | tf_op jit(solution)/shard_map/while/body/eval_jaxpr/pallas_call | solution.py:85
  284.0 3.0 scatter_fusion
  287.1 4.4 fusion.57
  295.3 7.6 collective-permute-start.6
  302.9 4.3 collective-permute-start.7
  308.3 36.9 %collective-permute-done.5 = f32[256,1024]{1,0:T(8,128)S(1)} collective-permute-done((f32[256,1024]{1,0:T(8,128)}, f32[256,1024]{1,0:T(8,128)S(1)}, u32[]{:S(2)}, u32[]{:S(2)}) %collective-permute-start.5) | collective-permute-done | bytes 1048608 | tf_op jit(solution)/shard_map/while/body/eval_jaxpr/ppermute | solution.py:20
  345.1 15.9 %collective-permute-done.4 = f32[256,1024]{1,0:T(8,128)} collective-permute-done((f32[256,1024]{1,0:T(8,128)}, f32[256,1024]{1,0:T(8,128)}, u32[]{:S(2)}, u32[]{:S(2)}) %collective-permute-start.4) | collective-permute-done | bytes 1048608 | tf_op jit(solution)/shard_map/while/body/eval_jaxpr/ppermute | solution.py:20
  361.0 15.6 %collective-permute-done.6 = f32[256,1024]{1,0:T(8,128)} collective-permute-done((f32[256,1024]{1,0:T(8,128)}, f32[256,1024]{1,0:T(8,128)}, u32[]{:S(2)}, u32[]{:S(2)}) %collective-permute-start.6) | collective-permute-done | bytes 1048608 | tf_op jit(solution)/shard_map/while/body/eval_jaxpr/ppermute | solution.py:20
  381.8 2.9 collective-permute-start.8
  394.2 7.6 collective-permute-start.1
  401.8 3.7 collective-permute-start
  408.3 5.0 collective-permute-done.3
  413.3 15.9 %collective-permute-done.2 = bf16[256,1024]{1,0:T(8,128)(2,1)S(1)} collective-permute-done((bf16[256,1024]{1,0:T(8,128)(2,1)S(1)}, bf16[256,1024]{1,0:T(8,128)(2,1)S(1)}, u32[]{:S(2)}, u32[]{:S(2)}) %collective-permute-start.2) | collective-permute-done | bytes 524320 | tf_op jit(solution)/shard_map/while/body/eval_jaxpr/ppermute | solution.py:20
  433.6 29.5 %eval_jaxpr.12 = (f32[256,512]{1,0:T(8,128)}, f32[512,512]{1,0:T(8,128)}, f32[512,512]{1,0:T(8,128)}) custom-call(bf16[256,512]{1,0:T(8,128)(2,1)} %slice.157.q_ref, bf16[512,512]{1,0:T(8,128)(2,1)} %get-tuple-element.550.k_ref, bf16[512,512]{1,0:T(8,128)(2,1)} %get-tuple-element.551.v_ref, bf16[256,512]{1,0:T(8,128)(2,1)} %convolution_convert_fusion.5.g_ref), custom_call_target="tpu_custom_call" | custom-call | flops 5368709120 | bytes 4194304 | tf_op jit(solution)/shard_map/while/body/eval_jaxpr/pallas_call | solution.py:85
  467.3 3.1 scatter_fusion
  470.4 4.4 fusion.57
  478.6 7.6 collective-permute-start.6
  486.2 4.4 collective-permute-start.7
  491.8 33.5 %collective-permute-done.5 = f32[256,1024]{1,0:T(8,128)S(1)} collective-permute-done((f32[256,1024]{1,0:T(8,128)}, f32[256,1024]{1,0:T(8,128)S(1)}, u32[]{:S(2)}, u32[]{:S(2)}) %collective-permute-start.5) | collective-permute-done | bytes 1048608 | tf_op jit(solution)/shard_map/while/body/eval_jaxpr/ppermute | solution.py:20
  525.3 17.8 %collective-permute-done.4 = f32[256,1024]{1,0:T(8,128)} collective-permute-done((f32[256,1024]{1,0:T(8,128)}, f32[256,1024]{1,0:T(8,128)}, u32[]{:S(2)}, u32[]{:S(2)}) %collective-permute-start.4) | collective-permute-done | bytes 1048608 | tf_op jit(solution)/shard_map/while/body/eval_jaxpr/ppermute | solution.py:20
  543.1 17.1 %collective-permute-done.6 = f32[256,1024]{1,0:T(8,128)} collective-permute-done((f32[256,1024]{1,0:T(8,128)}, f32[256,1024]{1,0:T(8,128)}, u32[]{:S(2)}, u32[]{:S(2)}) %collective-permute-start.6) | collective-permute-done | bytes 1048608 | tf_op jit(solution)/shard_map/while/body/eval_jaxpr/ppermute | solution.py:20
  565.4 3.4 collective-permute-start.8
  578.3 7.6 collective-permute-start.1
  585.9 3.7 collective-permute-start
  592.4 5.5 collective-permute-done.3
  597.9 15.9 %collective-permute-done.2 = bf16[256,1024]{1,0:T(8,128)(2,1)S(1)} collective-permute-done((bf16[256,1024]{1,0:T(8,128)(2,1)S(1)}, bf16[256,1024]{1,0:T(8,128)(2,1)S(1)}, u32[]{:S(2)}, u32[]{:S(2)}) %collective-permute-start.2) | collective-permute-done | bytes 524320 | tf_op jit(solution)/shard_map/while/body/eval_jaxpr/ppermute | solution.py:20
  617.6 29.6 %eval_jaxpr.12 = (f32[256,512]{1,0:T(8,128)}, f32[512,512]{1,0:T(8,128)}, f32[512,512]{1,0:T(8,128)}) custom-call(bf16[256,512]{1,0:T(8,128)(2,1)} %slice.157.q_ref, bf16[512,512]{1,0:T(8,128)(2,1)} %get-tuple-element.550.k_ref, bf16[512,512]{1,0:T(8,128)(2,1)} %get-tuple-element.551.v_ref, bf16[256,512]{1,0:T(8,128)(2,1)} %convolution_convert_fusion.5.g_ref), custom_call_target="tpu_custom_call" | custom-call | flops 5368709120 | bytes 4194304 | tf_op jit(solution)/shard_map/while/body/eval_jaxpr/pallas_call | solution.py:85
  651.4 2.9 scatter_fusion
  654.3 4.4 fusion.57
  662.5 7.6 collective-permute-start.6
  670.1 4.6 collective-permute-start.7
  675.8 32.7 %collective-permute-done.5 = f32[256,1024]{1,0:T(8,128)S(1)} collective-permute-done((f32[256,1024]{1,0:T(8,128)}, f32[256,1024]{1,0:T(8,128)S(1)}, u32[]{:S(2)}, u32[]{:S(2)}) %collective-permute-start.5) | collective-permute-done | bytes 1048608 | tf_op jit(solution)/shard_map/while/body/eval_jaxpr/ppermute | solution.py:20
  708.5 18.3 %collective-permute-done.4 = f32[256,1024]{1,0:T(8,128)} collective-permute-done((f32[256,1024]{1,0:T(8,128)}, f32[256,1024]{1,0:T(8,128)}, u32[]{:S(2)}, u32[]{:S(2)}) %collective-permute-start.4) | collective-permute-done | bytes 1048608 | tf_op jit(solution)/shard_map/while/body/eval_jaxpr/ppermute | solution.py:20
  726.8 18.3 %collective-permute-done.6 = f32[256,1024]{1,0:T(8,128)} collective-permute-done((f32[256,1024]{1,0:T(8,128)}, f32[256,1024]{1,0:T(8,128)}, u32[]{:S(2)}, u32[]{:S(2)}) %collective-permute-start.6) | collective-permute-done | bytes 1048608 | tf_op jit(solution)/shard_map/while/body/eval_jaxpr/ppermute | solution.py:20
  750.2 3.2 collective-permute-start.8
  762.9 7.6 collective-permute-start.1
  770.5 3.7 collective-permute-start
  777.0 4.8 collective-permute-done.3
  781.9 16.0 %collective-permute-done.2 = bf16[256,1024]{1,0:T(8,128)(2,1)S(1)} collective-permute-done((bf16[256,1024]{1,0:T(8,128)(2,1)S(1)}, bf16[256,1024]{1,0:T(8,128)(2,1)S(1)}, u32[]{:S(2)}, u32[]{:S(2)}) %collective-permute-start.2) | collective-permute-done | bytes 524320 | tf_op jit(solution)/shard_map/while/body/eval_jaxpr/ppermute | solution.py:20
  802.3 29.6 %eval_jaxpr.12 = (f32[256,512]{1,0:T(8,128)}, f32[512,512]{1,0:T(8,128)}, f32[512,512]{1,0:T(8,128)}) custom-call(bf16[256,512]{1,0:T(8,128)(2,1)} %slice.157.q_ref, bf16[512,512]{1,0:T(8,128)(2,1)} %get-tuple-element.550.k_ref, bf16[512,512]{1,0:T(8,128)(2,1)} %get-tuple-element.551.v_ref, bf16[256,512]{1,0:T(8,128)(2,1)} %convolution_convert_fusion.5.g_ref), custom_call_target="tpu_custom_call" | custom-call | flops 5368709120 | bytes 4194304 | tf_op jit(solution)/shard_map/while/body/eval_jaxpr/pallas_call | solution.py:85
  839.0 4.4 fusion.57
  847.2 7.6 collective-permute-start.6
  854.8 4.6 collective-permute-start.7
  860.5 32.7 %collective-permute-done.5 = f32[256,1024]{1,0:T(8,128)S(1)} collective-permute-done((f32[256,1024]{1,0:T(8,128)}, f32[256,1024]{1,0:T(8,128)S(1)}, u32[]{:S(2)}, u32[]{:S(2)}) %collective-permute-start.5) | collective-permute-done | bytes 1048608 | tf_op jit(solution)/shard_map/while/body/eval_jaxpr/ppermute | solution.py:20
  893.2 18.3 %collective-permute-done.4 = f32[256,1024]{1,0:T(8,128)} collective-permute-done((f32[256,1024]{1,0:T(8,128)}, f32[256,1024]{1,0:T(8,128)}, u32[]{:S(2)}, u32[]{:S(2)}) %collective-permute-start.4) | collective-permute-done | bytes 1048608 | tf_op jit(solution)/shard_map/while/body/eval_jaxpr/ppermute | solution.py:20
  911.5 17.5 %collective-permute-done.6 = f32[256,1024]{1,0:T(8,128)} collective-permute-done((f32[256,1024]{1,0:T(8,128)}, f32[256,1024]{1,0:T(8,128)}, u32[]{:S(2)}, u32[]{:S(2)}) %collective-permute-start.6) | collective-permute-done | bytes 1048608 | tf_op jit(solution)/shard_map/while/body/eval_jaxpr/ppermute | solution.py:20
  934.1 3.2 collective-permute-start.8
  (220 shorter events, 157.2 us)
Async XLA Ops:
  4.1 19.4 %copy-start.2 = (bf16[512,512]{1,0:T(8,128)(2,1)S(1)}, bf16[512,512]{1,0:T(8,128)(2,1)}, u32[]{:S(2)}) copy-start(bf16[512,512]{1,0:T(8,128)(2,1)} %get-tuple-element.611) | copy-start | bytes 1572868 | tf_op jit(solution)/shard_map/while
  6.4 20.0 %collective-permute-start.3 = (bf16[256,1024]{1,0:T(8,128)(2,1)S(1)}, bf16[256,1024]{1,0:T(8,128)(2,1)S(1)}, u32[]{:S(2)}, u32[]{:S(2)}) collective-permute-start(bf16[256,1024]{1,0:T(8,128)(2,1)S(1)} %slice.158), channel_id=1, source_target_pairs={{0,2},{1,3},{2,4},{3,5},{4,6},{5,7},{6,8},{7,9},{8,10},{9,11},{10,... | collective-permute-start | bytes 1572872 | tf_op jit(solution)/shard_map/while/body/eval_jaxpr/ppermute | solution.py:20
  11.2 26.4 %collective-permute-start.2 = (bf16[256,1024]{1,0:T(8,128)(2,1)S(1)}, bf16[256,1024]{1,0:T(8,128)(2,1)S(1)}, u32[]{:S(2)}, u32[]{:S(2)}) collective-permute-start(bf16[256,1024]{1,0:T(8,128)(2,1)S(1)} %slice.158), channel_id=1, source_target_pairs={{0,1},{1,2},{2,3},{3,4},{4,5},{5,6},{6,7},{7,8},{8,9},{9,10},{10,1... | collective-permute-start | bytes 1572872 | tf_op jit(solution)/shard_map/while/body/eval_jaxpr/ppermute | solution.py:20
  13.5 40.8 %collective-permute-start.1 = (bf16[256,1024]{1,0:T(8,128)(2,1)S(1)}, bf16[256,1024]{1,0:T(8,128)(2,1)S(1)}, u32[]{:S(2)}, u32[]{:S(2)}) collective-permute-start(bf16[256,1024]{1,0:T(8,128)(2,1)S(1)} %slice.158), channel_id=1, source_target_pairs={{1,0},{2,1},{3,2},{4,3},{5,4},{6,5},{7,6},{8,7},{9,8},{10,9},{11,1... | collective-permute-start | bytes 1572872 | tf_op jit(solution)/shard_map/while/body/eval_jaxpr/ppermute | solution.py:20
  20.7 33.6 %collective-permute-start = (bf16[256,1024]{1,0:T(8,128)(2,1)S(1)}, bf16[256,1024]{1,0:T(8,128)(2,1)S(1)}, u32[]{:S(2)}, u32[]{:S(2)}) collective-permute-start(bf16[256,1024]{1,0:T(8,128)(2,1)S(1)} %slice.158), channel_id=1, source_target_pairs={{2,0},{3,1},{4,2},{5,3},{6,4},{7,5},{8,6},{9,7},{10,8},{11,9},{12,... | collective-permute-start | bytes 1572872 | tf_op jit(solution)/shard_map/while/body/eval_jaxpr/ppermute | solution.py:20
  97.6 51.4 %collective-permute-start.5 = (f32[256,1024]{1,0:T(8,128)}, f32[256,1024]{1,0:T(8,128)S(1)}, u32[]{:S(2)}, u32[]{:S(2)}) collective-permute-start(f32[256,1024]{1,0:T(8,128)} %bitcast.137), channel_id=1, source_target_pairs={{0,1},{1,2},{2,3},{3,4},{4,5},{5,6},{6,7},{7,8},{8,9},{9,10},{10,1... | collective-permute-start | bytes 3145736 | tf_op jit(solution)/shard_map/while/body/eval_jaxpr/ppermute | solution.py:20
  99.5 49.5 %collective-permute-start.4 = (f32[256,1024]{1,0:T(8,128)}, f32[256,1024]{1,0:T(8,128)}, u32[]{:S(2)}, u32[]{:S(2)}) collective-permute-start(f32[256,1024]{1,0:T(8,128)} %bitcast.136), channel_id=1, source_target_pairs={{0,2},{1,3},{2,4},{3,5},{4,6},{5,7},{6,8},{7,9},{8,10},{9,11},{10,... | collective-permute-start | bytes 3145736 | tf_op jit(solution)/shard_map/while/body/eval_jaxpr/ppermute | solution.py:20
  101.4 88.8 %collective-permute-start.6 = (f32[256,1024]{1,0:T(8,128)}, f32[256,1024]{1,0:T(8,128)}, u32[]{:S(2)}, u32[]{:S(2)}) collective-permute-start(f32[256,1024]{1,0:T(8,128)} %bitcast.138), channel_id=1, source_target_pairs={{1,0},{2,1},{3,2},{4,3},{5,4},{6,5},{7,6},{8,7},{9,8},{10,9},{11,1... | collective-permute-start | bytes 3145736 | tf_op jit(solution)/shard_map/while/body/eval_jaxpr/ppermute | solution.py:20
  109.0 81.2 %collective-permute-start.7 = (f32[256,1024]{1,0:T(8,128)}, f32[256,1024]{1,0:T(8,128)}, u32[]{:S(2)}, u32[]{:S(2)}) collective-permute-start(f32[256,1024]{1,0:T(8,128)} %bitcast.139), channel_id=1, source_target_pairs={{2,0},{3,1},{4,2},{5,3},{6,4},{7,5},{8,6},{9,7},{10,8},{11,9},{12,... | collective-permute-start | bytes 3145736 | tf_op jit(solution)/shard_map/while/body/eval_jaxpr/ppermute | solution.py:20
  114.4 78.1 %copy-start.1 = (bf16[1,4,256,512]{3,2,1,0:T(8,128)(2,1)S(1)}, bf16[1,4,256,512]{3,2,1,0:T(8,128)(2,1)}, u32[]{:S(2)}) copy-start(bf16[1,4,256,512]{3,2,1,0:T(8,128)(2,1)} %get-tuple-element.606) | copy-start | bytes 3145732 | tf_op jit(solution)/shard_map/while
  114.4 78.1 %copy-start.3 = (bf16[512,1536]{1,0:T(8,128)(2,1)S(1)}, bf16[512,1536]{1,0:T(8,128)(2,1)}, u32[]{:S(2)}) copy-start(bf16[512,1536]{1,0:T(8,128)(2,1)} %get-tuple-element.608) | copy-start | bytes 4718596 | tf_op jit(solution)/shard_map/while
  114.4 78.1 %copy-start.4 = (f32[1,512]{1,0:T(1,128)S(1)}, f32[1,512]{1,0:T(1,128)}, u32[]{:S(2)}) copy-start(f32[1,512]{1,0:T(1,128)} %get-tuple-element.607) | copy-start | bytes 6148 | tf_op jit(solution)/shard_map/while
  195.3 5.3 collective-permute-start.8
  202.8 18.3 %copy-start.2 = (bf16[512,512]{1,0:T(8,128)(2,1)S(1)}, bf16[512,512]{1,0:T(8,128)(2,1)}, u32[]{:S(2)}) copy-start(bf16[512,512]{1,0:T(8,128)(2,1)} %get-tuple-element.611) | copy-start | bytes 1572868 | tf_op jit(solution)/shard_map/while
  205.1 20.0 %collective-permute-start.3 = (bf16[256,1024]{1,0:T(8,128)(2,1)S(1)}, bf16[256,1024]{1,0:T(8,128)(2,1)S(1)}, u32[]{:S(2)}, u32[]{:S(2)}) collective-permute-start(bf16[256,1024]{1,0:T(8,128)(2,1)S(1)} %slice.158), channel_id=1, source_target_pairs={{0,2},{1,3},{2,4},{3,5},{4,6},{5,7},{6,8},{7,9},{8,10},{9,11},{10,... | collective-permute-start | bytes 1572872 | tf_op jit(solution)/shard_map/while/body/eval_jaxpr/ppermute | solution.py:20
  207.1 37.6 %collective-permute-start.2 = (bf16[256,1024]{1,0:T(8,128)(2,1)S(1)}, bf16[256,1024]{1,0:T(8,128)(2,1)S(1)}, u32[]{:S(2)}, u32[]{:S(2)}) collective-permute-start(bf16[256,1024]{1,0:T(8,128)(2,1)S(1)} %slice.158), channel_id=1, source_target_pairs={{0,1},{1,2},{2,3},{3,4},{4,5},{5,6},{6,7},{7,8},{8,9},{9,10},{10,1... | collective-permute-start | bytes 1572872 | tf_op jit(solution)/shard_map/while/body/eval_jaxpr/ppermute | solution.py:20
  209.0 39.2 %collective-permute-start.1 = (bf16[256,1024]{1,0:T(8,128)(2,1)S(1)}, bf16[256,1024]{1,0:T(8,128)(2,1)S(1)}, u32[]{:S(2)}, u32[]{:S(2)}) collective-permute-start(bf16[256,1024]{1,0:T(8,128)(2,1)S(1)} %slice.158), channel_id=1, source_target_pairs={{1,0},{2,1},{3,2},{4,3},{5,4},{6,5},{7,6},{8,7},{9,8},{10,9},{11,1... | collective-permute-start | bytes 1572872 | tf_op jit(solution)/shard_map/while/body/eval_jaxpr/ppermute | solution.py:20
  216.6 31.6 %collective-permute-start = (bf16[256,1024]{1,0:T(8,128)(2,1)S(1)}, bf16[256,1024]{1,0:T(8,128)(2,1)S(1)}, u32[]{:S(2)}, u32[]{:S(2)}) collective-permute-start(bf16[256,1024]{1,0:T(8,128)(2,1)S(1)} %slice.158), channel_id=1, source_target_pairs={{2,0},{3,1},{4,2},{5,3},{6,4},{7,5},{8,6},{9,7},{10,8},{11,9},{12,... | collective-permute-start | bytes 1572872 | tf_op jit(solution)/shard_map/while/body/eval_jaxpr/ppermute | solution.py:20
  291.4 53.7 %collective-permute-start.5 = (f32[256,1024]{1,0:T(8,128)}, f32[256,1024]{1,0:T(8,128)S(1)}, u32[]{:S(2)}, u32[]{:S(2)}) collective-permute-start(f32[256,1024]{1,0:T(8,128)} %bitcast.137), channel_id=1, source_target_pairs={{0,1},{1,2},{2,3},{3,4},{4,5},{5,6},{6,7},{7,8},{8,9},{9,10},{10,1... | collective-permute-start | bytes 3145736 | tf_op jit(solution)/shard_map/while/body/eval_jaxpr/ppermute | solution.py:20
  293.4 67.7 %collective-permute-start.4 = (f32[256,1024]{1,0:T(8,128)}, f32[256,1024]{1,0:T(8,128)}, u32[]{:S(2)}, u32[]{:S(2)}) collective-permute-start(f32[256,1024]{1,0:T(8,128)} %bitcast.136), channel_id=1, source_target_pairs={{0,2},{1,3},{2,4},{3,5},{4,6},{5,7},{6,8},{7,9},{8,10},{9,11},{10,... | collective-permute-start | bytes 3145736 | tf_op jit(solution)/shard_map/while/body/eval_jaxpr/ppermute | solution.py:20
  295.3 81.3 %collective-permute-start.6 = (f32[256,1024]{1,0:T(8,128)}, f32[256,1024]{1,0:T(8,128)}, u32[]{:S(2)}, u32[]{:S(2)}) collective-permute-start(f32[256,1024]{1,0:T(8,128)} %bitcast.138), channel_id=1, source_target_pairs={{1,0},{2,1},{3,2},{4,3},{5,4},{6,5},{7,6},{8,7},{9,8},{10,9},{11,1... | collective-permute-start | bytes 3145736 | tf_op jit(solution)/shard_map/while/body/eval_jaxpr/ppermute | solution.py:20
  302.9 73.8 %collective-permute-start.7 = (f32[256,1024]{1,0:T(8,128)}, f32[256,1024]{1,0:T(8,128)}, u32[]{:S(2)}, u32[]{:S(2)}) collective-permute-start(f32[256,1024]{1,0:T(8,128)} %bitcast.139), channel_id=1, source_target_pairs={{2,0},{3,1},{4,2},{5,3},{6,4},{7,5},{8,6},{9,7},{10,8},{11,9},{12,... | collective-permute-start | bytes 3145736 | tf_op jit(solution)/shard_map/while/body/eval_jaxpr/ppermute | solution.py:20
  308.2 70.7 %copy-start.1 = (bf16[1,4,256,512]{3,2,1,0:T(8,128)(2,1)S(1)}, bf16[1,4,256,512]{3,2,1,0:T(8,128)(2,1)}, u32[]{:S(2)}) copy-start(bf16[1,4,256,512]{3,2,1,0:T(8,128)(2,1)} %get-tuple-element.606) | copy-start | bytes 3145732 | tf_op jit(solution)/shard_map/while
  308.3 70.7 %copy-start.3 = (bf16[512,1536]{1,0:T(8,128)(2,1)S(1)}, bf16[512,1536]{1,0:T(8,128)(2,1)}, u32[]{:S(2)}) copy-start(bf16[512,1536]{1,0:T(8,128)(2,1)} %get-tuple-element.608) | copy-start | bytes 4718596 | tf_op jit(solution)/shard_map/while
  308.3 70.7 %copy-start.4 = (f32[1,512]{1,0:T(1,128)S(1)}, f32[1,512]{1,0:T(1,128)}, u32[]{:S(2)}) copy-start(f32[1,512]{1,0:T(1,128)} %get-tuple-element.607) | copy-start | bytes 6148 | tf_op jit(solution)/shard_map/while
  381.8 4.0 collective-permute-start.8
  388.1 18.3 %copy-start.2 = (bf16[512,512]{1,0:T(8,128)(2,1)S(1)}, bf16[512,512]{1,0:T(8,128)(2,1)}, u32[]{:S(2)}) copy-start(bf16[512,512]{1,0:T(8,128)(2,1)} %get-tuple-element.611) | copy-start | bytes 1572868 | tf_op jit(solution)/shard_map/while
  390.3 22.9 %collective-permute-start.3 = (bf16[256,1024]{1,0:T(8,128)(2,1)S(1)}, bf16[256,1024]{1,0:T(8,128)(2,1)S(1)}, u32[]{:S(2)}, u32[]{:S(2)}) collective-permute-start(bf16[256,1024]{1,0:T(8,128)(2,1)S(1)} %slice.158), channel_id=1, source_target_pairs={{0,2},{1,3},{2,4},{3,5},{4,6},{5,7},{6,8},{7,9},{8,10},{9,11},{10,... | collective-permute-start | bytes 1572872 | tf_op jit(solution)/shard_map/while/body/eval_jaxpr/ppermute | solution.py:20
  392.3 36.9 %collective-permute-start.2 = (bf16[256,1024]{1,0:T(8,128)(2,1)S(1)}, bf16[256,1024]{1,0:T(8,128)(2,1)S(1)}, u32[]{:S(2)}, u32[]{:S(2)}) collective-permute-start(bf16[256,1024]{1,0:T(8,128)(2,1)S(1)} %slice.158), channel_id=1, source_target_pairs={{0,1},{1,2},{2,3},{3,4},{4,5},{5,6},{6,7},{7,8},{8,9},{9,10},{10,1... | collective-permute-start | bytes 1572872 | tf_op jit(solution)/shard_map/while/body/eval_jaxpr/ppermute | solution.py:20
  394.2 35.0 %collective-permute-start.1 = (bf16[256,1024]{1,0:T(8,128)(2,1)S(1)}, bf16[256,1024]{1,0:T(8,128)(2,1)S(1)}, u32[]{:S(2)}, u32[]{:S(2)}) collective-permute-start(bf16[256,1024]{1,0:T(8,128)(2,1)S(1)} %slice.158), channel_id=1, source_target_pairs={{1,0},{2,1},{3,2},{4,3},{5,4},{6,5},{7,6},{8,7},{9,8},{10,9},{11,1... | collective-permute-start | bytes 1572872 | tf_op jit(solution)/shard_map/while/body/eval_jaxpr/ppermute | solution.py:20
  401.8 29.7 %collective-permute-start = (bf16[256,1024]{1,0:T(8,128)(2,1)S(1)}, bf16[256,1024]{1,0:T(8,128)(2,1)S(1)}, u32[]{:S(2)}, u32[]{:S(2)}) collective-permute-start(bf16[256,1024]{1,0:T(8,128)(2,1)S(1)} %slice.158), channel_id=1, source_target_pairs={{2,0},{3,1},{4,2},{5,3},{6,4},{7,5},{8,6},{9,7},{10,8},{11,9},{12,... | collective-permute-start | bytes 1572872 | tf_op jit(solution)/shard_map/while/body/eval_jaxpr/ppermute | solution.py:20
  474.8 50.5 %collective-permute-start.5 = (f32[256,1024]{1,0:T(8,128)}, f32[256,1024]{1,0:T(8,128)S(1)}, u32[]{:S(2)}, u32[]{:S(2)}) collective-permute-start(f32[256,1024]{1,0:T(8,128)} %bitcast.137), channel_id=1, source_target_pairs={{0,1},{1,2},{2,3},{3,4},{4,5},{5,6},{6,7},{7,8},{8,9},{9,10},{10,1... | collective-permute-start | bytes 3145736 | tf_op jit(solution)/shard_map/while/body/eval_jaxpr/ppermute | solution.py:20
  476.7 66.4 %collective-permute-start.4 = (f32[256,1024]{1,0:T(8,128)}, f32[256,1024]{1,0:T(8,128)}, u32[]{:S(2)}, u32[]{:S(2)}) collective-permute-start(f32[256,1024]{1,0:T(8,128)} %bitcast.136), channel_id=1, source_target_pairs={{0,2},{1,3},{2,4},{3,5},{4,6},{5,7},{6,8},{7,9},{8,10},{9,11},{10,... | collective-permute-start | bytes 3145736 | tf_op jit(solution)/shard_map/while/body/eval_jaxpr/ppermute | solution.py:20
  478.6 81.6 %collective-permute-start.6 = (f32[256,1024]{1,0:T(8,128)}, f32[256,1024]{1,0:T(8,128)}, u32[]{:S(2)}, u32[]{:S(2)}) collective-permute-start(f32[256,1024]{1,0:T(8,128)} %bitcast.138), channel_id=1, source_target_pairs={{1,0},{2,1},{3,2},{4,3},{5,4},{6,5},{7,6},{8,7},{9,8},{10,9},{11,1... | collective-permute-start | bytes 3145736 | tf_op jit(solution)/shard_map/while/body/eval_jaxpr/ppermute | solution.py:20
  486.2 74.0 %collective-permute-start.7 = (f32[256,1024]{1,0:T(8,128)}, f32[256,1024]{1,0:T(8,128)}, u32[]{:S(2)}, u32[]{:S(2)}) collective-permute-start(f32[256,1024]{1,0:T(8,128)} %bitcast.139), channel_id=1, source_target_pairs={{2,0},{3,1},{4,2},{5,3},{6,4},{7,5},{8,6},{9,7},{10,8},{11,9},{12,... | collective-permute-start | bytes 3145736 | tf_op jit(solution)/shard_map/while/body/eval_jaxpr/ppermute | solution.py:20
  491.7 70.9 %copy-start.1 = (bf16[1,4,256,512]{3,2,1,0:T(8,128)(2,1)S(1)}, bf16[1,4,256,512]{3,2,1,0:T(8,128)(2,1)}, u32[]{:S(2)}) copy-start(bf16[1,4,256,512]{3,2,1,0:T(8,128)(2,1)} %get-tuple-element.606) | copy-start | bytes 3145732 | tf_op jit(solution)/shard_map/while
  491.7 70.9 %copy-start.3 = (bf16[512,1536]{1,0:T(8,128)(2,1)S(1)}, bf16[512,1536]{1,0:T(8,128)(2,1)}, u32[]{:S(2)}) copy-start(bf16[512,1536]{1,0:T(8,128)(2,1)} %get-tuple-element.608) | copy-start | bytes 4718596 | tf_op jit(solution)/shard_map/while
  491.7 70.9 %copy-start.4 = (f32[1,512]{1,0:T(1,128)S(1)}, f32[1,512]{1,0:T(1,128)}, u32[]{:S(2)}) copy-start(f32[1,512]{1,0:T(1,128)} %get-tuple-element.607) | copy-start | bytes 6148 | tf_op jit(solution)/shard_map/while
  565.4 4.5 collective-permute-start.8
  574.4 23.5 %collective-permute-start.3 = (bf16[256,1024]{1,0:T(8,128)(2,1)S(1)}, bf16[256,1024]{1,0:T(8,128)(2,1)S(1)}, u32[]{:S(2)}, u32[]{:S(2)}) collective-permute-start(bf16[256,1024]{1,0:T(8,128)(2,1)S(1)} %slice.158), channel_id=1, source_target_pairs={{0,2},{1,3},{2,4},{3,5},{4,6},{5,7},{6,8},{7,9},{8,10},{9,11},{10,... | collective-permute-start | bytes 1572872 | tf_op jit(solution)/shard_map/while/body/eval_jaxpr/ppermute | solution.py:20
  576.4 37.5 %collective-permute-start.2 = (bf16[256,1024]{1,0:T(8,128)(2,1)S(1)}, bf16[256,1024]{1,0:T(8,128)(2,1)S(1)}, u32[]{:S(2)}, u32[]{:S(2)}) collective-permute-start(bf16[256,1024]{1,0:T(8,128)(2,1)S(1)} %slice.158), channel_id=1, source_target_pairs={{0,1},{1,2},{2,3},{3,4},{4,5},{5,6},{6,7},{7,8},{8,9},{9,10},{10,1... | collective-permute-start | bytes 1572872 | tf_op jit(solution)/shard_map/while/body/eval_jaxpr/ppermute | solution.py:20
  578.3 35.6 %collective-permute-start.1 = (bf16[256,1024]{1,0:T(8,128)(2,1)S(1)}, bf16[256,1024]{1,0:T(8,128)(2,1)S(1)}, u32[]{:S(2)}, u32[]{:S(2)}) collective-permute-start(bf16[256,1024]{1,0:T(8,128)(2,1)S(1)} %slice.158), channel_id=1, source_target_pairs={{1,0},{2,1},{3,2},{4,3},{5,4},{6,5},{7,6},{8,7},{9,8},{10,9},{11,1... | collective-permute-start | bytes 1572872 | tf_op jit(solution)/shard_map/while/body/eval_jaxpr/ppermute | solution.py:20
  585.9 29.7 %collective-permute-start = (bf16[256,1024]{1,0:T(8,128)(2,1)S(1)}, bf16[256,1024]{1,0:T(8,128)(2,1)S(1)}, u32[]{:S(2)}, u32[]{:S(2)}) collective-permute-start(bf16[256,1024]{1,0:T(8,128)(2,1)S(1)} %slice.158), channel_id=1, source_target_pairs={{2,0},{3,1},{4,2},{5,3},{6,4},{7,5},{8,6},{9,7},{10,8},{11,9},{12,... | collective-permute-start | bytes 1572872 | tf_op jit(solution)/shard_map/while/body/eval_jaxpr/ppermute | solution.py:20
  658.6 49.8 %collective-permute-start.5 = (f32[256,1024]{1,0:T(8,128)}, f32[256,1024]{1,0:T(8,128)S(1)}, u32[]{:S(2)}, u32[]{:S(2)}) collective-permute-start(f32[256,1024]{1,0:T(8,128)} %bitcast.137), channel_id=1, source_target_pairs={{0,1},{1,2},{2,3},{3,4},{4,5},{5,6},{6,7},{7,8},{8,9},{9,10},{10,1... | collective-permute-start | bytes 3145736 | tf_op jit(solution)/shard_map/while/body/eval_jaxpr/ppermute | solution.py:20
  660.5 66.2 %collective-permute-start.4 = (f32[256,1024]{1,0:T(8,128)}, f32[256,1024]{1,0:T(8,128)}, u32[]{:S(2)}, u32[]{:S(2)}) collective-permute-start(f32[256,1024]{1,0:T(8,128)} %bitcast.136), channel_id=1, source_target_pairs={{0,2},{1,3},{2,4},{3,5},{4,6},{5,7},{6,8},{7,9},{8,10},{9,11},{10,... | collective-permute-start | bytes 3145736 | tf_op jit(solution)/shard_map/while/body/eval_jaxpr/ppermute | solution.py:20
  662.5 82.6 %collective-permute-start.6 = (f32[256,1024]{1,0:T(8,128)}, f32[256,1024]{1,0:T(8,128)}, u32[]{:S(2)}, u32[]{:S(2)}) collective-permute-start(f32[256,1024]{1,0:T(8,128)} %bitcast.138), channel_id=1, source_target_pairs={{1,0},{2,1},{3,2},{4,3},{5,4},{6,5},{7,6},{8,7},{9,8},{10,9},{11,1... | collective-permute-start | bytes 3145736 | tf_op jit(solution)/shard_map/while/body/eval_jaxpr/ppermute | solution.py:20
  670.1 75.0 %collective-permute-start.7 = (f32[256,1024]{1,0:T(8,128)}, f32[256,1024]{1,0:T(8,128)}, u32[]{:S(2)}, u32[]{:S(2)}) collective-permute-start(f32[256,1024]{1,0:T(8,128)} %bitcast.139), channel_id=1, source_target_pairs={{2,0},{3,1},{4,2},{5,3},{6,4},{7,5},{8,6},{9,7},{10,8},{11,9},{12,... | collective-permute-start | bytes 3145736 | tf_op jit(solution)/shard_map/while/body/eval_jaxpr/ppermute | solution.py:20
  675.7 71.6 %copy-start.1 = (bf16[1,4,256,512]{3,2,1,0:T(8,128)(2,1)S(1)}, bf16[1,4,256,512]{3,2,1,0:T(8,128)(2,1)}, u32[]{:S(2)}) copy-start(bf16[1,4,256,512]{3,2,1,0:T(8,128)(2,1)} %get-tuple-element.606) | copy-start | bytes 3145732 | tf_op jit(solution)/shard_map/while
  675.8 71.6 %copy-start.3 = (bf16[512,1536]{1,0:T(8,128)(2,1)S(1)}, bf16[512,1536]{1,0:T(8,128)(2,1)}, u32[]{:S(2)}) copy-start(bf16[512,1536]{1,0:T(8,128)(2,1)} %get-tuple-element.608) | copy-start | bytes 4718596 | tf_op jit(solution)/shard_map/while
  675.8 71.6 %copy-start.4 = (f32[1,512]{1,0:T(1,128)S(1)}, f32[1,512]{1,0:T(1,128)}, u32[]{:S(2)}) copy-start(f32[1,512]{1,0:T(1,128)} %get-tuple-element.607) | copy-start | bytes 6148 | tf_op jit(solution)/shard_map/while
  750.2 4.3 collective-permute-start.8
  756.8 18.3 %copy-start.2 = (bf16[512,512]{1,0:T(8,128)(2,1)S(1)}, bf16[512,512]{1,0:T(8,128)(2,1)}, u32[]{:S(2)}) copy-start(bf16[512,512]{1,0:T(8,128)(2,1)} %get-tuple-element.611) | copy-start | bytes 1572868 | tf_op jit(solution)/shard_map/while
  759.1 22.8 %collective-permute-start.3 = (bf16[256,1024]{1,0:T(8,128)(2,1)S(1)}, bf16[256,1024]{1,0:T(8,128)(2,1)S(1)}, u32[]{:S(2)}, u32[]{:S(2)}) collective-permute-start(bf16[256,1024]{1,0:T(8,128)(2,1)S(1)} %slice.158), channel_id=1, source_target_pairs={{0,2},{1,3},{2,4},{3,5},{4,6},{5,7},{6,8},{7,9},{8,10},{9,11},{10,... | collective-permute-start | bytes 1572872 | tf_op jit(solution)/shard_map/while/body/eval_jaxpr/ppermute | solution.py:20
  761.0 36.9 %collective-permute-start.2 = (bf16[256,1024]{1,0:T(8,128)(2,1)S(1)}, bf16[256,1024]{1,0:T(8,128)(2,1)S(1)}, u32[]{:S(2)}, u32[]{:S(2)}) collective-permute-start(bf16[256,1024]{1,0:T(8,128)(2,1)S(1)} %slice.158), channel_id=1, source_target_pairs={{0,1},{1,2},{2,3},{3,4},{4,5},{5,6},{6,7},{7,8},{8,9},{9,10},{10,1... | collective-permute-start | bytes 1572872 | tf_op jit(solution)/shard_map/while/body/eval_jaxpr/ppermute | solution.py:20
  762.9 35.0 %collective-permute-start.1 = (bf16[256,1024]{1,0:T(8,128)(2,1)S(1)}, bf16[256,1024]{1,0:T(8,128)(2,1)S(1)}, u32[]{:S(2)}, u32[]{:S(2)}) collective-permute-start(bf16[256,1024]{1,0:T(8,128)(2,1)S(1)} %slice.158), channel_id=1, source_target_pairs={{1,0},{2,1},{3,2},{4,3},{5,4},{6,5},{7,6},{8,7},{9,8},{10,9},{11,1... | collective-permute-start | bytes 1572872 | tf_op jit(solution)/shard_map/while/body/eval_jaxpr/ppermute | solution.py:20
  770.5 29.7 %collective-permute-start = (bf16[256,1024]{1,0:T(8,128)(2,1)S(1)}, bf16[256,1024]{1,0:T(8,128)(2,1)S(1)}, u32[]{:S(2)}, u32[]{:S(2)}) collective-permute-start(bf16[256,1024]{1,0:T(8,128)(2,1)S(1)} %slice.158), channel_id=1, source_target_pairs={{2,0},{3,1},{4,2},{5,3},{6,4},{7,5},{8,6},{9,7},{10,8},{11,9},{12,... | collective-permute-start | bytes 1572872 | tf_op jit(solution)/shard_map/while/body/eval_jaxpr/ppermute | solution.py:20
  843.3 49.9 %collective-permute-start.5 = (f32[256,1024]{1,0:T(8,128)}, f32[256,1024]{1,0:T(8,128)S(1)}, u32[]{:S(2)}, u32[]{:S(2)}) collective-permute-start(f32[256,1024]{1,0:T(8,128)} %bitcast.137), channel_id=1, source_target_pairs={{0,1},{1,2},{2,3},{3,4},{4,5},{5,6},{6,7},{7,8},{8,9},{9,10},{10,1... | collective-permute-start | bytes 3145736 | tf_op jit(solution)/shard_map/while/body/eval_jaxpr/ppermute | solution.py:20
  845.3 66.2 %collective-permute-start.4 = (f32[256,1024]{1,0:T(8,128)}, f32[256,1024]{1,0:T(8,128)}, u32[]{:S(2)}, u32[]{:S(2)}) collective-permute-start(f32[256,1024]{1,0:T(8,128)} %bitcast.136), channel_id=1, source_target_pairs={{0,2},{1,3},{2,4},{3,5},{4,6},{5,7},{6,8},{7,9},{8,10},{9,11},{10,... | collective-permute-start | bytes 3145736 | tf_op jit(solution)/shard_map/while/body/eval_jaxpr/ppermute | solution.py:20
  847.2 81.8 %collective-permute-start.6 = (f32[256,1024]{1,0:T(8,128)}, f32[256,1024]{1,0:T(8,128)}, u32[]{:S(2)}, u32[]{:S(2)}) collective-permute-start(f32[256,1024]{1,0:T(8,128)} %bitcast.138), channel_id=1, source_target_pairs={{1,0},{2,1},{3,2},{4,3},{5,4},{6,5},{7,6},{8,7},{9,8},{10,9},{11,1... | collective-permute-start | bytes 3145736 | tf_op jit(solution)/shard_map/while/body/eval_jaxpr/ppermute | solution.py:20
  854.8 74.2 %collective-permute-start.7 = (f32[256,1024]{1,0:T(8,128)}, f32[256,1024]{1,0:T(8,128)}, u32[]{:S(2)}, u32[]{:S(2)}) collective-permute-start(f32[256,1024]{1,0:T(8,128)} %bitcast.139), channel_id=1, source_target_pairs={{2,0},{3,1},{4,2},{5,3},{6,4},{7,5},{8,6},{9,7},{10,8},{11,9},{12,... | collective-permute-start | bytes 3145736 | tf_op jit(solution)/shard_map/while/body/eval_jaxpr/ppermute | solution.py:20
  860.4 70.9 %copy-start.1 = (bf16[1,4,256,512]{3,2,1,0:T(8,128)(2,1)S(1)}, bf16[1,4,256,512]{3,2,1,0:T(8,128)(2,1)}, u32[]{:S(2)}) copy-start(bf16[1,4,256,512]{3,2,1,0:T(8,128)(2,1)} %get-tuple-element.606) | copy-start | bytes 3145732 | tf_op jit(solution)/shard_map/while
  860.5 70.9 %copy-start.3 = (bf16[512,1536]{1,0:T(8,128)(2,1)S(1)}, bf16[512,1536]{1,0:T(8,128)(2,1)}, u32[]{:S(2)}) copy-start(bf16[512,1536]{1,0:T(8,128)(2,1)} %get-tuple-element.608) | copy-start | bytes 4718596 | tf_op jit(solution)/shard_map/while
  860.5 70.9 %copy-start.4 = (f32[1,512]{1,0:T(1,128)S(1)}, f32[1,512]{1,0:T(1,128)}, u32[]{:S(2)}) copy-start(f32[1,512]{1,0:T(1,128)} %get-tuple-element.607) | copy-start | bytes 6148 | tf_op jit(solution)/shard_map/while
  934.1 4.3 collective-permute-start.8
  (6 other events, 26.0 us)

commit v2 on v1

--- a/solution.py
+++ b/solution.py
@@ -109,10 +109,32 @@
     model_width = cotangent.shape[2]
     weight_in = project_in[0]
     weight_out = project_out[0]
+    weight_pairs = weight_in[:, model_width:]
     gain_row = norm_gains[0]
     block_count = points // BLK
     offsets = [shift_by for shift_by in range(-REACH, REACH + 1) if shift_by != 0]
-    local_lists = neighbour_blocks[0, :, 0, :]
+    lists = neighbour_blocks[0, :, 0, :]
+    owners = lists // block_count
+    within = lists % block_count
+    distance = owners - myself
+    slot = jnp.where(distance < 0, distance + REACH, distance + REACH - 1)
+
+    scaled, inverse, normed = normalize(saved_inputs[0], gain_row)
+    projected = jnp.dot(normed, weight_in, preferred_element_type=jnp.float32).astype(jnp.bfloat16)
+    queries = projected[:, :, :model_width]
+    own_pairs = projected[:, :, model_width:]
+    received = jnp.stack([shifted(normed, "space", -shift_by) for shift_by in offsets])
+    received = received.reshape(len(offsets) * micro_count * block_count, BLK, model_width)
+    micro_ids = lax.broadcasted_iota(jnp.int32, lists.shape, 0)
+    gather_at = (slot * micro_count + micro_ids) * block_count + within
+    fetched_normed = jnp.take(received, gather_at.reshape(-1), axis=0).reshape(
+        micro_count, -1, model_width
+    )
+    fetched_pairs = jnp.dot(
+        fetched_normed, weight_pairs, preferred_element_type=jnp.float32
+    ).astype(jnp.bfloat16)
+    pairs = jnp.concatenate([own_pairs, fetched_pairs], 1)
+    scatter_at = slot * block_count + within
 
     def step(step_index, state_pair):
         incoming, collected = state_pair
@@ -124,49 +146,37 @@
             lax.dynamic_index_in_dim(cotangent, chosen, 0, keepdims=False),
             incoming,
         )
-        points_in = lax.dynamic_index_in_dim(saved_inputs[0], chosen, 0, keepdims=False)
-        block_ids = lax.dynamic_index_in_dim(local_lists, chosen, 0, keepdims=False)
-        owners = block_ids // block_count
-        within = block_ids % block_count
-        distance = owners - myself
-        scaled, inverse, normed = normalize(points_in, gain_row)
-        projected = jnp.dot(normed, weight_in, preferred_element_type=jnp.float32).astype(
-            jnp.bfloat16
-        )
-        queries = projected[:, :model_width]
-        own_pairs = projected[:, model_width:]
+        query_rows = lax.dynamic_index_in_dim(queries, chosen, 0, keepdims=False)
+        pair_rows = lax.dynamic_index_in_dim(pairs, chosen, 0, keepdims=False)
+        scaled_rows = lax.dynamic_index_in_dim(scaled, chosen, 0, keepdims=False)
+        inverse_rows = lax.dynamic_index_in_dim(inverse, chosen, 0, keepdims=False)
+        targets = lax.dynamic_index_in_dim(scatter_at, chosen, 0, keepdims=False)
         grad_attn = jnp.dot(grad_out, weight_out.T, preferred_element_type=jnp.float32).astype(
             jnp.bfloat16
         )
-        received = []
-        for shift_by in offsets:
-            received.append(shifted(own_pairs, "space", -shift_by))
-        window_blocks = jnp.stack(received).reshape(
-            len(offsets) * block_count, BLK, 2 * model_width
-        )
-        position = (
-            jnp.where(distance < 0, distance + REACH, distance + REACH - 1) * block_count + within
-        )
-        fetched = jnp.take(window_blocks, position, axis=0)
-        combined = jnp.concatenate([own_pairs, fetched.reshape(-1, 2 * model_width)], 0)
         grad_query, grad_key, grad_value = attend_backward(
-            queries, combined[:, :model_width], combined[:, model_width:], grad_attn
+            query_rows, pair_rows[:, :model_width], pair_rows[:, model_width:], grad_attn
         )
         grad_pairs = jnp.concatenate([grad_key, grad_value], 1)
         grad_own = grad_pairs[:points]
-        grad_remote = grad_pairs[points:].reshape(-1, BLK, 2 * model_width)
+        grad_remote = jnp.dot(
+            grad_pairs[points:].astype(jnp.bfloat16),
+            weight_pairs.T,
+            preferred_element_type=jnp.float32,
+        ).reshape(-1, BLK, model_width)
         window_grads = (
-            jnp.zeros((len(offsets) * block_count, BLK, 2 * model_width), jnp.float32)
-            .at[position]
+            jnp.zeros((len(offsets) * block_count, BLK, model_width), jnp.float32)
+            .at[targets]
             .add(grad_remote)
         )
-        window_grads = window_grads.reshape(len(offsets), points, 2 * model_width)
-        for slot_index, shift_by in enumerate(offsets):
-            grad_own = grad_own + shifted(window_grads[slot_index], "space", shift_by)
+        window_grads = window_grads.reshape(len(offsets), points, model_width)
         grad_project = jnp.concatenate([grad_query, grad_own], 1).astype(jnp.bfloat16)
         grad_normed = jnp.dot(grad_project, weight_in.T, preferred_element_type=jnp.float32)
+        for slot_index, shift_by in enumerate(offsets):
+            grad_normed = grad_normed + shifted(window_grads[slot_index], "space", shift_by)
         result = (
-            grad_out.astype(jnp.float32) + norm_backward(grad_normed, scaled, inverse, gain_row)
+            grad_out.astype(jnp.float32)
+            + norm_backward(grad_normed, scaled_rows, inverse_rows, gain_row)
         ).astype(jnp.bfloat16)
         collected = jnp.where(
             active, lax.dynamic_update_index_in_dim(collected, result, chosen, 0), collected

time: 941 us -> 603 us (0.64)
  waiting for transfers between devices: 480 us -> 223 us
  starting transfers between devices: 172 us -> 107 us
  other arithmetic: 60.9 us -> 47.8 us
  local copies, waits for them, and re-layouts: 52 us -> 39.1 us
  matrix products: 24.5 us -> 34.8 us
    ppermute x45 -> x29, waiting for transfers between devices: 480 us -> 223 us  [shifted(): return lax.ppermute(x, axis, pairs)]
    ppermute x45 -> x29, starting transfers between devices: 172 us -> 107 us  [shifted(): return lax.ppermute(x, axis, pairs)]
    squeeze x0 -> x11, local copies, waits for them, and re-layouts: none -> 16.8 us  [the longest x5 8.38 us: step(): pair_rows = lax.dynamic_index_in_dim(pairs, chosen, 0, keepdims=False)]
    slice x20 -> x19, local copies, waits for them, and re-layouts: 26.3 us -> 13.9 us  [the longest x5 6.95 us: step(): window_grads[slot_index]]
    dot_general x5, matrix products: 3.66 us -> 15.2 us  [step(): jnp.dot(grad_project, weight_in.T, preferred_element_type=jnp.float32)]
    another operation x5, local copies, waits for them, and re-layouts: 12.4 us -> 1.24 us
  transfers between devices with their start and end apart: 45 -> 29, of which waited for: 34 -> 23; matrix products, arithmetic and copies ran while one was open for 2% -> 2% of each run, Pallas kernels for 0% -> 0%
where the time goes in v2:
time: 603 us; the launch traced here: 600 us
  waiting for transfers between devices  223 us (37%)
  Pallas kernels  148 us (25%)
  starting transfers between devices  107 us (18%)
  other arithmetic  47.8 us (8%)
  local copies, waits for them, and re-layouts  39.1 us (6%)
  matrix products  34.8 us (6%)
    ppermute x29, waiting for transfers between devices, shifted(): return lax.ppermute(x, axis, pairs)  223 us
    pallas_call x5, Pallas kernels, attend_backward(): pl.pallas_call(attention_kernel, grid=(groups,), in_specs=[row_spec, key_...  148 us
    ppermute x29, starting transfers between devices, shifted(): return lax.ppermute(x, axis, pairs)  107 us
    dot_general x5, matrix products, step(): jnp.dot(grad_project, weight_in.T, preferred_element_type=jnp.float32)  15.2 us
    another operation x10, other arithmetic  13.8 us
  transfers between devices with their start and end apart: 29, of which 23 were waited for; matrix products, arithmetic and copies ran while one was open for 2% of the time, Pallas kernels for 0%

profile of v2, /device:TPU:5, one launch (start us, length us, event | category | flops | bytes accessed | tf_op | source)
XLA Modules:
  0.0 600.4 jit_solution(16268283009258036687)
XLA Ops:
  3.3 2.1 fusion.20
  5.4 4.8 collective-permute-start.5
  10.2 2.3 collective-permute-start.6
  12.5 7.2 %collective-permute-start.7 = (bf16[4,256,512]{2,1,0:T(8,128)(2,1)}, bf16[4,256,512]{2,1,0:T(8,128)(2,1)}, u32[]{:S(2)}, u32[]{:S(2)}) collective-permute-start(bf16[4,256,512]{2,1,0:T(8,128)(2,1)} %get-tuple-element.407), channel_id=1, source_target_pairs={{1,0},{2,1},{3,2},{4,3},{5,4},{6,5},{7,6},{8,7},{9,8},{10,9},{11,1... | collective-permute-start | bytes 3145736 | tf_op jit(solution)/shard_map/ppermute | solution.py:20
  19.7 1.9 collective-permute-start.8
  26.9 9.9 %collective-permute-done.5 = bf16[4,256,512]{2,1,0:T(8,128)(2,1)} collective-permute-done((bf16[4,256,512]{2,1,0:T(8,128)(2,1)}, bf16[4,256,512]{2,1,0:T(8,128)(2,1)}, u32[]{:S(2)}, u32[]{:S(2)}) %collective-permute-start.5) | collective-permute-done | bytes 1048608 | tf_op jit(solution)/shard_map/ppermute | solution.py:20
  36.9 22.5 %collective-permute-done.6 = bf16[4,256,512]{2,1,0:T(8,128)(2,1)} collective-permute-done((bf16[4,256,512]{2,1,0:T(8,128)(2,1)}, bf16[4,256,512]{2,1,0:T(8,128)(2,1)}, u32[]{:S(2)}, u32[]{:S(2)}) %collective-permute-start.6) | collective-permute-done | bytes 1048608 | tf_op jit(solution)/shard_map/ppermute | solution.py:20
  59.3 41.5 %collective-permute-done.7 = bf16[4,256,512]{2,1,0:T(8,128)(2,1)} collective-permute-done((bf16[4,256,512]{2,1,0:T(8,128)(2,1)}, bf16[4,256,512]{2,1,0:T(8,128)(2,1)}, u32[]{:S(2)}, u32[]{:S(2)}) %collective-permute-start.7) | collective-permute-done | bytes 1048608 | tf_op jit(solution)/shard_map/ppermute | solution.py:20
  100.8 3.7 pad_maximum_fusion
  104.5 3.8 gather_fusion
  111.3 2.4 pad_maximum_fusion.1
  114.8 485.6 %while.17 = (s32[]{:T(128)}, bf16[256,512]{1,0:T(8,128)(2,1)S(1)}, bf16[4,256,512]{2,1,0:T(8,128)(2,1)}, pred[]{:T(512)}, s32[]{:T(128)}, /*index=5*/bf16[4,256,...) while((s32[]{:T(128)}, bf16[256,512]{1,0:T(8,128)(2,1)S(1)}, ...), condition=%wide.region_6.7_spmd, body=%wide.region_2.6_spmd.sunk | while | flops 6180438016 | bytes 63453860 | solution.py:191
  119.3 2.0 convolution_convert_fusion.4.g_ref
  121.3 29.6 %eval_jaxpr.7 = (f32[256,512]{1,0:T(8,128)}, f32[512,512]{1,0:T(8,128)}, f32[512,512]{1,0:T(8,128)}) custom-call(bf16[256,512]{1,0:T(8,128)(2,1)} %dynamic-slice_bitcast_fusion.4.q_ref, bf16[512,512]{1,0:T(8,128)(2,1)} %get-tuple-element.515.k_ref, bf16[512,512]{1,0:T(8,128)(2,1)} %get-tuple-element.516.v_ref, bf16[256,512]{1,0:T(8,128)(2,1)} %convolution_convert_fusion.4.g_ref), custom_call_target="tpu_custom_call" | custom-call | flops 5368709120 | bytes 4194304 | tf_op jit(solution)/shard_map/while/body/eval_jaxpr/pallas_call | solution.py:85
  159.2 1.9 collective-permute-start.1
  161.1 7.6 %collective-permute-start.2 = (f32[256,512]{1,0:T(8,128)}, f32[256,512]{1,0:T(8,128)}, u32[]{:S(2)}, u32[]{:S(2)}) collective-permute-start(f32[256,512]{1,0:T(8,128)} %bitcast.142), channel_id=1, source_target_pairs={{1,0},{2,1},{3,2},{4,3},{5,4},{6,5},{7,6},{8,7},{9,8},{10,9},{11,1... | collective-permute-start | bytes 1572872 | tf_op jit(solution)/shard_map/while/body/eval_jaxpr/ppermute | solution.py:20
  168.7 3.7 collective-permute-start.3
  173.5 2.8 collective-permute-done
  176.3 17.3 %collective-permute-done.1 = f32[256,512]{1,0:T(8,128)S(1)} collective-permute-done((f32[256,512]{1,0:T(8,128)}, f32[256,512]{1,0:T(8,128)S(1)}, u32[]{:S(2)}, u32[]{:S(2)}) %collective-permute-start.1) | collective-permute-done | bytes 524320 | tf_op jit(solution)/shard_map/while/body/eval_jaxpr/ppermute | solution.py:20
  193.7 8.7 %collective-permute-done.2 = f32[256,512]{1,0:T(8,128)} collective-permute-done((f32[256,512]{1,0:T(8,128)}, f32[256,512]{1,0:T(8,128)}, u32[]{:S(2)}, u32[]{:S(2)}) %collective-permute-start.2) | collective-permute-done | bytes 524320 | tf_op jit(solution)/shard_map/while/body/eval_jaxpr/ppermute | solution.py:20
  202.4 3.0 fusion.64
  205.4 2.4 fusion.65
  207.8 3.7 collective-permute-start.4
  217.4 2.0 convolution_convert_fusion.4.g_ref
  219.4 29.6 %eval_jaxpr.7 = (f32[256,512]{1,0:T(8,128)}, f32[512,512]{1,0:T(8,128)}, f32[512,512]{1,0:T(8,128)}) custom-call(bf16[256,512]{1,0:T(8,128)(2,1)} %dynamic-slice_bitcast_fusion.4.q_ref, bf16[512,512]{1,0:T(8,128)(2,1)} %get-tuple-element.515.k_ref, bf16[512,512]{1,0:T(8,128)(2,1)} %get-tuple-element.516.v_ref, bf16[256,512]{1,0:T(8,128)(2,1)} %convolution_convert_fusion.4.g_ref), custom_call_target="tpu_custom_call" | custom-call | flops 5368709120 | bytes 4194304 | tf_op jit(solution)/shard_map/while/body/eval_jaxpr/pallas_call | solution.py:85
  257.3 1.9 collective-permute-start.1
  259.2 7.6 %collective-permute-start.2 = (f32[256,512]{1,0:T(8,128)}, f32[256,512]{1,0:T(8,128)}, u32[]{:S(2)}, u32[]{:S(2)}) collective-permute-start(f32[256,512]{1,0:T(8,128)} %bitcast.142), channel_id=1, source_target_pairs={{1,0},{2,1},{3,2},{4,3},{5,4},{6,5},{7,6},{8,7},{9,8},{10,9},{11,1... | collective-permute-start | bytes 1572872 | tf_op jit(solution)/shard_map/while/body/eval_jaxpr/ppermute | solution.py:20
  266.8 3.7 collective-permute-start.3
  271.6 4.0 collective-permute-done
  275.6 17.9 %collective-permute-done.1 = f32[256,512]{1,0:T(8,128)S(1)} collective-permute-done((f32[256,512]{1,0:T(8,128)}, f32[256,512]{1,0:T(8,128)S(1)}, u32[]{:S(2)}, u32[]{:S(2)}) %collective-permute-start.1) | collective-permute-done | bytes 524320 | tf_op jit(solution)/shard_map/while/body/eval_jaxpr/ppermute | solution.py:20
  293.5 4.7 collective-permute-done.2
  298.2 3.0 fusion.64
  301.3 2.4 fusion.65
  303.7 2.8 collective-permute-start.4
  312.3 2.0 convolution_convert_fusion.4.g_ref
  314.3 29.6 %eval_jaxpr.7 = (f32[256,512]{1,0:T(8,128)}, f32[512,512]{1,0:T(8,128)}, f32[512,512]{1,0:T(8,128)}) custom-call(bf16[256,512]{1,0:T(8,128)(2,1)} %dynamic-slice_bitcast_fusion.4.q_ref, bf16[512,512]{1,0:T(8,128)(2,1)} %get-tuple-element.515.k_ref, bf16[512,512]{1,0:T(8,128)(2,1)} %get-tuple-element.516.v_ref, bf16[256,512]{1,0:T(8,128)(2,1)} %convolution_convert_fusion.4.g_ref), custom_call_target="tpu_custom_call" | custom-call | flops 5368709120 | bytes 4194304 | tf_op jit(solution)/shard_map/while/body/eval_jaxpr/pallas_call | solution.py:85
  354.1 7.6 %collective-permute-start.2 = (f32[256,512]{1,0:T(8,128)}, f32[256,512]{1,0:T(8,128)}, u32[]{:S(2)}, u32[]{:S(2)}) collective-permute-start(f32[256,512]{1,0:T(8,128)} %bitcast.142), channel_id=1, source_target_pairs={{1,0},{2,1},{3,2},{4,3},{5,4},{6,5},{7,6},{8,7},{9,8},{10,9},{11,1... | collective-permute-start | bytes 1572872 | tf_op jit(solution)/shard_map/while/body/eval_jaxpr/ppermute | solution.py:20
  361.7 3.7 collective-permute-start.3
  366.6 4.0 collective-permute-done
  370.6 15.7 %collective-permute-done.1 = f32[256,512]{1,0:T(8,128)S(1)} collective-permute-done((f32[256,512]{1,0:T(8,128)}, f32[256,512]{1,0:T(8,128)S(1)}, u32[]{:S(2)}, u32[]{:S(2)}) %collective-permute-start.1) | collective-permute-done | bytes 524320 | tf_op jit(solution)/shard_map/while/body/eval_jaxpr/ppermute | solution.py:20
  386.3 10.1 %collective-permute-done.2 = f32[256,512]{1,0:T(8,128)} collective-permute-done((f32[256,512]{1,0:T(8,128)}, f32[256,512]{1,0:T(8,128)}, u32[]{:S(2)}, u32[]{:S(2)}) %collective-permute-start.2) | collective-permute-done | bytes 524320 | tf_op jit(solution)/shard_map/while/body/eval_jaxpr/ppermute | solution.py:20
  396.4 3.0 fusion.64
  399.4 2.4 fusion.65
  401.8 2.8 collective-permute-start.4
  410.4 2.0 convolution_convert_fusion.4.g_ref
  412.4 29.6 %eval_jaxpr.7 = (f32[256,512]{1,0:T(8,128)}, f32[512,512]{1,0:T(8,128)}, f32[512,512]{1,0:T(8,128)}) custom-call(bf16[256,512]{1,0:T(8,128)(2,1)} %dynamic-slice_bitcast_fusion.4.q_ref, bf16[512,512]{1,0:T(8,128)(2,1)} %get-tuple-element.515.k_ref, bf16[512,512]{1,0:T(8,128)(2,1)} %get-tuple-element.516.v_ref, bf16[256,512]{1,0:T(8,128)(2,1)} %convolution_convert_fusion.4.g_ref), custom_call_target="tpu_custom_call" | custom-call | flops 5368709120 | bytes 4194304 | tf_op jit(solution)/shard_map/while/body/eval_jaxpr/pallas_call | solution.py:85
  452.3 7.6 %collective-permute-start.2 = (f32[256,512]{1,0:T(8,128)}, f32[256,512]{1,0:T(8,128)}, u32[]{:S(2)}, u32[]{:S(2)}) collective-permute-start(f32[256,512]{1,0:T(8,128)} %bitcast.142), channel_id=1, source_target_pairs={{1,0},{2,1},{3,2},{4,3},{5,4},{6,5},{7,6},{8,7},{9,8},{10,9},{11,1... | collective-permute-start | bytes 1572872 | tf_op jit(solution)/shard_map/while/body/eval_jaxpr/ppermute | solution.py:20
  459.9 3.7 collective-permute-start.3
  464.7 3.9 collective-permute-done
  468.6 18.1 %collective-permute-done.1 = f32[256,512]{1,0:T(8,128)S(1)} collective-permute-done((f32[256,512]{1,0:T(8,128)}, f32[256,512]{1,0:T(8,128)S(1)}, u32[]{:S(2)}, u32[]{:S(2)}) %collective-permute-start.1) | collective-permute-done | bytes 524320 | tf_op jit(solution)/shard_map/while/body/eval_jaxpr/ppermute | solution.py:20
  486.7 7.7 %collective-permute-done.2 = f32[256,512]{1,0:T(8,128)} collective-permute-done((f32[256,512]{1,0:T(8,128)}, f32[256,512]{1,0:T(8,128)}, u32[]{:S(2)}, u32[]{:S(2)}) %collective-permute-start.2) | collective-permute-done | bytes 524320 | tf_op jit(solution)/shard_map/while/body/eval_jaxpr/ppermute | solution.py:20
  494.5 3.0 fusion.64
  497.6 2.4 fusion.65
  500.0 2.8 collective-permute-start.4
  508.5 2.0 convolution_convert_fusion.4.g_ref
  510.5 29.6 %eval_jaxpr.7 = (f32[256,512]{1,0:T(8,128)}, f32[512,512]{1,0:T(8,128)}, f32[512,512]{1,0:T(8,128)}) custom-call(bf16[256,512]{1,0:T(8,128)(2,1)} %dynamic-slice_bitcast_fusion.4.q_ref, bf16[512,512]{1,0:T(8,128)(2,1)} %get-tuple-element.515.k_ref, bf16[512,512]{1,0:T(8,128)(2,1)} %get-tuple-element.516.v_ref, bf16[256,512]{1,0:T(8,128)(2,1)} %convolution_convert_fusion.4.g_ref), custom_call_target="tpu_custom_call" | custom-call | flops 5368709120 | bytes 4194304 | tf_op jit(solution)/shard_map/while/body/eval_jaxpr/pallas_call | solution.py:85
  550.4 7.6 %collective-permute-start.2 = (f32[256,512]{1,0:T(8,128)}, f32[256,512]{1,0:T(8,128)}, u32[]{:S(2)}, u32[]{:S(2)}) collective-permute-start(f32[256,512]{1,0:T(8,128)} %bitcast.142), channel_id=1, source_target_pairs={{1,0},{2,1},{3,2},{4,3},{5,4},{6,5},{7,6},{8,7},{9,8},{10,9},{11,1... | collective-permute-start | bytes 1572872 | tf_op jit(solution)/shard_map/while/body/eval_jaxpr/ppermute | solution.py:20
  558.0 3.7 collective-permute-start.3
  562.8 3.9 collective-permute-done
  566.7 18.0 %collective-permute-done.1 = f32[256,512]{1,0:T(8,128)S(1)} collective-permute-done((f32[256,512]{1,0:T(8,128)}, f32[256,512]{1,0:T(8,128)S(1)}, u32[]{:S(2)}, u32[]{:S(2)}) %collective-permute-start.1) | collective-permute-done | bytes 524320 | tf_op jit(solution)/shard_map/while/body/eval_jaxpr/ppermute | solution.py:20
  584.7 6.0 %collective-permute-done.2 = f32[256,512]{1,0:T(8,128)} collective-permute-done((f32[256,512]{1,0:T(8,128)}, f32[256,512]{1,0:T(8,128)}, u32[]{:S(2)}, u32[]{:S(2)}) %collective-permute-start.2) | collective-permute-done | bytes 524320 | tf_op jit(solution)/shard_map/while/body/eval_jaxpr/ppermute | solution.py:20
  590.8 3.0 fusion.64
  593.8 2.4 fusion.65
  596.3 2.8 collective-permute-start.4
  (180 shorter events, 94.5 us)
Async XLA Ops:
  0.0 3.2 copy-start.8
  0.0 3.3 copy-start.10
  3.3 18.4 %copy-start = (bf16[1,512,1536]{2,1,0:T(8,128)(2,1)S(1)}, bf16[1,512,1536]{2,1,0:T(8,128)(2,1)}, u32[]{:S(2)}) copy-start(bf16[1,512,1536]{2,1,0:T(8,128)(2,1)} %param.9) | copy-start | bytes 4718596
  5.4 31.5 %collective-permute-start.5 = (bf16[4,256,512]{2,1,0:T(8,128)(2,1)}, bf16[4,256,512]{2,1,0:T(8,128)(2,1)}, u32[]{:S(2)}, u32[]{:S(2)}) collective-permute-start(bf16[4,256,512]{2,1,0:T(8,128)(2,1)} %get-tuple-element.407), channel_id=1, source_target_pairs={{0,2},{1,3},{2,4},{3,5},{4,6},{5,7},{6,8},{7,9},{8,10},{9,11},{10,... | collective-permute-start | bytes 3145736 | tf_op jit(solution)/shard_map/ppermute | solution.py:20
  10.2 49.2 %collective-permute-start.6 = (bf16[4,256,512]{2,1,0:T(8,128)(2,1)}, bf16[4,256,512]{2,1,0:T(8,128)(2,1)}, u32[]{:S(2)}, u32[]{:S(2)}) collective-permute-start(bf16[4,256,512]{2,1,0:T(8,128)(2,1)} %get-tuple-element.407), channel_id=1, source_target_pairs={{0,1},{1,2},{2,3},{3,4},{4,5},{5,6},{6,7},{7,8},{8,9},{9,10},{10,1... | collective-permute-start | bytes 3145736 | tf_op jit(solution)/shard_map/ppermute | solution.py:20
  12.5 88.3 %collective-permute-start.7 = (bf16[4,256,512]{2,1,0:T(8,128)(2,1)}, bf16[4,256,512]{2,1,0:T(8,128)(2,1)}, u32[]{:S(2)}, u32[]{:S(2)}) collective-permute-start(bf16[4,256,512]{2,1,0:T(8,128)(2,1)} %get-tuple-element.407), channel_id=1, source_target_pairs={{1,0},{2,1},{3,2},{4,3},{5,4},{6,5},{7,6},{8,7},{9,8},{10,9},{11,1... | collective-permute-start | bytes 3145736 | tf_op jit(solution)/shard_map/ppermute | solution.py:20
  19.7 81.1 %collective-permute-start.8 = (bf16[4,256,512]{2,1,0:T(8,128)(2,1)}, bf16[4,256,512]{2,1,0:T(8,128)(2,1)}, u32[]{:S(2)}, u32[]{:S(2)}) collective-permute-start(bf16[4,256,512]{2,1,0:T(8,128)(2,1)} %get-tuple-element.407), channel_id=1, source_target_pairs={{2,0},{3,1},{4,2},{5,3},{6,4},{7,5},{8,6},{9,7},{10,8},{11,9},{12,... | collective-permute-start | bytes 3145736 | tf_op jit(solution)/shard_map/ppermute | solution.py:20
  23.5 1.7 copy-start.9
  111.3 3.5 copy-start.6
  114.8 37.7 %copy-start.2 = (bf16[512,1024]{1,0:T(8,128)(2,1)}, bf16[512,1024]{1,0:T(8,128)(2,1)S(1)}, u32[]{:S(2)}) copy-start(bf16[512,1024]{1,0:T(8,128)(2,1)S(1)} %get-tuple-element.583) | copy-start | bytes 3145732 | tf_op jit(solution)/shard_map/while
  157.3 19.1 %collective-permute-start = (f32[256,512]{1,0:T(8,128)}, f32[256,512]{1,0:T(8,128)S(1)}, u32[]{:S(2)}, u32[]{:S(2)}) collective-permute-start(f32[256,512]{1,0:T(8,128)} %bitcast.140), channel_id=1, source_target_pairs={{0,2},{1,3},{2,4},{3,5},{4,6},{5,7},{6,8},{7,9},{8,10},{9,11},{10,... | collective-permute-start | bytes 1572872 | tf_op jit(solution)/shard_map/while/body/eval_jaxpr/ppermute | solution.py:20
  159.2 34.5 %collective-permute-start.1 = (f32[256,512]{1,0:T(8,128)}, f32[256,512]{1,0:T(8,128)S(1)}, u32[]{:S(2)}, u32[]{:S(2)}) collective-permute-start(f32[256,512]{1,0:T(8,128)} %bitcast.141), channel_id=1, source_target_pairs={{0,1},{1,2},{2,3},{3,4},{4,5},{5,6},{6,7},{7,8},{8,9},{9,10},{10,1... | collective-permute-start | bytes 1572872 | tf_op jit(solution)/shard_map/while/body/eval_jaxpr/ppermute | solution.py:20
  161.1 41.2 %collective-permute-start.2 = (f32[256,512]{1,0:T(8,128)}, f32[256,512]{1,0:T(8,128)}, u32[]{:S(2)}, u32[]{:S(2)}) collective-permute-start(f32[256,512]{1,0:T(8,128)} %bitcast.142), channel_id=1, source_target_pairs={{1,0},{2,1},{3,2},{4,3},{5,4},{6,5},{7,6},{8,7},{9,8},{10,9},{11,1... | collective-permute-start | bytes 1572872 | tf_op jit(solution)/shard_map/while/body/eval_jaxpr/ppermute | solution.py:20
  168.7 33.6 %collective-permute-start.3 = (f32[256,512]{1,0:T(8,128)}, f32[256,512]{1,0:T(8,128)}, u32[]{:S(2)}, u32[]{:S(2)}) collective-permute-start(f32[256,512]{1,0:T(8,128)} %bitcast.143), channel_id=1, source_target_pairs={{2,0},{3,1},{4,2},{5,3},{6,4},{7,5},{8,6},{9,7},{10,8},{11,9},{12,... | collective-permute-start | bytes 1572872 | tf_op jit(solution)/shard_map/while/body/eval_jaxpr/ppermute | solution.py:20
  176.3 26.0 %copy-start.4 = (f32[256,512]{1,0:T(8,128)}, f32[256,512]{1,0:T(8,128)S(1)}, u32[]{:S(2)}) copy-start(f32[256,512]{1,0:T(8,128)S(1)} %collective-permute-done) | copy-start | bytes 1572868 | tf_op jit(solution)/shard_map/while
  193.7 8.7 %copy-start.5 = (f32[256,512]{1,0:T(8,128)}, f32[256,512]{1,0:T(8,128)S(1)}, u32[]{:S(2)}) copy-start(f32[256,512]{1,0:T(8,128)S(1)} %collective-permute-done.1) | copy-start | bytes 1572868 | tf_op jit(solution)/shard_map/while
  202.3 10.6 %copy-start.3 = (bf16[512,1024]{1,0:T(8,128)(2,1)S(1)}, bf16[512,1024]{1,0:T(8,128)(2,1)}, u32[]{:S(2)}) copy-start(bf16[512,1024]{1,0:T(8,128)(2,1)} %copy-done.2) | copy-start | bytes 3145732 | tf_op jit(solution)/shard_map/while
  205.4 7.5 %copy-start.1 = (bf16[1,512,1536]{2,1,0:T(8,128)(2,1)S(1)}, bf16[1,512,1536]{2,1,0:T(8,128)(2,1)}, u32[]{:S(2)}) copy-start(bf16[1,512,1536]{2,1,0:T(8,128)(2,1)} %get-tuple-element.611) | copy-start | bytes 4718596 | tf_op jit(solution)/shard_map/while
  205.4 7.5 %copy-start.7 = (bf16[1,512,512]{2,1,0:T(8,128)(2,1)S(1)}, bf16[1,512,512]{2,1,0:T(8,128)(2,1)}, u32[]{:S(2)}) copy-start(bf16[1,512,512]{2,1,0:T(8,128)(2,1)} %get-tuple-element.636) | copy-start | bytes 1572868 | tf_op jit(solution)/shard_map/while
  207.8 5.1 collective-permute-start.4
  212.9 37.7 %copy-start.2 = (bf16[512,1024]{1,0:T(8,128)(2,1)}, bf16[512,1024]{1,0:T(8,128)(2,1)S(1)}, u32[]{:S(2)}) copy-start(bf16[512,1024]{1,0:T(8,128)(2,1)S(1)} %get-tuple-element.583) | copy-start | bytes 3145732 | tf_op jit(solution)/shard_map/while
  255.4 20.2 %collective-permute-start = (f32[256,512]{1,0:T(8,128)}, f32[256,512]{1,0:T(8,128)S(1)}, u32[]{:S(2)}, u32[]{:S(2)}) collective-permute-start(f32[256,512]{1,0:T(8,128)} %bitcast.140), channel_id=1, source_target_pairs={{0,2},{1,3},{2,4},{3,5},{4,6},{5,7},{6,8},{7,9},{8,10},{9,11},{10,... | collective-permute-start | bytes 1572872 | tf_op jit(solution)/shard_map/while/body/eval_jaxpr/ppermute | solution.py:20
  257.3 36.2 %collective-permute-start.1 = (f32[256,512]{1,0:T(8,128)}, f32[256,512]{1,0:T(8,128)S(1)}, u32[]{:S(2)}, u32[]{:S(2)}) collective-permute-start(f32[256,512]{1,0:T(8,128)} %bitcast.141), channel_id=1, source_target_pairs={{0,1},{1,2},{2,3},{3,4},{4,5},{5,6},{6,7},{7,8},{8,9},{9,10},{10,1... | collective-permute-start | bytes 1572872 | tf_op jit(solution)/shard_map/while/body/eval_jaxpr/ppermute | solution.py:20
  259.2 39.0 %collective-permute-start.2 = (f32[256,512]{1,0:T(8,128)}, f32[256,512]{1,0:T(8,128)}, u32[]{:S(2)}, u32[]{:S(2)}) collective-permute-start(f32[256,512]{1,0:T(8,128)} %bitcast.142), channel_id=1, source_target_pairs={{1,0},{2,1},{3,2},{4,3},{5,4},{6,5},{7,6},{8,7},{9,8},{10,9},{11,1... | collective-permute-start | bytes 1572872 | tf_op jit(solution)/shard_map/while/body/eval_jaxpr/ppermute | solution.py:20
  266.8 31.4 %collective-permute-start.3 = (f32[256,512]{1,0:T(8,128)}, f32[256,512]{1,0:T(8,128)}, u32[]{:S(2)}, u32[]{:S(2)}) collective-permute-start(f32[256,512]{1,0:T(8,128)} %bitcast.143), channel_id=1, source_target_pairs={{2,0},{3,1},{4,2},{5,3},{6,4},{7,5},{8,6},{9,7},{10,8},{11,9},{12,... | collective-permute-start | bytes 1572872 | tf_op jit(solution)/shard_map/while/body/eval_jaxpr/ppermute | solution.py:20
  275.6 22.6 %copy-start.4 = (f32[256,512]{1,0:T(8,128)}, f32[256,512]{1,0:T(8,128)S(1)}, u32[]{:S(2)}) copy-start(f32[256,512]{1,0:T(8,128)S(1)} %collective-permute-done) | copy-start | bytes 1572868 | tf_op jit(solution)/shard_map/while
  293.5 4.7 copy-start.5
  298.2 9.7 %copy-start.3 = (bf16[512,1024]{1,0:T(8,128)(2,1)S(1)}, bf16[512,1024]{1,0:T(8,128)(2,1)}, u32[]{:S(2)}) copy-start(bf16[512,1024]{1,0:T(8,128)(2,1)} %copy-done.2) | copy-start | bytes 3145732 | tf_op jit(solution)/shard_map/while
  301.2 6.6 %copy-start.1 = (bf16[1,512,1536]{2,1,0:T(8,128)(2,1)S(1)}, bf16[1,512,1536]{2,1,0:T(8,128)(2,1)}, u32[]{:S(2)}) copy-start(bf16[1,512,1536]{2,1,0:T(8,128)(2,1)} %get-tuple-element.611) | copy-start | bytes 4718596 | tf_op jit(solution)/shard_map/while
  301.3 6.6 %copy-start.7 = (bf16[1,512,512]{2,1,0:T(8,128)(2,1)S(1)}, bf16[1,512,512]{2,1,0:T(8,128)(2,1)}, u32[]{:S(2)}) copy-start(bf16[1,512,512]{2,1,0:T(8,128)(2,1)} %get-tuple-element.636) | copy-start | bytes 1572868 | tf_op jit(solution)/shard_map/while
  303.7 4.2 collective-permute-start.4
  307.9 37.7 %copy-start.2 = (bf16[512,1024]{1,0:T(8,128)(2,1)}, bf16[512,1024]{1,0:T(8,128)(2,1)S(1)}, u32[]{:S(2)}) copy-start(bf16[512,1024]{1,0:T(8,128)(2,1)S(1)} %get-tuple-element.583) | copy-start | bytes 3145732 | tf_op jit(solution)/shard_map/while
  350.3 20.3 %collective-permute-start = (f32[256,512]{1,0:T(8,128)}, f32[256,512]{1,0:T(8,128)S(1)}, u32[]{:S(2)}, u32[]{:S(2)}) collective-permute-start(f32[256,512]{1,0:T(8,128)} %bitcast.140), channel_id=1, source_target_pairs={{0,2},{1,3},{2,4},{3,5},{4,6},{5,7},{6,8},{7,9},{8,10},{9,11},{10,... | collective-permute-start | bytes 1572872 | tf_op jit(solution)/shard_map/while/body/eval_jaxpr/ppermute | solution.py:20
  352.2 34.1 %collective-permute-start.1 = (f32[256,512]{1,0:T(8,128)}, f32[256,512]{1,0:T(8,128)S(1)}, u32[]{:S(2)}, u32[]{:S(2)}) collective-permute-start(f32[256,512]{1,0:T(8,128)} %bitcast.141), channel_id=1, source_target_pairs={{0,1},{1,2},{2,3},{3,4},{4,5},{5,6},{6,7},{7,8},{8,9},{9,10},{10,1... | collective-permute-start | bytes 1572872 | tf_op jit(solution)/shard_map/while/body/eval_jaxpr/ppermute | solution.py:20
  354.1 42.2 %collective-permute-start.2 = (f32[256,512]{1,0:T(8,128)}, f32[256,512]{1,0:T(8,128)}, u32[]{:S(2)}, u32[]{:S(2)}) collective-permute-start(f32[256,512]{1,0:T(8,128)} %bitcast.142), channel_id=1, source_target_pairs={{1,0},{2,1},{3,2},{4,3},{5,4},{6,5},{7,6},{8,7},{9,8},{10,9},{11,1... | collective-permute-start | bytes 1572872 | tf_op jit(solution)/shard_map/while/body/eval_jaxpr/ppermute | solution.py:20
  361.7 34.6 %collective-permute-start.3 = (f32[256,512]{1,0:T(8,128)}, f32[256,512]{1,0:T(8,128)}, u32[]{:S(2)}, u32[]{:S(2)}) collective-permute-start(f32[256,512]{1,0:T(8,128)} %bitcast.143), channel_id=1, source_target_pairs={{2,0},{3,1},{4,2},{5,3},{6,4},{7,5},{8,6},{9,7},{10,8},{11,9},{12,... | collective-permute-start | bytes 1572872 | tf_op jit(solution)/shard_map/while/body/eval_jaxpr/ppermute | solution.py:20
  370.6 25.8 %copy-start.4 = (f32[256,512]{1,0:T(8,128)}, f32[256,512]{1,0:T(8,128)S(1)}, u32[]{:S(2)}) copy-start(f32[256,512]{1,0:T(8,128)S(1)} %collective-permute-done) | copy-start | bytes 1572868 | tf_op jit(solution)/shard_map/while
  386.3 10.1 %copy-start.5 = (f32[256,512]{1,0:T(8,128)}, f32[256,512]{1,0:T(8,128)S(1)}, u32[]{:S(2)}) copy-start(f32[256,512]{1,0:T(8,128)S(1)} %collective-permute-done.1) | copy-start | bytes 1572868 | tf_op jit(solution)/shard_map/while
  396.4 9.7 %copy-start.3 = (bf16[512,1024]{1,0:T(8,128)(2,1)S(1)}, bf16[512,1024]{1,0:T(8,128)(2,1)}, u32[]{:S(2)}) copy-start(bf16[512,1024]{1,0:T(8,128)(2,1)} %copy-done.2) | copy-start | bytes 3145732 | tf_op jit(solution)/shard_map/while
  399.4 6.6 %copy-start.1 = (bf16[1,512,1536]{2,1,0:T(8,128)(2,1)S(1)}, bf16[1,512,1536]{2,1,0:T(8,128)(2,1)}, u32[]{:S(2)}) copy-start(bf16[1,512,1536]{2,1,0:T(8,128)(2,1)} %get-tuple-element.611) | copy-start | bytes 4718596 | tf_op jit(solution)/shard_map/while
  399.4 6.6 %copy-start.7 = (bf16[1,512,512]{2,1,0:T(8,128)(2,1)S(1)}, bf16[1,512,512]{2,1,0:T(8,128)(2,1)}, u32[]{:S(2)}) copy-start(bf16[1,512,512]{2,1,0:T(8,128)(2,1)} %get-tuple-element.636) | copy-start | bytes 1572868 | tf_op jit(solution)/shard_map/while
  401.8 4.2 collective-permute-start.4
  406.0 37.7 %copy-start.2 = (bf16[512,1024]{1,0:T(8,128)(2,1)}, bf16[512,1024]{1,0:T(8,128)(2,1)S(1)}, u32[]{:S(2)}) copy-start(bf16[512,1024]{1,0:T(8,128)(2,1)S(1)} %get-tuple-element.583) | copy-start | bytes 3145732 | tf_op jit(solution)/shard_map/while
  448.5 20.2 %collective-permute-start = (f32[256,512]{1,0:T(8,128)}, f32[256,512]{1,0:T(8,128)S(1)}, u32[]{:S(2)}, u32[]{:S(2)}) collective-permute-start(f32[256,512]{1,0:T(8,128)} %bitcast.140), channel_id=1, source_target_pairs={{0,2},{1,3},{2,4},{3,5},{4,6},{5,7},{6,8},{7,9},{8,10},{9,11},{10,... | collective-permute-start | bytes 1572872 | tf_op jit(solution)/shard_map/while/body/eval_jaxpr/ppermute | solution.py:20
  450.4 36.4 %collective-permute-start.1 = (f32[256,512]{1,0:T(8,128)}, f32[256,512]{1,0:T(8,128)S(1)}, u32[]{:S(2)}, u32[]{:S(2)}) collective-permute-start(f32[256,512]{1,0:T(8,128)} %bitcast.141), channel_id=1, source_target_pairs={{0,1},{1,2},{2,3},{3,4},{4,5},{5,6},{6,7},{7,8},{8,9},{9,10},{10,1... | collective-permute-start | bytes 1572872 | tf_op jit(solution)/shard_map/while/body/eval_jaxpr/ppermute | solution.py:20
  452.3 42.2 %collective-permute-start.2 = (f32[256,512]{1,0:T(8,128)}, f32[256,512]{1,0:T(8,128)}, u32[]{:S(2)}, u32[]{:S(2)}) collective-permute-start(f32[256,512]{1,0:T(8,128)} %bitcast.142), channel_id=1, source_target_pairs={{1,0},{2,1},{3,2},{4,3},{5,4},{6,5},{7,6},{8,7},{9,8},{10,9},{11,1... | collective-permute-start | bytes 1572872 | tf_op jit(solution)/shard_map/while/body/eval_jaxpr/ppermute | solution.py:20
  459.9 34.6 %collective-permute-start.3 = (f32[256,512]{1,0:T(8,128)}, f32[256,512]{1,0:T(8,128)}, u32[]{:S(2)}, u32[]{:S(2)}) collective-permute-start(f32[256,512]{1,0:T(8,128)} %bitcast.143), channel_id=1, source_target_pairs={{2,0},{3,1},{4,2},{5,3},{6,4},{7,5},{8,6},{9,7},{10,8},{11,9},{12,... | collective-permute-start | bytes 1572872 | tf_op jit(solution)/shard_map/while/body/eval_jaxpr/ppermute | solution.py:20
  468.6 25.8 %copy-start.4 = (f32[256,512]{1,0:T(8,128)}, f32[256,512]{1,0:T(8,128)S(1)}, u32[]{:S(2)}) copy-start(f32[256,512]{1,0:T(8,128)S(1)} %collective-permute-done) | copy-start | bytes 1572868 | tf_op jit(solution)/shard_map/while
  486.7 7.7 %copy-start.5 = (f32[256,512]{1,0:T(8,128)}, f32[256,512]{1,0:T(8,128)S(1)}, u32[]{:S(2)}) copy-start(f32[256,512]{1,0:T(8,128)S(1)} %collective-permute-done.1) | copy-start | bytes 1572868 | tf_op jit(solution)/shard_map/while
  494.5 9.6 %copy-start.3 = (bf16[512,1024]{1,0:T(8,128)(2,1)S(1)}, bf16[512,1024]{1,0:T(8,128)(2,1)}, u32[]{:S(2)}) copy-start(bf16[512,1024]{1,0:T(8,128)(2,1)} %copy-done.2) | copy-start | bytes 3145732 | tf_op jit(solution)/shard_map/while
  497.5 6.6 %copy-start.1 = (bf16[1,512,1536]{2,1,0:T(8,128)(2,1)S(1)}, bf16[1,512,1536]{2,1,0:T(8,128)(2,1)}, u32[]{:S(2)}) copy-start(bf16[1,512,1536]{2,1,0:T(8,128)(2,1)} %get-tuple-element.611) | copy-start | bytes 4718596 | tf_op jit(solution)/shard_map/while
  497.5 6.6 %copy-start.7 = (bf16[1,512,512]{2,1,0:T(8,128)(2,1)S(1)}, bf16[1,512,512]{2,1,0:T(8,128)(2,1)}, u32[]{:S(2)}) copy-start(bf16[1,512,512]{2,1,0:T(8,128)(2,1)} %get-tuple-element.636) | copy-start | bytes 1572868 | tf_op jit(solution)/shard_map/while
  500.0 4.1 collective-permute-start.4
  504.1 37.7 %copy-start.2 = (bf16[512,1024]{1,0:T(8,128)(2,1)}, bf16[512,1024]{1,0:T(8,128)(2,1)S(1)}, u32[]{:S(2)}) copy-start(bf16[512,1024]{1,0:T(8,128)(2,1)S(1)} %get-tuple-element.583) | copy-start | bytes 3145732 | tf_op jit(solution)/shard_map/while
  546.5 20.2 %collective-permute-start = (f32[256,512]{1,0:T(8,128)}, f32[256,512]{1,0:T(8,128)S(1)}, u32[]{:S(2)}, u32[]{:S(2)}) collective-permute-start(f32[256,512]{1,0:T(8,128)} %bitcast.140), channel_id=1, source_target_pairs={{0,2},{1,3},{2,4},{3,5},{4,6},{5,7},{6,8},{7,9},{8,10},{9,11},{10,... | collective-permute-start | bytes 1572872 | tf_op jit(solution)/shard_map/while/body/eval_jaxpr/ppermute | solution.py:20
  548.5 36.3 %collective-permute-start.1 = (f32[256,512]{1,0:T(8,128)}, f32[256,512]{1,0:T(8,128)S(1)}, u32[]{:S(2)}, u32[]{:S(2)}) collective-permute-start(f32[256,512]{1,0:T(8,128)} %bitcast.141), channel_id=1, source_target_pairs={{0,1},{1,2},{2,3},{3,4},{4,5},{5,6},{6,7},{7,8},{8,9},{9,10},{10,1... | collective-permute-start | bytes 1572872 | tf_op jit(solution)/shard_map/while/body/eval_jaxpr/ppermute | solution.py:20
  550.4 40.4 %collective-permute-start.2 = (f32[256,512]{1,0:T(8,128)}, f32[256,512]{1,0:T(8,128)}, u32[]{:S(2)}, u32[]{:S(2)}) collective-permute-start(f32[256,512]{1,0:T(8,128)} %bitcast.142), channel_id=1, source_target_pairs={{1,0},{2,1},{3,2},{4,3},{5,4},{6,5},{7,6},{8,7},{9,8},{10,9},{11,1... | collective-permute-start | bytes 1572872 | tf_op jit(solution)/shard_map/while/body/eval_jaxpr/ppermute | solution.py:20
  558.0 32.8 %collective-permute-start.3 = (f32[256,512]{1,0:T(8,128)}, f32[256,512]{1,0:T(8,128)}, u32[]{:S(2)}, u32[]{:S(2)}) collective-permute-start(f32[256,512]{1,0:T(8,128)} %bitcast.143), channel_id=1, source_target_pairs={{2,0},{3,1},{4,2},{5,3},{6,4},{7,5},{8,6},{9,7},{10,8},{11,9},{12,... | collective-permute-start | bytes 1572872 | tf_op jit(solution)/shard_map/while/body/eval_jaxpr/ppermute | solution.py:20
  566.7 24.0 %copy-start.4 = (f32[256,512]{1,0:T(8,128)}, f32[256,512]{1,0:T(8,128)S(1)}, u32[]{:S(2)}) copy-start(f32[256,512]{1,0:T(8,128)S(1)} %collective-permute-done) | copy-start | bytes 1572868 | tf_op jit(solution)/shard_map/while
  584.7 6.0 %copy-start.5 = (f32[256,512]{1,0:T(8,128)}, f32[256,512]{1,0:T(8,128)S(1)}, u32[]{:S(2)}) copy-start(f32[256,512]{1,0:T(8,128)S(1)} %collective-permute-done.1) | copy-start | bytes 1572868 | tf_op jit(solution)/shard_map/while
  590.8 9.6 %copy-start.3 = (bf16[512,1024]{1,0:T(8,128)(2,1)S(1)}, bf16[512,1024]{1,0:T(8,128)(2,1)}, u32[]{:S(2)}) copy-start(bf16[512,1024]{1,0:T(8,128)(2,1)} %copy-done.2) | copy-start | bytes 3145732 | tf_op jit(solution)/shard_map/while
  593.8 6.6 %copy-start.1 = (bf16[1,512,1536]{2,1,0:T(8,128)(2,1)S(1)}, bf16[1,512,1536]{2,1,0:T(8,128)(2,1)}, u32[]{:S(2)}) copy-start(bf16[1,512,1536]{2,1,0:T(8,128)(2,1)} %get-tuple-element.611) | copy-start | bytes 4718596 | tf_op jit(solution)/shard_map/while
  593.8 6.6 %copy-start.7 = (bf16[1,512,512]{2,1,0:T(8,128)(2,1)S(1)}, bf16[1,512,512]{2,1,0:T(8,128)(2,1)}, u32[]{:S(2)}) copy-start(bf16[1,512,512]{2,1,0:T(8,128)(2,1)} %get-tuple-element.636) | copy-start | bytes 1572868 | tf_op jit(solution)/shard_map/while
  596.3 4.2 collective-permute-start.4
  (2 other events, 2.7 us)

commit v3 on v2

--- a/solution.py
+++ b/solution.py
@@ -173,7 +173,9 @@
         grad_project = jnp.concatenate([grad_query, grad_own], 1).astype(jnp.bfloat16)
         grad_normed = jnp.dot(grad_project, weight_in.T, preferred_element_type=jnp.float32)
         for slot_index, shift_by in enumerate(offsets):
-            grad_normed = grad_normed + shifted(window_grads[slot_index], "space", shift_by)
+            grad_normed = grad_normed + shifted(
+                window_grads[slot_index].astype(jnp.bfloat16), "space", shift_by
+            ).astype(jnp.float32)
         result = (
             grad_out.astype(jnp.float32)
             + norm_backward(grad_normed, scaled_rows, inverse_rows, gain_row)

time: 603 us -> 488 us (0.81)
  the two profiles are of different devices: /device:TPU:5 before, /device:TPU:113 now
where the time goes in v3:
time: 488 us; the launch traced here: 486 us
  Pallas kernels  148 us (30%)
  waiting for transfers between devices  122 us (25%)
  starting transfers between devices  110 us (23%)
  other arithmetic  41.4 us (8%)
  matrix products  33.2 us (7%)
  local copies, waits for them, and re-layouts  30.4 us (6%)
    pallas_call x5, Pallas kernels, attend_backward(): pl.pallas_call(attention_kernel, grid=(groups,), in_specs=[row_spec, key_...  148 us
    ppermute x29, waiting for transfers between devices, shifted(): return lax.ppermute(x, axis, pairs)  122 us
    ppermute x29, starting transfers between devices, shifted(): return lax.ppermute(x, axis, pairs)  110 us
    dot_general x5, matrix products, step(): jnp.dot(grad_project, weight_in.T, preferred_element_type=jnp.float32)  13.7 us
    select_n x5, other arithmetic, step(): jnp.where(active, lax.dynamic_update_index_in_dim(collected, result, chos...  11.8 us
    squeeze x5, local copies, waits for them, and re-layouts, step(): pair_rows = lax.dynamic_index_in_dim(pairs, chosen, 0, keepdims=False)  10.2 us
    dot_general x5, matrix products, step(): jnp.dot(grad_out, weight_out.T, preferred_element_type=jnp.float32)  10 us
  transfers between devices with their start and end apart: 29, of which 18 were waited for; matrix products, arithmetic and copies ran while one was open for 1% of the time, Pallas kernels for 0%

profile of v3, /device:TPU:113, one launch (start us, length us, event | category | flops | bytes accessed | tf_op | source)
XLA Modules:
  0.0 485.8 jit_solution(1088482019923405126)
XLA Ops:
  7.0 3.4 collective-permute-start.6
  10.5 2.6 collective-permute-start.7
  13.1 6.3 %collective-permute-start.8 = (bf16[4,256,512]{2,1,0:T(8,128)(2,1)S(1)}, bf16[4,256,512]{2,1,0:T(8,128)(2,1)}, u32[]{:S(2)}, u32[]{:S(2)}) collective-permute-start(bf16[4,256,512]{2,1,0:T(8,128)(2,1)S(1)} %get-tuple-element.407), channel_id=1, source_target_pairs={{2,0},{3,1},{4,2},{5,3},{6,4},{7,5},{8,6},{9,7},{10,8},{11,9},{12,... | collective-permute-start | bytes 3145736 | tf_op jit(solution)/shard_map/ppermute | solution.py:20
  25.3 7.3 %collective-permute-done.5 = bf16[4,256,512]{2,1,0:T(8,128)(2,1)S(1)} collective-permute-done((bf16[4,256,512]{2,1,0:T(8,128)(2,1)S(1)}, bf16[4,256,512]{2,1,0:T(8,128)(2,1)S(1)}, u32[]{:S(2)}, u32[]{:S(2)}) %collective-permute-start.5) | collective-permute-done | bytes 1048608 | tf_op jit(solution)/shard_map/ppermute | solution.py:20
  32.6 24.6 %collective-permute-done.6 = bf16[4,256,512]{2,1,0:T(8,128)(2,1)} collective-permute-done((bf16[4,256,512]{2,1,0:T(8,128)(2,1)S(1)}, bf16[4,256,512]{2,1,0:T(8,128)(2,1)}, u32[]{:S(2)}, u32[]{:S(2)}) %collective-permute-start.6) | collective-permute-done | bytes 1048608 | tf_op jit(solution)/shard_map/ppermute | solution.py:20
  57.2 31.2 %collective-permute-done.8 = bf16[4,256,512]{2,1,0:T(8,128)(2,1)} collective-permute-done((bf16[4,256,512]{2,1,0:T(8,128)(2,1)S(1)}, bf16[4,256,512]{2,1,0:T(8,128)(2,1)}, u32[]{:S(2)}, u32[]{:S(2)}) %collective-permute-start.8) | collective-permute-done | bytes 1048608 | tf_op jit(solution)/shard_map/ppermute | solution.py:20
  88.4 3.5 pad_maximum_fusion
  91.9 2.8 gather_fusion
  97.8 2.4 pad_maximum_fusion.1
  101.2 384.5 %while.17 = (s32[]{:T(128)}, bf16[256,512]{1,0:T(8,128)(2,1)S(1)}, bf16[4,256,512]{2,1,0:T(8,128)(2,1)}, pred[]{:T(512)}, s32[]{:T(128)}, /*index=5*/bf16[4,256,...) while((s32[]{:T(128)}, bf16[256,512]{1,0:T(8,128)(2,1)S(1)}, ...), condition=%wide.region_6.7_spmd, body=%wide.region_2.6_spmd.sunk | while | flops 6181486592 | bytes 59259548 | solution.py:193
  101.3 2.0 dynamic-slice_bitcast_fusion.5
  107.1 29.5 %eval_jaxpr.7 = (f32[256,512]{1,0:T(8,128)}, f32[512,512]{1,0:T(8,128)}, f32[512,512]{1,0:T(8,128)}) custom-call(bf16[256,512]{1,0:T(8,128)(2,1)} %dynamic-slice_bitcast_fusion.4.q_ref, bf16[512,512]{1,0:T(8,128)(2,1)} %get-tuple-element.515.k_ref, bf16[512,512]{1,0:T(8,128)(2,1)} %get-tuple-element.516.v_ref, bf16[256,512]{1,0:T(8,128)(2,1)} %convolution_convert_fusion.4.g_ref), custom_call_target="tpu_custom_call" | custom-call | flops 5368709120 | bytes 4194304 | tf_op jit(solution)/shard_map/while/body/eval_jaxpr/pallas_call | solution.py:85
  141.9 13.6 %collective-permute-start = (bf16[256,512]{1,0:T(8,128)(2,1)S(1)}, bf16[256,512]{1,0:T(8,128)(2,1)}, u32[]{:S(2)}, u32[]{:S(2)}) collective-permute-start(bf16[256,512]{1,0:T(8,128)(2,1)S(1)} %bitcast.152), channel_id=1, source_target_pairs={{0,2},{1,3},{2,4},{3,5},{4,6},{5,7},{6,8},{7,9},{8,10},{9,11},{10,... | collective-permute-start | bytes 786440 | tf_op jit(solution)/shard_map/while/body/eval_jaxpr/ppermute | solution.py:20
  157.4 3.4 collective-permute-start.2
  162.9 6.6 %collective-permute-done.1 = bf16[256,512]{1,0:T(8,128)(2,1)} collective-permute-done((bf16[256,512]{1,0:T(8,128)(2,1)S(1)}, bf16[256,512]{1,0:T(8,128)(2,1)}, u32[]{:S(2)}, u32[]{:S(2)}) %collective-permute-start.1) | collective-permute-done | bytes 262176 | tf_op jit(solution)/shard_map/while/body/eval_jaxpr/ppermute | solution.py:20
  169.4 6.5 %collective-permute-done.3 = bf16[256,512]{1,0:T(8,128)(2,1)} collective-permute-done((bf16[256,512]{1,0:T(8,128)(2,1)S(1)}, bf16[256,512]{1,0:T(8,128)(2,1)}, u32[]{:S(2)}, u32[]{:S(2)}) %collective-permute-start.3) | collective-permute-done | bytes 262176 | tf_op jit(solution)/shard_map/while/body/eval_jaxpr/ppermute | solution.py:20
  175.9 2.7 fusion.63
  178.7 2.4 fusion.64
  181.1 4.2 collective-permute-start.4
  186.6 2.0 dynamic-slice_bitcast_fusion.5
  190.5 2.0 convolution_convert_fusion.4.g_ref
  192.5 29.5 %eval_jaxpr.7 = (f32[256,512]{1,0:T(8,128)}, f32[512,512]{1,0:T(8,128)}, f32[512,512]{1,0:T(8,128)}) custom-call(bf16[256,512]{1,0:T(8,128)(2,1)} %dynamic-slice_bitcast_fusion.4.q_ref, bf16[512,512]{1,0:T(8,128)(2,1)} %get-tuple-element.515.k_ref, bf16[512,512]{1,0:T(8,128)(2,1)} %get-tuple-element.516.v_ref, bf16[256,512]{1,0:T(8,128)(2,1)} %convolution_convert_fusion.4.g_ref), custom_call_target="tpu_custom_call" | custom-call | flops 5368709120 | bytes 4194304 | tf_op jit(solution)/shard_map/while/body/eval_jaxpr/pallas_call | solution.py:85
  227.3 2.1 collective-permute-start
  229.3 2.5 collective-permute-start.1
  231.9 3.1 collective-permute-start.2
  235.0 6.6 %collective-permute-start.3 = (bf16[256,512]{1,0:T(8,128)(2,1)S(1)}, bf16[256,512]{1,0:T(8,128)(2,1)}, u32[]{:S(2)}, u32[]{:S(2)}) collective-permute-start(bf16[256,512]{1,0:T(8,128)(2,1)S(1)} %bitcast.149), channel_id=1, source_target_pairs={{2,0},{3,1},{4,2},{5,3},{6,4},{7,5},{8,6},{9,7},{10,8},{11,9},{12,... | collective-permute-start | bytes 786440 | tf_op jit(solution)/shard_map/while/body/eval_jaxpr/ppermute | solution.py:20
  241.7 3.7 collective-permute-done.1
  245.4 5.0 %collective-permute-done.3 = bf16[256,512]{1,0:T(8,128)(2,1)} collective-permute-done((bf16[256,512]{1,0:T(8,128)(2,1)S(1)}, bf16[256,512]{1,0:T(8,128)(2,1)}, u32[]{:S(2)}, u32[]{:S(2)}) %collective-permute-start.3) | collective-permute-done | bytes 262176 | tf_op jit(solution)/shard_map/while/body/eval_jaxpr/ppermute | solution.py:20
  250.5 2.7 fusion.63
  253.2 2.4 fusion.64
  255.6 3.1 collective-permute-start.4
  260.1 2.0 dynamic-slice_bitcast_fusion.5
  265.9 29.5 %eval_jaxpr.7 = (f32[256,512]{1,0:T(8,128)}, f32[512,512]{1,0:T(8,128)}, f32[512,512]{1,0:T(8,128)}) custom-call(bf16[256,512]{1,0:T(8,128)(2,1)} %dynamic-slice_bitcast_fusion.4.q_ref, bf16[512,512]{1,0:T(8,128)(2,1)} %get-tuple-element.515.k_ref, bf16[512,512]{1,0:T(8,128)(2,1)} %get-tuple-element.516.v_ref, bf16[256,512]{1,0:T(8,128)(2,1)} %convolution_convert_fusion.4.g_ref), custom_call_target="tpu_custom_call" | custom-call | flops 5368709120 | bytes 4194304 | tf_op jit(solution)/shard_map/while/body/eval_jaxpr/pallas_call | solution.py:85
  300.7 2.1 collective-permute-start
  302.8 2.7 collective-permute-start.1
  305.5 3.1 collective-permute-start.2
  308.6 6.5 %collective-permute-start.3 = (bf16[256,512]{1,0:T(8,128)(2,1)S(1)}, bf16[256,512]{1,0:T(8,128)(2,1)}, u32[]{:S(2)}, u32[]{:S(2)}) collective-permute-start(bf16[256,512]{1,0:T(8,128)(2,1)S(1)} %bitcast.149), channel_id=1, source_target_pairs={{2,0},{3,1},{4,2},{5,3},{6,4},{7,5},{8,6},{9,7},{10,8},{11,9},{12,... | collective-permute-start | bytes 786440 | tf_op jit(solution)/shard_map/while/body/eval_jaxpr/ppermute | solution.py:20
  315.2 3.7 collective-permute-done.1
  318.9 5.1 %collective-permute-done.3 = bf16[256,512]{1,0:T(8,128)(2,1)} collective-permute-done((bf16[256,512]{1,0:T(8,128)(2,1)S(1)}, bf16[256,512]{1,0:T(8,128)(2,1)}, u32[]{:S(2)}, u32[]{:S(2)}) %collective-permute-start.3) | collective-permute-done | bytes 262176 | tf_op jit(solution)/shard_map/while/body/eval_jaxpr/ppermute | solution.py:20
  324.0 2.7 fusion.63
  326.8 2.4 fusion.64
  329.2 3.1 collective-permute-start.4
  333.7 2.0 dynamic-slice_bitcast_fusion.5
  337.5 2.0 convolution_convert_fusion.4.g_ref
  339.5 29.5 %eval_jaxpr.7 = (f32[256,512]{1,0:T(8,128)}, f32[512,512]{1,0:T(8,128)}, f32[512,512]{1,0:T(8,128)}) custom-call(bf16[256,512]{1,0:T(8,128)(2,1)} %dynamic-slice_bitcast_fusion.4.q_ref, bf16[512,512]{1,0:T(8,128)(2,1)} %get-tuple-element.515.k_ref, bf16[512,512]{1,0:T(8,128)(2,1)} %get-tuple-element.516.v_ref, bf16[256,512]{1,0:T(8,128)(2,1)} %convolution_convert_fusion.4.g_ref), custom_call_target="tpu_custom_call" | custom-call | flops 5368709120 | bytes 4194304 | tf_op jit(solution)/shard_map/while/body/eval_jaxpr/pallas_call | solution.py:85
  374.3 2.1 collective-permute-start
  376.4 2.7 collective-permute-start.1
  379.0 3.1 collective-permute-start.2
  382.1 6.5 %collective-permute-start.3 = (bf16[256,512]{1,0:T(8,128)(2,1)S(1)}, bf16[256,512]{1,0:T(8,128)(2,1)}, u32[]{:S(2)}, u32[]{:S(2)}) collective-permute-start(bf16[256,512]{1,0:T(8,128)(2,1)S(1)} %bitcast.149), channel_id=1, source_target_pairs={{2,0},{3,1},{4,2},{5,3},{6,4},{7,5},{8,6},{9,7},{10,8},{11,9},{12,... | collective-permute-start | bytes 786440 | tf_op jit(solution)/shard_map/while/body/eval_jaxpr/ppermute | solution.py:20
  388.8 3.7 collective-permute-done.1
  392.5 5.2 %collective-permute-done.3 = bf16[256,512]{1,0:T(8,128)(2,1)} collective-permute-done((bf16[256,512]{1,0:T(8,128)(2,1)S(1)}, bf16[256,512]{1,0:T(8,128)(2,1)}, u32[]{:S(2)}, u32[]{:S(2)}) %collective-permute-start.3) | collective-permute-done | bytes 262176 | tf_op jit(solution)/shard_map/while/body/eval_jaxpr/ppermute | solution.py:20
  397.7 2.7 fusion.63
  400.4 2.4 fusion.64
  402.8 3.1 collective-permute-start.4
  407.3 2.0 dynamic-slice_bitcast_fusion.5
  413.1 29.5 %eval_jaxpr.7 = (f32[256,512]{1,0:T(8,128)}, f32[512,512]{1,0:T(8,128)}, f32[512,512]{1,0:T(8,128)}) custom-call(bf16[256,512]{1,0:T(8,128)(2,1)} %dynamic-slice_bitcast_fusion.4.q_ref, bf16[512,512]{1,0:T(8,128)(2,1)} %get-tuple-element.515.k_ref, bf16[512,512]{1,0:T(8,128)(2,1)} %get-tuple-element.516.v_ref, bf16[256,512]{1,0:T(8,128)(2,1)} %convolution_convert_fusion.4.g_ref), custom_call_target="tpu_custom_call" | custom-call | flops 5368709120 | bytes 4194304 | tf_op jit(solution)/shard_map/while/body/eval_jaxpr/pallas_call | solution.py:85
  447.9 2.1 collective-permute-start
  450.0 4.6 collective-permute-start.1
  456.5 5.7 %collective-permute-start.3 = (bf16[256,512]{1,0:T(8,128)(2,1)S(1)}, bf16[256,512]{1,0:T(8,128)(2,1)}, u32[]{:S(2)}, u32[]{:S(2)}) collective-permute-start(bf16[256,512]{1,0:T(8,128)(2,1)S(1)} %bitcast.149), channel_id=1, source_target_pairs={{2,0},{3,1},{4,2},{5,3},{6,4},{7,5},{8,6},{9,7},{10,8},{11,9},{12,... | collective-permute-start | bytes 786440 | tf_op jit(solution)/shard_map/while/body/eval_jaxpr/ppermute | solution.py:20
  462.4 3.7 collective-permute-done.1
  466.1 9.4 %collective-permute-done.3 = bf16[256,512]{1,0:T(8,128)(2,1)} collective-permute-done((bf16[256,512]{1,0:T(8,128)(2,1)S(1)}, bf16[256,512]{1,0:T(8,128)(2,1)}, u32[]{:S(2)}, u32[]{:S(2)}) %collective-permute-start.3) | collective-permute-done | bytes 262176 | tf_op jit(solution)/shard_map/while/body/eval_jaxpr/ppermute | solution.py:20
  475.5 2.7 fusion.63
  478.3 2.4 fusion.64
  480.6 3.8 collective-permute-start.4
  (188 shorter events, 70.8 us)
Async XLA Ops:
  0.0 3.2 copy-start.5
  0.0 3.3 copy-start.12
  3.3 16.1 %copy-start.9 = (bf16[1,512,1536]{2,1,0:T(8,128)(2,1)S(1)}, bf16[1,512,1536]{2,1,0:T(8,128)(2,1)}, u32[]{:S(2)}) copy-start(bf16[1,512,1536]{2,1,0:T(8,128)(2,1)} %param.9) | copy-start | bytes 4718596
  5.1 27.5 %collective-permute-start.5 = (bf16[4,256,512]{2,1,0:T(8,128)(2,1)S(1)}, bf16[4,256,512]{2,1,0:T(8,128)(2,1)S(1)}, u32[]{:S(2)}, u32[]{:S(2)}) collective-permute-start(bf16[4,256,512]{2,1,0:T(8,128)(2,1)S(1)} %get-tuple-element.407), channel_id=1, source_target_pairs={{0,2},{1,3},{2,4},{3,5},{4,6},{5,7},{6,8},{7,9},{8,10},{9,11},{10,... | collective-permute-start | bytes 3145736 | tf_op jit(solution)/shard_map/ppermute | solution.py:20
  7.0 50.1 %collective-permute-start.6 = (bf16[4,256,512]{2,1,0:T(8,128)(2,1)S(1)}, bf16[4,256,512]{2,1,0:T(8,128)(2,1)}, u32[]{:S(2)}, u32[]{:S(2)}) collective-permute-start(bf16[4,256,512]{2,1,0:T(8,128)(2,1)S(1)} %get-tuple-element.407), channel_id=1, source_target_pairs={{0,1},{1,2},{2,3},{3,4},{4,5},{5,6},{6,7},{7,8},{8,9},{9,10},{10,1... | collective-permute-start | bytes 3145736 | tf_op jit(solution)/shard_map/ppermute | solution.py:20
  10.5 46.7 %collective-permute-start.7 = (bf16[4,256,512]{2,1,0:T(8,128)(2,1)S(1)}, bf16[4,256,512]{2,1,0:T(8,128)(2,1)}, u32[]{:S(2)}, u32[]{:S(2)}) collective-permute-start(bf16[4,256,512]{2,1,0:T(8,128)(2,1)S(1)} %get-tuple-element.407), channel_id=1, source_target_pairs={{1,0},{2,1},{3,2},{4,3},{5,4},{6,5},{7,6},{8,7},{9,8},{10,9},{11,1... | collective-permute-start | bytes 3145736 | tf_op jit(solution)/shard_map/ppermute | solution.py:20
  13.1 75.3 %collective-permute-start.8 = (bf16[4,256,512]{2,1,0:T(8,128)(2,1)S(1)}, bf16[4,256,512]{2,1,0:T(8,128)(2,1)}, u32[]{:S(2)}, u32[]{:S(2)}) collective-permute-start(bf16[4,256,512]{2,1,0:T(8,128)(2,1)S(1)} %get-tuple-element.407), channel_id=1, source_target_pairs={{2,0},{3,1},{4,2},{5,3},{6,4},{7,5},{8,6},{9,7},{10,8},{11,9},{12,... | collective-permute-start | bytes 3145736 | tf_op jit(solution)/shard_map/ppermute | solution.py:20
  97.8 3.5 copy-start.2
  97.8 3.5 slice-start.1
  101.3 3.1 copy-start.7
  101.3 37.0 %copy-start = (bf16[512,1024]{1,0:T(8,128)(2,1)}, bf16[512,1024]{1,0:T(8,128)(2,1)S(1)}, u32[]{:S(2)}) copy-start(bf16[512,1024]{1,0:T(8,128)(2,1)S(1)} %get-tuple-element.583) | copy-start | bytes 3145732 | tf_op jit(solution)/shard_map/while
  141.8 21.0 %copy-start.4 = (f32[256,512]{1,0:T(8,128)S(1)}, f32[256,512]{1,0:T(8,128)}, u32[]{:S(2)}) copy-start(f32[256,512]{1,0:T(8,128)} %get-tuple-element.523) | copy-start | bytes 1572868 | tf_op jit(solution)/shard_map/while
  141.9 21.0 %collective-permute-start = (bf16[256,512]{1,0:T(8,128)(2,1)S(1)}, bf16[256,512]{1,0:T(8,128)(2,1)}, u32[]{:S(2)}, u32[]{:S(2)}) collective-permute-start(bf16[256,512]{1,0:T(8,128)(2,1)S(1)} %bitcast.152), channel_id=1, source_target_pairs={{0,2},{1,3},{2,4},{3,5},{4,6},{5,7},{6,8},{7,9},{8,10},{9,11},{10,... | collective-permute-start | bytes 786440 | tf_op jit(solution)/shard_map/while/body/eval_jaxpr/ppermute | solution.py:20
  155.5 13.9 %collective-permute-start.1 = (bf16[256,512]{1,0:T(8,128)(2,1)S(1)}, bf16[256,512]{1,0:T(8,128)(2,1)}, u32[]{:S(2)}, u32[]{:S(2)}) collective-permute-start(bf16[256,512]{1,0:T(8,128)(2,1)S(1)} %bitcast.151), channel_id=1, source_target_pairs={{0,1},{1,2},{2,3},{3,4},{4,5},{5,6},{6,7},{7,8},{8,9},{9,10},{10,1... | collective-permute-start | bytes 786440 | tf_op jit(solution)/shard_map/while/body/eval_jaxpr/ppermute | solution.py:20
  157.4 12.0 %collective-permute-start.2 = (bf16[256,512]{1,0:T(8,128)(2,1)S(1)}, bf16[256,512]{1,0:T(8,128)(2,1)}, u32[]{:S(2)}, u32[]{:S(2)}) collective-permute-start(bf16[256,512]{1,0:T(8,128)(2,1)S(1)} %bitcast.150), channel_id=1, source_target_pairs={{1,0},{2,1},{3,2},{4,3},{5,4},{6,5},{7,6},{8,7},{9,8},{10,9},{11,1... | collective-permute-start | bytes 786440 | tf_op jit(solution)/shard_map/while/body/eval_jaxpr/ppermute | solution.py:20
  160.8 15.1 %collective-permute-start.3 = (bf16[256,512]{1,0:T(8,128)(2,1)S(1)}, bf16[256,512]{1,0:T(8,128)(2,1)}, u32[]{:S(2)}, u32[]{:S(2)}) collective-permute-start(bf16[256,512]{1,0:T(8,128)(2,1)S(1)} %bitcast.149), channel_id=1, source_target_pairs={{2,0},{3,1},{4,2},{5,3},{6,4},{7,5},{8,6},{9,7},{10,8},{11,9},{12,... | collective-permute-start | bytes 786440 | tf_op jit(solution)/shard_map/while/body/eval_jaxpr/ppermute | solution.py:20
  175.9 10.7 %copy-start.8 = (bf16[4,256,512]{2,1,0:T(8,128)(2,1)S(1)}, bf16[4,256,512]{2,1,0:T(8,128)(2,1)}, u32[]{:S(2)}) copy-start(bf16[4,256,512]{2,1,0:T(8,128)(2,1)} %copy-done.7) | copy-start | bytes 3145732 | tf_op jit(solution)/shard_map/while
  178.7 8.0 %copy-start.1 = (bf16[512,1024]{1,0:T(8,128)(2,1)S(1)}, bf16[512,1024]{1,0:T(8,128)(2,1)}, u32[]{:S(2)}) copy-start(bf16[512,1024]{1,0:T(8,128)(2,1)} %copy-done) | copy-start | bytes 3145732 | tf_op jit(solution)/shard_map/while
  178.7 7.9 %copy-start.3 = (bf16[1,512,512]{2,1,0:T(8,128)(2,1)S(1)}, bf16[1,512,512]{2,1,0:T(8,128)(2,1)}, u32[]{:S(2)}) copy-start(bf16[1,512,512]{2,1,0:T(8,128)(2,1)} %get-tuple-element.612) | copy-start | bytes 1572868 | tf_op jit(solution)/shard_map/while
  181.1 5.5 %collective-permute-start.4 = (bf16[256,512]{1,0:T(8,128)(2,1)}, bf16[256,512]{1,0:T(8,128)(2,1)S(1)}, u32[]{:S(2)}, u32[]{:S(2)}) collective-permute-start(bf16[256,512]{1,0:T(8,128)(2,1)} %get-tuple-element.529), channel_id=1, source_target_pairs={{64,0},{65,1},{66,2},{67,3},{68,4},{69,5},{70,6},{71,7},{72,8},{73... | collective-permute-start | bytes 786440 | tf_op jit(solution)/shard_map/while/body/eval_jaxpr/ppermute | solution.py:20
  186.6 3.1 copy-start.7
  186.6 37.1 %copy-start = (bf16[512,1024]{1,0:T(8,128)(2,1)}, bf16[512,1024]{1,0:T(8,128)(2,1)S(1)}, u32[]{:S(2)}) copy-start(bf16[512,1024]{1,0:T(8,128)(2,1)S(1)} %get-tuple-element.583) | copy-start | bytes 3145732 | tf_op jit(solution)/shard_map/while
  227.2 14.5 %copy-start.4 = (f32[256,512]{1,0:T(8,128)S(1)}, f32[256,512]{1,0:T(8,128)}, u32[]{:S(2)}) copy-start(f32[256,512]{1,0:T(8,128)} %get-tuple-element.523) | copy-start | bytes 1572868 | tf_op jit(solution)/shard_map/while
  227.3 14.5 %collective-permute-start = (bf16[256,512]{1,0:T(8,128)(2,1)S(1)}, bf16[256,512]{1,0:T(8,128)(2,1)}, u32[]{:S(2)}, u32[]{:S(2)}) collective-permute-start(bf16[256,512]{1,0:T(8,128)(2,1)S(1)} %bitcast.152), channel_id=1, source_target_pairs={{0,2},{1,3},{2,4},{3,5},{4,6},{5,7},{6,8},{7,9},{8,10},{9,11},{10,... | collective-permute-start | bytes 786440 | tf_op jit(solution)/shard_map/while/body/eval_jaxpr/ppermute | solution.py:20
  229.3 16.1 %collective-permute-start.1 = (bf16[256,512]{1,0:T(8,128)(2,1)S(1)}, bf16[256,512]{1,0:T(8,128)(2,1)}, u32[]{:S(2)}, u32[]{:S(2)}) collective-permute-start(bf16[256,512]{1,0:T(8,128)(2,1)S(1)} %bitcast.151), channel_id=1, source_target_pairs={{0,1},{1,2},{2,3},{3,4},{4,5},{5,6},{6,7},{7,8},{8,9},{9,10},{10,1... | collective-permute-start | bytes 786440 | tf_op jit(solution)/shard_map/while/body/eval_jaxpr/ppermute | solution.py:20
  231.9 13.6 %collective-permute-start.2 = (bf16[256,512]{1,0:T(8,128)(2,1)S(1)}, bf16[256,512]{1,0:T(8,128)(2,1)}, u32[]{:S(2)}, u32[]{:S(2)}) collective-permute-start(bf16[256,512]{1,0:T(8,128)(2,1)S(1)} %bitcast.150), channel_id=1, source_target_pairs={{1,0},{2,1},{3,2},{4,3},{5,4},{6,5},{7,6},{8,7},{9,8},{10,9},{11,1... | collective-permute-start | bytes 786440 | tf_op jit(solution)/shard_map/while/body/eval_jaxpr/ppermute | solution.py:20
  235.0 15.5 %collective-permute-start.3 = (bf16[256,512]{1,0:T(8,128)(2,1)S(1)}, bf16[256,512]{1,0:T(8,128)(2,1)}, u32[]{:S(2)}, u32[]{:S(2)}) collective-permute-start(bf16[256,512]{1,0:T(8,128)(2,1)S(1)} %bitcast.149), channel_id=1, source_target_pairs={{2,0},{3,1},{4,2},{5,3},{6,4},{7,5},{8,6},{9,7},{10,8},{11,9},{12,... | collective-permute-start | bytes 786440 | tf_op jit(solution)/shard_map/while/body/eval_jaxpr/ppermute | solution.py:20
  250.5 9.6 %copy-start.8 = (bf16[4,256,512]{2,1,0:T(8,128)(2,1)S(1)}, bf16[4,256,512]{2,1,0:T(8,128)(2,1)}, u32[]{:S(2)}) copy-start(bf16[4,256,512]{2,1,0:T(8,128)(2,1)} %copy-done.7) | copy-start | bytes 3145732 | tf_op jit(solution)/shard_map/while
  253.2 6.9 %copy-start.1 = (bf16[512,1024]{1,0:T(8,128)(2,1)S(1)}, bf16[512,1024]{1,0:T(8,128)(2,1)}, u32[]{:S(2)}) copy-start(bf16[512,1024]{1,0:T(8,128)(2,1)} %copy-done) | copy-start | bytes 3145732 | tf_op jit(solution)/shard_map/while
  253.2 6.9 %copy-start.3 = (bf16[1,512,512]{2,1,0:T(8,128)(2,1)S(1)}, bf16[1,512,512]{2,1,0:T(8,128)(2,1)}, u32[]{:S(2)}) copy-start(bf16[1,512,512]{2,1,0:T(8,128)(2,1)} %get-tuple-element.612) | copy-start | bytes 1572868 | tf_op jit(solution)/shard_map/while
  255.6 4.5 collective-permute-start.4
  260.1 3.1 copy-start.7
  260.1 37.1 %copy-start = (bf16[512,1024]{1,0:T(8,128)(2,1)}, bf16[512,1024]{1,0:T(8,128)(2,1)S(1)}, u32[]{:S(2)}) copy-start(bf16[512,1024]{1,0:T(8,128)(2,1)S(1)} %get-tuple-element.583) | copy-start | bytes 3145732 | tf_op jit(solution)/shard_map/while
  300.6 14.5 %copy-start.4 = (f32[256,512]{1,0:T(8,128)S(1)}, f32[256,512]{1,0:T(8,128)}, u32[]{:S(2)}) copy-start(f32[256,512]{1,0:T(8,128)} %get-tuple-element.523) | copy-start | bytes 1572868 | tf_op jit(solution)/shard_map/while
  300.7 14.5 %collective-permute-start = (bf16[256,512]{1,0:T(8,128)(2,1)S(1)}, bf16[256,512]{1,0:T(8,128)(2,1)}, u32[]{:S(2)}, u32[]{:S(2)}) collective-permute-start(bf16[256,512]{1,0:T(8,128)(2,1)S(1)} %bitcast.152), channel_id=1, source_target_pairs={{0,2},{1,3},{2,4},{3,5},{4,6},{5,7},{6,8},{7,9},{8,10},{9,11},{10,... | collective-permute-start | bytes 786440 | tf_op jit(solution)/shard_map/while/body/eval_jaxpr/ppermute | solution.py:20
  302.8 16.1 %collective-permute-start.1 = (bf16[256,512]{1,0:T(8,128)(2,1)S(1)}, bf16[256,512]{1,0:T(8,128)(2,1)}, u32[]{:S(2)}, u32[]{:S(2)}) collective-permute-start(bf16[256,512]{1,0:T(8,128)(2,1)S(1)} %bitcast.151), channel_id=1, source_target_pairs={{0,1},{1,2},{2,3},{3,4},{4,5},{5,6},{6,7},{7,8},{8,9},{9,10},{10,1... | collective-permute-start | bytes 786440 | tf_op jit(solution)/shard_map/while/body/eval_jaxpr/ppermute | solution.py:20
  305.5 13.4 %collective-permute-start.2 = (bf16[256,512]{1,0:T(8,128)(2,1)S(1)}, bf16[256,512]{1,0:T(8,128)(2,1)}, u32[]{:S(2)}, u32[]{:S(2)}) collective-permute-start(bf16[256,512]{1,0:T(8,128)(2,1)S(1)} %bitcast.150), channel_id=1, source_target_pairs={{1,0},{2,1},{3,2},{4,3},{5,4},{6,5},{7,6},{8,7},{9,8},{10,9},{11,1... | collective-permute-start | bytes 786440 | tf_op jit(solution)/shard_map/while/body/eval_jaxpr/ppermute | solution.py:20
  308.6 15.5 %collective-permute-start.3 = (bf16[256,512]{1,0:T(8,128)(2,1)S(1)}, bf16[256,512]{1,0:T(8,128)(2,1)}, u32[]{:S(2)}, u32[]{:S(2)}) collective-permute-start(bf16[256,512]{1,0:T(8,128)(2,1)S(1)} %bitcast.149), channel_id=1, source_target_pairs={{2,0},{3,1},{4,2},{5,3},{6,4},{7,5},{8,6},{9,7},{10,8},{11,9},{12,... | collective-permute-start | bytes 786440 | tf_op jit(solution)/shard_map/while/body/eval_jaxpr/ppermute | solution.py:20
  324.0 9.6 %copy-start.8 = (bf16[4,256,512]{2,1,0:T(8,128)(2,1)S(1)}, bf16[4,256,512]{2,1,0:T(8,128)(2,1)}, u32[]{:S(2)}) copy-start(bf16[4,256,512]{2,1,0:T(8,128)(2,1)} %copy-done.7) | copy-start | bytes 3145732 | tf_op jit(solution)/shard_map/while
  326.8 6.9 %copy-start.1 = (bf16[512,1024]{1,0:T(8,128)(2,1)S(1)}, bf16[512,1024]{1,0:T(8,128)(2,1)}, u32[]{:S(2)}) copy-start(bf16[512,1024]{1,0:T(8,128)(2,1)} %copy-done) | copy-start | bytes 3145732 | tf_op jit(solution)/shard_map/while
  326.8 6.9 %copy-start.3 = (bf16[1,512,512]{2,1,0:T(8,128)(2,1)S(1)}, bf16[1,512,512]{2,1,0:T(8,128)(2,1)}, u32[]{:S(2)}) copy-start(bf16[1,512,512]{2,1,0:T(8,128)(2,1)} %get-tuple-element.612) | copy-start | bytes 1572868 | tf_op jit(solution)/shard_map/while
  329.2 4.5 collective-permute-start.4
  333.7 3.1 copy-start.7
  333.7 37.1 %copy-start = (bf16[512,1024]{1,0:T(8,128)(2,1)}, bf16[512,1024]{1,0:T(8,128)(2,1)S(1)}, u32[]{:S(2)}) copy-start(bf16[512,1024]{1,0:T(8,128)(2,1)S(1)} %get-tuple-element.583) | copy-start | bytes 3145732 | tf_op jit(solution)/shard_map/while
  374.2 14.5 %copy-start.4 = (f32[256,512]{1,0:T(8,128)S(1)}, f32[256,512]{1,0:T(8,128)}, u32[]{:S(2)}) copy-start(f32[256,512]{1,0:T(8,128)} %get-tuple-element.523) | copy-start | bytes 1572868 | tf_op jit(solution)/shard_map/while
  374.3 14.5 %collective-permute-start = (bf16[256,512]{1,0:T(8,128)(2,1)S(1)}, bf16[256,512]{1,0:T(8,128)(2,1)}, u32[]{:S(2)}, u32[]{:S(2)}) collective-permute-start(bf16[256,512]{1,0:T(8,128)(2,1)S(1)} %bitcast.152), channel_id=1, source_target_pairs={{0,2},{1,3},{2,4},{3,5},{4,6},{5,7},{6,8},{7,9},{8,10},{9,11},{10,... | collective-permute-start | bytes 786440 | tf_op jit(solution)/shard_map/while/body/eval_jaxpr/ppermute | solution.py:20
  376.4 16.1 %collective-permute-start.1 = (bf16[256,512]{1,0:T(8,128)(2,1)S(1)}, bf16[256,512]{1,0:T(8,128)(2,1)}, u32[]{:S(2)}, u32[]{:S(2)}) collective-permute-start(bf16[256,512]{1,0:T(8,128)(2,1)S(1)} %bitcast.151), channel_id=1, source_target_pairs={{0,1},{1,2},{2,3},{3,4},{4,5},{5,6},{6,7},{7,8},{8,9},{9,10},{10,1... | collective-permute-start | bytes 786440 | tf_op jit(solution)/shard_map/while/body/eval_jaxpr/ppermute | solution.py:20
  379.0 13.4 %collective-permute-start.2 = (bf16[256,512]{1,0:T(8,128)(2,1)S(1)}, bf16[256,512]{1,0:T(8,128)(2,1)}, u32[]{:S(2)}, u32[]{:S(2)}) collective-permute-start(bf16[256,512]{1,0:T(8,128)(2,1)S(1)} %bitcast.150), channel_id=1, source_target_pairs={{1,0},{2,1},{3,2},{4,3},{5,4},{6,5},{7,6},{8,7},{9,8},{10,9},{11,1... | collective-permute-start | bytes 786440 | tf_op jit(solution)/shard_map/while/body/eval_jaxpr/ppermute | solution.py:20
  382.1 15.5 %collective-permute-start.3 = (bf16[256,512]{1,0:T(8,128)(2,1)S(1)}, bf16[256,512]{1,0:T(8,128)(2,1)}, u32[]{:S(2)}, u32[]{:S(2)}) collective-permute-start(bf16[256,512]{1,0:T(8,128)(2,1)S(1)} %bitcast.149), channel_id=1, source_target_pairs={{2,0},{3,1},{4,2},{5,3},{6,4},{7,5},{8,6},{9,7},{10,8},{11,9},{12,... | collective-permute-start | bytes 786440 | tf_op jit(solution)/shard_map/while/body/eval_jaxpr/ppermute | solution.py:20
  397.7 9.6 %copy-start.8 = (bf16[4,256,512]{2,1,0:T(8,128)(2,1)S(1)}, bf16[4,256,512]{2,1,0:T(8,128)(2,1)}, u32[]{:S(2)}) copy-start(bf16[4,256,512]{2,1,0:T(8,128)(2,1)} %copy-done.7) | copy-start | bytes 3145732 | tf_op jit(solution)/shard_map/while
  400.4 6.9 %copy-start.1 = (bf16[512,1024]{1,0:T(8,128)(2,1)S(1)}, bf16[512,1024]{1,0:T(8,128)(2,1)}, u32[]{:S(2)}) copy-start(bf16[512,1024]{1,0:T(8,128)(2,1)} %copy-done) | copy-start | bytes 3145732 | tf_op jit(solution)/shard_map/while
  400.4 6.9 %copy-start.3 = (bf16[1,512,512]{2,1,0:T(8,128)(2,1)S(1)}, bf16[1,512,512]{2,1,0:T(8,128)(2,1)}, u32[]{:S(2)}) copy-start(bf16[1,512,512]{2,1,0:T(8,128)(2,1)} %get-tuple-element.612) | copy-start | bytes 1572868 | tf_op jit(solution)/shard_map/while
  402.8 4.5 collective-permute-start.4
  407.3 3.1 copy-start.7
  407.3 37.1 %copy-start = (bf16[512,1024]{1,0:T(8,128)(2,1)}, bf16[512,1024]{1,0:T(8,128)(2,1)S(1)}, u32[]{:S(2)}) copy-start(bf16[512,1024]{1,0:T(8,128)(2,1)S(1)} %get-tuple-element.583) | copy-start | bytes 3145732 | tf_op jit(solution)/shard_map/while
  447.8 14.5 %copy-start.4 = (f32[256,512]{1,0:T(8,128)S(1)}, f32[256,512]{1,0:T(8,128)}, u32[]{:S(2)}) copy-start(f32[256,512]{1,0:T(8,128)} %get-tuple-element.523) | copy-start | bytes 1572868 | tf_op jit(solution)/shard_map/while
  447.9 14.5 %collective-permute-start = (bf16[256,512]{1,0:T(8,128)(2,1)S(1)}, bf16[256,512]{1,0:T(8,128)(2,1)}, u32[]{:S(2)}, u32[]{:S(2)}) collective-permute-start(bf16[256,512]{1,0:T(8,128)(2,1)S(1)} %bitcast.152), channel_id=1, source_target_pairs={{0,2},{1,3},{2,4},{3,5},{4,6},{5,7},{6,8},{7,9},{8,10},{9,11},{10,... | collective-permute-start | bytes 786440 | tf_op jit(solution)/shard_map/while/body/eval_jaxpr/ppermute | solution.py:20
  450.0 16.1 %collective-permute-start.1 = (bf16[256,512]{1,0:T(8,128)(2,1)S(1)}, bf16[256,512]{1,0:T(8,128)(2,1)}, u32[]{:S(2)}, u32[]{:S(2)}) collective-permute-start(bf16[256,512]{1,0:T(8,128)(2,1)S(1)} %bitcast.151), channel_id=1, source_target_pairs={{0,1},{1,2},{2,3},{3,4},{4,5},{5,6},{6,7},{7,8},{8,9},{9,10},{10,1... | collective-permute-start | bytes 786440 | tf_op jit(solution)/shard_map/while/body/eval_jaxpr/ppermute | solution.py:20
  454.6 11.5 %collective-permute-start.2 = (bf16[256,512]{1,0:T(8,128)(2,1)S(1)}, bf16[256,512]{1,0:T(8,128)(2,1)}, u32[]{:S(2)}, u32[]{:S(2)}) collective-permute-start(bf16[256,512]{1,0:T(8,128)(2,1)S(1)} %bitcast.150), channel_id=1, source_target_pairs={{1,0},{2,1},{3,2},{4,3},{5,4},{6,5},{7,6},{8,7},{9,8},{10,9},{11,1... | collective-permute-start | bytes 786440 | tf_op jit(solution)/shard_map/while/body/eval_jaxpr/ppermute | solution.py:20
  456.5 19.0 %collective-permute-start.3 = (bf16[256,512]{1,0:T(8,128)(2,1)S(1)}, bf16[256,512]{1,0:T(8,128)(2,1)}, u32[]{:S(2)}, u32[]{:S(2)}) collective-permute-start(bf16[256,512]{1,0:T(8,128)(2,1)S(1)} %bitcast.149), channel_id=1, source_target_pairs={{2,0},{3,1},{4,2},{5,3},{6,4},{7,5},{8,6},{9,7},{10,8},{11,9},{12,... | collective-permute-start | bytes 786440 | tf_op jit(solution)/shard_map/while/body/eval_jaxpr/ppermute | solution.py:20
  475.5 10.2 %copy-start.8 = (bf16[4,256,512]{2,1,0:T(8,128)(2,1)S(1)}, bf16[4,256,512]{2,1,0:T(8,128)(2,1)}, u32[]{:S(2)}) copy-start(bf16[4,256,512]{2,1,0:T(8,128)(2,1)} %copy-done.7) | copy-start | bytes 3145732 | tf_op jit(solution)/shard_map/while
  478.2 7.5 %copy-start.1 = (bf16[512,1024]{1,0:T(8,128)(2,1)S(1)}, bf16[512,1024]{1,0:T(8,128)(2,1)}, u32[]{:S(2)}) copy-start(bf16[512,1024]{1,0:T(8,128)(2,1)} %copy-done) | copy-start | bytes 3145732 | tf_op jit(solution)/shard_map/while
  478.3 7.5 %copy-start.3 = (bf16[1,512,512]{2,1,0:T(8,128)(2,1)S(1)}, bf16[1,512,512]{2,1,0:T(8,128)(2,1)}, u32[]{:S(2)}) copy-start(bf16[1,512,512]{2,1,0:T(8,128)(2,1)} %get-tuple-element.612) | copy-start | bytes 1572868 | tf_op jit(solution)/shard_map/while
  480.6 5.1 %collective-permute-start.4 = (bf16[256,512]{1,0:T(8,128)(2,1)}, bf16[256,512]{1,0:T(8,128)(2,1)S(1)}, u32[]{:S(2)}, u32[]{:S(2)}) collective-permute-start(bf16[256,512]{1,0:T(8,128)(2,1)} %get-tuple-element.529), channel_id=1, source_target_pairs={{64,0},{65,1},{66,2},{67,3},{68,4},{69,5},{70,6},{71,7},{72,8},{73... | collective-permute-start | bytes 786440 | tf_op jit(solution)/shard_map/while/body/eval_jaxpr/ppermute | solution.py:20
  (4 other events, 5.4 us)

commit v4 on v1

--- a/solution.py
+++ b/solution.py
@@ -100,86 +100,122 @@
     )(queries, key_rows, value_rows, grad_attn)
 
 
+def swap_cores(value):
+    return lax.ppermute(value, "pipe", [(0, 1), (1, 0)])
+
+
+def pick(own, other, core, section):
+    return jnp.where(core == section, own, other)
+
+
+def prepare(rows, lists, weight_in, gain_row, myself):
+    points, model_width = rows.shape
+    block_count = points // BLK
+    offsets = [shift_by for shift_by in range(-REACH, REACH + 1) if shift_by != 0]
+    scaled, inverse, normed = normalize(rows, gain_row)
+    projected = jnp.dot(normed, weight_in, preferred_element_type=jnp.float32).astype(jnp.bfloat16)
+    received = jnp.stack([shifted(normed, "space", -shift_by) for shift_by in offsets])
+    received = received.reshape(len(offsets) * block_count, BLK, model_width)
+    owners = lists // block_count
+    within = lists % block_count
+    distance = owners - myself
+    slot = jnp.where(distance < 0, distance + REACH, distance + REACH - 1)
+    window_at = slot * block_count + within
+    fetched = jnp.take(received, window_at, axis=0).reshape(-1, model_width)
+    fetched_pairs = jnp.dot(
+        fetched, weight_in[:, model_width:], preferred_element_type=jnp.float32
+    ).astype(jnp.bfloat16)
+    pairs = jnp.concatenate([projected[:, model_width:], fetched_pairs], 0)
+    return scaled, inverse, projected[:, :model_width], pairs, window_at
+
+
+def block_backward(grad_out, prepared, weight_in, weight_out, gain_row):
+    scaled, inverse, queries, pairs, window_at = prepared
+    points, model_width = grad_out.shape
+    block_count = points // BLK
+    offsets = [shift_by for shift_by in range(-REACH, REACH + 1) if shift_by != 0]
+    weight_pairs = weight_in[:, model_width:]
+    grad_attn = jnp.dot(grad_out, weight_out.T, preferred_element_type=jnp.float32).astype(
+        jnp.bfloat16
+    )
+    grad_query, grad_key, grad_value = attend_backward(
+        queries, pairs[:, :model_width], pairs[:, model_width:], grad_attn
+    )
+    grad_pairs = jnp.concatenate([grad_key, grad_value], 1)
+    grad_remote = jnp.dot(
+        grad_pairs[points:].astype(jnp.bfloat16), weight_pairs.T, preferred_element_type=jnp.float32
+    ).reshape(-1, BLK, model_width)
+    window_grads = (
+        jnp.zeros((len(offsets) * block_count, BLK, model_width), jnp.float32)
+        .at[window_at]
+        .add(grad_remote)
+    ).reshape(len(offsets), points, model_width)
+    grad_project = jnp.concatenate([grad_query, grad_pairs[:points]], 1).astype(jnp.bfloat16)
+    grad_normed = jnp.dot(grad_project, weight_in.T, preferred_element_type=jnp.float32)
+    for slot_index, shift_by in enumerate(offsets):
+        grad_normed = grad_normed + shifted(
+            window_grads[slot_index].astype(jnp.bfloat16), "space", shift_by
+        ).astype(jnp.float32)
+    return (
+        grad_out.astype(jnp.float32) + norm_backward(grad_normed, scaled, inverse, gain_row)
+    ).astype(jnp.bfloat16)
+
+
 def shards(saved_inputs, project_in, project_out, norm_gains, neighbour_blocks, cotangent):
     sections = lax.axis_size("pipe")
-    segment_index = lax.axis_index("pipe")
+    core = lax.axis_index("pipe")
+    other = sections - 1 - core
     myself = lax.axis_index("space")
     micro_count = cotangent.shape[0]
-    points = cotangent.shape[1]
-    model_width = cotangent.shape[2]
-    weight_in = project_in[0]
-    weight_out = project_out[0]
-    gain_row = norm_gains[0]
-    block_count = points // BLK
-    offsets = [shift_by for shift_by in range(-REACH, REACH + 1) if shift_by != 0]
+    half = micro_count // sections
+
+    def mine(array, whose):
+        grouped = array.reshape((half, sections) + array.shape[1:])
+        return lax.dynamic_index_in_dim(grouped, whose, 1, keepdims=False)
+
     local_lists = neighbour_blocks[0, :, 0, :]
-
-    def step(step_index, state_pair):
-        incoming, collected = state_pair
-        micro_index = step_index - (sections - 1 - segment_index)
-        active = (micro_index >= 0) & (micro_index < micro_count)
-        chosen = jnp.clip(micro_index, 0, micro_count - 1)
-        grad_out = jnp.where(
-            segment_index == sections - 1,
-            lax.dynamic_index_in_dim(cotangent, chosen, 0, keepdims=False),
-            incoming,
-        )
-        points_in = lax.dynamic_index_in_dim(saved_inputs[0], chosen, 0, keepdims=False)
-        block_ids = lax.dynamic_index_in_dim(local_lists, chosen, 0, keepdims=False)
-        owners = block_ids // block_count
-        within = block_ids % block_count
-        distance = owners - myself
-        scaled, inverse, normed = normalize(points_in, gain_row)
-        projected = jnp.dot(normed, weight_in, preferred_element_type=jnp.float32).astype(
-            jnp.bfloat16
-        )
-        queries = projected[:, :model_width]
-        own_pairs = projected[:, model_width:]
-        grad_attn = jnp.dot(grad_out, weight_out.T, preferred_element_type=jnp.float32).astype(
-            jnp.bfloat16
-        )
-        received = []
-        for shift_by in offsets:
-            received.append(shifted(own_pairs, "space", -shift_by))
-        window_blocks = jnp.stack(received).reshape(
-            len(offsets) * block_count, BLK, 2 * model_width
-        )
-        position = (
-            jnp.where(distance < 0, distance + REACH, distance + REACH - 1) * block_count + within
-        )
-        fetched = jnp.take(window_blocks, position, axis=0)
-        combined = jnp.concatenate([own_pairs, fetched.reshape(-1, 2 * model_width)], 0)
-        grad_query, grad_key, grad_value = attend_backward(
-            queries, combined[:, :model_width], combined[:, model_width:], grad_attn
-        )
-        grad_pairs = jnp.concatenate([grad_key, grad_value], 1)
-        grad_own = grad_pairs[:points]
-        grad_remote = grad_pairs[points:].reshape(-1, BLK, 2 * model_width)
-        window_grads = (
-            jnp.zeros((len(offsets) * block_count, BLK, 2 * model_width), jnp.float32)
-            .at[position]
-            .add(grad_remote)
-        )
-        window_grads = window_grads.reshape(len(offsets), points, 2 * model_width)
-        for slot_index, shift_by in enumerate(offsets):
-            grad_own = grad_own + shifted(window_grads[slot_index], "space", shift_by)
-        grad_project = jnp.concatenate([grad_query, grad_own], 1).astype(jnp.bfloat16)
-        grad_normed = jnp.dot(grad_project, weight_in.T, preferred_element_type=jnp.float32)
-        result = (
-            grad_out.astype(jnp.float32) + norm_backward(grad_normed, scaled, inverse, gain_row)
-        ).astype(jnp.bfloat16)
-        collected = jnp.where(
-            active, lax.dynamic_update_index_in_dim(collected, result, chosen, 0), collected
-        )
-        passed = shifted(result, "pipe", -1)
-        return (passed, collected)
-
-    start_state = (
-        jnp.zeros((points, model_width), jnp.bfloat16),
-        jnp.zeros((micro_count, points, model_width), jnp.bfloat16),
-    )
-    final_state = lax.fori_loop(0, micro_count + sections - 1, step, start_state)
-    return final_state[1][None]
+    own = (
+        mine(saved_inputs[0], core),
+        mine(local_lists, core),
+        project_in[0],
+        project_out[0],
+        norm_gains[0],
+    )
+    got = swap_cores(
+        (mine(saved_inputs[0], other), mine(local_lists, other), project_in[0], project_out[0], norm_gains[0])
+    )
+    params = [
+        [pick(own_part, got_part, core, section) for own_part, got_part in zip(own, got)]
+        for section in range(sections)
+    ]
+    cotangent_mine = mine(cotangent, core)
+    prepared = [
+        [
+            prepare(params[section][0][j], params[section][1][j], params[section][2], params[section][4], myself)
+            for j in range(half)
+        ]
+        for section in range(sections)
+    ]
+    results = [[None] * half for _ in range(sections)]
+    exchanged = [[None] * half for _ in range(sections)]
+    for section in range(sections - 1, -1, -1):
+        _, _, weight_in, weight_out, gain_row = params[section]
+        for j in range(half):
+            grad_out = cotangent_mine[j] if section == sections - 1 else results[section + 1][j]
+            results[section][j] = block_backward(
+                grad_out, prepared[section][j], weight_in, weight_out, gain_row
+            )
+            exchanged[section][j] = swap_cores(results[section][j])
+    own_out = jnp.stack(
+        [pick(results[0][j], results[1][j], core, 0) for j in range(half)]
+    )
+    other_out = jnp.stack(
+        [pick(exchanged[0][j], exchanged[1][j], core, 0) for j in range(half)]
+    )
+    grouped = jnp.stack(
+        [pick(own_out, other_out, core, parity) for parity in range(sections)], 1
+    )
+    return grouped.reshape((1, micro_count) + grouped.shape[2:])
 
 
 def solution(mesh):

time: 941 us -> 367 us (0.39)
  the two profiles are of different devices: /device:TPU:5 before, /device:TPU:15 now
where the time goes in v4:
time: 367 us; the launch traced here: 363 us
  starting transfers between devices  141 us (38%)
  Pallas kernels  118 us (32%)
  other arithmetic  43.7 us (12%)
  matrix products  19.9 us (5%)
  waiting for transfers between devices  19.6 us (5%)
  local copies, waits for them, and re-layouts  19.5 us (5%)
    ppermute x32, starting transfers between devices, shifted(): return lax.ppermute(x, axis, pairs)  126 us
    pallas_call x4, Pallas kernels, attend_backward(): pl.pallas_call(attention_kernel, grid=(groups,), in_specs=[row_spec, key_...  118 us
    ppermute x32, waiting for transfers between devices, shifted(): return lax.ppermute(x, axis, pairs)  17.6 us
    ppermute x9, starting transfers between devices, swap_cores(): return lax.ppermute(value, 'pipe', [(0, 1), (1, 0)])  15.8 us
    another operation x12, other arithmetic  13.8 us
    scatter-add x4, other arithmetic, block_backward(): window_grads = jnp.zeros((len(offsets) * block_count, BLK, model_width),...  10.6 us
  transfers between devices with their start and end apart: 41, of which 8 were waited for; matrix products, arithmetic and copies ran while one was open for 11% of the time, Pallas kernels for 8%

profile of v4, /device:TPU:15, one launch (start us, length us, event | category | flops | bytes accessed | tf_op | source)
XLA Modules:
  0.0 363.5 jit_solution(18390190114941614128)
XLA Ops:
  6.9 7.8 %collective-permute-start.24 = (bf16[256,512]{1,0:T(8,128)(2,1)S(1)}, bf16[256,512]{1,0:T(8,128)(2,1)S(1)}, u32[]{:S(2)}, u32[]{:S(2)}) collective-permute-start(bf16[256,512]{1,0:T(8,128)(2,1)S(1)} %get-tuple-element.93), channel_id=1, source_target_pairs={{2,0},{3,1},{4,2},{5,3},{6,4},{7,5},{8,6},{9,7},{10,8},{11,9},{12,... | collective-permute-start | bytes 786440 | tf_op jit(solution)/shard_map/ppermute | solution.py:20
  14.7 3.0 collective-permute-start.23
  17.7 2.3 collective-permute-start.22
  20.0 1.9 collective-permute-start.21
  23.3 8.0 %collective-permute-start.6 = (bf16[256,512]{1,0:T(8,128)(2,1)S(1)}, bf16[256,512]{1,0:T(8,128)(2,1)S(1)}, u32[]{:S(2)}, u32[]{:S(2)}) collective-permute-start(bf16[256,512]{1,0:T(8,128)(2,1)S(1)} %get-tuple-element.92), channel_id=1, source_target_pairs={{2,0},{3,1},{4,2},{5,3},{6,4},{7,5},{8,6},{9,7},{10,8},{11,9},{12,... | collective-permute-start | bytes 786440 | tf_op jit(solution)/shard_map/ppermute | solution.py:20
  31.3 3.0 collective-permute-start.5
  34.3 2.3 collective-permute-start.4
  36.6 1.9 collective-permute-start.3
  40.5 3.5 collective-permute-start.2
  44.0 8.3 %collective-permute-start.32 = (bf16[256,512]{1,0:T(8,128)(2,1)S(1)}, bf16[256,512]{1,0:T(8,128)(2,1)}, u32[]{:S(2)}, u32[]{:S(2)}) collective-permute-start(bf16[256,512]{1,0:T(8,128)(2,1)S(1)} %get-tuple-element.90), channel_id=1, source_target_pairs={{2,0},{3,1},{4,2},{5,3},{6,4},{7,5},{8,6},{9,7},{10,8},{11,9},{12,... | collective-permute-start | bytes 786440 | tf_op jit(solution)/shard_map/ppermute | solution.py:20
  52.3 3.1 collective-permute-start.31
  55.5 2.2 collective-permute-start.30
  57.7 1.9 collective-permute-start.29
  61.4 9.4 %collective-permute-start.16 = (bf16[256,512]{1,0:T(8,128)(2,1)}, bf16[256,512]{1,0:T(8,128)(2,1)}, u32[]{:S(2)}, u32[]{:S(2)}) collective-permute-start(bf16[256,512]{1,0:T(8,128)(2,1)} %get-tuple-element.91), channel_id=1, source_target_pairs={{2,0},{3,1},{4,2},{5,3},{6,4},{7,5},{8,6},{9,7},{10,8},{11,9},{12,... | collective-permute-start | bytes 786440 | tf_op jit(solution)/shard_map/ppermute | solution.py:20
  70.8 3.1 collective-permute-start.15
  73.9 2.2 collective-permute-start.14
  76.1 2.3 collective-permute-done.29
  78.4 1.9 collective-permute-start.13
  82.1 1.3 pad_maximum_fusion.3
  84.1 10.2 %collective-permute-done.13 = bf16[256,512]{1,0:T(8,128)(2,1)} collective-permute-done((bf16[256,512]{1,0:T(8,128)(2,1)}, bf16[256,512]{1,0:T(8,128)(2,1)}, u32[]{:S(2)}, u32[]{:S(2)}) %collective-permute-start.13) | collective-permute-done | bytes 262176 | tf_op jit(solution)/shard_map/ppermute | solution.py:20
  99.4 2.1 broadcast_select_fusion
  104.4 29.5 %shard_map.66 = (f32[256,512]{1,0:T(8,128)}, f32[512,512]{1,0:T(8,128)}, f32[512,512]{1,0:T(8,128)}) custom-call(bf16[256,512]{1,0:T(8,128)(2,1)} %slice.289.q_ref, bf16[512,512]{1,0:T(8,128)(2,1)} %get-tuple-element.89.k_ref, bf16[512,512]{1,0:T(8,128)(2,1)} %get-tuple-element.88.v_ref, bf16[256,512]{1,0:T(8,128)(2,1)} %convolution_convert_fusion.9.g_ref), custom_call_target="tpu_custom_call" | custom-call | flops 5368709120 | bytes 4194304 | tf_op jit(solution)/shard_map/pallas_call | solution.py:85
  133.9 1.7 maximum_convert_fusion.2
  139.7 29.5 %shard_map.64 = (f32[256,512]{1,0:T(8,128)}, f32[512,512]{1,0:T(8,128)}, f32[512,512]{1,0:T(8,128)}) custom-call(bf16[256,512]{1,0:T(8,128)(2,1)} %slice.265.q_ref, bf16[512,512]{1,0:T(8,128)(2,1)} %get-tuple-element.83.k_ref, bf16[512,512]{1,0:T(8,128)(2,1)} %get-tuple-element.82.v_ref, bf16[256,512]{1,0:T(8,128)(2,1)} %convolution_convert_fusion.11.g_ref), custom_call_target="tpu_custom_call" | custom-call | flops 5368709120 | bytes 4194304 | tf_op jit(solution)/shard_map/pallas_call | solution.py:85
  169.2 1.7 maximum_convert_fusion
  173.6 1.6 convolution_convert_fusion.2
  176.9 1.6 broadcast.691.clone
  178.5 2.7 scatter_fusion.2
  181.2 1.7 convert.64
  183.9 1.9 collective-permute-start.28
  185.8 2.1 collective-permute-start.27
  188.0 3.4 collective-permute-start.26
  191.3 7.9 %collective-permute-start.25 = (bf16[256,512]{1,0:T(8,128)(2,1)}, bf16[256,512]{1,0:T(8,128)(2,1)}, u32[]{:S(2)}, u32[]{:S(2)}) collective-permute-start(bf16[256,512]{1,0:T(8,128)(2,1)} %bitcast.53), channel_id=1, source_target_pairs={{2,0},{3,1},{4,2},{5,3},{6,4},{7,5},{8,6},{9,7},{10,8},{11,9},{12,... | collective-permute-start | bytes 786440 | tf_op jit(solution)/shard_map/ppermute | solution.py:20
  199.2 1.6 broadcast.691.clone.1
  200.8 2.6 scatter_fusion
  203.5 1.7 convert.58
  205.3 2.1 collective-permute-start.12
  210.6 2.6 collective-permute-start.11
  213.2 3.7 %collective-permute-start.10 = (bf16[256,512]{1,0:T(8,128)(2,1)S(1)}, bf16[256,512]{1,0:T(8,128)(2,1)S(1)}, u32[]{:S(2)}, u32[]{:S(2)}) collective-permute-start(bf16[256,512]{1,0:T(8,128)(2,1)S(1)} %bitcast.392), channel_id=1, source_target_pairs={{1,0},{2,1},{3,2},{4,3},{5,4},{6,5},{7,6},{8,7},{9,8},{10,9},{11,1... | collective-permute-start | bytes 786440 | tf_op jit(solution)/shard_map/ppermute | solution.py:20
  217.0 7.0 %collective-permute-start.9 = (bf16[256,512]{1,0:T(8,128)(2,1)S(1)}, bf16[256,512]{1,0:T(8,128)(2,1)S(1)}, u32[]{:S(2)}, u32[]{:S(2)}) collective-permute-start(bf16[256,512]{1,0:T(8,128)(2,1)S(1)} %bitcast.391), channel_id=1, source_target_pairs={{2,0},{3,1},{4,2},{5,3},{6,4},{7,5},{8,6},{9,7},{10,8},{11,9},{12,... | collective-permute-start | bytes 786440 | tf_op jit(solution)/shard_map/ppermute | solution.py:20
  224.0 1.9 fusion.7
  225.9 1.5 collective-permute-done.9
  230.6 29.5 %shard_map.67 = (f32[256,512]{1,0:T(8,128)}, f32[512,512]{1,0:T(8,128)}, f32[512,512]{1,0:T(8,128)}) custom-call(bf16[256,512]{1,0:T(8,128)(2,1)} %slice.300.q_ref, bf16[512,512]{1,0:T(8,128)(2,1)} %get-tuple-element.71.k_ref, bf16[512,512]{1,0:T(8,128)(2,1)} %get-tuple-element.70.v_ref, bf16[256,512]{1,0:T(8,128)(2,1)} %convolution_convert_fusion.8.g_ref), custom_call_target="tpu_custom_call" | custom-call | flops 5368709120 | bytes 4194304 | tf_op jit(solution)/shard_map/pallas_call | solution.py:85
  260.1 1.7 maximum_convert_fusion.3
  263.1 1.6 broadcast.691.clone.2
  264.7 2.7 scatter_fusion.3
  267.4 1.7 convert.67
  270.2 2.2 collective-permute-start.36
  272.4 3.2 collective-permute-start.35
  275.6 4.3 %collective-permute-start.34 = (bf16[256,512]{1,0:T(8,128)(2,1)}, bf16[256,512]{1,0:T(8,128)(2,1)}, u32[]{:S(2)}, u32[]{:S(2)}) collective-permute-start(bf16[256,512]{1,0:T(8,128)(2,1)} %bitcast.69), channel_id=1, source_target_pairs={{1,0},{2,1},{3,2},{4,3},{5,4},{6,5},{7,6},{8,7},{9,8},{10,9},{11,1... | collective-permute-start | bytes 786440 | tf_op jit(solution)/shard_map/ppermute | solution.py:20
  279.9 7.3 %collective-permute-start.33 = (bf16[256,512]{1,0:T(8,128)(2,1)}, bf16[256,512]{1,0:T(8,128)(2,1)}, u32[]{:S(2)}, u32[]{:S(2)}) collective-permute-start(bf16[256,512]{1,0:T(8,128)(2,1)} %bitcast.68), channel_id=1, source_target_pairs={{2,0},{3,1},{4,2},{5,3},{6,4},{7,5},{8,6},{9,7},{10,8},{11,9},{12,... | collective-permute-start | bytes 786440 | tf_op jit(solution)/shard_map/ppermute | solution.py:20
  288.3 29.5 %shard_map.65 = (f32[256,512]{1,0:T(8,128)}, f32[512,512]{1,0:T(8,128)}, f32[512,512]{1,0:T(8,128)}) custom-call(bf16[256,512]{1,0:T(8,128)(2,1)} %slice.277.q_ref, bf16[512,512]{1,0:T(8,128)(2,1)} %get-tuple-element.77.k_ref, bf16[512,512]{1,0:T(8,128)(2,1)} %get-tuple-element.76.v_ref, bf16[256,512]{1,0:T(8,128)(2,1)} %convolution_convert_fusion.10.g_ref), custom_call_target="tpu_custom_call" | custom-call | flops 5368709120 | bytes 4194304 | tf_op jit(solution)/shard_map/pallas_call | solution.py:85
  317.8 1.7 maximum_convert_fusion.1
  320.7 6.2 %collective-permute-start.40 = (bf16[256,512]{1,0:T(8,128)(2,1)S(1)}, bf16[256,512]{1,0:T(8,128)(2,1)S(1)}, u32[]{:S(2)}, u32[]{:S(2)}) collective-permute-start(bf16[256,512]{1,0:T(8,128)(2,1)S(1)} %get-tuple-element.61), channel_id=1, source_target_pairs={{0,64},{64,0},{1,65},{65,1},{2,66},{66,2},{3,67},{67,3},{4,68},{68... | collective-permute-start | bytes 786440 | tf_op jit(solution)/shard_map/ppermute | solution.py:104
  327.0 1.6 broadcast.691.clone.3
  328.6 2.5 scatter_fusion.1
  331.2 1.8 convert.61
  333.1 1.9 collective-permute-start.20
  335.1 3.4 collective-permute-start.19
  338.5 3.7 %collective-permute-start.18 = (bf16[256,512]{1,0:T(8,128)(2,1)S(1)}, bf16[256,512]{1,0:T(8,128)(2,1)S(1)}, u32[]{:S(2)}, u32[]{:S(2)}) collective-permute-start(bf16[256,512]{1,0:T(8,128)(2,1)S(1)} %bitcast.396), channel_id=1, source_target_pairs={{1,0},{2,1},{3,2},{4,3},{5,4},{6,5},{7,6},{8,7},{9,8},{10,9},{11,1... | collective-permute-start | bytes 786440 | tf_op jit(solution)/shard_map/ppermute | solution.py:20
  342.2 6.8 %collective-permute-start.17 = (bf16[256,512]{1,0:T(8,128)(2,1)S(1)}, bf16[256,512]{1,0:T(8,128)(2,1)S(1)}, u32[]{:S(2)}, u32[]{:S(2)}) collective-permute-start(bf16[256,512]{1,0:T(8,128)(2,1)S(1)} %bitcast.395), channel_id=1, source_target_pairs={{2,0},{3,1},{4,2},{5,3},{6,4},{7,5},{8,6},{9,7},{10,8},{11,9},{12,... | collective-permute-start | bytes 786440 | tf_op jit(solution)/shard_map/ppermute | solution.py:20
  349.1 1.9 fusion.3
  351.0 3.5 collective-permute-done.17
  356.2 4.2 %collective-permute-start.39 = (bf16[256,512]{1,0:T(8,128)(2,1)S(1)}, bf16[256,512]{1,0:T(8,128)(2,1)S(1)}, u32[]{:S(2)}, u32[]{:S(2)}) collective-permute-start(bf16[256,512]{1,0:T(8,128)(2,1)S(1)} %get-tuple-element.95), channel_id=1, source_target_pairs={{0,64},{64,0},{1,65},{65,1},{2,66},{66,2},{3,67},{67,3},{4,68},{68... | collective-permute-start | bytes 786440 | tf_op jit(solution)/shard_map/ppermute | solution.py:104
  (216 shorter events, 47.6 us)
Async XLA Ops:
  1.1 3.9 %collective-permute-start = (bf16[2,256,512]{2,1,0:T(8,128)(2,1)S(1)}, bf16[2,256,512]{2,1,0:T(8,128)(2,1)S(1)}, u32[]{:S(2)}, u32[]{:S(2)}) collective-permute-start(bf16[2,256,512]{2,1,0:T(8,128)(2,1)S(1)} %dynamic-slice_bitcast_fusion), channel_id=1, source_target_pairs={{0,64},{64,0},{1,65},{65,1},{2,66},{66,2},{3,67},{67,3},{4,68},{68... | collective-permute-start | bytes 1572872 | tf_op jit(solution)/shard_map/ppermute | solution.py:104
  1.8 2.4 collective-permute-start.1
  2.9 1.2 collective-permute-start.7
  3.3 19.1 %collective-permute-start.8 = (bf16[512,512]{1,0:T(8,128)(2,1)}, bf16[512,512]{1,0:T(8,128)(2,1)S(1)}, u32[]{:S(2)}, u32[]{:S(2)}) collective-permute-start(bf16[512,512]{1,0:T(8,128)(2,1)} %bitcast.402), channel_id=1, source_target_pairs={{0,64},{64,0},{1,65},{65,1},{2,66},{66,2},{3,67},{67,3},{4,68},{68... | collective-permute-start | bytes 1572872 | tf_op jit(solution)/shard_map/ppermute | solution.py:104
  6.1 16.3 %copy-start = (bf16[2,256,512]{2,1,0:T(8,128)(2,1)}, bf16[2,256,512]{2,1,0:T(8,128)(2,1)S(1)}, u32[]{:S(2)}) copy-start(bf16[2,256,512]{2,1,0:T(8,128)(2,1)S(1)} %get-tuple-element.63) | copy-start | bytes 1572868
  6.1 32.5 %copy-start.2 = (bf16[2,256,512]{2,1,0:T(8,128)(2,1)}, bf16[2,256,512]{2,1,0:T(8,128)(2,1)S(1)}, u32[]{:S(2)}) copy-start(bf16[2,256,512]{2,1,0:T(8,128)(2,1)S(1)} %get-tuple-element.62) | copy-start | bytes 1572868
  6.6 32.9 %copy-start.23 = (bf16[4,256,512]{2,1,0:T(8,128)(2,1)S(1)}, bf16[4,256,512]{2,1,0:T(8,128)(2,1)}, u32[]{:S(2)}) copy-start(bf16[4,256,512]{2,1,0:T(8,128)(2,1)} %param.13) | copy-start | bytes 3145732
  6.6 32.9 %copy-start.31 = (bf16[1,512,512]{2,1,0:T(8,128)(2,1)S(1)}, bf16[1,512,512]{2,1,0:T(8,128)(2,1)}, u32[]{:S(2)}) copy-start(bf16[1,512,512]{2,1,0:T(8,128)(2,1)} %param.10) | copy-start | bytes 1572868
  6.9 33.7 %copy-start.12 = (bf16[256,512]{1,0:T(8,128)(2,1)}, bf16[256,512]{1,0:T(8,128)(2,1)S(1)}, u32[]{:S(2)}) copy-start(bf16[256,512]{1,0:T(8,128)(2,1)S(1)} %get-tuple-element.92) | copy-start | bytes 786436
  6.9 33.7 %copy-start.14 = (bf16[256,512]{1,0:T(8,128)(2,1)}, bf16[256,512]{1,0:T(8,128)(2,1)S(1)}, u32[]{:S(2)}) copy-start(bf16[256,512]{1,0:T(8,128)(2,1)S(1)} %get-tuple-element.93) | copy-start | bytes 786436
  6.9 24.4 %collective-permute-start.24 = (bf16[256,512]{1,0:T(8,128)(2,1)S(1)}, bf16[256,512]{1,0:T(8,128)(2,1)S(1)}, u32[]{:S(2)}, u32[]{:S(2)}) collective-permute-start(bf16[256,512]{1,0:T(8,128)(2,1)S(1)} %get-tuple-element.93), channel_id=1, source_target_pairs={{2,0},{3,1},{4,2},{5,3},{6,4},{7,5},{8,6},{9,7},{10,8},{11,9},{12,... | collective-permute-start | bytes 786440 | tf_op jit(solution)/shard_map/ppermute | solution.py:20
  14.7 19.6 %collective-permute-start.23 = (bf16[256,512]{1,0:T(8,128)(2,1)S(1)}, bf16[256,512]{1,0:T(8,128)(2,1)S(1)}, u32[]{:S(2)}, u32[]{:S(2)}) collective-permute-start(bf16[256,512]{1,0:T(8,128)(2,1)S(1)} %get-tuple-element.93), channel_id=1, source_target_pairs={{1,0},{2,1},{3,2},{4,3},{5,4},{6,5},{7,6},{8,7},{9,8},{10,9},{11,1... | collective-permute-start | bytes 786440 | tf_op jit(solution)/shard_map/ppermute | solution.py:20
  17.7 18.9 %collective-permute-start.22 = (bf16[256,512]{1,0:T(8,128)(2,1)S(1)}, bf16[256,512]{1,0:T(8,128)(2,1)S(1)}, u32[]{:S(2)}, u32[]{:S(2)}) collective-permute-start(bf16[256,512]{1,0:T(8,128)(2,1)S(1)} %get-tuple-element.93), channel_id=1, source_target_pairs={{0,1},{1,2},{2,3},{3,4},{4,5},{5,6},{6,7},{7,8},{8,9},{9,10},{10,1... | collective-permute-start | bytes 786440 | tf_op jit(solution)/shard_map/ppermute | solution.py:20
  20.0 20.6 %collective-permute-start.21 = (bf16[256,512]{1,0:T(8,128)(2,1)S(1)}, bf16[256,512]{1,0:T(8,128)(2,1)S(1)}, u32[]{:S(2)}, u32[]{:S(2)}) collective-permute-start(bf16[256,512]{1,0:T(8,128)(2,1)S(1)} %get-tuple-element.93), channel_id=1, source_target_pairs={{0,2},{1,3},{2,4},{3,5},{4,6},{5,7},{6,8},{7,9},{8,10},{9,11},{10,... | collective-permute-start | bytes 786440 | tf_op jit(solution)/shard_map/ppermute | solution.py:20
  22.1 18.5 %copy-start.10 = (bf16[1,512,1536]{2,1,0:T(8,128)(2,1)S(1)}, bf16[1,512,1536]{2,1,0:T(8,128)(2,1)}, u32[]{:S(2)}) copy-start(bf16[1,512,1536]{2,1,0:T(8,128)(2,1)} %param.9) | copy-start | bytes 4718596
  23.3 36.4 %copy-start.35 = (bf16[512,512]{1,0:T(8,128)(2,1)S(1)}, bf16[512,512]{1,0:T(8,128)(2,1)}, u32[]{:S(2)}) copy-start(bf16[512,512]{1,0:T(8,128)(2,1)} %copy-done.34) | copy-start | bytes 1572868
  23.3 20.8 %collective-permute-start.6 = (bf16[256,512]{1,0:T(8,128)(2,1)S(1)}, bf16[256,512]{1,0:T(8,128)(2,1)S(1)}, u32[]{:S(2)}, u32[]{:S(2)}) collective-permute-start(bf16[256,512]{1,0:T(8,128)(2,1)S(1)} %get-tuple-element.92), channel_id=1, source_target_pairs={{2,0},{3,1},{4,2},{5,3},{6,4},{7,5},{8,6},{9,7},{10,8},{11,9},{12,... | collective-permute-start | bytes 786440 | tf_op jit(solution)/shard_map/ppermute | solution.py:20
  31.3 21.0 %collective-permute-start.5 = (bf16[256,512]{1,0:T(8,128)(2,1)S(1)}, bf16[256,512]{1,0:T(8,128)(2,1)S(1)}, u32[]{:S(2)}, u32[]{:S(2)}) collective-permute-start(bf16[256,512]{1,0:T(8,128)(2,1)S(1)} %get-tuple-element.92), channel_id=1, source_target_pairs={{1,0},{2,1},{3,2},{4,3},{5,4},{6,5},{7,6},{8,7},{9,8},{10,9},{11,1... | collective-permute-start | bytes 786440 | tf_op jit(solution)/shard_map/ppermute | solution.py:20
  34.3 21.2 %collective-permute-start.4 = (bf16[256,512]{1,0:T(8,128)(2,1)S(1)}, bf16[256,512]{1,0:T(8,128)(2,1)S(1)}, u32[]{:S(2)}, u32[]{:S(2)}) collective-permute-start(bf16[256,512]{1,0:T(8,128)(2,1)S(1)} %get-tuple-element.92), channel_id=1, source_target_pairs={{0,1},{1,2},{2,3},{3,4},{4,5},{5,6},{6,7},{7,8},{8,9},{9,10},{10,1... | collective-permute-start | bytes 786440 | tf_op jit(solution)/shard_map/ppermute | solution.py:20
  36.6 21.1 %collective-permute-start.3 = (bf16[256,512]{1,0:T(8,128)(2,1)S(1)}, bf16[256,512]{1,0:T(8,128)(2,1)S(1)}, u32[]{:S(2)}, u32[]{:S(2)}) collective-permute-start(bf16[256,512]{1,0:T(8,128)(2,1)S(1)} %get-tuple-element.92), channel_id=1, source_target_pairs={{0,2},{1,3},{2,4},{3,5},{4,6},{5,7},{6,8},{7,9},{8,10},{9,11},{10,... | collective-permute-start | bytes 786440 | tf_op jit(solution)/shard_map/ppermute | solution.py:20
  39.5 21.2 %copy-start.16 = (bf16[256,512]{1,0:T(8,128)(2,1)}, bf16[256,512]{1,0:T(8,128)(2,1)S(1)}, u32[]{:S(2)}) copy-start(bf16[256,512]{1,0:T(8,128)(2,1)S(1)} %get-tuple-element.90) | copy-start | bytes 786436
  40.5 58.9 %collective-permute-start.2 = (bf16[512,1536]{1,0:T(8,128)(2,1)S(1)}, bf16[512,1536]{1,0:T(8,128)(2,1)}, u32[]{:S(2)}, u32[]{:S(2)}) collective-permute-start(bf16[512,1536]{1,0:T(8,128)(2,1)S(1)} %bitcast.369), channel_id=1, source_target_pairs={{0,64},{64,0},{1,65},{65,1},{2,66},{66,2},{3,67},{67,3},{4,68},{68... | collective-permute-start | bytes 4718600 | tf_op jit(solution)/shard_map/ppermute | solution.py:104
  44.0 17.4 %collective-permute-start.32 = (bf16[256,512]{1,0:T(8,128)(2,1)S(1)}, bf16[256,512]{1,0:T(8,128)(2,1)}, u32[]{:S(2)}, u32[]{:S(2)}) collective-permute-start(bf16[256,512]{1,0:T(8,128)(2,1)S(1)} %get-tuple-element.90), channel_id=1, source_target_pairs={{2,0},{3,1},{4,2},{5,3},{6,4},{7,5},{8,6},{9,7},{10,8},{11,9},{12,... | collective-permute-start | bytes 786440 | tf_op jit(solution)/shard_map/ppermute | solution.py:20
  52.3 8.5 %copy-start.28 = (bf16[256,512]{1,0:T(8,128)(2,1)}, bf16[256,512]{1,0:T(8,128)(2,1)S(1)}, u32[]{:S(2)}) copy-start(bf16[256,512]{1,0:T(8,128)(2,1)S(1)} %collective-permute-done.5) | copy-start | bytes 786436
  52.3 18.5 %collective-permute-start.31 = (bf16[256,512]{1,0:T(8,128)(2,1)S(1)}, bf16[256,512]{1,0:T(8,128)(2,1)}, u32[]{:S(2)}, u32[]{:S(2)}) collective-permute-start(bf16[256,512]{1,0:T(8,128)(2,1)S(1)} %get-tuple-element.90), channel_id=1, source_target_pairs={{1,0},{2,1},{3,2},{4,3},{5,4},{6,5},{7,6},{8,7},{9,8},{10,9},{11,1... | collective-permute-start | bytes 786440 | tf_op jit(solution)/shard_map/ppermute | solution.py:20
  55.5 5.4 %copy-start.29 = (bf16[256,512]{1,0:T(8,128)(2,1)}, bf16[256,512]{1,0:T(8,128)(2,1)S(1)}, u32[]{:S(2)}) copy-start(bf16[256,512]{1,0:T(8,128)(2,1)S(1)} %collective-permute-done.4) | copy-start | bytes 786436
  55.5 18.4 %collective-permute-start.30 = (bf16[256,512]{1,0:T(8,128)(2,1)S(1)}, bf16[256,512]{1,0:T(8,128)(2,1)}, u32[]{:S(2)}, u32[]{:S(2)}) collective-permute-start(bf16[256,512]{1,0:T(8,128)(2,1)S(1)} %get-tuple-element.90), channel_id=1, source_target_pairs={{0,1},{1,2},{2,3},{3,4},{4,5},{5,6},{6,7},{7,8},{8,9},{9,10},{10,1... | collective-permute-start | bytes 786440 | tf_op jit(solution)/shard_map/ppermute | solution.py:20
  57.7 20.7 %collective-permute-start.29 = (bf16[256,512]{1,0:T(8,128)(2,1)S(1)}, bf16[256,512]{1,0:T(8,128)(2,1)}, u32[]{:S(2)}, u32[]{:S(2)}) collective-permute-start(bf16[256,512]{1,0:T(8,128)(2,1)S(1)} %get-tuple-element.90), channel_id=1, source_target_pairs={{0,2},{1,3},{2,4},{3,5},{4,6},{5,7},{6,8},{7,9},{8,10},{9,11},{10,... | collective-permute-start | bytes 786440 | tf_op jit(solution)/shard_map/ppermute | solution.py:20
  61.4 22.6 %collective-permute-start.16 = (bf16[256,512]{1,0:T(8,128)(2,1)}, bf16[256,512]{1,0:T(8,128)(2,1)}, u32[]{:S(2)}, u32[]{:S(2)}) collective-permute-start(bf16[256,512]{1,0:T(8,128)(2,1)} %get-tuple-element.91), channel_id=1, source_target_pairs={{2,0},{3,1},{4,2},{5,3},{6,4},{7,5},{8,6},{9,7},{10,8},{11,9},{12,... | collective-permute-start | bytes 786440 | tf_op jit(solution)/shard_map/ppermute | solution.py:20
  70.8 13.2 %collective-permute-start.15 = (bf16[256,512]{1,0:T(8,128)(2,1)}, bf16[256,512]{1,0:T(8,128)(2,1)}, u32[]{:S(2)}, u32[]{:S(2)}) collective-permute-start(bf16[256,512]{1,0:T(8,128)(2,1)} %get-tuple-element.91), channel_id=1, source_target_pairs={{1,0},{2,1},{3,2},{4,3},{5,4},{6,5},{7,6},{8,7},{9,8},{10,9},{11,1... | collective-permute-start | bytes 786440 | tf_op jit(solution)/shard_map/ppermute | solution.py:20
  73.9 10.1 %collective-permute-start.14 = (bf16[256,512]{1,0:T(8,128)(2,1)}, bf16[256,512]{1,0:T(8,128)(2,1)}, u32[]{:S(2)}, u32[]{:S(2)}) collective-permute-start(bf16[256,512]{1,0:T(8,128)(2,1)} %get-tuple-element.91), channel_id=1, source_target_pairs={{0,1},{1,2},{2,3},{3,4},{4,5},{5,6},{6,7},{7,8},{8,9},{9,10},{10,1... | collective-permute-start | bytes 786440 | tf_op jit(solution)/shard_map/ppermute | solution.py:20
  78.4 15.9 %collective-permute-start.13 = (bf16[256,512]{1,0:T(8,128)(2,1)}, bf16[256,512]{1,0:T(8,128)(2,1)}, u32[]{:S(2)}, u32[]{:S(2)}) collective-permute-start(bf16[256,512]{1,0:T(8,128)(2,1)} %get-tuple-element.91), channel_id=1, source_target_pairs={{0,2},{1,3},{2,4},{3,5},{4,6},{5,7},{6,8},{7,9},{8,10},{9,11},{10,... | collective-permute-start | bytes 786440 | tf_op jit(solution)/shard_map/ppermute | solution.py:20
  173.6 3.2 copy-start.20
  183.9 26.7 %collective-permute-start.28 = (bf16[256,512]{1,0:T(8,128)(2,1)}, bf16[256,512]{1,0:T(8,128)(2,1)}, u32[]{:S(2)}, u32[]{:S(2)}) collective-permute-start(bf16[256,512]{1,0:T(8,128)(2,1)} %bitcast.56), channel_id=1, source_target_pairs={{0,2},{1,3},{2,4},{3,5},{4,6},{5,7},{6,8},{7,9},{8,10},{9,11},{10,... | collective-permute-start | bytes 786440 | tf_op jit(solution)/shard_map/ppermute | solution.py:20
  185.8 27.4 %collective-permute-start.27 = (bf16[256,512]{1,0:T(8,128)(2,1)}, bf16[256,512]{1,0:T(8,128)(2,1)}, u32[]{:S(2)}, u32[]{:S(2)}) collective-permute-start(bf16[256,512]{1,0:T(8,128)(2,1)} %bitcast.55), channel_id=1, source_target_pairs={{0,1},{1,2},{2,3},{3,4},{4,5},{5,6},{6,7},{7,8},{8,9},{9,10},{10,1... | collective-permute-start | bytes 786440 | tf_op jit(solution)/shard_map/ppermute | solution.py:20
  188.0 29.0 %collective-permute-start.26 = (bf16[256,512]{1,0:T(8,128)(2,1)}, bf16[256,512]{1,0:T(8,128)(2,1)}, u32[]{:S(2)}, u32[]{:S(2)}) collective-permute-start(bf16[256,512]{1,0:T(8,128)(2,1)} %bitcast.54), channel_id=1, source_target_pairs={{1,0},{2,1},{3,2},{4,3},{5,4},{6,5},{7,6},{8,7},{9,8},{10,9},{11,1... | collective-permute-start | bytes 786440 | tf_op jit(solution)/shard_map/ppermute | solution.py:20
  191.3 32.6 %collective-permute-start.25 = (bf16[256,512]{1,0:T(8,128)(2,1)}, bf16[256,512]{1,0:T(8,128)(2,1)}, u32[]{:S(2)}, u32[]{:S(2)}) collective-permute-start(bf16[256,512]{1,0:T(8,128)(2,1)} %bitcast.53), channel_id=1, source_target_pairs={{2,0},{3,1},{4,2},{5,3},{6,4},{7,5},{8,6},{9,7},{10,8},{11,9},{12,... | collective-permute-start | bytes 786440 | tf_op jit(solution)/shard_map/ppermute | solution.py:20
  205.3 20.6 %collective-permute-start.12 = (bf16[256,512]{1,0:T(8,128)(2,1)S(1)}, bf16[256,512]{1,0:T(8,128)(2,1)S(1)}, u32[]{:S(2)}, u32[]{:S(2)}) collective-permute-start(bf16[256,512]{1,0:T(8,128)(2,1)S(1)} %bitcast.394), channel_id=1, source_target_pairs={{0,2},{1,3},{2,4},{3,5},{4,6},{5,7},{6,8},{7,9},{8,10},{9,11},{10,... | collective-permute-start | bytes 786440 | tf_op jit(solution)/shard_map/ppermute | solution.py:20
  209.5 14.4 %slice-start.3 = ((bf16[512,1024]{1,0:T(8,128)(2,1)}), bf16[256,1024]{1,0:T(8,128)(2,1)S(1)}, s32[]{:S(2)}) async-start(bf16[512,1024]{1,0:T(8,128)(2,1)} %copy-done.7), calls=%async_computation.3 | async-start | bytes 1048576 | tf_op jit(solution)/shard_map/slice | solution.py:153
  210.6 15.3 %collective-permute-start.11 = (bf16[256,512]{1,0:T(8,128)(2,1)S(1)}, bf16[256,512]{1,0:T(8,128)(2,1)S(1)}, u32[]{:S(2)}, u32[]{:S(2)}) collective-permute-start(bf16[256,512]{1,0:T(8,128)(2,1)S(1)} %bitcast.393), channel_id=1, source_target_pairs={{0,1},{1,2},{2,3},{3,4},{4,5},{5,6},{6,7},{7,8},{8,9},{9,10},{10,1... | collective-permute-start | bytes 786440 | tf_op jit(solution)/shard_map/ppermute | solution.py:20
  213.2 12.7 %collective-permute-start.10 = (bf16[256,512]{1,0:T(8,128)(2,1)S(1)}, bf16[256,512]{1,0:T(8,128)(2,1)S(1)}, u32[]{:S(2)}, u32[]{:S(2)}) collective-permute-start(bf16[256,512]{1,0:T(8,128)(2,1)S(1)} %bitcast.392), channel_id=1, source_target_pairs={{1,0},{2,1},{3,2},{4,3},{5,4},{6,5},{7,6},{8,7},{9,8},{10,9},{11,1... | collective-permute-start | bytes 786440 | tf_op jit(solution)/shard_map/ppermute | solution.py:20
  216.9 10.5 %copy-start.1 = (bf16[2,256,512]{2,1,0:T(8,128)(2,1)S(1)}, bf16[2,256,512]{2,1,0:T(8,128)(2,1)}, u32[]{:S(2)}) copy-start(bf16[2,256,512]{2,1,0:T(8,128)(2,1)} %copy-done) | copy-start | bytes 1572868
  217.0 10.5 %slice-start.4 = ((bf16[512,1024]{1,0:T(8,128)(2,1)}), bf16[256,1024]{1,0:T(8,128)(2,1)S(1)}, s32[]{:S(2)}) async-start(bf16[512,1024]{1,0:T(8,128)(2,1)} %copy-done.8), calls=%async_computation.4 | async-start | bytes 1048576 | tf_op jit(solution)/shard_map/slice | solution.py:153
  217.0 10.5 %collective-permute-start.9 = (bf16[256,512]{1,0:T(8,128)(2,1)S(1)}, bf16[256,512]{1,0:T(8,128)(2,1)S(1)}, u32[]{:S(2)}, u32[]{:S(2)}) collective-permute-start(bf16[256,512]{1,0:T(8,128)(2,1)S(1)} %bitcast.391), channel_id=1, source_target_pairs={{2,0},{3,1},{4,2},{5,3},{6,4},{7,5},{8,6},{9,7},{10,8},{11,9},{12,... | collective-permute-start | bytes 786440 | tf_op jit(solution)/shard_map/ppermute | solution.py:20
  261.8 58.9 %copy-start.5 = (bf16[512,1024]{1,0:T(8,128)(2,1)}, bf16[512,1024]{1,0:T(8,128)(2,1)S(1)}, u32[]{:S(2)}) copy-start(bf16[512,1024]{1,0:T(8,128)(2,1)S(1)} %maximum_convert_fusion.3) | copy-start | bytes 3145732
  269.1 18.0 %copy-start.33 = (bf16[1,512,512]{2,1,0:T(8,128)(2,1)S(1)}, bf16[1,512,512]{2,1,0:T(8,128)(2,1)}, u32[]{:S(2)}) copy-start(bf16[1,512,512]{2,1,0:T(8,128)(2,1)} %param.10) | copy-start | bytes 1572868
  269.1 18.0 %copy-start.37 = (bf16[512,512]{1,0:T(8,128)(2,1)S(1)}, bf16[512,512]{1,0:T(8,128)(2,1)}, u32[]{:S(2)}) copy-start(bf16[512,512]{1,0:T(8,128)(2,1)} %copy-done.34) | copy-start | bytes 1572868
  270.2 63.0 %collective-permute-start.36 = (bf16[256,512]{1,0:T(8,128)(2,1)}, bf16[256,512]{1,0:T(8,128)(2,1)}, u32[]{:S(2)}, u32[]{:S(2)}) collective-permute-start(bf16[256,512]{1,0:T(8,128)(2,1)} %bitcast.71), channel_id=1, source_target_pairs={{0,2},{1,3},{2,4},{3,5},{4,6},{5,7},{6,8},{7,9},{8,10},{9,11},{10,... | collective-permute-start | bytes 786440 | tf_op jit(solution)/shard_map/ppermute | solution.py:20
  272.4 62.6 %collective-permute-start.35 = (bf16[256,512]{1,0:T(8,128)(2,1)}, bf16[256,512]{1,0:T(8,128)(2,1)}, u32[]{:S(2)}, u32[]{:S(2)}) collective-permute-start(bf16[256,512]{1,0:T(8,128)(2,1)} %bitcast.70), channel_id=1, source_target_pairs={{0,1},{1,2},{2,3},{3,4},{4,5},{5,6},{6,7},{7,8},{8,9},{9,10},{10,1... | collective-permute-start | bytes 786440 | tf_op jit(solution)/shard_map/ppermute | solution.py:20
  275.6 62.8 %collective-permute-start.34 = (bf16[256,512]{1,0:T(8,128)(2,1)}, bf16[256,512]{1,0:T(8,128)(2,1)}, u32[]{:S(2)}, u32[]{:S(2)}) collective-permute-start(bf16[256,512]{1,0:T(8,128)(2,1)} %bitcast.69), channel_id=1, source_target_pairs={{1,0},{2,1},{3,2},{4,3},{5,4},{6,5},{7,6},{8,7},{9,8},{10,9},{11,1... | collective-permute-start | bytes 786440 | tf_op jit(solution)/shard_map/ppermute | solution.py:20
  279.9 62.3 %collective-permute-start.33 = (bf16[256,512]{1,0:T(8,128)(2,1)}, bf16[256,512]{1,0:T(8,128)(2,1)}, u32[]{:S(2)}, u32[]{:S(2)}) collective-permute-start(bf16[256,512]{1,0:T(8,128)(2,1)} %bitcast.68), channel_id=1, source_target_pairs={{2,0},{3,1},{4,2},{5,3},{6,4},{7,5},{8,6},{9,7},{10,8},{11,9},{12,... | collective-permute-start | bytes 786440 | tf_op jit(solution)/shard_map/ppermute | solution.py:20
  320.7 6.2 %copy-start.19 = (f32[256,512]{1,0:T(8,128)S(1)}, f32[256,512]{1,0:T(8,128)}, u32[]{:S(2)}) copy-start(f32[256,512]{1,0:T(8,128)} %get-tuple-element.27) | copy-start | bytes 1572868
  320.7 7.9 %copy-start.22 = (f32[256,512]{1,0:T(8,128)S(1)}, f32[256,512]{1,0:T(8,128)}, u32[]{:S(2)}) copy-start(f32[256,512]{1,0:T(8,128)} %fusion.31) | copy-start | bytes 1572868
  320.7 40.1 %collective-permute-start.40 = (bf16[256,512]{1,0:T(8,128)(2,1)S(1)}, bf16[256,512]{1,0:T(8,128)(2,1)S(1)}, u32[]{:S(2)}, u32[]{:S(2)}) collective-permute-start(bf16[256,512]{1,0:T(8,128)(2,1)S(1)} %get-tuple-element.61), channel_id=1, source_target_pairs={{0,64},{64,0},{1,65},{65,1},{2,66},{66,2},{3,67},{67,3},{4,68},{68... | collective-permute-start | bytes 786440 | tf_op jit(solution)/shard_map/ppermute | solution.py:104
  333.0 16.1 %slice-start.1 = ((bf16[512,1024]{1,0:T(8,128)(2,1)}), bf16[256,1024]{1,0:T(8,128)(2,1)S(1)}, s32[]{:S(2)}) async-start(bf16[512,1024]{1,0:T(8,128)(2,1)} %copy-done.5), calls=%async_computation.1 | async-start | bytes 1048576 | tf_op jit(solution)/shard_map/slice | solution.py:153
  333.1 17.8 %collective-permute-start.20 = (bf16[256,512]{1,0:T(8,128)(2,1)S(1)}, bf16[256,512]{1,0:T(8,128)(2,1)S(1)}, u32[]{:S(2)}, u32[]{:S(2)}) collective-permute-start(bf16[256,512]{1,0:T(8,128)(2,1)S(1)} %bitcast.398), channel_id=1, source_target_pairs={{0,2},{1,3},{2,4},{3,5},{4,6},{5,7},{6,8},{7,9},{8,10},{9,11},{10,... | collective-permute-start | bytes 786440 | tf_op jit(solution)/shard_map/ppermute | solution.py:20
  335.1 15.9 %collective-permute-start.19 = (bf16[256,512]{1,0:T(8,128)(2,1)S(1)}, bf16[256,512]{1,0:T(8,128)(2,1)S(1)}, u32[]{:S(2)}, u32[]{:S(2)}) collective-permute-start(bf16[256,512]{1,0:T(8,128)(2,1)S(1)} %bitcast.397), channel_id=1, source_target_pairs={{0,1},{1,2},{2,3},{3,4},{4,5},{5,6},{6,7},{7,8},{8,9},{9,10},{10,1... | collective-permute-start | bytes 786440 | tf_op jit(solution)/shard_map/ppermute | solution.py:20
  338.5 12.5 %collective-permute-start.18 = (bf16[256,512]{1,0:T(8,128)(2,1)S(1)}, bf16[256,512]{1,0:T(8,128)(2,1)S(1)}, u32[]{:S(2)}, u32[]{:S(2)}) collective-permute-start(bf16[256,512]{1,0:T(8,128)(2,1)S(1)} %bitcast.396), channel_id=1, source_target_pairs={{1,0},{2,1},{3,2},{4,3},{5,4},{6,5},{7,6},{8,7},{9,8},{10,9},{11,1... | collective-permute-start | bytes 786440 | tf_op jit(solution)/shard_map/ppermute | solution.py:20
  342.2 12.3 %copy-start.3 = (bf16[2,256,512]{2,1,0:T(8,128)(2,1)S(1)}, bf16[2,256,512]{2,1,0:T(8,128)(2,1)}, u32[]{:S(2)}) copy-start(bf16[2,256,512]{2,1,0:T(8,128)(2,1)} %copy-done.2) | copy-start | bytes 1572868
  342.2 12.3 %slice-start.2 = ((bf16[512,1024]{1,0:T(8,128)(2,1)}), bf16[256,1024]{1,0:T(8,128)(2,1)S(1)}, s32[]{:S(2)}) async-start(bf16[512,1024]{1,0:T(8,128)(2,1)} %copy-done.6), calls=%async_computation.2 | async-start | bytes 1048576 | tf_op jit(solution)/shard_map/slice | solution.py:153
  342.2 12.3 %collective-permute-start.17 = (bf16[256,512]{1,0:T(8,128)(2,1)S(1)}, bf16[256,512]{1,0:T(8,128)(2,1)S(1)}, u32[]{:S(2)}, u32[]{:S(2)}) collective-permute-start(bf16[256,512]{1,0:T(8,128)(2,1)S(1)} %bitcast.395), channel_id=1, source_target_pairs={{2,0},{3,1},{4,2},{5,3},{6,4},{7,5},{8,6},{9,7},{10,8},{11,9},{12,... | collective-permute-start | bytes 786440 | tf_op jit(solution)/shard_map/ppermute | solution.py:20
  356.2 5.3 %collective-permute-start.39 = (bf16[256,512]{1,0:T(8,128)(2,1)S(1)}, bf16[256,512]{1,0:T(8,128)(2,1)S(1)}, u32[]{:S(2)}, u32[]{:S(2)}) collective-permute-start(bf16[256,512]{1,0:T(8,128)(2,1)S(1)} %get-tuple-element.95), channel_id=1, source_target_pairs={{0,64},{64,0},{1,65},{65,1},{2,66},{66,2},{3,67},{67,3},{4,68},{68... | collective-permute-start | bytes 786440 | tf_op jit(solution)/shard_map/ppermute | solution.py:104
  360.3 1.5 collective-permute-start.38
  360.4 1.8 collective-permute-start.37
  (20 other events, 34.3 us)

commit v5 on v4

--- a/solution.py
+++ b/solution.py
@@ -1,3 +1,5 @@
+import functools
+
 import jax
 import jax.numpy as jnp
 from jax import lax
@@ -100,6 +102,83 @@
     )(queries, key_rows, value_rows, grad_attn)
 
 
+MESH = pl.DeviceIdType.MESH
+OFFSETS = [shift_by for shift_by in range(-REACH, REACH + 1) if shift_by != 0]
+
+
+def exchange_kernel(per_target, x_ref, out_ref, send_sems, recv_sems):
+    core = lax.axis_index("pipe")
+    me = lax.axis_index("space")
+    peers = lax.axis_size("space")
+    barrier = pltpu.get_barrier_semaphore()
+
+    def exists(shift_by):
+        return (me + shift_by >= 0) & (me + shift_by < peers)
+
+    for shift_by in OFFSETS:
+        @pl.when(exists(shift_by))
+        def _():
+            pl.semaphore_signal(barrier, 1, device_id=(core, me + shift_by), device_id_type=MESH)
+
+    pl.semaphore_wait(barrier, sum(jnp.where(exists(shift_by), 1, 0) for shift_by in OFFSETS))
+
+    def copy_to(index, shift_by):
+        landing = OFFSETS.index(-shift_by)
+        return pltpu.make_async_remote_copy(
+            src_ref=x_ref.at[index] if per_target else x_ref,
+            dst_ref=out_ref.at[landing],
+            send_sem=send_sems.at[index],
+            recv_sem=recv_sems.at[landing],
+            device_id=(core, me + shift_by),
+            device_id_type=MESH,
+        )
+
+    def copy_from(index, shift_by):
+        return pltpu.make_async_remote_copy(
+            src_ref=x_ref.at[index] if per_target else x_ref,
+            dst_ref=out_ref.at[index],
+            send_sem=send_sems.at[index],
+            recv_sem=recv_sems.at[index],
+            device_id=(core, me + shift_by),
+            device_id_type=MESH,
+        )
+
+    for index, shift_by in enumerate(OFFSETS):
+        @pl.when(exists(shift_by))
+        def _():
+            copy_to(index, shift_by).start()
+
+    for index, shift_by in enumerate(OFFSETS):
+        @pl.when(jnp.logical_not(exists(shift_by)))
+        def _():
+            out_ref[index] = jnp.zeros(out_ref.shape[1:], out_ref.dtype)
+
+    for index, shift_by in enumerate(OFFSETS):
+        @pl.when(exists(shift_by))
+        def _():
+            copy_to(index, shift_by).wait_send()
+
+    for index, shift_by in enumerate(OFFSETS):
+        @pl.when(exists(shift_by))
+        def _():
+            copy_from(index, shift_by).wait_recv()
+
+
+def exchange(payload, per_target, collective_id):
+    shape = payload.shape[1:] if per_target else payload.shape
+    return pl.pallas_call(
+        functools.partial(exchange_kernel, per_target),
+        out_shape=jax.ShapeDtypeStruct((len(OFFSETS),) + shape, payload.dtype),
+        in_specs=[pl.BlockSpec(memory_space=pltpu.VMEM)],
+        out_specs=pl.BlockSpec(memory_space=pltpu.VMEM),
+        scratch_shapes=[
+            pltpu.SemaphoreType.DMA((len(OFFSETS),)),
+            pltpu.SemaphoreType.DMA((len(OFFSETS),)),
+        ],
+        compiler_params=pltpu.CompilerParams(collective_id=collective_id, has_side_effects=True),
+    )(payload)
+
+
 def swap_cores(value):
     return lax.ppermute(value, "pipe", [(0, 1), (1, 0)])
 
@@ -108,13 +187,13 @@
     return jnp.where(core == section, own, other)
 
 
-def prepare(rows, lists, weight_in, gain_row, myself):
+def prepare(rows, lists, weight_in, gain_row, myself, collective_id):
     points, model_width = rows.shape
     block_count = points // BLK
     offsets = [shift_by for shift_by in range(-REACH, REACH + 1) if shift_by != 0]
     scaled, inverse, normed = normalize(rows, gain_row)
     projected = jnp.dot(normed, weight_in, preferred_element_type=jnp.float32).astype(jnp.bfloat16)
-    received = jnp.stack([shifted(normed, "space", -shift_by) for shift_by in offsets])
+    received = exchange(normed, False, collective_id)
     received = received.reshape(len(offsets) * block_count, BLK, model_width)
     owners = lists // block_count
     within = lists % block_count
@@ -129,7 +208,7 @@
     return scaled, inverse, projected[:, :model_width], pairs, window_at
 
 
-def block_backward(grad_out, prepared, weight_in, weight_out, gain_row):
+def block_backward(grad_out, prepared, weight_in, weight_out, gain_row, collective_id):
     scaled, inverse, queries, pairs, window_at = prepared
     points, model_width = grad_out.shape
     block_count = points // BLK
@@ -152,10 +231,8 @@
     ).reshape(len(offsets), points, model_width)
     grad_project = jnp.concatenate([grad_query, grad_pairs[:points]], 1).astype(jnp.bfloat16)
     grad_normed = jnp.dot(grad_project, weight_in.T, preferred_element_type=jnp.float32)
-    for slot_index, shift_by in enumerate(offsets):
-        grad_normed = grad_normed + shifted(
-            window_grads[slot_index].astype(jnp.bfloat16), "space", shift_by
-        ).astype(jnp.float32)
+    returned = exchange(window_grads.astype(jnp.bfloat16), True, collective_id)
+    grad_normed = grad_normed + jnp.sum(returned.astype(jnp.float32), axis=0)
     return (
         grad_out.astype(jnp.float32) + norm_backward(grad_normed, scaled, inverse, gain_row)
     ).astype(jnp.bfloat16)
@@ -191,7 +268,14 @@
     cotangent_mine = mine(cotangent, core)
     prepared = [
         [
-            prepare(params[section][0][j], params[section][1][j], params[section][2], params[section][4], myself)
+            prepare(
+                params[section][0][j],
+                params[section][1][j],
+                params[section][2],
+                params[section][4],
+                myself,
+                section * half + j,
+            )
             for j in range(half)
         ]
         for section in range(sections)
@@ -203,7 +287,12 @@
         for j in range(half):
             grad_out = cotangent_mine[j] if section == sections - 1 else results[section + 1][j]
             results[section][j] = block_backward(
-                grad_out, prepared[section][j], weight_in, weight_out, gain_row
+                grad_out,
+                prepared[section][j],
+                weight_in,
+                weight_out,
+                gain_row,
+                sections * half + section * half + j,
             )
             exchanged[section][j] = swap_cores(results[section][j])
     own_out = jnp.stack(

time: 367 us -> 415 us (1.13)
  Pallas kernels: 118 us -> 312 us
  starting transfers between devices: 141 us -> 4.78 us
  waiting for transfers between devices: 19.6 us -> 4.09 us
  other arithmetic: 43.7 us -> 50.4 us
    pallas_call x0 -> x8, Pallas kernels: none -> 195 us  [exchange(): pl.pallas_call(functools.partial(exchange_kernel, per_target), out_shape=...]
    ppermute x32 -> x0, starting transfers between devices: 126 us -> none  [shifted(): return lax.ppermute(x, axis, pairs)]
    ppermute x32 -> x0, waiting for transfers between devices: 17.6 us -> none  [shifted(): return lax.ppermute(x, axis, pairs)]
    ppermute x9, starting transfers between devices: 15.8 us -> 4.78 us  [swap_cores(): return lax.ppermute(value, 'pipe', [(0, 1), (1, 0)])]
    another operation x16 -> x8, other arithmetic: 17.8 us -> 6.85 us
    convert_element_type x0 -> x4, other arithmetic: none -> 10.8 us  [block_backward(): returned = exchange(window_grads.astype(jnp.bfloat16), True, collective_id)]
    reduce_sum x0 -> x4, other arithmetic: none -> 6.72 us  [block_backward(): grad_normed = grad_normed + jnp.sum(returned.astype(jnp.float32), axis=0)]
    gather x4, local copies, waits for them, and re-layouts: 2.98 us -> 7.15 us  [prepare(): fetched = jnp.take(received, window_at, axis=0).reshape(-1, model_width)]
  transfers between devices with their start and end apart: 41 -> 9, of which waited for: 8 -> 5; matrix products, arithmetic and copies ran while one was open for 11% -> 4% of each run, Pallas kernels for 8% -> 25%
where the time goes in v5:
time: 415 us; the launch traced here: 411 us
  Pallas kernels  312 us (75%)
  other arithmetic  50.4 us (12%)
  local copies, waits for them, and re-layouts  22.4 us (5%)
  matrix products  16.1 us (4%)
  starting transfers between devices  4.78 us (1%)
    pallas_call x8, Pallas kernels, exchange(): pl.pallas_call(functools.partial(exchange_kernel, per_target), out_shape=...  195 us
    pallas_call x4, Pallas kernels, attend_backward(): pl.pallas_call(attention_kernel, grid=(groups,), in_specs=[row_spec, key_...  118 us
    convert_element_type x4, other arithmetic, block_backward(): returned = exchange(window_grads.astype(jnp.bfloat16), True, collective_id)  10.8 us
    scatter-add x4, other arithmetic, block_backward(): window_grads = jnp.zeros((len(offsets) * block_count, BLK, model_width),...  10.7 us
  transfers between devices with their start and end apart: 9, of which 5 were waited for; matrix products, arithmetic and copies ran while one was open for 4% of the time, Pallas kernels for 25%

profile of v5, /device:TPU:15, one launch (start us, length us, event | category | flops | bytes accessed | tf_op | source)
XLA Modules:
  0.0 410.9 jit_solution(13357787051630406451)
XLA Ops:
  0.0 1.1 dynamic-slice_bitcast_fusion
  1.1 0.8 collective-permute-start
  1.8 0.8 reshape_squeeze.9
  4.0 2.4 collective-permute-done.1
  7.2 1.1 bitcast_select_fusion
  9.3 1.5 fusion.34
  10.8 25.7 %shard_map.70 = bf16[4,256,512]{2,1,0:T(8,128)(2,1)} custom-call(bf16[256,512]{1,0:T(8,128)(2,1)} %get-tuple-element.77.x_ref), custom_call_target="tpu_custom_call" | custom-call | tf_op jit(solution)/shard_map/pallas_call | solution.py:169
  36.5 24.8 %shard_map.64 = bf16[4,256,512]{2,1,0:T(8,128)(2,1)} custom-call(bf16[256,512]{1,0:T(8,128)(2,1)} %get-tuple-element.76.x_ref), custom_call_target="tpu_custom_call" | custom-call | tf_op jit(solution)/shard_map/pallas_call | solution.py:169
  61.3 1.8 gather_fusion.2
  63.1 1.8 gather_fusion
  64.9 0.8 broadcast_select_fusion.7
  65.8 25.8 %shard_map.73 = bf16[4,256,512]{2,1,0:T(8,128)(2,1)} custom-call(bf16[256,512]{1,0:T(8,128)(2,1)} %get-tuple-element.103.x_ref), custom_call_target="tpu_custom_call" | custom-call | tf_op jit(solution)/shard_map/pallas_call | solution.py:169
  91.7 25.2 %shard_map.67 = bf16[4,256,512]{2,1,0:T(8,128)(2,1)} custom-call(bf16[256,512]{1,0:T(8,128)(2,1)} %get-tuple-element.102.x_ref), custom_call_target="tpu_custom_call" | custom-call | tf_op jit(solution)/shard_map/pallas_call | solution.py:169
  116.9 1.8 gather_fusion.3
  118.7 1.8 gather_fusion.1
  120.5 0.8 broadcast_select_fusion.6
  121.3 0.8 broadcast_select_fusion.8
  122.1 1.1 convolution_convert_fusion.11.g_ref
  123.2 1.1 convolution_convert_fusion.9.g_ref
  124.3 1.7 broadcast_select_fusion
  127.8 1.1 pad_maximum_fusion.2
  128.9 29.5 %shard_map.71 = (f32[256,512]{1,0:T(8,128)}, f32[512,512]{1,0:T(8,128)}, f32[512,512]{1,0:T(8,128)}) custom-call(bf16[256,512]{1,0:T(8,128)(2,1)} %slice.185.q_ref, bf16[512,512]{1,0:T(8,128)(2,1)} %get-tuple-element.73.k_ref, bf16[512,512]{1,0:T(8,128)(2,1)} %get-tuple-element.72.v_ref, bf16[256,512]{1,0:T(8,128)(2,1)} %convolution_convert_fusion.9.g_ref), custom_call_target="tpu_custom_call" | custom-call | flops 5368709120 | bytes 4194304 | tf_op jit(solution)/shard_map/pallas_call | solution.py:87
  158.4 1.7 maximum_convert_fusion.2
  160.1 1.3 fusion.22
  163.1 1.1 pad_maximum_fusion.4
  164.2 29.5 %shard_map.65 = (f32[256,512]{1,0:T(8,128)}, f32[512,512]{1,0:T(8,128)}, f32[512,512]{1,0:T(8,128)}) custom-call(bf16[256,512]{1,0:T(8,128)(2,1)} %slice.169.q_ref, bf16[512,512]{1,0:T(8,128)(2,1)} %get-tuple-element.71.k_ref, bf16[512,512]{1,0:T(8,128)(2,1)} %get-tuple-element.70.v_ref, bf16[256,512]{1,0:T(8,128)(2,1)} %convolution_convert_fusion.11.g_ref), custom_call_target="tpu_custom_call" | custom-call | flops 5368709120 | bytes 4194304 | tf_op jit(solution)/shard_map/pallas_call | solution.py:87
  193.7 1.7 maximum_convert_fusion
  195.4 1.3 fusion.25
  197.3 0.7 slice.192.q_ref
  198.0 0.9 slice.193
  198.9 1.6 broadcast.691.clone
  200.5 2.7 scatter_fusion.2
  203.2 2.7 convert_element_type.165
  205.9 20.5 %shard_map.72 = bf16[4,256,512]{2,1,0:T(8,128)(2,1)} custom-call(bf16[4,256,512]{2,1,0:T(8,128)(2,1)} %bitcast.337), custom_call_target="tpu_custom_call" | custom-call | tf_op jit(solution)/shard_map/pallas_call | solution.py:169
  226.4 2.3 convert_reduce_fusion.1
  228.7 1.6 broadcast.691.clone.1
  230.3 2.6 scatter_fusion
  232.9 2.7 convert_element_type.143
  235.6 27.3 %shard_map.66 = bf16[4,256,512]{2,1,0:T(8,128)(2,1)} custom-call(bf16[4,256,512]{2,1,0:T(8,128)(2,1)} %bitcast.338), custom_call_target="tpu_custom_call" | custom-call | tf_op jit(solution)/shard_map/pallas_call | solution.py:169
  263.0 1.5 convert_reduce_fusion.3
  265.8 0.8 fusion.119
  267.7 1.1 pad_maximum_fusion.1
  270.0 1.1 convolution_convert_fusion.8.g_ref
  271.1 29.5 %shard_map.74 = (f32[256,512]{1,0:T(8,128)}, f32[512,512]{1,0:T(8,128)}, f32[512,512]{1,0:T(8,128)}) custom-call(bf16[256,512]{1,0:T(8,128)(2,1)} %slice.192.q_ref, bf16[512,512]{1,0:T(8,128)(2,1)} %get-tuple-element.67.k_ref, bf16[512,512]{1,0:T(8,128)(2,1)} %get-tuple-element.66.v_ref, bf16[256,512]{1,0:T(8,128)(2,1)} %convolution_convert_fusion.8.g_ref), custom_call_target="tpu_custom_call" | custom-call | flops 5368709120 | bytes 4194304 | tf_op jit(solution)/shard_map/pallas_call | solution.py:87
  300.5 1.7 maximum_convert_fusion.3
  302.2 1.3 fusion.16
  305.4 1.1 pad_maximum_fusion.3
  306.5 1.0 convolution_convert_fusion.10.g_ref
  307.5 29.5 %shard_map.68 = (f32[256,512]{1,0:T(8,128)}, f32[512,512]{1,0:T(8,128)}, f32[512,512]{1,0:T(8,128)}) custom-call(bf16[256,512]{1,0:T(8,128)(2,1)} %slice.177.q_ref, bf16[512,512]{1,0:T(8,128)(2,1)} %get-tuple-element.69.k_ref, bf16[512,512]{1,0:T(8,128)(2,1)} %get-tuple-element.68.v_ref, bf16[256,512]{1,0:T(8,128)(2,1)} %convolution_convert_fusion.10.g_ref), custom_call_target="tpu_custom_call" | custom-call | flops 5368709120 | bytes 4194304 | tf_op jit(solution)/shard_map/pallas_call | solution.py:87
  337.0 1.7 maximum_convert_fusion.1
  338.7 1.3 fusion.19
  340.0 1.6 broadcast.691.clone.2
  341.6 2.6 scatter_fusion.3
  344.2 2.7 convert_element_type.176
  346.9 22.9 %shard_map.75 = bf16[4,256,512]{2,1,0:T(8,128)(2,1)} custom-call(bf16[4,256,512]{2,1,0:T(8,128)(2,1)} %bitcast.339), custom_call_target="tpu_custom_call" | custom-call | tf_op jit(solution)/shard_map/pallas_call | solution.py:169
  369.8 1.4 convert_reduce_fusion
  371.3 1.6 broadcast.691.clone.3
  372.9 2.7 scatter_fusion.1
  375.6 2.7 convert_element_type.154
  378.3 22.4 %shard_map.69 = bf16[4,256,512]{2,1,0:T(8,128)(2,1)} custom-call(bf16[4,256,512]{2,1,0:T(8,128)(2,1)} %bitcast.340), custom_call_target="tpu_custom_call" | custom-call | tf_op jit(solution)/shard_map/pallas_call | solution.py:169
  400.7 1.5 convert_reduce_fusion.2
  403.5 0.8 fusion.118
  405.0 2.4 collective-permute-start.7
  409.9 1.1 pad_maximum_fusion
  (140 shorter events, 17.1 us)
Async XLA Ops:
  1.1 6.1 %collective-permute-start = (bf16[2,256,512]{2,1,0:T(8,128)(2,1)S(1)}, bf16[2,256,512]{2,1,0:T(8,128)(2,1)S(1)}, u32[]{:S(2)}, u32[]{:S(2)}) collective-permute-start(bf16[2,256,512]{2,1,0:T(8,128)(2,1)S(1)} %dynamic-slice_bitcast_fusion), channel_id=1, source_target_pairs={{0,64},{64,0},{1,65},{65,1},{2,66},{66,2},{3,67},{67,3},{4,68},{68... | collective-permute-start | bytes 1572872 | tf_op jit(solution)/shard_map/ppermute | solution.py:183
  2.8 1.1 collective-permute-start.3
  2.8 121.5 %collective-permute-start.2 = (bf16[512,1536]{1,0:T(8,128)(2,1)}, bf16[512,1536]{1,0:T(8,128)(2,1)}, u32[]{:S(2)}, u32[]{:S(2)}) collective-permute-start(bf16[512,1536]{1,0:T(8,128)(2,1)} %bitcast.345), channel_id=1, source_target_pairs={{0,64},{64,0},{1,65},{65,1},{2,66},{66,2},{3,67},{67,3},{4,68},{68... | collective-permute-start | bytes 4718600 | tf_op jit(solution)/shard_map/ppermute | solution.py:183
  3.3 3.2 collective-permute-start.1
  3.4 118.7 %collective-permute-start.4 = (bf16[512,512]{1,0:T(8,128)(2,1)}, bf16[512,512]{1,0:T(8,128)(2,1)S(1)}, u32[]{:S(2)}, u32[]{:S(2)}) collective-permute-start(bf16[512,512]{1,0:T(8,128)(2,1)} %bitcast.362), channel_id=1, source_target_pairs={{0,64},{64,0},{1,65},{65,1},{2,66},{66,2},{3,67},{67,3},{4,68},{68... | collective-permute-start | bytes 1572872 | tf_op jit(solution)/shard_map/ppermute | solution.py:183
  8.3 2.6 copy-start
  8.3 2.6 copy-start.2
  91.7 30.4 %copy-start.19 = (bf16[4,256,512]{2,1,0:T(8,128)(2,1)S(1)}, bf16[4,256,512]{2,1,0:T(8,128)(2,1)}, u32[]{:S(2)}) copy-start(bf16[4,256,512]{2,1,0:T(8,128)(2,1)} %param.13) | copy-start | bytes 3145732
  91.7 30.4 %copy-start.24 = (bf16[1,512,512]{2,1,0:T(8,128)(2,1)S(1)}, bf16[1,512,512]{2,1,0:T(8,128)(2,1)}, u32[]{:S(2)}) copy-start(bf16[1,512,512]{2,1,0:T(8,128)(2,1)} %param.10) | copy-start | bytes 1572868
  122.1 2.2 copy-start.27
  122.1 2.2 copy-start.13
  124.2 1.7 copy-start.11
  125.9 1.4 copy-start.23
  160.0 1.3 copy-start.4
  160.0 1.3 copy-start.10
  195.4 1.3 copy-start.5
  195.4 1.3 copy-start.9
  226.4 2.3 copy-start.15
  263.0 1.6 copy-start.17
  263.0 1.6 slice-start
  263.0 1.7 copy-start.14
  264.6 1.0 copy-start.1
  264.6 1.2 slice-start.1
  265.8 0.9 copy-start.22
  266.6 1.1 copy-start.12
  266.8 2.0 copy-start.20
  268.8 1.0 copy-start.25
  268.8 1.2 copy-start.28
  302.2 1.3 copy-start.6
  302.2 1.3 copy-start.8
  303.5 1.4 copy-start.21
  304.9 1.6 copy-start.26
  304.9 1.6 copy-start.29
  338.7 1.3 copy-start.7
  346.9 24.3 %copy-start.16 = (f32[256,512]{1,0:T(8,128)S(1)}, f32[256,512]{1,0:T(8,128)}, u32[]{:S(2)}) copy-start(f32[256,512]{1,0:T(8,128)} %get-tuple-element.27) | copy-start | bytes 1572868
  400.7 1.5 copy-start.18
  400.7 1.6 slice-start.2
  402.3 1.0 copy-start.3
  402.3 1.2 slice-start.3
  405.0 3.6 collective-permute-start.7
  407.4 1.5 collective-permute-start.8
  407.5 1.8 collective-permute-start.5
  407.9 1.8 collective-permute-start.6

commit v6 on v4

v6 whole, which is shorter than its diff:
```python
import functools

import jax
import jax.numpy as jnp
from jax import lax
from jax.experimental import pallas as pl
from jax.experimental.pallas import tpu as pltpu
from jax.sharding import PartitionSpec as P

HEADS = 32
HD = 16
BLK = 128
REACH = 2


epsilon = 1e-05


def shifted(x, axis, by):
    peers = lax.axis_size(axis)
    pairs = [(i, i + by) for i in range(peers) if 0 <= i + by < peers]
    return lax.ppermute(x, axis, pairs)


def normalize(points, gain_row):
    values = points.astype(jnp.float32)
    centre = jnp.mean(values, axis=-1, keepdims=True)
    spread = jnp.mean(jnp.square(values - centre), axis=-1, keepdims=True)
    inverse = lax.rsqrt(spread + epsilon)
    scaled = (values - centre) * inverse
    return (scaled, inverse, (scaled * gain_row).astype(jnp.bfloat16))


def norm_backward(grad_normed, scaled, inverse, gain_row):
    weighted = grad_normed * gain_row
    return inverse * (
        weighted
        - jnp.mean(weighted, axis=-1, keepdims=True)
        - scaled * jnp.mean(weighted * scaled, axis=-1, keepdims=True)
    )


MESH = pl.DeviceIdType.MESH
OFFSETS = [shift_by for shift_by in range(-REACH, REACH + 1) if shift_by != 0]


def attention_body(q_ref, k_ref, v_ref, g_ref, dq_ref, dk_ref, dv_ref):
    factor = HD ** (-0.5)
    group = 128
    nt = (((1,), (1,)), ((), ()))
    tn = (((0,), (0,)), ((), ()))
    head_of = lax.broadcasted_iota(jnp.int32, (1, group), 1) // HD
    dq_ref[...] = jnp.zeros_like(dq_ref)
    dk_ref[...] = jnp.zeros_like(dk_ref)
    dv_ref[...] = jnp.zeros_like(dv_ref)
    for first in range(0, q_ref.shape[1], group):
        cols = slice(first, first + group)
        q = q_ref[:, cols]
        k = k_ref[:, cols]
        v = v_ref[:, cols]
        g = g_ref[:, cols]

        def head(h, carry, q=q, k=k, v=v, g=g, cols=cols):
            mask = head_of == h
            qm = jnp.where(mask, q, jnp.zeros_like(q))
            km = jnp.where(mask, k, jnp.zeros_like(k))
            gm = jnp.where(mask, g, jnp.zeros_like(g))
            scores = lax.dot_general(qm, k, nt, preferred_element_type=jnp.float32) * factor
            top = jnp.max(scores, axis=-1, keepdims=True)
            exps = jnp.exp(scores - top)
            attention = exps / jnp.sum(exps, axis=-1, keepdims=True)
            grad_probs = lax.dot_general(gm, v, nt, preferred_element_type=jnp.float32)
            row = jnp.sum(attention * grad_probs, axis=-1, keepdims=True)
            grad_scores = (attention * (grad_probs - row) * factor).astype(jnp.bfloat16)
            dq_ref[:, cols] += jnp.dot(grad_scores, km, preferred_element_type=jnp.float32)
            dk_ref[:, cols] += lax.dot_general(
                grad_scores, qm, tn, preferred_element_type=jnp.float32
            )
            dv_ref[:, cols] += lax.dot_general(
                attention.astype(jnp.bfloat16), gm, tn, preferred_element_type=jnp.float32
            )
            return carry

        lax.fori_loop(0, group // HD, head, 0)


def exchange_start(spreads, payload_refs, out_refs, send_sems, recv_sems):
    core = lax.axis_index("pipe")
    me = lax.axis_index("space")
    peers = lax.axis_size("space")
    barrier = pltpu.get_barrier_semaphore()

    def exists(shift_by):
        return (me + shift_by >= 0) & (me + shift_by < peers)

    for shift_by in OFFSETS:

        @pl.when(exists(shift_by))
        def _():
            pl.semaphore_signal(barrier, 1, device_id=(core, me + shift_by), device_id_type=MESH)

    pl.semaphore_wait(barrier, sum(jnp.where(exists(shift_by), 1, 0) for shift_by in OFFSETS))

    def describe(which, index, landing, shift_by):
        spread, x_ref, out_ref = spreads[which], payload_refs[which], out_refs[which]
        return pltpu.make_async_remote_copy(
            src_ref=x_ref.at[index] if spread else x_ref,
            dst_ref=out_ref.at[landing],
            send_sem=send_sems.at[which, index],
            recv_sem=recv_sems.at[which, landing],
            device_id=(core, me + shift_by),
            device_id_type=MESH,
        )

    for which in range(len(spreads)):
        for index, shift_by in enumerate(OFFSETS):

            @pl.when(exists(shift_by))
            def _():
                describe(which, index, OFFSETS.index(-shift_by), shift_by).start()

        for index, shift_by in enumerate(OFFSETS):

            @pl.when(jnp.logical_not(exists(shift_by)))
            def _():
                out_refs[which][index] = jnp.zeros(out_refs[which].shape[1:], out_refs[which].dtype)

    def finish():
        for which in range(len(spreads)):
            for index, shift_by in enumerate(OFFSETS):

                @pl.when(exists(shift_by))
                def _():
                    describe(which, index, OFFSETS.index(-shift_by), shift_by).wait_send()

            for index, shift_by in enumerate(OFFSETS):

                @pl.when(exists(shift_by))
                def _():
                    describe(which, index, index, shift_by).wait_recv()

    return finish


def fused_kernel(spreads, with_attention, *refs):
    count = len(spreads)
    inputs = 4 if with_attention else 0
    outputs = 3 if with_attention else 0
    attention_in = refs[:inputs]
    payload_refs = refs[inputs : inputs + count]
    attention_out = refs[inputs + count : inputs + count + outputs]
    out_refs = refs[inputs + count + outputs : inputs + 2 * count + outputs]
    send_sems, recv_sems = refs[inputs + 2 * count + outputs :]
    finish = exchange_start(spreads, payload_refs, out_refs, send_sems, recv_sems)
    if with_attention:
        attention_body(*attention_in, *attention_out)
    finish()


def fused_step(attention_args, payloads, spreads, collective_id):
    vmem = pl.BlockSpec(memory_space=pltpu.VMEM)
    out_shapes = []
    flops = 0
    if attention_args:
        queries, key_rows, value_rows, grad_attn = attention_args
        rows, width = queries.shape
        keys = key_rows.shape[0]
        out_shapes = [
            jax.ShapeDtypeStruct((rows, width), jnp.float32),
            jax.ShapeDtypeStruct((keys, width), jnp.float32),
            jax.ShapeDtypeStruct((keys, width), jnp.float32),
        ]
        flops = 2 * 5 * rows * keys * width * (128 // HD)
    for payload, spread in zip(payloads, spreads):
        shape = payload.shape[1:] if spread else payload.shape
        out_shapes.append(jax.ShapeDtypeStruct((len(OFFSETS),) + shape, payload.dtype))
    moved = sum(len(OFFSETS) * x.size * x.dtype.itemsize for x in payloads)
    outs = pl.pallas_call(
        functools.partial(fused_kernel, tuple(spreads), bool(attention_args)),
        out_shape=out_shapes,
        in_specs=[vmem] * (len(attention_args) + len(payloads)),
        out_specs=[vmem] * len(out_shapes),
        scratch_shapes=[
            pltpu.SemaphoreType.DMA((len(payloads), len(OFFSETS))),
            pltpu.SemaphoreType.DMA((len(payloads), len(OFFSETS))),
        ],
        compiler_params=pltpu.CompilerParams(
            collective_id=collective_id,
            has_side_effects=True,
            vmem_limit_bytes=48 * 1024 * 1024,
        ),
        cost_estimate=pl.CostEstimate(
            flops=flops, transcendentals=flops // 160, bytes_accessed=moved + 1
        ),
    )(*attention_args, *payloads)
    return list(outs)


def swap_cores(value):
    return lax.ppermute(value, "pipe", [(0, 1), (1, 0)])


def pick(own, other, core, section):
    return jnp.where(core == section, own, other)


def prepare(rows, lists, weight_in, gain_row, myself):
    points, model_width = rows.shape
    block_count = points // BLK
    scaled, inverse, normed = normalize(rows, gain_row)
    projected = jnp.dot(normed, weight_in, preferred_element_type=jnp.float32).astype(jnp.bfloat16)
    owners = lists // block_count
    within = lists % block_count
    distance = owners - myself
    slot = jnp.where(distance < 0, distance + REACH, distance + REACH - 1)
    window_at = slot * block_count + within
    return dict(
        scaled=scaled,
        inverse=inverse,
        normed=normed,
        queries=projected[:, :model_width],
        own_pairs=projected[:, model_width:],
        window_at=window_at,
    )


def attach(unit, received, weight_in):
    points, model_width = unit["queries"].shape
    received = received.reshape(len(OFFSETS) * (points // BLK), BLK, model_width)
    fetched = jnp.take(received, unit["window_at"], axis=0).reshape(-1, model_width)
    fetched_pairs = jnp.dot(
        fetched, weight_in[:, model_width:], preferred_element_type=jnp.float32
    ).astype(jnp.bfloat16)
    unit["pairs"] = jnp.concatenate([unit["own_pairs"], fetched_pairs], 0)


def outgoing(unit, grad_key, grad_value, weight_in):
    points, model_width = unit["queries"].shape
    block_count = points // BLK
    grad_pairs = jnp.concatenate([grad_key, grad_value], 1)
    grad_remote = jnp.dot(
        grad_pairs[points:].astype(jnp.bfloat16),
        weight_in[:, model_width:].T,
        preferred_element_type=jnp.float32,
    ).reshape(-1, BLK, model_width)
    window_grads = (
        jnp.zeros((len(OFFSETS) * block_count, BLK, model_width), jnp.float32)
        .at[unit["window_at"]]
        .add(grad_remote)
    ).reshape(len(OFFSETS), points, model_width)
    unit["own_grad"] = grad_pairs[:points]
    return window_grads.astype(jnp.bfloat16)


def complete(unit, grad_out, grad_query, returned, weight_in, gain_row):
    grad_project = jnp.concatenate([grad_query, unit["own_grad"]], 1).astype(jnp.bfloat16)
    grad_normed = jnp.dot(grad_project, weight_in.T, preferred_element_type=jnp.float32)
    grad_normed = grad_normed + jnp.sum(returned.astype(jnp.float32), axis=0)
    return (
        grad_out.astype(jnp.float32)
        + norm_backward(grad_normed, unit["scaled"], unit["inverse"], gain_row)
    ).astype(jnp.bfloat16)


def shards(saved_inputs, project_in, project_out, norm_gains, neighbour_blocks, cotangent):
    sections = lax.axis_size("pipe")
    core = lax.axis_index("pipe")
    other = sections - 1 - core
    myself = lax.axis_index("space")
    micro_count = cotangent.shape[0]
    half = micro_count // sections
    model_width = cotangent.shape[2]

    def mine(array, whose):
        grouped = array.reshape((half, sections) + array.shape[1:])
        return lax.dynamic_index_in_dim(grouped, whose, 1, keepdims=False)

    local_lists = neighbour_blocks[0, :, 0, :]
    own = (
        mine(saved_inputs[0], core),
        mine(local_lists, core),
        project_in[0],
        project_out[0],
        norm_gains[0],
    )
    got = swap_cores(
        (
            mine(saved_inputs[0], other),
            mine(local_lists, other),
            project_in[0],
            project_out[0],
            norm_gains[0],
        )
    )
    params = [
        [pick(own_part, got_part, core, section) for own_part, got_part in zip(own, got)]
        for section in range(sections)
    ]
    cotangent_mine = mine(cotangent, core)
    order = [(section, j) for section in range(sections - 1, -1, -1) for j in range(half)]
    units = [
        prepare(params[section][0][j], params[section][1][j], params[section][2], params[section][4], myself)
        for section, j in order
    ]
    results = {}
    exchanged = {}
    ids = iter(range(len(order) + 2))
    (first_received,) = fused_step((), [units[0]["normed"]], [False], next(ids))
    attach(units[0], first_received, params[order[0][0]][2])
    pending = None
    for step, (section, j) in enumerate(order):
        unit = units[step]
        _, _, weight_in, weight_out, gain_row = params[section]
        grad_out = cotangent_mine[j] if section == sections - 1 else results[(section + 1, j)]
        unit["grad_out"] = grad_out
        grad_attn = jnp.dot(grad_out, weight_out.T, preferred_element_type=jnp.float32).astype(
            jnp.bfloat16
        )
        payloads, spreads = [], []
        if pending is not None:
            payloads.append(pending[1])
            spreads.append(True)
        if step + 1 < len(order):
            payloads.append(units[step + 1]["normed"])
            spreads.append(False)
        outs = fused_step(
            (unit["queries"], unit["pairs"][:, :model_width], unit["pairs"][:, model_width:], grad_attn),
            payloads,
            spreads,
            next(ids),
        )
        grad_query, grad_key, grad_value = outs[:3]
        received = outs[3:]
        if pending is not None:
            done_step, _ = pending
            done_section, done_j = order[done_step]
            done_unit = units[done_step]
            results[(done_section, done_j)] = complete(
                done_unit,
                done_unit["grad_out"],
                done_unit["grad_query"],
                received[0],
                params[done_section][2],
                params[done_section][4],
            )
            exchanged[(done_section, done_j)] = swap_cores(results[(done_section, done_j)])
            received = received[1:]
        if step + 1 < len(order):
            next_section = order[step + 1][0]
            attach(units[step + 1], received[0], params[next_section][2])
        unit["grad_query"] = grad_query
        pending = (step, outgoing(unit, grad_key, grad_value, weight_in))
    done_step, window = pending
    done_section, done_j = order[done_step]
    done_unit = units[done_step]
    (returned,) = fused_step((), [window], [True], next(ids))
    results[(done_section, done_j)] = complete(
        done_unit,
        done_unit["grad_out"],
        done_unit["grad_query"],
        returned,
        params[done_section][2],
        params[done_section][4],
    )
    exchanged[(done_section, done_j)] = swap_cores(results[(done_section, done_j)])
    own_out = jnp.stack([pick(results[(0, j)], results[(1, j)], core, 0) for j in range(half)])
    other_out = jnp.stack(
        [pick(exchanged[(0, j)], exchanged[(1, j)], core, 0) for j in range(half)]
    )
    grouped = jnp.stack([pick(own_out, other_out, core, parity) for parity in range(sections)], 1)
    return grouped.reshape((1, micro_count) + grouped.shape[2:])


def solution(mesh):
    return jax.shard_map(
        shards,
        mesh=mesh,
        in_specs=(
            P("pipe", None, "space", None),
            P("pipe", None, None),
            P("pipe", None, None),
            P("pipe", None),
            P("pipe", None, "space", None),
            P(None, "space", None),
        ),
        out_specs=P("pipe", None, "space", None),
        check_vma=False,
    )
```

time: 367 us -> 297 us (0.81)
  starting transfers between devices: 141 us -> 2.96 us
  Pallas kernels: 118 us -> 211 us
  waiting for transfers between devices: 19.6 us -> 1.87 us
  other arithmetic: 43.7 us -> 32.4 us
  local copies, waits for them, and re-layouts: 19.5 us -> 27.7 us
    ppermute x32 -> x0, starting transfers between devices: 126 us -> none  [shifted(): return lax.ppermute(x, axis, pairs)]
    pallas_call x4 -> x6, Pallas kernels: 118 us -> 211 us  [fused_step(): pl.pallas_call(functools.partial(fused_kernel, tuple(spreads), bool(atten...]
    ppermute x32 -> x0, waiting for transfers between devices: 17.6 us -> none  [shifted(): return lax.ppermute(x, axis, pairs)]
    another operation x19 -> x11, other arithmetic: 18.5 us -> 1.39 us  [the longest x1 0.68 us: shards(): jnp.stack([pick(results[0, j], results[1, j], core, 0) for j in range(hal...]
    ppermute x9, starting transfers between devices: 15.8 us -> 2.96 us  [swap_cores(): return lax.ppermute(value, 'pipe', [(0, 1), (1, 0)])]
    convert_element_type x1 -> x6, other arithmetic: 0.41 us -> 12.3 us  [the longest x4 9.86 us: outgoing(): return window_grads.astype(jnp.bfloat16)]
    unnamed x76 -> x60, local copies, waits for them, and re-layouts: 1.71 us -> 12.5 us
    slice x21 -> x19, local copies, waits for them, and re-layouts: 6.24 us -> 1.96 us  [the longest x7 1.61 us: prepare(): projected[:, model_width:]]
  transfers between devices with their start and end apart: 41 -> 9, of which waited for: 8 -> 5; matrix products, arithmetic and copies ran while one was open for 11% -> 3% of each run, Pallas kernels for 8% -> 8%
where the time goes in v6:
time: 297 us; the launch traced here: 296 us
  Pallas kernels  211 us (71%)
  other arithmetic  32.4 us (11%)
  local copies, waits for them, and re-layouts  27.7 us (9%)
  matrix products  19.2 us (6%)
    pallas_call x6, Pallas kernels, fused_step(): pl.pallas_call(functools.partial(fused_kernel, tuple(spreads), bool(atten...  211 us
    unnamed x60, local copies, waits for them, and re-layouts  12.5 us
    scatter-add x4, other arithmetic, outgoing(): window_grads = jnp.zeros((len(OFFSETS) * block_count, BLK, model_width),...  10.2 us
    convert_element_type x4, other arithmetic, outgoing(): return window_grads.astype(jnp.bfloat16)  9.86 us
    another operation x4, local copies, waits for them, and re-layouts  6.47 us
    dot_general x4, matrix products, shards(): jnp.dot(grad_out, weight_out.T, preferred_element_type=jnp.float32)  6.46 us
  transfers between devices with their start and end apart: 9, of which 5 were waited for; matrix products, arithmetic and copies ran while one was open for 3% of the time, Pallas kernels for 8%

profile of v6, /device:TPU:15, one launch (start us, length us, event | category | flops | bytes accessed | tf_op | source)
XLA Modules:
  0.0 296.2 jit_solution(14394051423401479145)
XLA Ops:
  0.0 1.1 dynamic-slice_bitcast_fusion
  1.1 0.8 collective-permute-start
  1.9 0.8 reshape_squeeze.9
  4.2 0.7 broadcast_select_fusion.15
  4.9 1.1 bitcast_select_fusion.1
  7.3 23.5 %shard_map.64 = bf16[4,256,512]{2,1,0:T(8,128)(2,1)S(1)} custom-call(bf16[256,512]{1,0:T(8,128)(2,1)S(1)} %get-tuple-element.86.refs_0_), custom_call_target="tpu_custom_call" | custom-call | bytes 1048577 | tf_op jit(solution)/shard_map/pallas_call | solution.py:178
  30.8 0.6 gather_fusion
  31.7 1.6 convolution_convert_fusion.11.refs_3_
  33.3 2.0 convolution_convert_fusion.10.refs_3_
  35.4 1.6 broadcast_select_fusion.1
  37.0 0.6 convolution_convert_fusion.3
  37.6 0.6 convolution_convert_fusion.2
  38.2 0.7 copy-done.16
  40.3 34.8 %shard_map.65 = (f32[256,512]{1,0:T(8,128)S(1)}, f32[512,512]{1,0:T(8,128)S(1)}, f32[512,512]{1,0:T(8,128)S(1)}, bf16[4,256,512]{2,1,0:T(8,128)(2,1)S(1)}) custom-call(bf16[256,512]{1,0:T(8,128)(2,1)S(1)} %slice.169.refs_0_, bf16[512,512]{1,0:T(8,128)(2,1)S(1)} %get-tuple-element.83.refs_1_, bf16[512,512]{1,0:T(8,128)(2,1)S(1)} %get-tuple-element.82.refs_2_, ...), custom_call_target="tpu_custom_call" | custom-call | flops 5368709120 | bytes 1048577 | tf_op jit(solution)/shard_map/pallas_call | solution.py:178
  75.8 0.5 copy-done.20
  76.3 0.6 convolution_convert_fusion.1
  76.9 0.9 copy-done.18
  77.8 1.6 broadcast.691.clone
  79.5 2.5 scatter_fusion
  82.0 2.7 convert_element_type.149
  84.7 0.6 gather_fusion.1
  85.4 1.7 convolution_convert_fusion.6
  87.2 37.9 %shard_map.66 = (f32[256,512]{1,0:T(8,128)S(1)}, f32[512,512]{1,0:T(8,128)S(1)}, f32[512,512]{1,0:T(8,128)S(1)}, bf16[4,256,512]{2,1,0:T(8,128)(2,1)S(1)}, bf16[4,256,512]{2,1,0:T(8,128)(2,1)}) custom-call(bf16[256,512]{1,0:T(8,128)(2,1)S(1)} %slice.176.refs_0_, bf16[512,512]{1,0:T(8,128)(2,1)S(1)} %get-tuple-element.81.refs_1_, ...), custom_call_target="tpu_custom_call" | custom-call | flops 5368709120 | bytes 5242881 | tf_op jit(solution)/shard_map/pallas_call | solution.py:178
  125.3 1.3 copy-done.8
  126.5 1.3 fusion.22
  127.8 0.7 copy-done.2
  128.5 0.6 convolution_convert_fusion
  129.1 0.9 slice.191
  130.0 1.6 broadcast.691.clone.1
  131.6 2.7 scatter_fusion.1
  134.3 2.7 convert_element_type.160
  137.0 1.8 gather_fusion.2
  138.9 1.7 convolution_convert_fusion.5
  140.8 1.2 copy-done.9
  142.1 0.7 fusion.120
  143.3 1.2 fusion.39
  144.5 1.5 convolution_convert_fusion.9.refs_3_
  146.0 51.5 %shard_map.67 = (f32[256,512]{1,0:T(8,128)S(1)}, f32[512,512]{1,0:T(8,128)S(1)}, f32[512,512]{1,0:T(8,128)S(1)}, bf16[4,256,512]{2,1,0:T(8,128)(2,1)S(1)}, bf16[4,256,512]{2,1,0:T(8,128)(2,1)}) custom-call(bf16[256,512]{1,0:T(8,128)(2,1)S(1)} %slice.182.refs_0_, bf16[512,512]{1,0:T(8,128)(2,1)S(1)} %get-tuple-element.79.refs_1_, ...), custom_call_target="tpu_custom_call" | custom-call | flops 5368709120 | bytes 5242881 | tf_op jit(solution)/shard_map/pallas_call | solution.py:178
  197.7 1.3 copy-done.3
  198.9 0.5 fusion.18
  199.4 0.5 copy-done.19
  199.9 1.6 broadcast.691.clone.2
  201.6 2.4 scatter_fusion.2
  204.0 2.8 convert_element_type.171
  207.0 1.2 copy-done.10
  208.3 1.5 fusion.119
  209.7 1.8 gather_fusion.3
  212.1 1.2 pad_maximum_fusion.1
  213.3 1.2 fusion.52
  214.5 1.4 convolution_convert_fusion.8.refs_3_
  215.9 39.5 %shard_map.68 = (f32[256,512]{1,0:T(8,128)S(1)}, f32[512,512]{1,0:T(8,128)S(1)}, f32[512,512]{1,0:T(8,128)S(1)}, bf16[4,256,512]{2,1,0:T(8,128)(2,1)S(1)}) custom-call(bf16[256,512]{1,0:T(8,128)(2,1)S(1)} %slice.190.refs_0_, bf16[512,512]{1,0:T(8,128)(2,1)S(1)} %get-tuple-element.77.refs_1_, bf16[512,512]{1,0:T(8,128)(2,1)S(1)} %get-tuple-element.76.refs_2_, ...), custom_call_target="tpu_custom_call" | custom-call | flops 5368709120 | bytes 4194305 | tf_op jit(solution)/shard_map/pallas_call | solution.py:178
  255.5 1.3 copy-done.5
  257.3 0.5 copy-done.22
  257.8 1.6 broadcast.691
  259.4 2.5 scatter_fusion.3
  261.9 1.7 convert_element_type.176
  263.6 23.9 %shard_map.69 = bf16[4,256,512]{2,1,0:T(8,128)(2,1)S(1)} custom-call(bf16[4,256,512]{2,1,0:T(8,128)(2,1)S(1)} %bitcast.337), custom_call_target="tpu_custom_call" | custom-call | bytes 4194305 | tf_op jit(solution)/shard_map/pallas_call | solution.py:178
  288.0 1.2 copy-done.6
  289.3 0.6 fusion
  290.5 0.8 fusion.118
  291.4 0.7 select_bitcast_fusion.3
  292.1 0.6 collective-permute-start.5
  293.3 0.6 collective-permute-done.5
  295.1 1.1 pad_maximum_fusion
  (138 shorter events, 10.9 us)
Async XLA Ops:
  1.1 3.9 %collective-permute-start = (bf16[2,256,512]{2,1,0:T(8,128)(2,1)S(1)}, bf16[2,256,512]{2,1,0:T(8,128)(2,1)S(1)}, u32[]{:S(2)}, u32[]{:S(2)}) collective-permute-start(bf16[2,256,512]{2,1,0:T(8,128)(2,1)S(1)} %dynamic-slice_bitcast_fusion), channel_id=1, source_target_pairs={{0,64},{64,0},{1,65},{65,1},{2,66},{66,2},{3,67},{67,3},{4,68},{68... | collective-permute-start | bytes 1572872 | tf_op jit(solution)/shard_map/ppermute | solution.py:200
  1.8 2.4 collective-permute-start.1
  2.9 1.2 collective-permute-start.3
  3.3 32.1 %collective-permute-start.2 = (bf16[512,1536]{1,0:T(8,128)(2,1)}, bf16[512,1536]{1,0:T(8,128)(2,1)}, u32[]{:S(2)}, u32[]{:S(2)}) collective-permute-start(bf16[512,1536]{1,0:T(8,128)(2,1)} %bitcast.340), channel_id=1, source_target_pairs={{0,64},{64,0},{1,65},{65,1},{2,66},{66,2},{3,67},{67,3},{4,68},{68... | collective-permute-start | bytes 4718600 | tf_op jit(solution)/shard_map/ppermute | solution.py:200
  3.4 28.3 %collective-permute-start.4 = (bf16[512,512]{1,0:T(8,128)(2,1)}, bf16[512,512]{1,0:T(8,128)(2,1)}, u32[]{:S(2)}, u32[]{:S(2)}) collective-permute-start(bf16[512,512]{1,0:T(8,128)(2,1)} %bitcast.363), channel_id=1, source_target_pairs={{0,64},{64,0},{1,65},{65,1},{2,66},{66,2},{3,67},{67,3},{4,68},{68... | collective-permute-start | bytes 1572872 | tf_op jit(solution)/shard_map/ppermute | solution.py:200
  6.1 1.2 copy-start.11
  6.1 25.4 %copy-start.14 = (bf16[2,256,512]{2,1,0:T(8,128)(2,1)}, bf16[2,256,512]{2,1,0:T(8,128)(2,1)S(1)}, u32[]{:S(2)}) copy-start(bf16[2,256,512]{2,1,0:T(8,128)(2,1)S(1)} %get-tuple-element.73) | copy-start | bytes 1572868
  31.3 2.0 copy-start.27
  31.7 3.6 %copy-start.23 = (bf16[1,512,1536]{2,1,0:T(8,128)(2,1)S(1)}, bf16[1,512,1536]{2,1,0:T(8,128)(2,1)}, u32[]{:S(2)}) copy-start(bf16[1,512,1536]{2,1,0:T(8,128)(2,1)} %param.9) | copy-start | bytes 4718596
  37.0 38.3 %copy-start.7 = (bf16[512,1536]{1,0:T(8,128)(2,1)}, bf16[512,1536]{1,0:T(8,128)(2,1)S(1)}, u32[]{:S(2)}) copy-start(bf16[512,1536]{1,0:T(8,128)(2,1)S(1)} %get-tuple-element.70) | copy-start | bytes 4718596
  37.0 39.3 %copy-start.1 = (bf16[512,1536]{1,0:T(8,128)(2,1)}, bf16[512,1536]{1,0:T(8,128)(2,1)S(1)}, u32[]{:S(2)}) copy-start(bf16[512,1536]{1,0:T(8,128)(2,1)S(1)} %get-tuple-element.71) | copy-start | bytes 4718596
  37.6 1.3 copy-start.16
  38.9 0.9 copy-start.17
  38.9 1.3 slice-start
  75.3 1.0 copy-start.20
  76.9 0.9 copy-start.18
  84.7 2.4 slice-start.1
  85.4 1.8 copy-start
  125.1 1.4 copy-start.8
  126.5 1.3 copy-start.21
  126.5 2.0 copy-start.2
  138.9 2.0 slice-start.4
  140.6 1.4 copy-start.9
  140.6 1.5 copy-start.12
  142.1 1.0 slice-start.2
  143.2 1.3 copy-start.28
  144.5 1.5 copy-start.24
  197.5 1.4 copy-start.3
  198.9 1.0 copy-start.19
  204.0 3.0 slice-start.5
  206.7 1.4 copy-start.10
  206.7 1.5 copy-start.13
  208.3 3.4 %copy-start.4 = (bf16[512,1536]{1,0:T(8,128)(2,1)S(1)}, bf16[512,1536]{1,0:T(8,128)(2,1)}, u32[]{:S(2)}) copy-start(bf16[512,1536]{1,0:T(8,128)(2,1)} %copy-done.1) | copy-start | bytes 4718596
  211.6 1.6 copy-start.26
  212.1 2.4 copy-start.29
  255.4 1.4 copy-start.5
  256.8 1.0 copy-start.22
  287.7 1.4 copy-start.6
  287.8 1.5 slice-start.6
  289.3 1.0 copy-start.15
  289.3 1.2 slice-start.3
  290.5 0.9 copy-start.25
  292.1 1.7 collective-permute-start.5
  292.7 1.5 collective-permute-start.6
  292.8 1.8 collective-permute-start.7
  293.2 1.8 collective-permute-start.8

commit v7 on v6

--- a/solution.py
+++ b/solution.py
@@ -243,13 +243,13 @@
         weight_in[:, model_width:].T,
         preferred_element_type=jnp.float32,
     ).reshape(-1, BLK, model_width)
-    window_grads = (
-        jnp.zeros((len(OFFSETS) * block_count, BLK, model_width), jnp.float32)
-        .at[unit["window_at"]]
-        .add(grad_remote)
-    ).reshape(len(OFFSETS), points, model_width)
+    slots = lax.broadcasted_iota(jnp.int32, (len(OFFSETS) * block_count, 1, 1), 0)
+    window_grads = sum(
+        jnp.where(slots == unit["window_at"][entry], grad_remote[entry][None], 0.0)
+        for entry in range(grad_remote.shape[0])
+    )
     unit["own_grad"] = grad_pairs[:points]
-    return window_grads.astype(jnp.bfloat16)
+    return window_grads.astype(jnp.bfloat16).reshape(len(OFFSETS), points, model_width)
 
 
 def complete(unit, grad_out, grad_query, returned, weight_in, gain_row):

time: 297 us -> 280 us (0.943)
  other arithmetic: 32.4 us -> 21.3 us
  local copies, waits for them, and re-layouts: 27.7 us -> 23.2 us
    scatter-add x4 -> x0, other arithmetic: 10.2 us -> none  [outgoing(): window_grads = jnp.zeros((len(OFFSETS) * block_count, BLK, model_width),...]
    another operation x4 -> x0, local copies, waits for them, and re-layouts: 6.47 us -> none
    convert_element_type x4, other arithmetic: 9.86 us -> 4.17 us  [outgoing(): window_grads.astype(jnp.bfloat16).reshape(len(OFFSETS), points, model_width)]
    eq x0 -> x8, other arithmetic: none -> 5.01 us  [outgoing(): slots == unit['window_at'][entry]]
    unnamed x60 -> x58, local copies, waits for them, and re-layouts: 12.5 us -> 9.28 us
  transfers between devices with their start and end apart: 9 -> 9, of which waited for: 5 -> 1; matrix products, arithmetic and copies ran while one was open for 3% -> 12% of each run, Pallas kernels for 8% -> 49%
where the time goes in v7:
time: 280 us; the launch traced here: 279 us
  Pallas kernels  209 us (75%)
  local copies, waits for them, and re-layouts  23.2 us (8%)
  other arithmetic  21.3 us (8%)
  matrix products  19.1 us (7%)
  starting transfers between devices  4.73 us (2%)
    pallas_call x6, Pallas kernels, fused_step(): pl.pallas_call(functools.partial(fused_kernel, tuple(spreads), bool(atten...  209 us
    unnamed x58, local copies, waits for them, and re-layouts  9.28 us
    gather x4, local copies, waits for them, and re-layouts, attach(): jnp.take(received, unit['window_at'], axis=0).reshape(-1, model_width)  6.63 us
  transfers between devices with their start and end apart: 9, of which 1 were waited for; matrix products, arithmetic and copies ran while one was open for 12% of the time, Pallas kernels for 49%

profile of v7, /device:TPU:15, one launch (start us, length us, event | category | flops | bytes accessed | tf_op | source)
XLA Modules:
  0.0 279.4 jit_solution(17698363127626907335)
XLA Ops:
  0.0 0.8 reshape_squeeze.9
  1.0 0.7 collective-permute-start.3
  1.8 1.1 dynamic-slice_bitcast_fusion
  2.9 0.5 collective-permute-start
  4.0 0.6 fusion.137
  4.7 0.6 fusion.135
  5.3 0.7 fusion.103
  6.1 0.7 fusion.102
  6.8 0.6 fusion.104
  7.5 0.7 fusion.105
  8.2 0.6 fusion.99
  8.9 0.6 fusion.98
  9.6 0.6 fusion.100
  10.3 0.6 fusion.101
  11.0 0.7 broadcast_select_fusion.15
  13.0 24.1 %shard_map.64 = bf16[4,256,512]{2,1,0:T(8,128)(2,1)S(1)} custom-call(bf16[256,512]{1,0:T(8,128)(2,1)S(1)} %get-tuple-element.86.refs_0_), custom_call_target="tpu_custom_call" | custom-call | bytes 1048577 | tf_op jit(solution)/shard_map/pallas_call | solution.py:178
  37.1 0.6 gather_fusion
  38.1 1.4 convolution_convert_fusion.11.refs_3_
  39.5 1.3 convolution_convert_fusion.10.refs_3_
  40.8 1.6 broadcast_select_fusion.1
  42.5 0.6 convolution_convert_fusion.3
  43.1 0.6 convolution_convert_fusion.2
  43.7 0.7 copy-done.13
  44.4 0.6 convolution_convert_fusion
  45.3 0.6 convolution_convert_fusion.1
  47.0 0.5 slice-done
  47.6 34.3 %shard_map.65 = (f32[256,512]{1,0:T(8,128)S(1)}, f32[512,512]{1,0:T(8,128)S(1)}, f32[512,512]{1,0:T(8,128)S(1)}, bf16[4,256,512]{2,1,0:T(8,128)(2,1)S(1)}) custom-call(bf16[256,512]{1,0:T(8,128)(2,1)S(1)} %slice.241.refs_0_, bf16[512,512]{1,0:T(8,128)(2,1)S(1)} %get-tuple-element.83.refs_1_, bf16[512,512]{1,0:T(8,128)(2,1)S(1)} %get-tuple-element.82.refs_2_, ...), custom_call_target="tpu_custom_call" | custom-call | flops 5368709120 | bytes 1048577 | tf_op jit(solution)/shard_map/pallas_call | solution.py:178
  82.0 0.8 copy-done
  82.8 0.5 fusion.32
  83.3 0.5 copy-done.17
  83.8 1.8 gather_fusion.1
  85.7 1.7 convolution_convert_fusion.6
  88.1 1.2 fusion.7.refs_4_
  89.3 37.8 %shard_map.66 = (f32[256,512]{1,0:T(8,128)S(1)}, f32[512,512]{1,0:T(8,128)S(1)}, f32[512,512]{1,0:T(8,128)S(1)}, bf16[4,256,512]{2,1,0:T(8,128)(2,1)S(1)}, bf16[4,256,512]{2,1,0:T(8,128)(2,1)}) custom-call(bf16[256,512]{1,0:T(8,128)(2,1)S(1)} %slice.248.refs_0_, bf16[512,512]{1,0:T(8,128)(2,1)S(1)} %get-tuple-element.81.refs_1_, ...), custom_call_target="tpu_custom_call" | custom-call | flops 5368709120 | bytes 5242881 | tf_op jit(solution)/shard_map/pallas_call | solution.py:178
  127.3 1.6 copy-done.6
  128.9 1.3 fusion.30
  130.4 0.9 copy-done.9
  131.4 1.4 fusion.124
  132.8 2.5 gather_fusion.2
  135.3 1.1 broadcast_select_fusion.7
  136.9 1.3 fusion.47
  138.2 1.9 collective-permute-start.6
  140.7 1.2 fusion.5.refs_4_
  142.0 1.4 convolution_convert_fusion.9.refs_3_
  143.3 47.5 %shard_map.67 = (f32[256,512]{1,0:T(8,128)S(1)}, f32[512,512]{1,0:T(8,128)S(1)}, f32[512,512]{1,0:T(8,128)S(1)}, bf16[4,256,512]{2,1,0:T(8,128)(2,1)S(1)}, bf16[4,256,512]{2,1,0:T(8,128)(2,1)}) custom-call(bf16[256,512]{1,0:T(8,128)(2,1)S(1)} %slice.256.refs_0_, bf16[512,512]{1,0:T(8,128)(2,1)S(1)} %get-tuple-element.79.refs_1_, ...), custom_call_target="tpu_custom_call" | custom-call | flops 5368709120 | bytes 5242881 | tf_op jit(solution)/shard_map/pallas_call | solution.py:178
  191.0 1.3 copy-done.3
  192.2 1.3 fusion.26
  193.5 1.8 gather_fusion.3
  195.5 1.8 convolution_convert_fusion.4
  197.5 0.7 fusion.123
  198.7 1.2 fusion.60
  200.5 1.2 fusion.3.refs_4_
  201.7 1.4 convolution_convert_fusion.8.refs_3_
  203.1 41.9 %shard_map.68 = (f32[256,512]{1,0:T(8,128)S(1)}, f32[512,512]{1,0:T(8,128)S(1)}, f32[512,512]{1,0:T(8,128)S(1)}, bf16[4,256,512]{2,1,0:T(8,128)(2,1)S(1)}) custom-call(bf16[256,512]{1,0:T(8,128)(2,1)S(1)} %slice.266.refs_0_, bf16[512,512]{1,0:T(8,128)(2,1)S(1)} %get-tuple-element.77.refs_1_, bf16[512,512]{1,0:T(8,128)(2,1)S(1)} %get-tuple-element.76.refs_2_, ...), custom_call_target="tpu_custom_call" | custom-call | flops 5368709120 | bytes 4194305 | tf_op jit(solution)/shard_map/pallas_call | solution.py:178
  245.1 1.3 copy-done.4
  246.9 0.5 copy-done.20
  248.6 23.9 %shard_map.69 = bf16[4,256,512]{2,1,0:T(8,128)(2,1)S(1)} custom-call(bf16[4,256,512]{2,1,0:T(8,128)(2,1)S(1)} %fusion.1.refs_0_), custom_call_target="tpu_custom_call" | custom-call | bytes 4194305 | tf_op jit(solution)/shard_map/pallas_call | solution.py:178
  272.8 0.6 fusion.8
  274.0 0.8 fusion.122
  274.8 0.7 select_bitcast_fusion.3
  275.5 0.6 collective-permute-start.5
  276.6 0.6 collective-permute-done.5
  277.2 1.0 select_bitcast_fusion.1
  278.4 1.1 pad_maximum_fusion
  (161 shorter events, 11.8 us)
Async XLA Ops:
  0.0 11.7 %copy-start.22 = (bf16[1,4,256,512]{3,2,1,0:T(8,128)(2,1)S(1)}, bf16[1,4,256,512]{3,2,1,0:T(8,128)(2,1)}, u32[]{:S(2)}) copy-start(bf16[1,4,256,512]{3,2,1,0:T(8,128)(2,1)} %param.8) | copy-start | bytes 3145732
  1.0 3.0 %collective-permute-start.3 = (s32[2,2]{1,0:T(2,128)S(1)}, s32[2,2]{1,0:T(2,128)S(1)}, u32[]{:S(2)}, u32[]{:S(2)}) collective-permute-start(s32[2,2]{1,0:T(2,128)S(1)} %bitcast.350), channel_id=1, source_target_pairs={{0,64},{64,0},{1,65},{65,1},{2,66},{66,2},{3,67},{67,3},{4,68},{68... | collective-permute-start | bytes 56 | tf_op jit(solution)/shard_map/ppermute | solution.py:200
  1.7 9.3 %collective-permute-start.1 = (f32[512]{0:T(512)}, f32[512]{0:T(512)S(1)}, u32[]{:S(2)}, u32[]{:S(2)}) collective-permute-start(f32[512]{0:T(512)} %bitcast.348), channel_id=1, source_target_pairs={{0,64},{64,0},{1,65},{65,1},{2,66},{66,2},{3,67},{67,3},{4,68},{68... | collective-permute-start | bytes 6152 | tf_op jit(solution)/shard_map/ppermute | solution.py:200
  2.9 8.9 %collective-permute-start = (bf16[2,256,512]{2,1,0:T(8,128)(2,1)S(1)}, bf16[2,256,512]{2,1,0:T(8,128)(2,1)S(1)}, u32[]{:S(2)}, u32[]{:S(2)}) collective-permute-start(bf16[2,256,512]{2,1,0:T(8,128)(2,1)S(1)} %dynamic-slice_bitcast_fusion), channel_id=1, source_target_pairs={{0,64},{64,0},{1,65},{65,1},{2,66},{66,2},{3,67},{67,3},{4,68},{68... | collective-permute-start | bytes 1572872 | tf_op jit(solution)/shard_map/ppermute | solution.py:200
  3.4 34.7 %collective-permute-start.4 = (bf16[512,512]{1,0:T(8,128)(2,1)}, bf16[512,512]{1,0:T(8,128)(2,1)}, u32[]{:S(2)}, u32[]{:S(2)}) collective-permute-start(bf16[512,512]{1,0:T(8,128)(2,1)} %bitcast.351), channel_id=1, source_target_pairs={{0,64},{64,0},{1,65},{65,1},{2,66},{66,2},{3,67},{67,3},{4,68},{68... | collective-permute-start | bytes 1572872 | tf_op jit(solution)/shard_map/ppermute | solution.py:200
  3.5 37.3 %collective-permute-start.2 = (bf16[512,1536]{1,0:T(8,128)(2,1)}, bf16[512,1536]{1,0:T(8,128)(2,1)}, u32[]{:S(2)}, u32[]{:S(2)}) collective-permute-start(bf16[512,1536]{1,0:T(8,128)(2,1)} %bitcast.335), channel_id=1, source_target_pairs={{0,64},{64,0},{1,65},{65,1},{2,66},{66,2},{3,67},{67,3},{4,68},{68... | collective-permute-start | bytes 4718600 | tf_op jit(solution)/shard_map/ppermute | solution.py:200
  11.8 1.2 copy-start.8
  11.8 26.0 %copy-start.11 = (bf16[2,256,512]{2,1,0:T(8,128)(2,1)}, bf16[2,256,512]{2,1,0:T(8,128)(2,1)S(1)}, u32[]{:S(2)}) copy-start(bf16[2,256,512]{2,1,0:T(8,128)(2,1)S(1)} %get-tuple-element.73) | copy-start | bytes 1572868
  13.0 25.0 %copy-start.26 = (bf16[1,512,512]{2,1,0:T(8,128)(2,1)S(1)}, bf16[1,512,512]{2,1,0:T(8,128)(2,1)}, u32[]{:S(2)}) copy-start(bf16[1,512,512]{2,1,0:T(8,128)(2,1)} %param.10) | copy-start | bytes 1572868
  38.1 2.8 copy-start.21
  42.4 2.8 %copy-start.1 = (bf16[512,1536]{1,0:T(8,128)(2,1)}, bf16[512,1536]{1,0:T(8,128)(2,1)S(1)}, u32[]{:S(2)}) copy-start(bf16[512,1536]{1,0:T(8,128)(2,1)S(1)} %get-tuple-element.71) | copy-start | bytes 4718596
  42.5 39.5 %copy-start.5 = (bf16[512,1536]{1,0:T(8,128)(2,1)}, bf16[512,1536]{1,0:T(8,128)(2,1)S(1)}, u32[]{:S(2)}) copy-start(bf16[512,1536]{1,0:T(8,128)(2,1)S(1)} %get-tuple-element.70) | copy-start | bytes 4718596
  43.0 1.3 copy-start.13
  44.4 0.9 copy-start.14
  45.3 0.9 copy-start.15
  46.1 0.9 copy-start.16
  46.2 1.3 slice-start
  81.8 1.0 copy-start
  82.8 1.0 copy-start.17
  85.7 1.8 slice-start.1
  127.2 1.8 copy-start.6
  127.3 2.9 %copy-start.18 = (bf16[512,1024]{1,0:T(8,128)(2,1)}, bf16[512,1024]{1,0:T(8,128)(2,1)S(1)}, u32[]{:S(2)}) copy-start(bf16[512,1024]{1,0:T(8,128)(2,1)S(1)} %maximum_convert_fusion.1) | copy-start | bytes 3145732
  130.2 1.0 copy-start.9
  130.2 1.2 slice-start.4
  131.4 5.0 %copy-start.2 = (bf16[512,1536]{1,0:T(8,128)(2,1)S(1)}, bf16[512,1536]{1,0:T(8,128)(2,1)}, u32[]{:S(2)}) copy-start(bf16[512,1536]{1,0:T(8,128)(2,1)} %copy-done.1) | copy-start | bytes 4718596
  135.3 1.6 copy-start.23
  136.4 3.6 %copy-start.24 = (f32[256,512]{1,0:T(8,128)S(1)}, f32[256,512]{1,0:T(8,128)}, u32[]{:S(2)}) copy-start(f32[256,512]{1,0:T(8,128)} %fusion.30) | copy-start | bytes 1572868
  136.9 3.2 %slice-start.3 = ((bf16[256,1536]{1,0:T(8,128)(2,1)}), bf16[256,1024]{1,0:T(8,128)(2,1)S(1)}, s32[]{:S(2)}) async-start(bf16[256,1536]{1,0:T(8,128)(2,1)} %copy-done.16), calls=%async_computation.3 | async-start | bytes 1048576 | tf_op jit(solution)/shard_map/slice | solution.py:222
  138.2 138.4 %collective-permute-start.6 = (bf16[256,512]{1,0:T(8,128)(2,1)S(1)}, bf16[256,512]{1,0:T(8,128)(2,1)}, u32[]{:S(2)}, u32[]{:S(2)}) collective-permute-start(bf16[256,512]{1,0:T(8,128)(2,1)S(1)} %fusion.47), channel_id=1, source_target_pairs={{0,64},{64,0},{1,65},{65,1},{2,66},{66,2},{3,67},{67,3},{4,68},{68... | collective-permute-start | bytes 786440 | tf_op jit(solution)/shard_map/ppermute | solution.py:200
  140.7 1.3 copy-start.27
  190.8 1.4 copy-start.3
  192.2 1.3 copy-start.19
  195.4 2.0 copy-start.7
  195.4 2.0 copy-start.10
  195.4 2.0 slice-start.5
  197.5 1.0 copy-start.25
  197.5 1.2 slice-start.2
  200.5 1.3 copy-start.28
  245.0 1.4 copy-start.4
  246.4 1.0 copy-start.20
  248.6 24.1 %slice-start.7 = ((bf16[512,1024]{1,0:T(8,128)(2,1)}), bf16[256,1024]{1,0:T(8,128)(2,1)S(1)}, s32[]{:S(2)}) async-start(bf16[512,1024]{1,0:T(8,128)(2,1)} %copy-done.20), calls=%async_computation.7 | async-start | bytes 1048576 | tf_op jit(solution)/shard_map/slice | solution.py:251
  272.8 1.0 copy-start.12
  272.8 1.2 slice-start.6
  275.5 1.7 collective-permute-start.5
  276.0 2.1 collective-permute-start.8
  276.1 2.1 collective-permute-start.7

commit v8 on v7

--- a/solution.py
+++ b/solution.py
@@ -44,7 +44,7 @@
 OFFSETS = [shift_by for shift_by in range(-REACH, REACH + 1) if shift_by != 0]
 
 
-def attention_body(q_ref, k_ref, v_ref, g_ref, dq_ref, dk_ref, dv_ref):
+def attention_body(q_ref, k_ref, v_ref, g_ref, dq_ref, dk_ref, dv_ref, after_first):
     factor = HD ** (-0.5)
     group = 128
     nt = (((1,), (1,)), ((), ()))
@@ -82,6 +82,8 @@
             return carry
 
         lax.fori_loop(0, group // HD, head, 0)
+        if first == 0:
+            after_first()
 
 
 def exchange_start(spreads, payload_refs, out_refs, send_sems, recv_sems):
@@ -93,6 +95,9 @@
     def exists(shift_by):
         return (me + shift_by >= 0) & (me + shift_by < peers)
 
+    def slot(shift_by):
+        return OFFSETS.index(shift_by)
+
     for shift_by in OFFSETS:
 
         @pl.when(exists(shift_by))
@@ -101,45 +106,85 @@
 
     pl.semaphore_wait(barrier, sum(jnp.where(exists(shift_by), 1, 0) for shift_by in OFFSETS))
 
-    def describe(which, index, landing, shift_by):
-        spread, x_ref, out_ref = spreads[which], payload_refs[which], out_refs[which]
+    def describe(which, source, landing, shift_by):
         return pltpu.make_async_remote_copy(
-            src_ref=x_ref.at[index] if spread else x_ref,
-            dst_ref=out_ref.at[landing],
-            send_sem=send_sems.at[which, index],
+            src_ref=source,
+            dst_ref=out_refs[which].at[landing],
+            send_sem=send_sems.at[which, landing],
             recv_sem=recv_sems.at[which, landing],
             device_id=(core, me + shift_by),
             device_id_type=MESH,
         )
 
-    for which in range(len(spreads)):
-        for index, shift_by in enumerate(OFFSETS):
+    def arrival(which, landing):
+        return describe(which, out_refs[which].at[landing], landing, OFFSETS[landing])
+
+    direct = []
+    relayed = []
+    for which, spread in enumerate(spreads):
+        x_ref = payload_refs[which]
+        targets = OFFSETS if spread else [-1, 1]
+        for shift_by in targets:
+            source = x_ref.at[slot(shift_by)] if spread else x_ref
+            copy = describe(which, source, slot(-shift_by), shift_by)
+            direct.append((copy, exists(shift_by)))
 
             @pl.when(exists(shift_by))
             def _():
-                describe(which, index, OFFSETS.index(-shift_by), shift_by).start()
-
-        for index, shift_by in enumerate(OFFSETS):
+                copy.start()
+
+        for shift_by in OFFSETS:
 
             @pl.when(jnp.logical_not(exists(shift_by)))
             def _():
-                out_refs[which][index] = jnp.zeros(out_refs[which].shape[1:], out_refs[which].dtype)
+                out_refs[which][slot(shift_by)] = jnp.zeros(
+                    out_refs[which].shape[1:], out_refs[which].dtype
+                )
+
+        if not spread:
+            for shift_by in (-1, 1):
+                forward = describe(
+                    which, out_refs[which].at[slot(-shift_by)], slot(-2 * shift_by), shift_by
+                )
+                relayed.append((which, shift_by, forward, exists(shift_by) & exists(-shift_by)))
+
+    def relay():
+        for which, shift_by, forward, valid in relayed:
+
+            @pl.when(exists(-shift_by))
+            def _():
+                arrival(which, slot(-shift_by)).wait_recv()
+
+        for which, shift_by, forward, valid in relayed:
+
+            @pl.when(valid)
+            def _():
+                forward.start()
 
     def finish():
+        for copy, valid in direct:
+
+            @pl.when(valid)
+            def _():
+                copy.wait_send()
+
+        for which, shift_by, forward, valid in relayed:
+
+            @pl.when(valid)
+            def _():
+                forward.wait_send()
+
+        relayed_slots = {(which, slot(-shift_by)) for which, shift_by, _, _ in relayed}
         for which in range(len(spreads)):
-            for index, shift_by in enumerate(OFFSETS):
+            for landing, shift_by in enumerate(OFFSETS):
+                if (which, landing) in relayed_slots:
+                    continue
 
                 @pl.when(exists(shift_by))
                 def _():
-                    describe(which, index, OFFSETS.index(-shift_by), shift_by).wait_send()
-
-            for index, shift_by in enumerate(OFFSETS):
-
-                @pl.when(exists(shift_by))
-                def _():
-                    describe(which, index, index, shift_by).wait_recv()
-
-    return finish
+                    arrival(which, landing).wait_recv()
+
+    return relay, finish
 
 
 def fused_kernel(spreads, with_attention, *refs):
@@ -151,9 +196,11 @@
     attention_out = refs[inputs + count : inputs + count + outputs]
     out_refs = refs[inputs + count + outputs : inputs + 2 * count + outputs]
     send_sems, recv_sems = refs[inputs + 2 * count + outputs :]
-    finish = exchange_start(spreads, payload_refs, out_refs, send_sems, recv_sems)
+    relay, finish = exchange_start(spreads, payload_refs, out_refs, send_sems, recv_sems)
     if with_attention:
-        attention_body(*attention_in, *attention_out)
+        attention_body(*attention_in, *attention_out, relay)
+    else:
+        relay()
     finish()
 
 

time: 280 us -> 292 us (1.043)
  Pallas kernels: 209 us -> 221 us
    pallas_call x6, Pallas kernels: 209 us -> 221 us  [fused_step(): pl.pallas_call(functools.partial(fused_kernel, tuple(spreads), bool(atten...]
  transfers between devices with their start and end apart: 9 -> 9, of which waited for: 1 -> 1; matrix products, arithmetic and copies ran while one was open for 12% -> 11% of each run, Pallas kernels for 49% -> 48%
where the time goes in v8:
time: 292 us; the launch traced here: 291 us
  Pallas kernels  221 us (76%)
  local copies, waits for them, and re-layouts  23.2 us (8%)
  other arithmetic  21.3 us (7%)
  matrix products  19.1 us (7%)
  starting transfers between devices  4.92 us (2%)
    pallas_call x6, Pallas kernels, fused_step(): pl.pallas_call(functools.partial(fused_kernel, tuple(spreads), bool(atten...  221 us
    unnamed x58, local copies, waits for them, and re-layouts  9.28 us
    gather x4, local copies, waits for them, and re-layouts, attach(): jnp.take(received, unit['window_at'], axis=0).reshape(-1, model_width)  6.63 us
  transfers between devices with their start and end apart: 9, of which 1 were waited for; matrix products, arithmetic and copies ran while one was open for 11% of the time, Pallas kernels for 48%

profile of v8, /device:TPU:15, one launch (start us, length us, event | category | flops | bytes accessed | tf_op | source)
XLA Modules:
  0.0 290.7 jit_solution(1791383885437812624)
XLA Ops:
  0.0 0.8 reshape_squeeze.9
  1.0 0.7 collective-permute-start.3
  1.8 1.1 dynamic-slice_bitcast_fusion
  2.9 0.5 collective-permute-start
  4.0 0.6 fusion.137
  4.7 0.6 fusion.135
  5.3 0.7 fusion.103
  6.1 0.7 fusion.102
  6.8 0.6 fusion.104
  7.5 0.7 fusion.105
  8.2 0.6 fusion.99
  8.9 0.6 fusion.98
  9.6 0.6 fusion.100
  10.3 0.6 fusion.101
  11.0 0.7 broadcast_select_fusion.15
  13.0 20.0 %shard_map.64 = bf16[4,256,512]{2,1,0:T(8,128)(2,1)S(1)} custom-call(bf16[256,512]{1,0:T(8,128)(2,1)S(1)} %get-tuple-element.86.refs_0_), custom_call_target="tpu_custom_call" | custom-call | bytes 1048577 | tf_op jit(solution)/shard_map/pallas_call | solution.py:225
  33.0 0.6 gather_fusion
  34.0 1.4 convolution_convert_fusion.11.refs_3_
  35.4 1.3 convolution_convert_fusion.10.refs_3_
  36.7 1.6 broadcast_select_fusion.1
  38.4 0.6 convolution_convert_fusion.3
  39.0 0.6 convolution_convert_fusion.2
  39.6 0.7 copy-done.13
  40.3 0.6 convolution_convert_fusion
  41.2 0.6 convolution_convert_fusion.1
  43.0 0.5 slice-done
  43.5 32.5 %shard_map.65 = (f32[256,512]{1,0:T(8,128)S(1)}, f32[512,512]{1,0:T(8,128)S(1)}, f32[512,512]{1,0:T(8,128)S(1)}, bf16[4,256,512]{2,1,0:T(8,128)(2,1)S(1)}) custom-call(bf16[256,512]{1,0:T(8,128)(2,1)S(1)} %slice.241.refs_0_, bf16[512,512]{1,0:T(8,128)(2,1)S(1)} %get-tuple-element.83.refs_1_, bf16[512,512]{1,0:T(8,128)(2,1)S(1)} %get-tuple-element.82.refs_2_, ...), custom_call_target="tpu_custom_call" | custom-call | flops 5368709120 | bytes 1048577 | tf_op jit(solution)/shard_map/pallas_call | solution.py:225
  76.2 0.8 copy-done
  77.0 0.5 fusion.32
  77.5 0.5 copy-done.17
  78.0 1.8 gather_fusion.1
  79.9 1.7 convolution_convert_fusion.6
  82.3 1.2 fusion.7.refs_4_
  83.5 48.6 %shard_map.66 = (f32[256,512]{1,0:T(8,128)S(1)}, f32[512,512]{1,0:T(8,128)S(1)}, f32[512,512]{1,0:T(8,128)S(1)}, bf16[4,256,512]{2,1,0:T(8,128)(2,1)S(1)}, bf16[4,256,512]{2,1,0:T(8,128)(2,1)}) custom-call(bf16[256,512]{1,0:T(8,128)(2,1)S(1)} %slice.248.refs_0_, bf16[512,512]{1,0:T(8,128)(2,1)S(1)} %get-tuple-element.81.refs_1_, ...), custom_call_target="tpu_custom_call" | custom-call | flops 5368709120 | bytes 5242881 | tf_op jit(solution)/shard_map/pallas_call | solution.py:225
  132.3 1.6 copy-done.6
  133.9 1.3 fusion.30
  135.4 0.9 copy-done.9
  136.4 1.4 fusion.124
  137.8 2.5 gather_fusion.2
  140.3 1.1 broadcast_select_fusion.7
  141.9 1.3 fusion.47
  143.2 2.2 collective-permute-start.6
  146.0 1.2 fusion.5.refs_4_
  147.3 1.4 convolution_convert_fusion.9.refs_3_
  148.6 54.1 %shard_map.67 = (f32[256,512]{1,0:T(8,128)S(1)}, f32[512,512]{1,0:T(8,128)S(1)}, f32[512,512]{1,0:T(8,128)S(1)}, bf16[4,256,512]{2,1,0:T(8,128)(2,1)S(1)}, bf16[4,256,512]{2,1,0:T(8,128)(2,1)}) custom-call(bf16[256,512]{1,0:T(8,128)(2,1)S(1)} %slice.256.refs_0_, bf16[512,512]{1,0:T(8,128)(2,1)S(1)} %get-tuple-element.79.refs_1_, ...), custom_call_target="tpu_custom_call" | custom-call | flops 5368709120 | bytes 5242881 | tf_op jit(solution)/shard_map/pallas_call | solution.py:225
  202.9 1.3 copy-done.3
  204.2 1.3 fusion.26
  205.5 1.8 gather_fusion.3
  207.4 1.8 convolution_convert_fusion.4
  209.4 0.7 fusion.123
  210.7 1.2 fusion.60
  212.4 1.2 fusion.3.refs_4_
  213.7 1.4 convolution_convert_fusion.8.refs_3_
  215.1 41.1 %shard_map.68 = (f32[256,512]{1,0:T(8,128)S(1)}, f32[512,512]{1,0:T(8,128)S(1)}, f32[512,512]{1,0:T(8,128)S(1)}, bf16[4,256,512]{2,1,0:T(8,128)(2,1)S(1)}) custom-call(bf16[256,512]{1,0:T(8,128)(2,1)S(1)} %slice.266.refs_0_, bf16[512,512]{1,0:T(8,128)(2,1)S(1)} %get-tuple-element.77.refs_1_, bf16[512,512]{1,0:T(8,128)(2,1)S(1)} %get-tuple-element.76.refs_2_, ...), custom_call_target="tpu_custom_call" | custom-call | flops 5368709120 | bytes 4194305 | tf_op jit(solution)/shard_map/pallas_call | solution.py:225
  256.4 1.3 copy-done.4
  258.1 0.5 copy-done.20
  259.9 24.1 %shard_map.69 = bf16[4,256,512]{2,1,0:T(8,128)(2,1)S(1)} custom-call(bf16[4,256,512]{2,1,0:T(8,128)(2,1)S(1)} %fusion.1.refs_0_), custom_call_target="tpu_custom_call" | custom-call | bytes 4194305 | tf_op jit(solution)/shard_map/pallas_call | solution.py:225
  284.2 0.6 fusion.8
  285.4 0.8 fusion.122
  286.2 0.7 select_bitcast_fusion.3
  286.9 0.5 collective-permute-start.5
  287.9 0.6 collective-permute-done.5
  288.5 1.0 select_bitcast_fusion.1
  289.7 1.1 pad_maximum_fusion
  (161 shorter events, 11.8 us)
Async XLA Ops:
  0.0 11.7 %copy-start.22 = (bf16[1,4,256,512]{3,2,1,0:T(8,128)(2,1)S(1)}, bf16[1,4,256,512]{3,2,1,0:T(8,128)(2,1)}, u32[]{:S(2)}) copy-start(bf16[1,4,256,512]{3,2,1,0:T(8,128)(2,1)} %param.8) | copy-start | bytes 3145732
  1.0 3.0 %collective-permute-start.3 = (s32[2,2]{1,0:T(2,128)S(1)}, s32[2,2]{1,0:T(2,128)S(1)}, u32[]{:S(2)}, u32[]{:S(2)}) collective-permute-start(s32[2,2]{1,0:T(2,128)S(1)} %bitcast.350), channel_id=1, source_target_pairs={{0,64},{64,0},{1,65},{65,1},{2,66},{66,2},{3,67},{67,3},{4,68},{68... | collective-permute-start | bytes 56 | tf_op jit(solution)/shard_map/ppermute | solution.py:247
  1.7 9.3 %collective-permute-start.1 = (f32[512]{0:T(512)}, f32[512]{0:T(512)S(1)}, u32[]{:S(2)}, u32[]{:S(2)}) collective-permute-start(f32[512]{0:T(512)} %bitcast.348), channel_id=1, source_target_pairs={{0,64},{64,0},{1,65},{65,1},{2,66},{66,2},{3,67},{67,3},{4,68},{68... | collective-permute-start | bytes 6152 | tf_op jit(solution)/shard_map/ppermute | solution.py:247
  2.9 8.9 %collective-permute-start = (bf16[2,256,512]{2,1,0:T(8,128)(2,1)S(1)}, bf16[2,256,512]{2,1,0:T(8,128)(2,1)S(1)}, u32[]{:S(2)}, u32[]{:S(2)}) collective-permute-start(bf16[2,256,512]{2,1,0:T(8,128)(2,1)S(1)} %dynamic-slice_bitcast_fusion), channel_id=1, source_target_pairs={{0,64},{64,0},{1,65},{65,1},{2,66},{66,2},{3,67},{67,3},{4,68},{68... | collective-permute-start | bytes 1572872 | tf_op jit(solution)/shard_map/ppermute | solution.py:247
  3.4 30.6 %collective-permute-start.4 = (bf16[512,512]{1,0:T(8,128)(2,1)}, bf16[512,512]{1,0:T(8,128)(2,1)}, u32[]{:S(2)}, u32[]{:S(2)}) collective-permute-start(bf16[512,512]{1,0:T(8,128)(2,1)} %bitcast.351), channel_id=1, source_target_pairs={{0,64},{64,0},{1,65},{65,1},{2,66},{66,2},{3,67},{67,3},{4,68},{68... | collective-permute-start | bytes 1572872 | tf_op jit(solution)/shard_map/ppermute | solution.py:247
  3.5 33.3 %collective-permute-start.2 = (bf16[512,1536]{1,0:T(8,128)(2,1)}, bf16[512,1536]{1,0:T(8,128)(2,1)}, u32[]{:S(2)}, u32[]{:S(2)}) collective-permute-start(bf16[512,1536]{1,0:T(8,128)(2,1)} %bitcast.335), channel_id=1, source_target_pairs={{0,64},{64,0},{1,65},{65,1},{2,66},{66,2},{3,67},{67,3},{4,68},{68... | collective-permute-start | bytes 4718600 | tf_op jit(solution)/shard_map/ppermute | solution.py:247
  11.8 1.2 copy-start.8
  11.8 21.9 %copy-start.11 = (bf16[2,256,512]{2,1,0:T(8,128)(2,1)}, bf16[2,256,512]{2,1,0:T(8,128)(2,1)S(1)}, u32[]{:S(2)}) copy-start(bf16[2,256,512]{2,1,0:T(8,128)(2,1)S(1)} %get-tuple-element.73) | copy-start | bytes 1572868
  13.0 20.9 %copy-start.26 = (bf16[1,512,512]{2,1,0:T(8,128)(2,1)S(1)}, bf16[1,512,512]{2,1,0:T(8,128)(2,1)}, u32[]{:S(2)}) copy-start(bf16[1,512,512]{2,1,0:T(8,128)(2,1)} %param.10) | copy-start | bytes 1572868
  34.0 2.8 copy-start.21
  38.4 2.8 copy-start.1
  38.4 37.8 %copy-start.5 = (bf16[512,1536]{1,0:T(8,128)(2,1)}, bf16[512,1536]{1,0:T(8,128)(2,1)S(1)}, u32[]{:S(2)}) copy-start(bf16[512,1536]{1,0:T(8,128)(2,1)S(1)} %get-tuple-element.70) | copy-start | bytes 4718596
  39.0 1.3 copy-start.13
  40.3 0.9 copy-start.14
  41.2 0.9 copy-start.15
  42.1 0.9 copy-start.16
  42.1 1.3 slice-start
  76.0 1.0 copy-start
  77.0 1.0 copy-start.17
  79.9 1.8 slice-start.1
  132.2 1.8 copy-start.6
  132.3 2.9 copy-start.18
  135.2 1.0 copy-start.9
  135.2 1.2 slice-start.4
  136.4 5.0 %copy-start.2 = (bf16[512,1536]{1,0:T(8,128)(2,1)S(1)}, bf16[512,1536]{1,0:T(8,128)(2,1)}, u32[]{:S(2)}) copy-start(bf16[512,1536]{1,0:T(8,128)(2,1)} %copy-done.1) | copy-start | bytes 4718596
  140.3 1.6 copy-start.23
  141.4 3.9 %copy-start.24 = (f32[256,512]{1,0:T(8,128)S(1)}, f32[256,512]{1,0:T(8,128)}, u32[]{:S(2)}) copy-start(f32[256,512]{1,0:T(8,128)} %fusion.30) | copy-start | bytes 1572868
  141.9 3.5 %slice-start.3 = ((bf16[256,1536]{1,0:T(8,128)(2,1)}), bf16[256,1024]{1,0:T(8,128)(2,1)S(1)}, s32[]{:S(2)}) async-start(bf16[256,1536]{1,0:T(8,128)(2,1)} %copy-done.16), calls=%async_computation.3 | async-start | bytes 1048576 | tf_op jit(solution)/shard_map/slice | solution.py:269
  143.2 144.7 %collective-permute-start.6 = (bf16[256,512]{1,0:T(8,128)(2,1)S(1)}, bf16[256,512]{1,0:T(8,128)(2,1)}, u32[]{:S(2)}, u32[]{:S(2)}) collective-permute-start(bf16[256,512]{1,0:T(8,128)(2,1)S(1)} %fusion.47), channel_id=1, source_target_pairs={{0,64},{64,0},{1,65},{65,1},{2,66},{66,2},{3,67},{67,3},{4,68},{68... | collective-permute-start | bytes 786440 | tf_op jit(solution)/shard_map/ppermute | solution.py:247
  146.0 1.3 copy-start.27
  202.8 1.4 copy-start.3
  204.2 1.3 copy-start.19
  207.4 2.0 copy-start.7
  207.4 2.0 copy-start.10
  207.4 2.0 slice-start.5
  209.4 1.0 copy-start.25
  209.4 1.2 slice-start.2
  212.4 1.3 copy-start.28
  256.2 1.4 copy-start.4
  257.6 1.0 copy-start.20
  259.9 24.3 %slice-start.7 = ((bf16[512,1024]{1,0:T(8,128)(2,1)}), bf16[256,1024]{1,0:T(8,128)(2,1)S(1)}, s32[]{:S(2)}) async-start(bf16[512,1024]{1,0:T(8,128)(2,1)} %copy-done.20), calls=%async_computation.7 | async-start | bytes 1048576 | tf_op jit(solution)/shard_map/slice | solution.py:298
  284.2 1.0 copy-start.12
  284.2 1.2 slice-start.6
  286.9 1.6 collective-permute-start.5
  287.4 2.1 collective-permute-start.8
  287.5 2.0 collective-permute-start.7

commit v9 on v8

--- a/solution.py
+++ b/solution.py
@@ -121,9 +121,10 @@
 
     direct = []
     relayed = []
+    relaying = not any(spreads)
     for which, spread in enumerate(spreads):
         x_ref = payload_refs[which]
-        targets = OFFSETS if spread else [-1, 1]
+        targets = OFFSETS if spread or not relaying else [-1, 1]
         for shift_by in targets:
             source = x_ref.at[slot(shift_by)] if spread else x_ref
             copy = describe(which, source, slot(-shift_by), shift_by)
@@ -141,7 +142,7 @@
                     out_refs[which].shape[1:], out_refs[which].dtype
                 )
 
-        if not spread:
+        if relaying and not spread:
             for shift_by in (-1, 1):
                 forward = describe(
                     which, out_refs[which].at[slot(-shift_by)], slot(-2 * shift_by), shift_by

time: 292 us -> 279 us (0.955)
  Pallas kernels: 221 us -> 208 us
    pallas_call x6, Pallas kernels: 221 us -> 208 us  [fused_step(): pl.pallas_call(functools.partial(fused_kernel, tuple(spreads), bool(atten...]
  transfers between devices with their start and end apart: 9 -> 9, of which waited for: 1 -> 1; matrix products, arithmetic and copies ran while one was open for 11% -> 12% of each run, Pallas kernels for 48% -> 50%
where the time goes in v9:
time: 279 us
  Pallas kernels  208 us (75%)
  local copies, waits for them, and re-layouts  23.2 us (8%)
  other arithmetic  21.3 us (8%)
  matrix products  19.1 us (7%)
  starting transfers between devices  5.55 us (2%)
    pallas_call x6, Pallas kernels, fused_step(): pl.pallas_call(functools.partial(fused_kernel, tuple(spreads), bool(atten...  208 us
    unnamed x58, local copies, waits for them, and re-layouts  9.28 us
    gather x4, local copies, waits for them, and re-layouts, attach(): jnp.take(received, unit['window_at'], axis=0).reshape(-1, model_width)  6.63 us
  transfers between devices with their start and end apart: 9, of which 1 were waited for; matrix products, arithmetic and copies ran while one was open for 12% of the time, Pallas kernels for 50%

profile of v9, /device:TPU:15, one launch (start us, length us, event | category | flops | bytes accessed | tf_op | source)
XLA Modules:
  0.0 278.5 jit_solution(4136574829331574607)
XLA Ops:
  0.0 0.8 reshape_squeeze.9
  1.0 0.7 collective-permute-start.3
  1.8 1.1 dynamic-slice_bitcast_fusion
  2.9 0.5 collective-permute-start
  4.0 0.6 fusion.137
  4.7 0.6 fusion.135
  5.3 0.7 fusion.103
  6.1 0.7 fusion.102
  6.8 0.6 fusion.104
  7.5 0.7 fusion.105
  8.2 0.6 fusion.99
  8.9 0.6 fusion.98
  9.6 0.6 fusion.100
  10.3 0.6 fusion.101
  11.0 0.7 broadcast_select_fusion.15
  13.0 20.0 %shard_map.64 = bf16[4,256,512]{2,1,0:T(8,128)(2,1)S(1)} custom-call(bf16[256,512]{1,0:T(8,128)(2,1)S(1)} %get-tuple-element.86.refs_0_), custom_call_target="tpu_custom_call" | custom-call | bytes 1048577 | tf_op jit(solution)/shard_map/pallas_call | solution.py:226
  33.0 0.6 gather_fusion
  34.0 1.4 convolution_convert_fusion.11.refs_3_
  35.4 1.3 convolution_convert_fusion.10.refs_3_
  36.7 1.6 broadcast_select_fusion.1
  38.4 0.6 convolution_convert_fusion.3
  39.0 0.6 convolution_convert_fusion.2
  39.6 0.7 copy-done.13
  40.3 0.6 convolution_convert_fusion
  41.2 0.6 convolution_convert_fusion.1
  43.0 0.5 slice-done
  43.5 32.5 %shard_map.65 = (f32[256,512]{1,0:T(8,128)S(1)}, f32[512,512]{1,0:T(8,128)S(1)}, f32[512,512]{1,0:T(8,128)S(1)}, bf16[4,256,512]{2,1,0:T(8,128)(2,1)S(1)}) custom-call(bf16[256,512]{1,0:T(8,128)(2,1)S(1)} %slice.241.refs_0_, bf16[512,512]{1,0:T(8,128)(2,1)S(1)} %get-tuple-element.83.refs_1_, bf16[512,512]{1,0:T(8,128)(2,1)S(1)} %get-tuple-element.82.refs_2_, ...), custom_call_target="tpu_custom_call" | custom-call | flops 5368709120 | bytes 1048577 | tf_op jit(solution)/shard_map/pallas_call | solution.py:226
  76.2 0.8 copy-done
  77.0 0.5 fusion.32
  77.5 0.5 copy-done.17
  78.0 1.8 gather_fusion.1
  79.9 1.7 convolution_convert_fusion.6
  82.3 1.2 fusion.7.refs_4_
  83.5 36.8 %shard_map.66 = (f32[256,512]{1,0:T(8,128)S(1)}, f32[512,512]{1,0:T(8,128)S(1)}, f32[512,512]{1,0:T(8,128)S(1)}, bf16[4,256,512]{2,1,0:T(8,128)(2,1)S(1)}, bf16[4,256,512]{2,1,0:T(8,128)(2,1)}) custom-call(bf16[256,512]{1,0:T(8,128)(2,1)S(1)} %slice.248.refs_0_, bf16[512,512]{1,0:T(8,128)(2,1)S(1)} %get-tuple-element.81.refs_1_, ...), custom_call_target="tpu_custom_call" | custom-call | flops 5368709120 | bytes 5242881 | tf_op jit(solution)/shard_map/pallas_call | solution.py:226
  120.5 1.6 copy-done.6
  122.1 1.3 fusion.30
  123.6 0.9 copy-done.9
  124.6 1.4 fusion.124
  126.0 2.5 gather_fusion.2
  128.5 1.1 broadcast_select_fusion.7
  130.1 1.3 fusion.47
  131.3 2.7 collective-permute-start.6
  134.7 1.2 fusion.5.refs_4_
  135.9 1.4 convolution_convert_fusion.9.refs_3_
  137.3 49.7 %shard_map.67 = (f32[256,512]{1,0:T(8,128)S(1)}, f32[512,512]{1,0:T(8,128)S(1)}, f32[512,512]{1,0:T(8,128)S(1)}, bf16[4,256,512]{2,1,0:T(8,128)(2,1)S(1)}, bf16[4,256,512]{2,1,0:T(8,128)(2,1)}) custom-call(bf16[256,512]{1,0:T(8,128)(2,1)S(1)} %slice.256.refs_0_, bf16[512,512]{1,0:T(8,128)(2,1)S(1)} %get-tuple-element.79.refs_1_, ...), custom_call_target="tpu_custom_call" | custom-call | flops 5368709120 | bytes 5242881 | tf_op jit(solution)/shard_map/pallas_call | solution.py:226
  187.2 1.3 copy-done.3
  188.4 1.3 fusion.26
  189.7 1.8 gather_fusion.3
  191.7 1.8 convolution_convert_fusion.4
  193.7 0.7 fusion.123
  195.0 1.2 fusion.60
  196.7 1.2 fusion.3.refs_4_
  198.0 1.4 convolution_convert_fusion.8.refs_3_
  199.3 44.7 %shard_map.68 = (f32[256,512]{1,0:T(8,128)S(1)}, f32[512,512]{1,0:T(8,128)S(1)}, f32[512,512]{1,0:T(8,128)S(1)}, bf16[4,256,512]{2,1,0:T(8,128)(2,1)S(1)}) custom-call(bf16[256,512]{1,0:T(8,128)(2,1)S(1)} %slice.266.refs_0_, bf16[512,512]{1,0:T(8,128)(2,1)S(1)} %get-tuple-element.77.refs_1_, bf16[512,512]{1,0:T(8,128)(2,1)S(1)} %get-tuple-element.76.refs_2_, ...), custom_call_target="tpu_custom_call" | custom-call | flops 5368709120 | bytes 4194305 | tf_op jit(solution)/shard_map/pallas_call | solution.py:226
  244.2 1.3 copy-done.4
  246.0 0.5 copy-done.20
  247.7 23.9 %shard_map.69 = bf16[4,256,512]{2,1,0:T(8,128)(2,1)S(1)} custom-call(bf16[4,256,512]{2,1,0:T(8,128)(2,1)S(1)} %fusion.1.refs_0_), custom_call_target="tpu_custom_call" | custom-call | bytes 4194305 | tf_op jit(solution)/shard_map/pallas_call | solution.py:226
  271.9 0.6 fusion.8
  273.0 0.8 fusion.122
  273.9 0.7 select_bitcast_fusion.3
  274.6 0.6 collective-permute-start.5
  275.6 0.6 collective-permute-done.5
  276.3 1.0 select_bitcast_fusion.1
  277.4 1.1 pad_maximum_fusion
  (161 shorter events, 11.8 us)
Async XLA Ops:
  0.0 11.7 %copy-start.22 = (bf16[1,4,256,512]{3,2,1,0:T(8,128)(2,1)S(1)}, bf16[1,4,256,512]{3,2,1,0:T(8,128)(2,1)}, u32[]{:S(2)}) copy-start(bf16[1,4,256,512]{3,2,1,0:T(8,128)(2,1)} %param.8) | copy-start | bytes 3145732
  1.0 3.0 %collective-permute-start.3 = (s32[2,2]{1,0:T(2,128)S(1)}, s32[2,2]{1,0:T(2,128)S(1)}, u32[]{:S(2)}, u32[]{:S(2)}) collective-permute-start(s32[2,2]{1,0:T(2,128)S(1)} %bitcast.350), channel_id=1, source_target_pairs={{0,64},{64,0},{1,65},{65,1},{2,66},{66,2},{3,67},{67,3},{4,68},{68... | collective-permute-start | bytes 56 | tf_op jit(solution)/shard_map/ppermute | solution.py:248
  1.7 9.3 %collective-permute-start.1 = (f32[512]{0:T(512)}, f32[512]{0:T(512)S(1)}, u32[]{:S(2)}, u32[]{:S(2)}) collective-permute-start(f32[512]{0:T(512)} %bitcast.348), channel_id=1, source_target_pairs={{0,64},{64,0},{1,65},{65,1},{2,66},{66,2},{3,67},{67,3},{4,68},{68... | collective-permute-start | bytes 6152 | tf_op jit(solution)/shard_map/ppermute | solution.py:248
  2.9 8.9 %collective-permute-start = (bf16[2,256,512]{2,1,0:T(8,128)(2,1)S(1)}, bf16[2,256,512]{2,1,0:T(8,128)(2,1)S(1)}, u32[]{:S(2)}, u32[]{:S(2)}) collective-permute-start(bf16[2,256,512]{2,1,0:T(8,128)(2,1)S(1)} %dynamic-slice_bitcast_fusion), channel_id=1, source_target_pairs={{0,64},{64,0},{1,65},{65,1},{2,66},{66,2},{3,67},{67,3},{4,68},{68... | collective-permute-start | bytes 1572872 | tf_op jit(solution)/shard_map/ppermute | solution.py:248
  3.4 30.6 %collective-permute-start.4 = (bf16[512,512]{1,0:T(8,128)(2,1)}, bf16[512,512]{1,0:T(8,128)(2,1)}, u32[]{:S(2)}, u32[]{:S(2)}) collective-permute-start(bf16[512,512]{1,0:T(8,128)(2,1)} %bitcast.351), channel_id=1, source_target_pairs={{0,64},{64,0},{1,65},{65,1},{2,66},{66,2},{3,67},{67,3},{4,68},{68... | collective-permute-start | bytes 1572872 | tf_op jit(solution)/shard_map/ppermute | solution.py:248
  3.5 33.3 %collective-permute-start.2 = (bf16[512,1536]{1,0:T(8,128)(2,1)}, bf16[512,1536]{1,0:T(8,128)(2,1)}, u32[]{:S(2)}, u32[]{:S(2)}) collective-permute-start(bf16[512,1536]{1,0:T(8,128)(2,1)} %bitcast.335), channel_id=1, source_target_pairs={{0,64},{64,0},{1,65},{65,1},{2,66},{66,2},{3,67},{67,3},{4,68},{68... | collective-permute-start | bytes 4718600 | tf_op jit(solution)/shard_map/ppermute | solution.py:248
  11.8 1.2 copy-start.8
  11.8 21.9 %copy-start.11 = (bf16[2,256,512]{2,1,0:T(8,128)(2,1)}, bf16[2,256,512]{2,1,0:T(8,128)(2,1)S(1)}, u32[]{:S(2)}) copy-start(bf16[2,256,512]{2,1,0:T(8,128)(2,1)S(1)} %get-tuple-element.73) | copy-start | bytes 1572868
  13.0 20.9 %copy-start.26 = (bf16[1,512,512]{2,1,0:T(8,128)(2,1)S(1)}, bf16[1,512,512]{2,1,0:T(8,128)(2,1)}, u32[]{:S(2)}) copy-start(bf16[1,512,512]{2,1,0:T(8,128)(2,1)} %param.10) | copy-start | bytes 1572868
  34.0 2.8 copy-start.21
  38.4 2.8 %copy-start.1 = (bf16[512,1536]{1,0:T(8,128)(2,1)}, bf16[512,1536]{1,0:T(8,128)(2,1)S(1)}, u32[]{:S(2)}) copy-start(bf16[512,1536]{1,0:T(8,128)(2,1)S(1)} %get-tuple-element.71) | copy-start | bytes 4718596
  38.4 37.8 %copy-start.5 = (bf16[512,1536]{1,0:T(8,128)(2,1)}, bf16[512,1536]{1,0:T(8,128)(2,1)S(1)}, u32[]{:S(2)}) copy-start(bf16[512,1536]{1,0:T(8,128)(2,1)S(1)} %get-tuple-element.70) | copy-start | bytes 4718596
  39.0 1.3 copy-start.13
  40.3 0.9 copy-start.14
  41.2 0.9 copy-start.15
  42.1 0.9 copy-start.16
  42.1 1.3 slice-start
  76.0 1.0 copy-start
  77.0 1.0 copy-start.17
  79.9 1.8 slice-start.1
  120.3 1.8 copy-start.6
  120.5 2.9 %copy-start.18 = (bf16[512,1024]{1,0:T(8,128)(2,1)}, bf16[512,1024]{1,0:T(8,128)(2,1)S(1)}, u32[]{:S(2)}) copy-start(bf16[512,1024]{1,0:T(8,128)(2,1)S(1)} %maximum_convert_fusion.1) | copy-start | bytes 3145732
  123.4 1.0 copy-start.9
  123.4 1.2 slice-start.4
  124.6 5.0 %copy-start.2 = (bf16[512,1536]{1,0:T(8,128)(2,1)S(1)}, bf16[512,1536]{1,0:T(8,128)(2,1)}, u32[]{:S(2)}) copy-start(bf16[512,1536]{1,0:T(8,128)(2,1)} %copy-done.1) | copy-start | bytes 4718596
  128.5 1.6 copy-start.23
  129.6 4.4 %copy-start.24 = (f32[256,512]{1,0:T(8,128)S(1)}, f32[256,512]{1,0:T(8,128)}, u32[]{:S(2)}) copy-start(f32[256,512]{1,0:T(8,128)} %fusion.30) | copy-start | bytes 1572868
  130.1 4.0 %slice-start.3 = ((bf16[256,1536]{1,0:T(8,128)(2,1)}), bf16[256,1024]{1,0:T(8,128)(2,1)S(1)}, s32[]{:S(2)}) async-start(bf16[256,1536]{1,0:T(8,128)(2,1)} %copy-done.16), calls=%async_computation.3 | async-start | bytes 1048576 | tf_op jit(solution)/shard_map/slice | solution.py:270
  131.3 144.3 %collective-permute-start.6 = (bf16[256,512]{1,0:T(8,128)(2,1)S(1)}, bf16[256,512]{1,0:T(8,128)(2,1)}, u32[]{:S(2)}, u32[]{:S(2)}) collective-permute-start(bf16[256,512]{1,0:T(8,128)(2,1)S(1)} %fusion.47), channel_id=1, source_target_pairs={{0,64},{64,0},{1,65},{65,1},{2,66},{66,2},{3,67},{67,3},{4,68},{68... | collective-permute-start | bytes 786440 | tf_op jit(solution)/shard_map/ppermute | solution.py:248
  134.7 1.3 copy-start.27
  187.0 1.4 copy-start.3
  188.4 1.3 copy-start.19
  191.6 2.0 copy-start.7
  191.7 2.0 copy-start.10
  191.7 2.0 slice-start.5
  193.7 1.0 copy-start.25
  193.7 1.2 slice-start.2
  196.7 1.3 copy-start.28
  244.1 1.4 copy-start.4
  245.5 1.0 copy-start.20
  247.7 24.1 %slice-start.7 = ((bf16[512,1024]{1,0:T(8,128)(2,1)}), bf16[256,1024]{1,0:T(8,128)(2,1)S(1)}, s32[]{:S(2)}) async-start(bf16[512,1024]{1,0:T(8,128)(2,1)} %copy-done.20), calls=%async_computation.7 | async-start | bytes 1048576 | tf_op jit(solution)/shard_map/slice | solution.py:299
  271.8 1.0 copy-start.12
  271.9 1.2 slice-start.6
  274.6 1.7 collective-permute-start.5
  275.1 2.1 collective-permute-start.8
  275.2 2.1 collective-permute-start.7

commit v10 on v9

--- a/solution.py
+++ b/solution.py
@@ -82,7 +82,7 @@
             return carry
 
         lax.fori_loop(0, group // HD, head, 0)
-        if first == 0:
+        if first == group:
             after_first()
 
 
@@ -368,9 +368,10 @@
         if pending is not None:
             payloads.append(pending[1])
             spreads.append(True)
-        if step + 1 < len(order):
-            payloads.append(units[step + 1]["normed"])
-            spreads.append(False)
+        if step == 0:
+            for later in units[1:]:
+                payloads.append(later["normed"])
+                spreads.append(False)
         outs = fused_step(
             (unit["queries"], unit["pairs"][:, :model_width], unit["pairs"][:, model_width:], grad_attn),
             payloads,
@@ -393,9 +394,9 @@
             )
             exchanged[(done_section, done_j)] = swap_cores(results[(done_section, done_j)])
             received = received[1:]
-        if step + 1 < len(order):
-            next_section = order[step + 1][0]
-            attach(units[step + 1], received[0], params[next_section][2])
+        if step == 0:
+            for later, (later_section, _), arrived in zip(units[1:], order[1:], received):
+                attach(later, arrived, params[later_section][2])
         unit["grad_query"] = grad_query
         pending = (step, outgoing(unit, grad_key, grad_value, weight_in))
     done_step, window = pending

time: 279 us -> 252 us (0.903)
  Pallas kernels: 208 us -> 179 us
    pallas_call x6, Pallas kernels: 208 us -> 179 us  [fused_step(): pl.pallas_call(functools.partial(fused_kernel, tuple(spreads), bool(atten...]
    unnamed x58 -> x54, local copies, waits for them, and re-layouts: 9.28 us -> 10.5 us
  transfers between devices with their start and end apart: 9 -> 9, of which waited for: 1 -> 1; matrix products, arithmetic and copies ran while one was open for 12% -> 12% of each run, Pallas kernels for 50% -> 42%
where the time goes in v10:
time: 252 us; the launch traced here: 250 us
  Pallas kernels  179 us (71%)
  local copies, waits for them, and re-layouts  23.1 us (9%)
  other arithmetic  20.3 us (8%)
  matrix products  17.7 us (7%)
  starting transfers between devices  8.33 us (3%)
    pallas_call x6, Pallas kernels, fused_step(): pl.pallas_call(functools.partial(fused_kernel, tuple(spreads), bool(atten...  179 us
    unnamed x54, local copies, waits for them, and re-layouts  10.5 us
    ppermute x9, starting transfers between devices, swap_cores(): return lax.ppermute(value, 'pipe', [(0, 1), (1, 0)])  8.33 us
    dot_general x4, matrix products, attach(): jnp.dot(fetched, weight_in[:, model_width:], preferred_element_type=jnp.f...  5.69 us
  transfers between devices with their start and end apart: 9, of which 1 were waited for; matrix products, arithmetic and copies ran while one was open for 12% of the time, Pallas kernels for 42%

profile of v10, /device:TPU:15, one launch (start us, length us, event | category | flops | bytes accessed | tf_op | source)
XLA Modules:
  0.0 250.1 jit_solution(1800294714270277957)
XLA Ops:
  0.0 0.8 reshape_squeeze.9
  1.0 0.7 collective-permute-start.3
  1.8 1.1 dynamic-slice_bitcast_fusion
  2.9 0.5 collective-permute-start
  4.0 0.7 fusion.137
  4.7 0.7 fusion.135
  5.4 0.7 fusion.103
  6.1 0.6 fusion.102
  6.8 0.6 fusion.104
  7.5 0.7 fusion.105
  8.3 0.6 fusion.99
  8.9 0.7 fusion.98
  9.7 0.6 fusion.100
  10.4 0.6 fusion.101
  11.1 0.7 broadcast_select_fusion.15
  13.1 20.0 %shard_map.64 = bf16[4,256,512]{2,1,0:T(8,128)(2,1)S(1)} custom-call(bf16[256,512]{1,0:T(8,128)(2,1)S(1)} %get-tuple-element.87.refs_0_), custom_call_target="tpu_custom_call" | custom-call | bytes 1048577 | tf_op jit(solution)/shard_map/pallas_call | solution.py:226
  33.1 0.6 gather_fusion
  34.1 0.7 copy-done.24
  35.4 0.7 copy-done.20
  36.1 1.6 broadcast_select_fusion.1
  37.8 0.6 convolution_convert_fusion.3
  38.4 0.6 convolution_convert_fusion.2
  39.0 0.7 copy-done.12
  39.7 0.6 convolution_convert_fusion
  40.6 0.6 convolution_convert_fusion.1
  41.5 0.9 copy-done.15
  43.0 39.9 %shard_map.65 = (f32[256,512]{1,0:T(8,128)S(1)}, f32[512,512]{1,0:T(8,128)S(1)}, f32[512,512]{1,0:T(8,128)S(1)}, bf16[4,256,512]{2,1,0:T(8,128)(2,1)S(1)}, bf16[...) custom-call(bf16[256,512]{1,0:T(8,128)(2,1)S(1)} %slice.241.refs_0_, ...), custom_call_target="tpu_custom_call" | custom-call | flops 5368709120 | bytes 3145729 | tf_op jit(solution)/shard_map/pallas_call | solution.py:226
  83.0 1.3 fusion.32
  84.2 0.6 gather_fusion.1
  84.9 1.7 convolution_convert_fusion.6
  86.6 1.1 fusion.134
  88.3 1.2 fusion.7.refs_4_
  89.6 33.5 %shard_map.66 = (f32[256,512]{1,0:T(8,128)S(1)}, f32[512,512]{1,0:T(8,128)S(1)}, f32[512,512]{1,0:T(8,128)S(1)}, bf16[4,256,512]{2,1,0:T(8,128)(2,1)S(1)}) custom-call(bf16[256,512]{1,0:T(8,128)(2,1)S(1)} %slice.250.refs_0_, bf16[512,512]{1,0:T(8,128)(2,1)S(1)} %get-tuple-element.79.refs_1_, bf16[512,512]{1,0:T(8,128)(2,1)S(1)} %get-tuple-element.78.refs_2_, ...), custom_call_target="tpu_custom_call" | custom-call | flops 5368709120 | bytes 4194305 | tf_op jit(solution)/shard_map/pallas_call | solution.py:226
  123.2 1.6 copy-done.4
  124.9 1.3 fusion.30
  126.2 1.8 gather_fusion.2
  128.1 1.8 convolution_convert_fusion.5
  130.1 0.7 fusion.124
  130.9 1.3 fusion.47
  132.2 5.9 %collective-permute-start.6 = (bf16[256,512]{1,0:T(8,128)(2,1)S(1)}, bf16[256,512]{1,0:T(8,128)(2,1)}, u32[]{:S(2)}, u32[]{:S(2)}) collective-permute-start(bf16[256,512]{1,0:T(8,128)(2,1)S(1)} %fusion.47), channel_id=1, source_target_pairs={{0,64},{64,0},{1,65},{65,1},{2,66},{66,2},{3,67},{67,3},{4,68},{68... | collective-permute-start | bytes 786440 | tf_op jit(solution)/shard_map/ppermute | solution.py:248
  138.7 1.2 fusion.5.refs_4_
  140.0 1.4 convolution_convert_fusion.9.refs_3_
  141.3 31.0 %shard_map.67 = (f32[256,512]{1,0:T(8,128)S(1)}, f32[512,512]{1,0:T(8,128)S(1)}, f32[512,512]{1,0:T(8,128)S(1)}, bf16[4,256,512]{2,1,0:T(8,128)(2,1)S(1)}) custom-call(bf16[256,512]{1,0:T(8,128)(2,1)S(1)} %slice.257.refs_0_, bf16[512,512]{1,0:T(8,128)(2,1)S(1)} %get-tuple-element.81.refs_1_, bf16[512,512]{1,0:T(8,128)(2,1)S(1)} %get-tuple-element.80.refs_2_, ...), custom_call_target="tpu_custom_call" | custom-call | flops 5368709120 | bytes 4194305 | tf_op jit(solution)/shard_map/pallas_call | solution.py:226
  172.6 1.3 copy-done.1
  173.8 0.5 fusion.26
  174.3 0.5 copy-done.18
  174.8 1.8 gather_fusion.3
  176.7 1.7 convolution_convert_fusion.4
  178.7 1.2 copy-done.6
  180.0 0.7 fusion.123
  181.1 1.2 fusion.60
  182.8 1.2 fusion.3.refs_4_
  184.1 1.4 convolution_convert_fusion.8.refs_3_
  185.5 32.5 %shard_map.68 = (f32[256,512]{1,0:T(8,128)S(1)}, f32[512,512]{1,0:T(8,128)S(1)}, f32[512,512]{1,0:T(8,128)S(1)}, bf16[4,256,512]{2,1,0:T(8,128)(2,1)S(1)}) custom-call(bf16[256,512]{1,0:T(8,128)(2,1)S(1)} %slice.266.refs_0_, bf16[512,512]{1,0:T(8,128)(2,1)S(1)} %get-tuple-element.77.refs_1_, bf16[512,512]{1,0:T(8,128)(2,1)S(1)} %get-tuple-element.76.refs_2_, ...), custom_call_target="tpu_custom_call" | custom-call | flops 5368709120 | bytes 4194305 | tf_op jit(solution)/shard_map/pallas_call | solution.py:226
  218.1 1.3 copy-done.2
  219.8 0.5 copy-done.19
  221.6 21.8 %shard_map.69 = bf16[4,256,512]{2,1,0:T(8,128)(2,1)S(1)} custom-call(bf16[4,256,512]{2,1,0:T(8,128)(2,1)S(1)} %fusion.1.refs_0_), custom_call_target="tpu_custom_call" | custom-call | bytes 4194305 | tf_op jit(solution)/shard_map/pallas_call | solution.py:226
  243.6 0.6 fusion.8
  244.7 0.8 fusion.122
  245.6 0.7 select_bitcast_fusion.3
  246.3 0.5 collective-permute-start.8
  246.9 0.9 collective-permute-done.5
  247.9 1.0 select_bitcast_fusion.1
  249.0 1.1 pad_maximum_fusion
  (157 shorter events, 11.2 us)
Async XLA Ops:
  0.0 11.8 %copy-start.21 = (bf16[1,4,256,512]{3,2,1,0:T(8,128)(2,1)S(1)}, bf16[1,4,256,512]{3,2,1,0:T(8,128)(2,1)}, u32[]{:S(2)}) copy-start(bf16[1,4,256,512]{3,2,1,0:T(8,128)(2,1)} %param.8) | copy-start | bytes 3145732
  1.0 3.0 %collective-permute-start.3 = (s32[2,2]{1,0:T(2,128)S(1)}, s32[2,2]{1,0:T(2,128)S(1)}, u32[]{:S(2)}, u32[]{:S(2)}) collective-permute-start(s32[2,2]{1,0:T(2,128)S(1)} %bitcast.350), channel_id=1, source_target_pairs={{0,64},{64,0},{1,65},{65,1},{2,66},{66,2},{3,67},{67,3},{4,68},{68... | collective-permute-start | bytes 56 | tf_op jit(solution)/shard_map/ppermute | solution.py:248
  1.7 9.4 %collective-permute-start.1 = (f32[512]{0:T(512)}, f32[512]{0:T(512)S(1)}, u32[]{:S(2)}, u32[]{:S(2)}) collective-permute-start(f32[512]{0:T(512)} %bitcast.348), channel_id=1, source_target_pairs={{0,64},{64,0},{1,65},{65,1},{2,66},{66,2},{3,67},{67,3},{4,68},{68... | collective-permute-start | bytes 6152 | tf_op jit(solution)/shard_map/ppermute | solution.py:248
  2.9 8.9 %collective-permute-start = (bf16[2,256,512]{2,1,0:T(8,128)(2,1)S(1)}, bf16[2,256,512]{2,1,0:T(8,128)(2,1)S(1)}, u32[]{:S(2)}, u32[]{:S(2)}) collective-permute-start(bf16[2,256,512]{2,1,0:T(8,128)(2,1)S(1)} %dynamic-slice_bitcast_fusion), channel_id=1, source_target_pairs={{0,64},{64,0},{1,65},{65,1},{2,66},{66,2},{3,67},{67,3},{4,68},{68... | collective-permute-start | bytes 1572872 | tf_op jit(solution)/shard_map/ppermute | solution.py:248
  3.4 30.7 %collective-permute-start.4 = (bf16[512,512]{1,0:T(8,128)(2,1)}, bf16[512,512]{1,0:T(8,128)(2,1)}, u32[]{:S(2)}, u32[]{:S(2)}) collective-permute-start(bf16[512,512]{1,0:T(8,128)(2,1)} %bitcast.351), channel_id=1, source_target_pairs={{0,64},{64,0},{1,65},{65,1},{2,66},{66,2},{3,67},{67,3},{4,68},{68... | collective-permute-start | bytes 1572872 | tf_op jit(solution)/shard_map/ppermute | solution.py:248
  3.5 32.0 %collective-permute-start.2 = (bf16[512,1536]{1,0:T(8,128)(2,1)}, bf16[512,1536]{1,0:T(8,128)(2,1)}, u32[]{:S(2)}, u32[]{:S(2)}) collective-permute-start(bf16[512,1536]{1,0:T(8,128)(2,1)} %bitcast.335), channel_id=1, source_target_pairs={{0,64},{64,0},{1,65},{65,1},{2,66},{66,2},{3,67},{67,3},{4,68},{68... | collective-permute-start | bytes 4718600 | tf_op jit(solution)/shard_map/ppermute | solution.py:248
  11.9 1.2 copy-start.7
  11.9 21.9 %copy-start.10 = (bf16[2,256,512]{2,1,0:T(8,128)(2,1)}, bf16[2,256,512]{2,1,0:T(8,128)(2,1)S(1)}, u32[]{:S(2)}) copy-start(bf16[2,256,512]{2,1,0:T(8,128)(2,1)S(1)} %get-tuple-element.73) | copy-start | bytes 1572868
  13.1 21.0 %copy-start.23 = (bf16[4,256,512]{2,1,0:T(8,128)(2,1)S(1)}, bf16[4,256,512]{2,1,0:T(8,128)(2,1)}, u32[]{:S(2)}) copy-start(bf16[4,256,512]{2,1,0:T(8,128)(2,1)} %param.13) | copy-start | bytes 3145732
  33.7 1.0 copy-start.24
  34.7 1.4 copy-start.20
  37.8 2.8 %copy-start = (bf16[512,1536]{1,0:T(8,128)(2,1)}, bf16[512,1536]{1,0:T(8,128)(2,1)S(1)}, u32[]{:S(2)}) copy-start(bf16[512,1536]{1,0:T(8,128)(2,1)S(1)} %get-tuple-element.71) | copy-start | bytes 4718596
  37.8 45.2 %copy-start.3 = (bf16[512,1536]{1,0:T(8,128)(2,1)}, bf16[512,1536]{1,0:T(8,128)(2,1)S(1)}, u32[]{:S(2)}) copy-start(bf16[512,1536]{1,0:T(8,128)(2,1)S(1)} %get-tuple-element.70) | copy-start | bytes 4718596
  38.3 1.3 copy-start.12
  39.7 0.9 copy-start.13
  40.6 0.9 copy-start.14
  41.5 0.9 copy-start.15
  41.5 1.4 slice-start
  83.0 1.3 copy-start.16
  84.9 2.8 %slice-start.1 = ((bf16[256,1536]{1,0:T(8,128)(2,1)}), bf16[256,1024]{1,0:T(8,128)(2,1)S(1)}, s32[]{:S(2)}) async-start(bf16[256,1536]{1,0:T(8,128)(2,1)} %copy-done.13), calls=%async_computation.1 | async-start | bytes 1048576 | tf_op jit(solution)/shard_map/slice | solution.py:270
  123.1 1.8 copy-start.4
  123.2 2.9 %copy-start.17 = (bf16[512,1024]{1,0:T(8,128)(2,1)}, bf16[512,1024]{1,0:T(8,128)(2,1)S(1)}, u32[]{:S(2)}) copy-start(bf16[512,1024]{1,0:T(8,128)(2,1)S(1)} %maximum_convert_fusion.1) | copy-start | bytes 3145732
  128.1 2.0 copy-start.5
  128.1 2.0 copy-start.8
  128.1 2.0 slice-start.4
  130.8 7.2 %copy-start.22 = (f32[256,512]{1,0:T(8,128)S(1)}, f32[256,512]{1,0:T(8,128)}, u32[]{:S(2)}) copy-start(f32[256,512]{1,0:T(8,128)} %fusion.30) | copy-start | bytes 1572868
  130.8 7.2 %slice-start.3 = ((bf16[256,1536]{1,0:T(8,128)(2,1)}), bf16[256,1024]{1,0:T(8,128)(2,1)S(1)}, s32[]{:S(2)}) async-start(bf16[256,1536]{1,0:T(8,128)(2,1)} %copy-done.15), calls=%async_computation.3 | async-start | bytes 1048576 | tf_op jit(solution)/shard_map/slice | solution.py:270
  132.2 114.8 %collective-permute-start.6 = (bf16[256,512]{1,0:T(8,128)(2,1)S(1)}, bf16[256,512]{1,0:T(8,128)(2,1)}, u32[]{:S(2)}, u32[]{:S(2)}) collective-permute-start(bf16[256,512]{1,0:T(8,128)(2,1)S(1)} %fusion.47), channel_id=1, source_target_pairs={{0,64},{64,0},{1,65},{65,1},{2,66},{66,2},{3,67},{67,3},{4,68},{68... | collective-permute-start | bytes 786440 | tf_op jit(solution)/shard_map/ppermute | solution.py:248
  138.7 1.3 copy-start.25
  172.4 1.4 copy-start.1
  173.8 1.0 copy-start.18
  176.7 2.0 slice-start.5
  178.5 1.4 copy-start.6
  178.5 1.5 copy-start.9
  180.0 1.0 slice-start.2
  182.8 1.3 copy-start.26
  218.0 1.4 copy-start.2
  219.4 1.0 copy-start.19
  221.6 21.9 %slice-start.7 = ((bf16[512,1024]{1,0:T(8,128)(2,1)}), bf16[256,1024]{1,0:T(8,128)(2,1)S(1)}, s32[]{:S(2)}) async-start(bf16[512,1024]{1,0:T(8,128)(2,1)} %copy-done.19), calls=%async_computation.7 | async-start | bytes 1048576 | tf_op jit(solution)/shard_map/slice | solution.py:299
  243.5 1.0 copy-start.11
  243.5 1.2 slice-start.6
  246.3 1.6 collective-permute-start.5
  246.3 2.5 %collective-permute-start.8 = (bf16[256,512]{1,0:T(8,128)(2,1)S(1)}, bf16[256,512]{1,0:T(8,128)(2,1)S(1)}, u32[]{:S(2)}, u32[]{:S(2)}) collective-permute-start(bf16[256,512]{1,0:T(8,128)(2,1)S(1)} %fusion.60), channel_id=1, source_target_pairs={{0,64},{64,0},{1,65},{65,1},{2,66},{66,2},{3,67},{67,3},{4,68},{68... | collective-permute-start | bytes 786440 | tf_op jit(solution)/shard_map/ppermute | solution.py:248
  246.8 2.0 collective-permute-start.7

commit v11 on v10

--- a/solution.py
+++ b/solution.py
@@ -68,7 +68,7 @@
             scores = lax.dot_general(qm, k, nt, preferred_element_type=jnp.float32) * factor
             top = jnp.max(scores, axis=-1, keepdims=True)
             exps = jnp.exp(scores - top)
-            attention = exps / jnp.sum(exps, axis=-1, keepdims=True)
+            attention = exps * (1.0 / jnp.sum(exps, axis=-1, keepdims=True))
             grad_probs = lax.dot_general(gm, v, nt, preferred_element_type=jnp.float32)
             row = jnp.sum(attention * grad_probs, axis=-1, keepdims=True)
             grad_scores = (attention * (grad_probs - row) * factor).astype(jnp.bfloat16)

time: 252 us -> 252 us (level)
  no operation moved by 1% of the time
where the time goes in v11:
time: 252 us; the launch traced here: 250 us
  Pallas kernels  179 us (71%)
  local copies, waits for them, and re-layouts  23.1 us (9%)
  other arithmetic  20.3 us (8%)
  matrix products  17.7 us (7%)
  starting transfers between devices  8.33 us (3%)
    pallas_call x6, Pallas kernels, fused_step(): pl.pallas_call(functools.partial(fused_kernel, tuple(spreads), bool(atten...  179 us
    unnamed x54, local copies, waits for them, and re-layouts  10.5 us
    ppermute x9, starting transfers between devices, swap_cores(): return lax.ppermute(value, 'pipe', [(0, 1), (1, 0)])  8.33 us
    dot_general x4, matrix products, attach(): jnp.dot(fetched, weight_in[:, model_width:], preferred_element_type=jnp.f...  5.69 us
  transfers between devices with their start and end apart: 9, of which 1 were waited for; matrix products, arithmetic and copies ran while one was open for 12% of the time, Pallas kernels for 42%

profile of v11, /device:TPU:15, one launch (start us, length us, event | category | flops | bytes accessed | tf_op | source)
XLA Modules:
  0.0 250.1 jit_solution(1800294714270277957)
XLA Ops:
  0.0 0.8 reshape_squeeze.9
  1.0 0.7 collective-permute-start.3
  1.8 1.1 dynamic-slice_bitcast_fusion
  2.9 0.5 collective-permute-start
  4.0 0.7 fusion.137
  4.7 0.7 fusion.135
  5.4 0.7 fusion.103
  6.1 0.6 fusion.102
  6.8 0.6 fusion.104
  7.5 0.7 fusion.105
  8.3 0.6 fusion.99
  8.9 0.7 fusion.98
  9.7 0.6 fusion.100
  10.4 0.6 fusion.101
  11.1 0.7 broadcast_select_fusion.15
  13.1 20.0 %shard_map.64 = bf16[4,256,512]{2,1,0:T(8,128)(2,1)S(1)} custom-call(bf16[256,512]{1,0:T(8,128)(2,1)S(1)} %get-tuple-element.87.refs_0_), custom_call_target="tpu_custom_call" | custom-call | bytes 1048577 | tf_op jit(solution)/shard_map/pallas_call | solution.py:226
  33.1 0.6 gather_fusion
  34.1 0.7 copy-done.24
  35.4 0.7 copy-done.20
  36.1 1.6 broadcast_select_fusion.1
  37.8 0.6 convolution_convert_fusion.3
  38.4 0.6 convolution_convert_fusion.2
  39.0 0.7 copy-done.12
  39.7 0.6 convolution_convert_fusion
  40.6 0.6 convolution_convert_fusion.1
  41.5 0.9 copy-done.15
  43.0 39.9 %shard_map.65 = (f32[256,512]{1,0:T(8,128)S(1)}, f32[512,512]{1,0:T(8,128)S(1)}, f32[512,512]{1,0:T(8,128)S(1)}, bf16[4,256,512]{2,1,0:T(8,128)(2,1)S(1)}, bf16[...) custom-call(bf16[256,512]{1,0:T(8,128)(2,1)S(1)} %slice.241.refs_0_, ...), custom_call_target="tpu_custom_call" | custom-call | flops 5368709120 | bytes 3145729 | tf_op jit(solution)/shard_map/pallas_call | solution.py:226
  83.0 1.3 fusion.32
  84.2 0.6 gather_fusion.1
  84.9 1.7 convolution_convert_fusion.6
  86.6 1.1 fusion.134
  88.3 1.2 fusion.7.refs_4_
  89.6 33.5 %shard_map.66 = (f32[256,512]{1,0:T(8,128)S(1)}, f32[512,512]{1,0:T(8,128)S(1)}, f32[512,512]{1,0:T(8,128)S(1)}, bf16[4,256,512]{2,1,0:T(8,128)(2,1)S(1)}) custom-call(bf16[256,512]{1,0:T(8,128)(2,1)S(1)} %slice.250.refs_0_, bf16[512,512]{1,0:T(8,128)(2,1)S(1)} %get-tuple-element.79.refs_1_, bf16[512,512]{1,0:T(8,128)(2,1)S(1)} %get-tuple-element.78.refs_2_, ...), custom_call_target="tpu_custom_call" | custom-call | flops 5368709120 | bytes 4194305 | tf_op jit(solution)/shard_map/pallas_call | solution.py:226
  123.2 1.6 copy-done.4
  124.9 1.3 fusion.30
  126.2 1.8 gather_fusion.2
  128.1 1.8 convolution_convert_fusion.5
  130.1 0.7 fusion.124
  130.9 1.3 fusion.47
  132.2 5.9 %collective-permute-start.6 = (bf16[256,512]{1,0:T(8,128)(2,1)S(1)}, bf16[256,512]{1,0:T(8,128)(2,1)}, u32[]{:S(2)}, u32[]{:S(2)}) collective-permute-start(bf16[256,512]{1,0:T(8,128)(2,1)S(1)} %fusion.47), channel_id=1, source_target_pairs={{0,64},{64,0},{1,65},{65,1},{2,66},{66,2},{3,67},{67,3},{4,68},{68... | collective-permute-start | bytes 786440 | tf_op jit(solution)/shard_map/ppermute | solution.py:248
  138.7 1.2 fusion.5.refs_4_
  140.0 1.4 convolution_convert_fusion.9.refs_3_
  141.3 31.0 %shard_map.67 = (f32[256,512]{1,0:T(8,128)S(1)}, f32[512,512]{1,0:T(8,128)S(1)}, f32[512,512]{1,0:T(8,128)S(1)}, bf16[4,256,512]{2,1,0:T(8,128)(2,1)S(1)}) custom-call(bf16[256,512]{1,0:T(8,128)(2,1)S(1)} %slice.257.refs_0_, bf16[512,512]{1,0:T(8,128)(2,1)S(1)} %get-tuple-element.81.refs_1_, bf16[512,512]{1,0:T(8,128)(2,1)S(1)} %get-tuple-element.80.refs_2_, ...), custom_call_target="tpu_custom_call" | custom-call | flops 5368709120 | bytes 4194305 | tf_op jit(solution)/shard_map/pallas_call | solution.py:226
  172.6 1.3 copy-done.1
  173.8 0.5 fusion.26
  174.3 0.5 copy-done.18
  174.8 1.8 gather_fusion.3
  176.7 1.7 convolution_convert_fusion.4
  178.7 1.2 copy-done.6
  180.0 0.7 fusion.123
  181.1 1.2 fusion.60
  182.8 1.2 fusion.3.refs_4_
  184.1 1.4 convolution_convert_fusion.8.refs_3_
  185.5 32.5 %shard_map.68 = (f32[256,512]{1,0:T(8,128)S(1)}, f32[512,512]{1,0:T(8,128)S(1)}, f32[512,512]{1,0:T(8,128)S(1)}, bf16[4,256,512]{2,1,0:T(8,128)(2,1)S(1)}) custom-call(bf16[256,512]{1,0:T(8,128)(2,1)S(1)} %slice.266.refs_0_, bf16[512,512]{1,0:T(8,128)(2,1)S(1)} %get-tuple-element.77.refs_1_, bf16[512,512]{1,0:T(8,128)(2,1)S(1)} %get-tuple-element.76.refs_2_, ...), custom_call_target="tpu_custom_call" | custom-call | flops 5368709120 | bytes 4194305 | tf_op jit(solution)/shard_map/pallas_call | solution.py:226
  218.1 1.3 copy-done.2
  219.8 0.5 copy-done.19
  221.6 21.8 %shard_map.69 = bf16[4,256,512]{2,1,0:T(8,128)(2,1)S(1)} custom-call(bf16[4,256,512]{2,1,0:T(8,128)(2,1)S(1)} %fusion.1.refs_0_), custom_call_target="tpu_custom_call" | custom-call | bytes 4194305 | tf_op jit(solution)/shard_map/pallas_call | solution.py:226
  243.6 0.6 fusion.8
  244.7 0.8 fusion.122
  245.6 0.7 select_bitcast_fusion.3
  246.3 0.5 collective-permute-start.8
  246.9 0.9 collective-permute-done.5
  247.9 1.0 select_bitcast_fusion.1
  249.0 1.1 pad_maximum_fusion
  (157 shorter events, 11.2 us)
Async XLA Ops:
  0.0 11.8 %copy-start.21 = (bf16[1,4,256,512]{3,2,1,0:T(8,128)(2,1)S(1)}, bf16[1,4,256,512]{3,2,1,0:T(8,128)(2,1)}, u32[]{:S(2)}) copy-start(bf16[1,4,256,512]{3,2,1,0:T(8,128)(2,1)} %param.8) | copy-start | bytes 3145732
  1.0 3.0 %collective-permute-start.3 = (s32[2,2]{1,0:T(2,128)S(1)}, s32[2,2]{1,0:T(2,128)S(1)}, u32[]{:S(2)}, u32[]{:S(2)}) collective-permute-start(s32[2,2]{1,0:T(2,128)S(1)} %bitcast.350), channel_id=1, source_target_pairs={{0,64},{64,0},{1,65},{65,1},{2,66},{66,2},{3,67},{67,3},{4,68},{68... | collective-permute-start | bytes 56 | tf_op jit(solution)/shard_map/ppermute | solution.py:248
  1.7 9.4 %collective-permute-start.1 = (f32[512]{0:T(512)}, f32[512]{0:T(512)S(1)}, u32[]{:S(2)}, u32[]{:S(2)}) collective-permute-start(f32[512]{0:T(512)} %bitcast.348), channel_id=1, source_target_pairs={{0,64},{64,0},{1,65},{65,1},{2,66},{66,2},{3,67},{67,3},{4,68},{68... | collective-permute-start | bytes 6152 | tf_op jit(solution)/shard_map/ppermute | solution.py:248
  2.9 8.9 %collective-permute-start = (bf16[2,256,512]{2,1,0:T(8,128)(2,1)S(1)}, bf16[2,256,512]{2,1,0:T(8,128)(2,1)S(1)}, u32[]{:S(2)}, u32[]{:S(2)}) collective-permute-start(bf16[2,256,512]{2,1,0:T(8,128)(2,1)S(1)} %dynamic-slice_bitcast_fusion), channel_id=1, source_target_pairs={{0,64},{64,0},{1,65},{65,1},{2,66},{66,2},{3,67},{67,3},{4,68},{68... | collective-permute-start | bytes 1572872 | tf_op jit(solution)/shard_map/ppermute | solution.py:248
  3.4 30.7 %collective-permute-start.4 = (bf16[512,512]{1,0:T(8,128)(2,1)}, bf16[512,512]{1,0:T(8,128)(2,1)}, u32[]{:S(2)}, u32[]{:S(2)}) collective-permute-start(bf16[512,512]{1,0:T(8,128)(2,1)} %bitcast.351), channel_id=1, source_target_pairs={{0,64},{64,0},{1,65},{65,1},{2,66},{66,2},{3,67},{67,3},{4,68},{68... | collective-permute-start | bytes 1572872 | tf_op jit(solution)/shard_map/ppermute | solution.py:248
  3.5 32.0 %collective-permute-start.2 = (bf16[512,1536]{1,0:T(8,128)(2,1)}, bf16[512,1536]{1,0:T(8,128)(2,1)}, u32[]{:S(2)}, u32[]{:S(2)}) collective-permute-start(bf16[512,1536]{1,0:T(8,128)(2,1)} %bitcast.335), channel_id=1, source_target_pairs={{0,64},{64,0},{1,65},{65,1},{2,66},{66,2},{3,67},{67,3},{4,68},{68... | collective-permute-start | bytes 4718600 | tf_op jit(solution)/shard_map/ppermute | solution.py:248
  11.9 1.2 copy-start.7
  11.9 21.9 %copy-start.10 = (bf16[2,256,512]{2,1,0:T(8,128)(2,1)}, bf16[2,256,512]{2,1,0:T(8,128)(2,1)S(1)}, u32[]{:S(2)}) copy-start(bf16[2,256,512]{2,1,0:T(8,128)(2,1)S(1)} %get-tuple-element.73) | copy-start | bytes 1572868
  13.1 21.0 %copy-start.23 = (bf16[4,256,512]{2,1,0:T(8,128)(2,1)S(1)}, bf16[4,256,512]{2,1,0:T(8,128)(2,1)}, u32[]{:S(2)}) copy-start(bf16[4,256,512]{2,1,0:T(8,128)(2,1)} %param.13) | copy-start | bytes 3145732
  33.7 1.0 copy-start.24
  34.7 1.4 copy-start.20
  37.8 2.8 %copy-start = (bf16[512,1536]{1,0:T(8,128)(2,1)}, bf16[512,1536]{1,0:T(8,128)(2,1)S(1)}, u32[]{:S(2)}) copy-start(bf16[512,1536]{1,0:T(8,128)(2,1)S(1)} %get-tuple-element.71) | copy-start | bytes 4718596
  37.8 45.2 %copy-start.3 = (bf16[512,1536]{1,0:T(8,128)(2,1)}, bf16[512,1536]{1,0:T(8,128)(2,1)S(1)}, u32[]{:S(2)}) copy-start(bf16[512,1536]{1,0:T(8,128)(2,1)S(1)} %get-tuple-element.70) | copy-start | bytes 4718596
  38.3 1.3 copy-start.12
  39.7 0.9 copy-start.13
  40.6 0.9 copy-start.14
  41.5 0.9 copy-start.15
  41.5 1.4 slice-start
  83.0 1.3 copy-start.16
  84.9 2.8 %slice-start.1 = ((bf16[256,1536]{1,0:T(8,128)(2,1)}), bf16[256,1024]{1,0:T(8,128)(2,1)S(1)}, s32[]{:S(2)}) async-start(bf16[256,1536]{1,0:T(8,128)(2,1)} %copy-done.13), calls=%async_computation.1 | async-start | bytes 1048576 | tf_op jit(solution)/shard_map/slice | solution.py:270
  123.1 1.8 copy-start.4
  123.2 2.9 %copy-start.17 = (bf16[512,1024]{1,0:T(8,128)(2,1)}, bf16[512,1024]{1,0:T(8,128)(2,1)S(1)}, u32[]{:S(2)}) copy-start(bf16[512,1024]{1,0:T(8,128)(2,1)S(1)} %maximum_convert_fusion.1) | copy-start | bytes 3145732
  128.1 2.0 copy-start.5
  128.1 2.0 copy-start.8
  128.1 2.0 slice-start.4
  130.8 7.2 %copy-start.22 = (f32[256,512]{1,0:T(8,128)S(1)}, f32[256,512]{1,0:T(8,128)}, u32[]{:S(2)}) copy-start(f32[256,512]{1,0:T(8,128)} %fusion.30) | copy-start | bytes 1572868
  130.8 7.2 %slice-start.3 = ((bf16[256,1536]{1,0:T(8,128)(2,1)}), bf16[256,1024]{1,0:T(8,128)(2,1)S(1)}, s32[]{:S(2)}) async-start(bf16[256,1536]{1,0:T(8,128)(2,1)} %copy-done.15), calls=%async_computation.3 | async-start | bytes 1048576 | tf_op jit(solution)/shard_map/slice | solution.py:270
  132.2 114.8 %collective-permute-start.6 = (bf16[256,512]{1,0:T(8,128)(2,1)S(1)}, bf16[256,512]{1,0:T(8,128)(2,1)}, u32[]{:S(2)}, u32[]{:S(2)}) collective-permute-start(bf16[256,512]{1,0:T(8,128)(2,1)S(1)} %fusion.47), channel_id=1, source_target_pairs={{0,64},{64,0},{1,65},{65,1},{2,66},{66,2},{3,67},{67,3},{4,68},{68... | collective-permute-start | bytes 786440 | tf_op jit(solution)/shard_map/ppermute | solution.py:248
  138.7 1.3 copy-start.25
  172.4 1.4 copy-start.1
  173.8 1.0 copy-start.18
  176.7 2.0 slice-start.5
  178.5 1.4 copy-start.6
  178.5 1.5 copy-start.9
  180.0 1.0 slice-start.2
  182.8 1.3 copy-start.26
  218.0 1.4 copy-start.2
  219.4 1.0 copy-start.19
  221.6 21.9 %slice-start.7 = ((bf16[512,1024]{1,0:T(8,128)(2,1)}), bf16[256,1024]{1,0:T(8,128)(2,1)S(1)}, s32[]{:S(2)}) async-start(bf16[512,1024]{1,0:T(8,128)(2,1)} %copy-done.19), calls=%async_computation.7 | async-start | bytes 1048576 | tf_op jit(solution)/shard_map/slice | solution.py:299
  243.5 1.0 copy-start.11
  243.5 1.2 slice-start.6
  246.3 1.6 collective-permute-start.5
  246.3 2.5 %collective-permute-start.8 = (bf16[256,512]{1,0:T(8,128)(2,1)S(1)}, bf16[256,512]{1,0:T(8,128)(2,1)S(1)}, u32[]{:S(2)}, u32[]{:S(2)}) collective-permute-start(bf16[256,512]{1,0:T(8,128)(2,1)S(1)} %fusion.60), channel_id=1, source_target_pairs={{0,64},{64,0},{1,65},{65,1},{2,66},{66,2},{3,67},{67,3},{4,68},{68... | collective-permute-start | bytes 786440 | tf_op jit(solution)/shard_map/ppermute | solution.py:248
  246.8 2.0 collective-permute-start.7
